TPU v7x, 256 devices: a whole 4x4x8 slice. The times are simulated.
256 devices in a mesh: cells: 64 (over y, z, core), rank: 4 (over x).
Axes of the slice: x: 4, y: 4, z: 8, core: 2. Of those that a mesh axis runs over, the one named last changes fastest.
Arguments:
- x_emb: bfloat16 [32768, 256], P('cells'), may hold values from -40 to 40, as said below
- y_emb: bfloat16 [32768, 256], P('cells'), may hold values from -40 to 40, as said below
- q_factor: float32 [32768, 512], P('cells', 'rank'), may hold values from 0 to 45, as said below
- r_factor: float32 [32768, 512], P('cells', 'rank'), may hold values from 0 to 45, as said below
- g_weights: float32 [512], P('rank'), may hold values from 16384 to 65536
- a_mass: float32 [32768], P('cells'), may hold values from 128 to 512
- b_mass: float32 [32768], P('cells'), may hold values from 128 to 512
- expr: bfloat16 [32768, 2048], P('cells', 'rank'), may hold values from -9 to 9, as said below
Outputs:
- q_new: float32 [32768, 512], P('cells', 'rank')
- r_new: float32 [32768, 512], P('cells', 'rank')
- rank_share: float32 [512], P('rank')
- predicted: bfloat16 [32768, 2048], P('cells', 'rank')
Inputs may be any that keep to these rules, and one draw needn't show every extreme that they name: `x_emb`: finite embedding values. `y_emb`: finite embedding values. `q_factor`: every entry is positive. `r_factor`: every entry is positive. `expr`: finite expression values.
All inputs are finite; a program needn't handle non-finite values. Where the computation divides by a largest or mean magnitude, that divisor is 1e-20 or more.
Results may differ from a plain program's by a relative error of at most 0.0075.
Values may be sent and summed in bfloat16 or wider, within the bound.
No kernel may reach another device: no remote copies, remote signals or barrier semaphores. Data moves between devices by JAX's collectives and lax.ppermute only.
A program may use at most 64 MiB of HBM per device.

v0:
```python
import jax
import jax.numpy as jnp
from jax import lax
from jax.sharding import PartitionSpec as P

PASSES = 10


SCALE = 0.0625
GAMMA = 10.0
POWER = 0.8


def contract_rows(left, right):
    return lax.dot_general(
        left, right, (((0,), (0,)), ((), ())), preferred_element_type=jnp.float32
    )


def marginal_passes(kern_q, kern_r, kern_g, a_mass, b_mass, rows_total, columns_total):
    width = kern_q.shape[1]
    count = kern_q.shape[0]

    def one_pass(step, carry):
        v_q, v_r, weights, u_q, u_r = carry
        s_q, s_r = rows_total(
            jnp.sum(kern_q * v_q[None, :], axis=1), jnp.sum(kern_r * v_r[None, :], axis=1)
        )
        u_q = (a_mass / s_q) ** POWER
        u_r = (b_mass / s_r) ** POWER
        t_q, t_r = columns_total(
            jnp.sum(kern_q * u_q[:, None], axis=0), jnp.sum(kern_r * u_r[:, None], axis=0)
        )
        weights = jnp.exp((jnp.log(kern_g) + jnp.log(v_q * t_q) + jnp.log(v_r * t_r)) / 3.0)
        return (weights / t_q, weights / t_r, weights, u_q, u_r)

    start = (
        jnp.ones((width,), jnp.float32),
        jnp.ones((width,), jnp.float32),
        kern_g,
        jnp.ones((count,), jnp.float32),
        jnp.ones((count,), jnp.float32),
    )
    return lax.fori_loop(0, PASSES, one_pass, start)


def shards(x_emb, y_emb, q_factor, r_factor, g_weights, a_mass, b_mass, expr):
    local_rows = q_factor.shape[0]
    cells_total = local_rows * lax.axis_size("cells")
    norms_one = jnp.sum(jnp.square(x_emb.astype(jnp.float32)), axis=1)
    norms_two = jnp.sum(jnp.square(y_emb.astype(jnp.float32)), axis=1)
    q_round = q_factor.astype(jnp.bfloat16)
    r_round = r_factor.astype(jnp.bfloat16)
    cross_xq, cross_yr, xq_vec, cq_vec, yr_vec, cr_vec = lax.psum(
        (
            contract_rows(x_emb, q_round),
            contract_rows(y_emb, r_round),
            jnp.sum(norms_one[:, None] * q_factor, axis=0),
            jnp.sum(q_factor, axis=0),
            jnp.sum(norms_two[:, None] * r_factor, axis=0),
            jnp.sum(r_factor, axis=0),
        ),
        "cells",
    )
    grad_q = (
        SCALE
        * (
            norms_one[:, None] * cr_vec[None, :]
            + yr_vec[None, :]
            - 2.0
            * jnp.dot(x_emb, cross_yr.astype(jnp.bfloat16), preferred_element_type=jnp.float32)
        )
        / g_weights[None, :]
    )
    grad_r = (
        SCALE
        * (
            norms_two[:, None] * cq_vec[None, :]
            + xq_vec[None, :]
            - 2.0
            * jnp.dot(y_emb, cross_xq.astype(jnp.bfloat16), preferred_element_type=jnp.float32)
        )
        / g_weights[None, :]
    )
    curvature = SCALE * (
        xq_vec * cr_vec + cq_vec * yr_vec - 2.0 * jnp.sum(cross_xq * cross_yr, axis=0)
    )
    grad_g = -curvature / jnp.square(g_weights)
    local_peak = jnp.maximum(
        jnp.max(jnp.abs(grad_q)), jnp.maximum(jnp.max(jnp.abs(grad_r)), jnp.max(jnp.abs(grad_g)))
    )
    peak = lax.pmax(local_peak, ("cells", "rank"))
    eta = GAMMA / (peak + 1e-06)
    kern_q = q_factor * jnp.exp(-eta * grad_q)
    kern_r = r_factor * jnp.exp(-eta * grad_r)
    kern_g = g_weights * jnp.exp(-eta * grad_g)

    def rank_rows(first, second):
        return lax.psum((first, second), "rank")

    def cell_columns(first, second):
        return lax.psum((first, second), "cells")

    v_q, v_r, weights_mine, u_q, u_r = marginal_passes(
        kern_q, kern_r, kern_g, a_mass, b_mass, rank_rows, cell_columns
    )
    q_new = u_q[:, None] * kern_q * v_q[None, :]
    r_new = u_r[:, None] * kern_r * v_r[None, :]
    row_mass = lax.psum(jnp.sum(q_new, axis=1), "rank")
    scaled_mine = (q_new / weights_mine[None, :]).astype(jnp.bfloat16)
    scaled_all, right_all = (
        lax.all_gather(scaled_mine, "rank", axis=1, tiled=True),
        lax.all_gather(r_new.astype(jnp.bfloat16), "rank", axis=1, tiled=True),
    )
    profiles = lax.psum(contract_rows(right_all, expr), "cells")
    mixed = jnp.dot(scaled_all, profiles.astype(jnp.bfloat16), preferred_element_type=jnp.float32)
    predicted = (mixed / row_mass[:, None]).astype(jnp.bfloat16)
    return (q_new, r_new, weights_mine / cells_total, predicted)


def solution(mesh):
    return jax.shard_map(
        shards,
        mesh=mesh,
        in_specs=(
            P("cells", None),
            P("cells", None),
            P("cells", "rank"),
            P("cells", "rank"),
            P("rank"),
            P("cells"),
            P("cells"),
            P("cells", "rank"),
        ),
        out_specs=(P("cells", "rank"), P("cells", "rank"), P("rank"), P("cells", "rank")),
        check_vma=False,
    )
```

profile of v0, /device:TPU:1, one launch (start us, length us, event | category | flops | bytes accessed | tf_op | source)
XLA Modules:
  0.0 1915.9 jit_solution(8022907149497716227)
XLA Ops:
  12.7 128.3 %all-reduce.2 = (f32[128]{0:T(128)S(1)}, f32[128]{0:T(128)S(1)}, f32[128]{0:T(128)S(1)}, f32[128]{0:T(128)S(1)}) all-reduce(f32[128]{0:T(128)S(1)} %get-tuple-element.228, f32[128]{0:T(128)S(1)} %reduce_sum.117, f32[128]{0:T(128)S(1)} %get-tuple-element.227, f32[128]{0:T(128)S(1)} %reduce_sum.120), channel_id=1, replica_groups=mesh['cells'=64,'rank'=4] {'cells'}, use_global_device_ids=true, to_apply=%region_5.0 | all-reduce | flops 512 | bytes 4096 | tf_op jit(solution)/shard_map/psum | solution.py:54
  141.0 50.4 %all-reduce.11.cloned.1.call-done = (f32[256,128]{1,0:T(8,128)}, f32[256,128]{1,0:T(8,128)}) async-done(((f32[256,128]{1,0:T(8,128)}, f32[256,128]{1,0:T(8,128)}), (f32[256,128]{1,0:T(8,128)}, f32[256,128]{1,0:T(8,128)})) %all-reduce.11.cloned.1.call-update) | async-done | bytes 262160 | tf_op jit(solution)/shard_map/psum | solution.py:54
  197.5 74.5 %pmax.7 = f32[]{:T(128)} all-reduce(f32[]{:T(128)S(6)} %max.9), channel_id=1, replica_groups=mesh['cells'=64,'rank'=4] {'cells','rank'}, use_global_device_ids=true, to_apply=%region_16.0 | all-reduce | flops 1 | bytes 8 | tf_op jit(solution)/shard_map/pmax | solution.py:92
  274.2 1348.8 %while.21 = (s32[]{:T(128)}, f32[128]{0:T(128)S(1)}, f32[128]{0:T(128)S(1)}, f32[128]{0:T(128)}, f32[512]{0:T(512)}, /*index=5*/f32[512]{0:T(512)}, f32[512,128]...) while((s32[]{:T(128)}, f32[128]{0:T(128)S(1)}, ...), condition=%wide.region_26.0_spmd.clone, body=%wide.region_17.0_spmd.clone.sunk | while | flops 526723 | bytes 1107165 | solution.py:44
  274.5 7.3 all-reduce.6
  283.0 126.1 %all-reduce.7 = (f32[128]{0:T(128)S(1)}, f32[128]{0:T(128)S(1)}) all-reduce(f32[128]{0:T(128)S(1)} %get-tuple-element.300, f32[128]{0:T(128)S(1)} %get-tuple-element.301), channel_id=1, replica_groups=mesh['cells'=64,'rank'=4] {'cells'}, use_global_device_ids=true, to_apply=%region_25.0 | all-reduce | flops 256 | bytes 2048 | tf_op jit(solution)/shard_map/while/body/eval_jaxpr/psum | solution.py:102
  417.5 126.3 %all-reduce.7 = (f32[128]{0:T(128)S(1)}, f32[128]{0:T(128)S(1)}) all-reduce(f32[128]{0:T(128)S(1)} %get-tuple-element.300, f32[128]{0:T(128)S(1)} %get-tuple-element.301), channel_id=1, replica_groups=mesh['cells'=64,'rank'=4] {'cells'}, use_global_device_ids=true, to_apply=%region_25.0 | all-reduce | flops 256 | bytes 2048 | tf_op jit(solution)/shard_map/while/body/eval_jaxpr/psum | solution.py:102
  544.6 6.8 all-reduce.6
  552.6 126.1 %all-reduce.7 = (f32[128]{0:T(128)S(1)}, f32[128]{0:T(128)S(1)}) all-reduce(f32[128]{0:T(128)S(1)} %get-tuple-element.300, f32[128]{0:T(128)S(1)} %get-tuple-element.301), channel_id=1, replica_groups=mesh['cells'=64,'rank'=4] {'cells'}, use_global_device_ids=true, to_apply=%region_25.0 | all-reduce | flops 256 | bytes 2048 | tf_op jit(solution)/shard_map/while/body/eval_jaxpr/psum | solution.py:102
  679.6 6.6 all-reduce.6
  687.4 126.1 %all-reduce.7 = (f32[128]{0:T(128)S(1)}, f32[128]{0:T(128)S(1)}) all-reduce(f32[128]{0:T(128)S(1)} %get-tuple-element.300, f32[128]{0:T(128)S(1)} %get-tuple-element.301), channel_id=1, replica_groups=mesh['cells'=64,'rank'=4] {'cells'}, use_global_device_ids=true, to_apply=%region_25.0 | all-reduce | flops 256 | bytes 2048 | tf_op jit(solution)/shard_map/while/body/eval_jaxpr/psum | solution.py:102
  814.3 6.8 all-reduce.6
  822.3 126.1 %all-reduce.7 = (f32[128]{0:T(128)S(1)}, f32[128]{0:T(128)S(1)}) all-reduce(f32[128]{0:T(128)S(1)} %get-tuple-element.300, f32[128]{0:T(128)S(1)} %get-tuple-element.301), channel_id=1, replica_groups=mesh['cells'=64,'rank'=4] {'cells'}, use_global_device_ids=true, to_apply=%region_25.0 | all-reduce | flops 256 | bytes 2048 | tf_op jit(solution)/shard_map/while/body/eval_jaxpr/psum | solution.py:102
  957.0 126.1 %all-reduce.7 = (f32[128]{0:T(128)S(1)}, f32[128]{0:T(128)S(1)}) all-reduce(f32[128]{0:T(128)S(1)} %get-tuple-element.300, f32[128]{0:T(128)S(1)} %get-tuple-element.301), channel_id=1, replica_groups=mesh['cells'=64,'rank'=4] {'cells'}, use_global_device_ids=true, to_apply=%region_25.0 | all-reduce | flops 256 | bytes 2048 | tf_op jit(solution)/shard_map/while/body/eval_jaxpr/psum | solution.py:102
  1084.0 6.8 all-reduce.6
  1092.0 126.1 %all-reduce.7 = (f32[128]{0:T(128)S(1)}, f32[128]{0:T(128)S(1)}) all-reduce(f32[128]{0:T(128)S(1)} %get-tuple-element.300, f32[128]{0:T(128)S(1)} %get-tuple-element.301), channel_id=1, replica_groups=mesh['cells'=64,'rank'=4] {'cells'}, use_global_device_ids=true, to_apply=%region_25.0 | all-reduce | flops 256 | bytes 2048 | tf_op jit(solution)/shard_map/while/body/eval_jaxpr/psum | solution.py:102
  1218.9 6.6 all-reduce.6
  1226.7 126.1 %all-reduce.7 = (f32[128]{0:T(128)S(1)}, f32[128]{0:T(128)S(1)}) all-reduce(f32[128]{0:T(128)S(1)} %get-tuple-element.300, f32[128]{0:T(128)S(1)} %get-tuple-element.301), channel_id=1, replica_groups=mesh['cells'=64,'rank'=4] {'cells'}, use_global_device_ids=true, to_apply=%region_25.0 | all-reduce | flops 256 | bytes 2048 | tf_op jit(solution)/shard_map/while/body/eval_jaxpr/psum | solution.py:102
  1353.6 6.8 all-reduce.6
  1361.6 126.1 %all-reduce.7 = (f32[128]{0:T(128)S(1)}, f32[128]{0:T(128)S(1)}) all-reduce(f32[128]{0:T(128)S(1)} %get-tuple-element.300, f32[128]{0:T(128)S(1)} %get-tuple-element.301), channel_id=1, replica_groups=mesh['cells'=64,'rank'=4] {'cells'}, use_global_device_ids=true, to_apply=%region_25.0 | all-reduce | flops 256 | bytes 2048 | tf_op jit(solution)/shard_map/while/body/eval_jaxpr/psum | solution.py:102
  1496.4 126.1 %all-reduce.7 = (f32[128]{0:T(128)S(1)}, f32[128]{0:T(128)S(1)}) all-reduce(f32[128]{0:T(128)S(1)} %get-tuple-element.300, f32[128]{0:T(128)S(1)} %get-tuple-element.301), channel_id=1, replica_groups=mesh['cells'=64,'rank'=4] {'cells'}, use_global_device_ids=true, to_apply=%region_25.0 | all-reduce | flops 256 | bytes 2048 | tf_op jit(solution)/shard_map/while/body/eval_jaxpr/psum | solution.py:102
  1626.6 9.9 all_gather.7
  1637.0 253.4 %all-reduce.12 = bf16[512,512]{1,0:T(8,128)(2,1)S(1)} all-reduce(f32[512,512]{1,0:T(8,128)S(1)} %fusion.20), channel_id=1, replica_groups=mesh['cells'=64,'rank'=4] {'cells'}, use_global_device_ids=true, to_apply=%region_27.0 | all-reduce | flops 262144 | bytes 1572864 | tf_op jit(solution)/shard_map/psum | solution.py:115
  1890.3 10.2 all_gather.6
  (212 shorter events, 63.4 us)
Async XLA Ops:
  7.2 1629.4 %copy-start = (bf16[512,512]{1,0:T(8,128)(2,1)S(1)}, bf16[512,512]{1,0:T(8,128)(2,1)}, u32[]{:S(2)}) copy-start(bf16[512,512]{1,0:T(8,128)(2,1)} %param.17) | copy-start | bytes 1572868
  7.2 2.1 copy-start.1
  7.2 2.1 copy-start.3
  7.2 184.2 %all-reduce.11.cloned.1.call-start = ((), (), s32[]{:S(2)}) async-start(), calls=%async_computation | async-start | bytes 524288 | tf_op jit(solution)/shard_map/psum | solution.py:54
  10.2 1.0 copy-start.2
  11.3 1.0 copy-start.4
  191.4 1.1 copy-start.6
  192.5 0.7 copy-start.15
  193.2 0.9 copy-start.5
  272.8 0.7 copy-start.12
  273.5 0.7 copy-start.11
  281.8 0.6 copy-start.9
  416.3 0.6 copy-start.9
  551.5 0.6 copy-start.9
  686.2 0.6 copy-start.9
  821.1 0.6 copy-start.9
  955.9 0.6 copy-start.9
  1090.8 0.6 copy-start.9
  1225.5 0.6 copy-start.9
  1360.5 0.6 copy-start.9
  1495.2 0.6 copy-start.9
  1623.0 0.7 copy-start.8
  1624.6 0.7 copy-start.14
  1625.9 0.7 copy-start.10
  (20 other events, 11.0 us)
Sparse Core Ops, SparseCore 0:
  12.2 179.2 all-reduce.10
where the time goes:
time: 1930 us; the launch traced here: 1920 us
  blocking collectives  1810 us (94%)
  waiting for transfers between devices  50.4 us (3%)
  local copies, waits for them, and re-layouts  21.5 us (1%)
    psum x10, blocking collectives, cell_columns(): return lax.psum((first, second), 'cells')  1260 us
    psum x1, blocking collectives, shards(): profiles = lax.psum(contract_rows(right_all, expr), 'cells')  253 us
    psum x1, blocking collectives, shards(): lax.psum((contract_rows(x_emb, q_round), contract_rows(y_emb, r_round), j...  128 us
    pmax x1, blocking collectives, shards(): peak = lax.pmax(local_peak, ('cells', 'rank'))  74.5 us
    psum x10, blocking collectives, rank_rows(): return lax.psum((first, second), 'rank')  67.5 us
    psum x1, waiting for transfers between devices, shards(): lax.psum((contract_rows(x_emb, q_round), contract_rows(y_emb, r_round), j...  50.4 us
  transfers between devices with their start and end apart: 1, of which 1 were waited for; matrix products, arithmetic and copies ran while one was open for 0% of the time, Pallas kernels for 0%

commit v1 on v0

v1 whole, which is shorter than its diff:
```python
import jax
import jax.numpy as jnp
from jax import lax
from jax.sharding import Mesh
from jax.sharding import PartitionSpec as P

PASSES = 10
SCALE = 0.0625
GAMMA = 10.0
POWER = 0.8

CELLS = ("y", "z", "c")
EVERY = ("y", "z", "c", "x")
F32 = jnp.float32
BF16 = jnp.bfloat16


def contract_rows(left, right):
    return lax.dot_general(
        left, right, (((0,), (0,)), ((), ())), preferred_element_type=F32
    )


def exchange(chunks, axes):
    return lax.all_to_all(chunks, axes, 0, 0, tiled=False)


def to_all(value, axes):
    count = lax.axis_size(axes)
    return exchange(jnp.broadcast_to(value[None], (count,) + value.shape), axes)


def split3(value):
    high = lax.reduce_precision(value, 8, 7)
    rest = value - high
    middle = lax.reduce_precision(rest, 8, 7)
    low = lax.reduce_precision(rest - middle, 8, 7)
    return jnp.stack([high, middle, low]).astype(BF16)


def join3(rows):
    parts = rows.astype(F32)
    return parts[..., 0, :] + (parts[..., 1, :] + parts[..., 2, :])


def shards(x_emb, y_emb, q_factor, r_factor, g_weights, a_mass, b_mass, expr):
    rows, width = q_factor.shape
    dim = x_emb.shape[1]
    genes = expr.shape[1]
    cell_devices = lax.axis_size(CELLS)
    ranks = lax.axis_size("x")
    cells_total = rows * cell_devices
    share = dim // cell_devices

    norms_one = jnp.sum(jnp.square(x_emb.astype(F32)), axis=1)
    norms_two = jnp.sum(jnp.square(y_emb.astype(F32)), axis=1)
    part_xq = contract_rows(x_emb, q_factor.astype(BF16))
    part_yr = contract_rows(y_emb, r_factor.astype(BF16))
    part_vec = jnp.stack(
        [
            jnp.sum(norms_one[:, None] * q_factor, axis=0),
            jnp.sum(q_factor, axis=0),
            jnp.sum(norms_two[:, None] * r_factor, axis=0),
            jnp.sum(r_factor, axis=0),
        ]
    )
    outgoing = jnp.concatenate(
        [
            part_xq.reshape(cell_devices, share, width),
            part_yr.reshape(cell_devices, share, width),
            jnp.broadcast_to(part_vec[None], (cell_devices, 4, width)),
        ],
        axis=1,
    )
    summed = jnp.sum(exchange(outgoing, CELLS), axis=0)
    mine_xq, mine_yr = summed[:share], summed[share : 2 * share]
    xq_vec, cq_vec, yr_vec, cr_vec = (summed[2 * share + i] for i in range(4))
    mine_dot = jnp.sum(mine_xq * mine_yr, axis=0)
    crosses = to_all(
        jnp.concatenate([mine_xq.astype(BF16), mine_yr.astype(BF16), split3(mine_dot)], axis=0),
        CELLS,
    )
    cross_xq = crosses[:, :share].reshape(dim, width)
    cross_yr = crosses[:, share : 2 * share].reshape(dim, width)
    cross_dot = jnp.sum(join3(crosses[:, 2 * share :]), axis=0)

    grad_q = (
        SCALE
        * (
            norms_one[:, None] * cr_vec[None, :]
            + yr_vec[None, :]
            - 2.0 * jnp.dot(x_emb, cross_yr, preferred_element_type=F32)
        )
        / g_weights[None, :]
    )
    grad_r = (
        SCALE
        * (
            norms_two[:, None] * cq_vec[None, :]
            + xq_vec[None, :]
            - 2.0 * jnp.dot(y_emb, cross_xq, preferred_element_type=F32)
        )
        / g_weights[None, :]
    )
    curvature = SCALE * (xq_vec * cr_vec + cq_vec * yr_vec - 2.0 * cross_dot)
    grad_g = -curvature / jnp.square(g_weights)
    local_peak = jnp.maximum(
        jnp.max(jnp.abs(grad_q), axis=0),
        jnp.maximum(jnp.max(jnp.abs(grad_r), axis=0), jnp.abs(grad_g)),
    )
    peak = jnp.max(to_all(local_peak[None], EVERY))
    eta = GAMMA / (peak + 1e-06)
    kern_q = q_factor * jnp.exp(-eta * grad_q)
    kern_r = r_factor * jnp.exp(-eta * grad_r)
    kern_g = g_weights * jnp.exp(-eta * grad_g)

    kerns = to_all(
        jnp.concatenate([kern_q.astype(BF16), kern_r.astype(BF16), split3(kern_g)], axis=0), "x"
    )
    all_q = kerns[:, :rows]
    all_r = kerns[:, rows : 2 * rows]
    log_g = jnp.log(join3(kerns[:, 2 * rows :]))

    def row_sums(v_q, v_r):
        return (
            jnp.sum(all_q.astype(F32) * v_q[:, None, :], axis=(0, 2)),
            jnp.sum(all_r.astype(F32) * v_r[:, None, :], axis=(0, 2)),
        )

    v_q = jnp.ones((ranks, width), F32)
    v_r = jnp.ones((ranks, width), F32)
    for step in range(PASSES):
        s_q, s_r = row_sums(v_q, v_r)
        u_q = (a_mass / s_q) ** POWER
        u_r = (b_mass / s_r) ** POWER
        part = jnp.concatenate(
            [
                jnp.sum(all_q.astype(F32) * u_q[None, :, None], axis=1),
                jnp.sum(all_r.astype(F32) * u_r[None, :, None], axis=1),
            ],
            axis=0,
        )
        total = jnp.sum(to_all(part, CELLS), axis=0)
        t_q, t_r = total[:ranks], total[ranks:]
        weights = jnp.exp((log_g + jnp.log(v_q * t_q) + jnp.log(v_r * t_r)) / 3.0)
        v_q = weights / t_q
        v_r = weights / t_r

    here = lax.axis_index("x")

    def own(value):
        return lax.dynamic_index_in_dim(value, here, 0, keepdims=False)

    q_new = u_q[:, None] * kern_q * own(v_q)[None, :]
    r_new = u_r[:, None] * kern_r * own(v_r)[None, :]
    s_q = jnp.sum(all_q.astype(F32) * v_q[:, None, :], axis=(0, 2))
    right = (all_r.astype(F32) * v_r[:, None, :] * u_r[None, :, None]).astype(BF16)
    scaled = (all_q.astype(F32) * (v_q / weights)[:, None, :]).astype(BF16)

    part = lax.dot_general(
        right, expr, (((1,), (0,)), ((), ())), preferred_element_type=F32
    ).reshape(2, ranks * width // 2, genes)
    half = jnp.sum(exchange(part, "c"), axis=0)
    others = lax.axis_size(("y", "z"))
    piece = jnp.sum(exchange(half.reshape(others, -1, genes), ("y", "z")), axis=0)
    half = to_all(piece.astype(BF16), ("y", "z")).reshape(-1, genes)
    profiles = lax.all_gather(half, "c", axis=0, tiled=True).reshape(ranks, width, genes)
    mixed = lax.dot_general(
        scaled, profiles, (((0, 2), (0, 1)), ((), ())), preferred_element_type=F32
    )
    predicted = (mixed / s_q[:, None]).astype(BF16)
    return (q_new, r_new, own(weights) / cells_total, predicted)


def solution(mesh):
    named = Mesh(mesh.devices.reshape(4, 8, 2, 4), EVERY)
    block = P(CELLS, "x")
    return jax.shard_map(
        shards,
        mesh=named,
        in_specs=(
            P(CELLS, None),
            P(CELLS, None),
            block,
            block,
            P("x"),
            P(CELLS),
            P(CELLS),
            block,
        ),
        out_specs=(block, block, P("x"), block),
        check_vma=False,
    )
```

time: 1930 us -> 334 us (0.17)
  blocking collectives: 1810 us -> 239 us
  starting transfers between devices: 0.04 us -> 25.6 us
    psum x23 -> x0, blocking collectives: 1720 us -> none  [the longest x10 1260 us: cell_columns(): return lax.psum((first, second), 'cells')]
    all_to_all x0 -> x13, blocking collectives: none -> 233 us  [exchange(): return lax.all_to_all(chunks, axes, 0, 0, tiled=False)]
    pmax x1 -> x0, blocking collectives: 74.5 us -> none  [shards(): peak = lax.pmax(local_peak, ('cells', 'rank'))]
    psum x1 -> x0, waiting for transfers between devices: 50.4 us -> none  [shards(): lax.psum((contract_rows(x_emb, q_round), contract_rows(y_emb, r_round), j...]
    all_to_all x0 -> x4, waiting for transfers between devices: none -> 45.2 us  [exchange(): return lax.all_to_all(chunks, axes, 0, 0, tiled=False)]
    all_to_all x0 -> x4, starting transfers between devices: none -> 25.6 us  [exchange(): return lax.all_to_all(chunks, axes, 0, 0, tiled=False)]
  transfers between devices with their start and end apart: 1 -> 4, of which waited for: 1 -> 4; matrix products, arithmetic and copies ran while one was open for 0% -> 1% of each run, Pallas kernels for 0% -> 0%
where the time goes in v1:
time: 334 us; the launch traced here: 333 us
  blocking collectives  239 us (72%)
  waiting for transfers between devices  45.2 us (14%)
  starting transfers between devices  25.6 us (8%)
  other arithmetic  11.7 us (4%)
  local copies, waits for them, and re-layouts  5.83 us (2%)
  matrix products  4.01 us (1%)
    all_to_all x13, blocking collectives, exchange(): return lax.all_to_all(chunks, axes, 0, 0, tiled=False)  233 us
    all_to_all x4, waiting for transfers between devices, exchange(): return lax.all_to_all(chunks, axes, 0, 0, tiled=False)  45.2 us
    all_to_all x4, starting transfers between devices, exchange(): return lax.all_to_all(chunks, axes, 0, 0, tiled=False)  25.6 us
  transfers between devices with their start and end apart: 4, of which 4 were waited for; matrix products, arithmetic and copies ran while one was open for 1% of the time, Pallas kernels for 0%

profile of v1, /device:TPU:1, one launch (start us, length us, event | category | flops | bytes accessed | tf_op | source)
XLA Modules:
  0.0 333.3 jit_solution(262849850262352990)
XLA Ops:
  1.9 1.3 fusion.59
  4.4 30.3 %all_to_all.85 = f32[64,12,128]{2,1,0:T(8,128)S(1)} all-to-all(f32[64,12,128]{2,1,0:T(8,128)S(1)} %pad_maximum_fusion), channel_id=1, replica_groups=mesh['y'=4,'z'=8,'c'=2,'x'=4] {'y','z','c'}, dimensions={0} | all-to-all | bytes 786432 | tf_op jit(solution)/shard_map/all_to_all | solution.py:25
  35.6 6.3 %all-to-all-start.1 = ((bf16[64,11,128]{2,1,0:T(8,128)(2,1)}), bf16[64,11,128]{2,1,0:T(8,128)(2,1)S(1)}, u32[]{:S(2)}, u32[]{:S(2)}) async-start(bf16[64,11,128]{2,1,0:T(8,128)(2,1)} %broadcast_in_dim.31), calls=%async_computation.1 | async-start | bytes 524288 | tf_op jit(solution)/shard_map/all_to_all | solution.py:25
  41.9 12.0 %all-to-all-done.1 = bf16[64,11,128]{2,1,0:T(8,128)(2,1)S(1)} async-done(((bf16[64,11,128]{2,1,0:T(8,128)(2,1)}), bf16[64,11,128]{2,1,0:T(8,128)(2,1)S(1)}, u32[]{:S(2)}, u32[]{:S(2)}) %all-to-all-start.1) | async-done | bytes 180256 | tf_op jit(solution)/shard_map/all_to_all | solution.py:25
  54.9 21.1 %all_to_all.86 = f32[256,1,128]{2,1,0:T(1,128)S(1)} all-to-all(f32[256,1,128]{2,1,0:T(1,128)S(1)} %broadcast_in_dim.32), channel_id=1, replica_groups=mesh['y'=4,'z'=8,'c'=2,'x'=4] {'y','z','c','x'}, dimensions={0} | all-to-all | bytes 262144 | tf_op jit(solution)/shard_map/all_to_all | solution.py:25
  78.3 16.7 %all_to_all.87 = bf16[4,1027,128]{2,1,0:T(8,128)(2,1)S(1)} all-to-all(bf16[4,1027,128]{2,1,0:T(8,128)(2,1)S(1)} %broadcast_in_dim.33), channel_id=1, replica_groups=mesh['y'=4,'z'=8,'c'=2,'x'=4] {'x'}, dimensions={0} | all-to-all | bytes 2103296 | tf_op jit(solution)/shard_map/all_to_all | solution.py:25
  96.7 6.0 %all-to-all-start.4 = ((f32[64,8,128]{2,1,0:T(8,128)}), f32[64,8,128]{2,1,0:T(8,128)S(1)}, u32[]{:S(2)}, u32[]{:S(2)}) async-start(f32[64,8,128]{2,1,0:T(8,128)} %broadcast_in_dim.34), calls=%async_computation.4 | async-start | bytes 524288 | tf_op jit(solution)/shard_map/all_to_all | solution.py:25
  102.7 12.0 %all-to-all-done.4 = f32[64,8,128]{2,1,0:T(8,128)S(1)} async-done(((f32[64,8,128]{2,1,0:T(8,128)}), f32[64,8,128]{2,1,0:T(8,128)S(1)}, u32[]{:S(2)}, u32[]{:S(2)}) %all-to-all-start.4) | async-done | bytes 262176 | tf_op jit(solution)/shard_map/all_to_all | solution.py:25
  115.5 17.9 %all_to_all.88 = f32[64,8,128]{2,1,0:T(8,128)S(1)} all-to-all(f32[64,8,128]{2,1,0:T(8,128)S(1)} %broadcast_in_dim.35), channel_id=1, replica_groups=mesh['y'=4,'z'=8,'c'=2,'x'=4] {'y','z','c'}, dimensions={0} | all-to-all | bytes 524288 | tf_op jit(solution)/shard_map/all_to_all | solution.py:25
  134.1 17.8 %all_to_all.89 = f32[64,8,128]{2,1,0:T(8,128)S(1)} all-to-all(f32[64,8,128]{2,1,0:T(8,128)S(1)} %broadcast_in_dim.36), channel_id=1, replica_groups=mesh['y'=4,'z'=8,'c'=2,'x'=4] {'y','z','c'}, dimensions={0} | all-to-all | bytes 524288 | tf_op jit(solution)/shard_map/all_to_all | solution.py:25
  152.7 18.0 %all_to_all.90 = f32[64,8,128]{2,1,0:T(8,128)S(1)} all-to-all(f32[64,8,128]{2,1,0:T(8,128)S(1)} %broadcast_in_dim.37), channel_id=1, replica_groups=mesh['y'=4,'z'=8,'c'=2,'x'=4] {'y','z','c'}, dimensions={0} | all-to-all | bytes 524288 | tf_op jit(solution)/shard_map/all_to_all | solution.py:25
  171.5 17.8 %all_to_all.91 = f32[64,8,128]{2,1,0:T(8,128)S(1)} all-to-all(f32[64,8,128]{2,1,0:T(8,128)S(1)} %broadcast_in_dim.38), channel_id=1, replica_groups=mesh['y'=4,'z'=8,'c'=2,'x'=4] {'y','z','c'}, dimensions={0} | all-to-all | bytes 524288 | tf_op jit(solution)/shard_map/all_to_all | solution.py:25
  190.1 17.8 %all_to_all.92 = f32[64,8,128]{2,1,0:T(8,128)S(1)} all-to-all(f32[64,8,128]{2,1,0:T(8,128)S(1)} %broadcast_in_dim.39), channel_id=1, replica_groups=mesh['y'=4,'z'=8,'c'=2,'x'=4] {'y','z','c'}, dimensions={0} | all-to-all | bytes 524288 | tf_op jit(solution)/shard_map/all_to_all | solution.py:25
  208.7 17.8 %all_to_all.93 = f32[64,8,128]{2,1,0:T(8,128)S(1)} all-to-all(f32[64,8,128]{2,1,0:T(8,128)S(1)} %broadcast_in_dim.40), channel_id=1, replica_groups=mesh['y'=4,'z'=8,'c'=2,'x'=4] {'y','z','c'}, dimensions={0} | all-to-all | bytes 524288 | tf_op jit(solution)/shard_map/all_to_all | solution.py:25
  227.3 17.8 %all_to_all.94 = f32[64,8,128]{2,1,0:T(8,128)S(1)} all-to-all(f32[64,8,128]{2,1,0:T(8,128)S(1)} %broadcast_in_dim.41), channel_id=1, replica_groups=mesh['y'=4,'z'=8,'c'=2,'x'=4] {'y','z','c'}, dimensions={0} | all-to-all | bytes 524288 | tf_op jit(solution)/shard_map/all_to_all | solution.py:25
  245.9 17.8 %all_to_all.95 = f32[64,8,128]{2,1,0:T(8,128)S(1)} all-to-all(f32[64,8,128]{2,1,0:T(8,128)S(1)} %broadcast_in_dim.42), channel_id=1, replica_groups=mesh['y'=4,'z'=8,'c'=2,'x'=4] {'y','z','c'}, dimensions={0} | all-to-all | bytes 524288 | tf_op jit(solution)/shard_map/all_to_all | solution.py:25
  264.6 17.8 %all_to_all.96 = f32[64,8,128]{2,1,0:T(8,128)S(1)} all-to-all(f32[64,8,128]{2,1,0:T(8,128)S(1)} %broadcast_in_dim.43), channel_id=1, replica_groups=mesh['y'=4,'z'=8,'c'=2,'x'=4] {'y','z','c'}, dimensions={0} | all-to-all | bytes 524288 | tf_op jit(solution)/shard_map/all_to_all | solution.py:25
  283.1 4.6 %all_to_all.97 = f32[2,256,512]{2,1,0:T(8,128)S(1)} all-to-all(f32[2,256,512]{2,1,0:T(8,128)S(1)} %bitcast.86), channel_id=1, replica_groups=mesh['y'=4,'z'=8,'c'=2,'x'=4] {'c'}, dimensions={0} | all-to-all | bytes 2097152 | tf_op jit(solution)/shard_map/all_to_all | solution.py:25
  288.6 5.3 %all-to-all-start.15 = ((f32[32,8,512]{2,1,0:T(8,128)}), f32[32,8,512]{2,1,0:T(8,128)S(1)}, u32[]{:S(2)}, u32[]{:S(2)}) async-start(f32[32,8,512]{2,1,0:T(8,128)} %bitcast.87), calls=%async_computation.15 | async-start | bytes 1048576 | tf_op jit(solution)/shard_map/all_to_all | solution.py:25
  294.0 14.0 %all-to-all-done.15 = f32[32,8,512]{2,1,0:T(8,128)S(1)} async-done(((f32[32,8,512]{2,1,0:T(8,128)}), f32[32,8,512]{2,1,0:T(8,128)S(1)}, u32[]{:S(2)}, u32[]{:S(2)}) %all-to-all-start.15) | async-done | bytes 524320 | tf_op jit(solution)/shard_map/all_to_all | solution.py:25
  308.8 8.1 %all-to-all-start.16 = ((bf16[32,8,512]{2,1,0:T(8,128)(2,1)}), bf16[32,8,512]{2,1,0:T(8,128)(2,1)S(1)}, u32[]{:S(2)}, u32[]{:S(2)}) async-start(bf16[32,8,512]{2,1,0:T(8,128)(2,1)} %broadcast_in_dim.44), calls=%async_computation.16 | async-start | bytes 524288 | tf_op jit(solution)/shard_map/all_to_all | solution.py:25
  319.4 7.2 %all-to-all-done.16 = bf16[32,8,512]{2,1,0:T(8,128)(2,1)S(1)} async-done(((bf16[32,8,512]{2,1,0:T(8,128)(2,1)}), bf16[32,8,512]{2,1,0:T(8,128)(2,1)S(1)}, u32[]{:S(2)}, u32[]{:S(2)}) %all-to-all-start.16) | async-done | bytes 262176 | tf_op jit(solution)/shard_map/all_to_all | solution.py:25
  326.6 5.4 %all_gather.3 = bf16[512,512]{1,0:T(8,128)(2,1)S(1)} all-gather(bf16[256,512]{1,0:T(8,128)(2,1)S(1)} %bitcast.88), channel_id=1, replica_groups=mesh['y'=4,'z'=8,'c'=2,'x'=4] {'c'}, dimensions={0}, use_global_device_ids=true | all-gather | bytes 786432 | tf_op jit(solution)/shard_map/all_gather | solution.py:167
  332.0 1.2 divide_convert_fusion
  (161 shorter events, 19.0 us)
Async XLA Ops:
  0.6 281.9 %copy-start = (bf16[512,512]{1,0:T(8,128)(2,1)S(1)}, bf16[512,512]{1,0:T(8,128)(2,1)}, u32[]{:S(2)}) copy-start(bf16[512,512]{1,0:T(8,128)(2,1)} %param.15) | copy-start | bytes 1572868
  0.6 2.5 copy-start.1
  0.7 2.6 copy-start.2
  0.7 2.7 copy-start.6
  34.7 19.4 %copy-start.5 = (bf16[512,256]{1,0:T(8,128)(2,1)S(1)}, bf16[512,256]{1,0:T(8,128)(2,1)}, u32[]{:S(2)}) copy-start(bf16[512,256]{1,0:T(8,128)(2,1)} %param.8) | copy-start | bytes 786436
  34.7 19.4 %copy-start.9 = (f32[128]{0:T(128)S(1)}, f32[128]{0:T(128)}, u32[]{:S(2)}) copy-start(f32[128]{0:T(128)} %param.12) | copy-start | bytes 1540
  35.6 18.3 %all-to-all-start.1 = ((bf16[64,11,128]{2,1,0:T(8,128)(2,1)}), bf16[64,11,128]{2,1,0:T(8,128)(2,1)S(1)}, u32[]{:S(2)}, u32[]{:S(2)}) async-start(bf16[64,11,128]{2,1,0:T(8,128)(2,1)} %broadcast_in_dim.31), calls=%async_computation.1 | async-start | bytes 524288 | tf_op jit(solution)/shard_map/all_to_all | solution.py:25
  54.8 23.1 %copy-start.3 = (f32[512,128]{0,1:T(8,128)}, f32[512,128]{0,1:T(8,128)S(1)}, u32[]{:S(2)}) copy-start(f32[512,128]{0,1:T(8,128)S(1)} %get-tuple-element.106) | copy-start | bytes 786436
  78.3 16.9 %copy-start.7 = (f32[512]{0:T(512)S(1)}, f32[512]{0:T(512)}, u32[]{:S(2)}) copy-start(f32[512]{0:T(512)} %param.13) | copy-start | bytes 6148
  94.9 0.7 copy-start.8
  96.7 18.0 %all-to-all-start.4 = ((f32[64,8,128]{2,1,0:T(8,128)}), f32[64,8,128]{2,1,0:T(8,128)S(1)}, u32[]{:S(2)}, u32[]{:S(2)}) async-start(f32[64,8,128]{2,1,0:T(8,128)} %broadcast_in_dim.34), calls=%async_computation.4 | async-start | bytes 524288 | tf_op jit(solution)/shard_map/all_to_all | solution.py:25
  288.6 5.3 %copy-start.4 = (f32[512,128]{0,1:T(8,128)S(1)}, f32[512,128]{0,1:T(8,128)}, u32[]{:S(2)}) copy-start(f32[512,128]{0,1:T(8,128)} %copy-done.3) | copy-start | bytes 786436
  288.6 19.4 %all-to-all-start.15 = ((f32[32,8,512]{2,1,0:T(8,128)}), f32[32,8,512]{2,1,0:T(8,128)S(1)}, u32[]{:S(2)}, u32[]{:S(2)}) async-start(f32[32,8,512]{2,1,0:T(8,128)} %bitcast.87), calls=%async_computation.15 | async-start | bytes 1048576 | tf_op jit(solution)/shard_map/all_to_all | solution.py:25
  308.8 17.8 %all-to-all-start.16 = ((bf16[32,8,512]{2,1,0:T(8,128)(2,1)}), bf16[32,8,512]{2,1,0:T(8,128)(2,1)S(1)}, u32[]{:S(2)}, u32[]{:S(2)}) async-start(bf16[32,8,512]{2,1,0:T(8,128)(2,1)} %broadcast_in_dim.44), calls=%async_computation.16 | async-start | bytes 524288 | tf_op jit(solution)/shard_map/all_to_all | solution.py:25

commit v2 on v1

v2 whole, which is shorter than its diff:
```python
import jax
import jax.numpy as jnp
from jax import lax
from jax.sharding import Mesh
from jax.sharding import PartitionSpec as P

PASSES = 10
SCALE = 0.0625
GAMMA = 10.0
POWER = 0.8

CHIPS = ("y", "z")
CELLS = ("y", "z", "c")
EVERY = ("y", "z", "c", "x")
F32 = jnp.float32
BF16 = jnp.bfloat16


def contract_rows(left, right):
    return lax.dot_general(
        left, right, (((0,), (0,)), ((), ())), preferred_element_type=F32
    )


def exchange(chunks, axes):
    return lax.all_to_all(chunks, axes, 0, 0, tiled=False)


def to_all(value, axes):
    count = lax.axis_size(axes)
    return exchange(jnp.broadcast_to(value[None], (count,) + value.shape), axes)


def swap(value):
    return lax.ppermute(value, "c", [(0, 1), (1, 0)])


def pick(value, index):
    return lax.dynamic_index_in_dim(value, index, 0, keepdims=False)


def split3(value):
    high = lax.reduce_precision(value, 8, 7)
    rest = value - high
    middle = lax.reduce_precision(rest, 8, 7)
    low = lax.reduce_precision(rest - middle, 8, 7)
    return jnp.stack([high, middle, low]).astype(BF16)


def join3(rows):
    parts = rows.astype(F32)
    return parts[..., 0, :] + (parts[..., 1, :] + parts[..., 2, :])


def shards(x_emb, y_emb, q_factor, r_factor, g_weights, a_mass, b_mass, expr):
    rows, width = q_factor.shape
    dim = x_emb.shape[1]
    genes = expr.shape[1]
    others = lax.axis_size(CHIPS)
    cell_devices = 2 * others
    ranks = lax.axis_size("x")
    cells_total = rows * cell_devices
    share = dim // cell_devices

    here = lax.axis_index("x")
    core = lax.axis_index("c")
    other_expr = swap(expr)
    masses = jnp.stack([a_mass, b_mass])
    masses = jnp.stack([masses, swap(masses)])
    norms_one = jnp.sum(jnp.square(x_emb.astype(F32)), axis=1)
    norms_two = jnp.sum(jnp.square(y_emb.astype(F32)), axis=1)
    part_xq = contract_rows(x_emb, q_factor.astype(BF16)).reshape(2, others, share, width)
    part_yr = contract_rows(y_emb, r_factor.astype(BF16)).reshape(2, others, share, width)
    part_cross = jnp.concatenate([part_xq, part_yr], axis=2)
    part_vec = jnp.stack(
        [
            jnp.sum(norms_one[:, None] * q_factor, axis=0),
            jnp.sum(q_factor, axis=0),
            jnp.sum(norms_two[:, None] * r_factor, axis=0),
            jnp.sum(r_factor, axis=0),
        ]
    )

    def with_vec(cross):
        return jnp.concatenate(
            [cross, jnp.broadcast_to(part_vec[None], (others, 4, width))], axis=1
        ).reshape(others, (2 * share + 4) // 4, 4, width)

    outgoing = with_vec(pick(part_cross, core)) + swap(with_vec(pick(part_cross, 1 - core)))
    summed = jnp.sum(exchange(outgoing, CHIPS), axis=0).reshape(2 * share + 4, width)
    mine_xq, mine_yr = summed[:share], summed[share : 2 * share]
    xq_vec, cq_vec, yr_vec, cr_vec = (summed[2 * share + i] for i in range(4))
    mine_dot = jnp.sum(mine_xq * mine_yr, axis=0)
    sent = jnp.concatenate(
        [
            mine_xq.astype(BF16),
            mine_yr.astype(BF16),
            split3(mine_dot),
            jnp.zeros((1, width), BF16),
        ],
        axis=0,
    ).reshape(share + 2, 2, width)
    crosses = lax.all_gather(to_all(sent, CHIPS), "c").reshape(2 * others, 2 * share + 4, width)
    cross_xq = crosses[:, :share].reshape(dim, width)
    cross_yr = crosses[:, share : 2 * share].reshape(dim, width)
    cross_dot = jnp.sum(join3(crosses[:, 2 * share : 2 * share + 3]), axis=0)

    grad_q = (
        SCALE
        * (
            norms_one[:, None] * cr_vec[None, :]
            + yr_vec[None, :]
            - 2.0 * jnp.dot(x_emb, cross_yr, preferred_element_type=F32)
        )
        / g_weights[None, :]
    )
    grad_r = (
        SCALE
        * (
            norms_two[:, None] * cq_vec[None, :]
            + xq_vec[None, :]
            - 2.0 * jnp.dot(y_emb, cross_xq, preferred_element_type=F32)
        )
        / g_weights[None, :]
    )
    curvature = SCALE * (xq_vec * cr_vec + cq_vec * yr_vec - 2.0 * cross_dot)
    grad_g = -curvature / jnp.square(g_weights)
    local_peak = jnp.maximum(
        jnp.max(jnp.abs(grad_q), axis=0),
        jnp.maximum(jnp.max(jnp.abs(grad_r), axis=0), jnp.abs(grad_g)),
    )
    peak = jnp.max(to_all(local_peak[None], EVERY))
    eta = GAMMA / (peak + 1e-06)
    kern_q = q_factor * jnp.exp(-eta * grad_q)
    kern_r = r_factor * jnp.exp(-eta * grad_r)
    kern_g = g_weights * jnp.exp(-eta * grad_g)

    mine = to_all(
        jnp.concatenate([kern_q.astype(BF16), kern_r.astype(BF16), split3(kern_g)], axis=0), "x"
    )
    log_g = jnp.log(join3(mine[:, 2 * rows :]))
    mine_q = mine[:, :rows]
    kerns = mine[:, : 2 * rows]
    pair = jnp.stack([kerns, swap(kerns)]).reshape(2, ranks, 2, rows, width)
    flat = jnp.ones((2, ranks, width), F32)

    def one_pass(v):
        s = jnp.sum(pair.astype(F32) * v.transpose(1, 0, 2)[None, :, :, None, :], axis=(1, 4))
        u = (masses / s) ** POWER
        parts = jnp.sum(pair.astype(F32) * u[:, None, :, :, None], axis=3)
        part = (parts[0] + parts[1]).transpose(1, 0, 2).reshape(2 * ranks, width)
        t = jnp.sum(to_all(part, CHIPS), axis=0).reshape(2, ranks, width)
        weights = jnp.exp((log_g + jnp.log(v[0] * t[0]) + jnp.log(v[1] * t[1])) / 3.0)
        return weights[None] / t, weights, u

    v = lax.fori_loop(0, PASSES - 1, lambda step, v: one_pass(v)[0], flat)
    (v_q, v_r), weights, u = one_pass(v)

    q_new = u[0, 0][:, None] * kern_q * pick(v_q, here)[None, :]
    r_new = u[0, 1][:, None] * kern_r * pick(v_r, here)[None, :]
    s_q = jnp.sum(mine_q.astype(F32) * v_q[:, None, :], axis=(0, 2))
    scaled = (mine_q.astype(F32) * (v_q / weights)[:, None, :]).astype(BF16)

    half = ranks // 2
    half_v = lax.dynamic_slice_in_dim(v_r, core * half, half, 0)

    def product(member, cells):
        kern = lax.dynamic_slice_in_dim(pair[member, :, 1], core * half, half, 0)
        right = (kern.astype(F32) * half_v[:, None, :] * u[member, 1][None, :, None]).astype(BF16)
        return lax.dot_general(right, cells, (((1,), (0,)), ((), ())), preferred_element_type=F32)

    part = product(0, expr) + product(1, other_expr)
    piece = jnp.sum(exchange(part.reshape(others, -1, genes), CHIPS), axis=0)
    profiles = lax.all_gather(to_all(piece.astype(BF16), CHIPS), "c").reshape(ranks, width, genes)
    mixed = lax.dot_general(
        scaled, profiles, (((0, 2), (0, 1)), ((), ())), preferred_element_type=F32
    )
    predicted = (mixed / s_q[:, None]).astype(BF16)
    return (q_new, r_new, pick(weights, here) / cells_total, predicted)


def solution(mesh):
    named = Mesh(mesh.devices.reshape(4, 8, 2, 4), EVERY)
    block = P(CELLS, "x")
    return jax.shard_map(
        shards,
        mesh=named,
        in_specs=(
            P(CELLS, None),
            P(CELLS, None),
            block,
            block,
            P("x"),
            P(CELLS),
            P(CELLS),
            block,
        ),
        out_specs=(block, block, P("x"), block),
        check_vma=False,
    )
```

time: 334 us -> 308 us (0.922)
  blocking collectives: 239 us -> 66.7 us
  waiting for transfers between devices: 45.2 us -> 113 us
  starting transfers between devices: 25.6 us -> 77.8 us
  other arithmetic: 11.7 us -> 24.1 us
  local copies, waits for them, and re-layouts: 5.83 us -> 14.7 us
    all_to_all x13 -> x3, blocking collectives: 233 us -> 54.4 us  [exchange(): return lax.all_to_all(chunks, axes, 0, 0, tiled=False)]
    all_to_all x4 -> x13, waiting for transfers between devices: 45.2 us -> 110 us  [exchange(): return lax.all_to_all(chunks, axes, 0, 0, tiled=False)]
    all_to_all x4 -> x13, starting transfers between devices: 25.6 us -> 61.2 us  [exchange(): return lax.all_to_all(chunks, axes, 0, 0, tiled=False)]
    ppermute x0 -> x4, starting transfers between devices: none -> 16.6 us  [swap(): return lax.ppermute(value, 'c', [(0, 1), (1, 0)])]
    all_gather x1 -> x2, blocking collectives: 5.42 us -> 12.3 us  [the longest x1 8.01 us: shards(): lax.all_gather(to_all(piece.astype(BF16), CHIPS), 'c')]
    pow x20 -> x10, other arithmetic: 0.25 us -> 6.58 us  [one_pass(): u = (masses / s) ** POWER]
    broadcast_in_dim x14 -> x15, local copies, waits for them, and re-layouts: 2.56 us -> 8.29 us  [to_all(): return exchange(jnp.broadcast_to(value[None], (count,) + value.shape), axes)]
    reduce_sum x35 -> x34, other arithmetic: 7.72 us -> 11.9 us  [the longest x10 6.26 us: one_pass(): jnp.sum(pair.astype(F32) * v.transpose(1, 0, 2)[None, :, :, None, :], axi...]
  transfers between devices with their start and end apart: 4 -> 17, of which waited for: 4 -> 15; matrix products, arithmetic and copies ran while one was open for 1% -> 2% of each run, Pallas kernels for 0% -> 0%
where the time goes in v2:
time: 308 us; the launch traced here: 306 us
  waiting for transfers between devices  113 us (37%)
  starting transfers between devices  77.8 us (25%)
  blocking collectives  66.7 us (22%)
  other arithmetic  24.1 us (8%)
  local copies, waits for them, and re-layouts  14.7 us (5%)
  matrix products  7.22 us (2%)
    all_to_all x13, waiting for transfers between devices, exchange(): return lax.all_to_all(chunks, axes, 0, 0, tiled=False)  110 us
    all_to_all x13, starting transfers between devices, exchange(): return lax.all_to_all(chunks, axes, 0, 0, tiled=False)  61.2 us
    all_to_all x3, blocking collectives, exchange(): return lax.all_to_all(chunks, axes, 0, 0, tiled=False)  54.4 us
    ppermute x4, starting transfers between devices, swap(): return lax.ppermute(value, 'c', [(0, 1), (1, 0)])  16.6 us
    broadcast_in_dim x15, local copies, waits for them, and re-layouts, to_all(): return exchange(jnp.broadcast_to(value[None], (count,) + value.shape), axes)  8.29 us
    all_gather x1, blocking collectives, shards(): lax.all_gather(to_all(piece.astype(BF16), CHIPS), 'c')  8.01 us
    pow x10, other arithmetic, one_pass(): u = (masses / s) ** POWER  6.58 us
    reduce_sum x10, other arithmetic, one_pass(): jnp.sum(pair.astype(F32) * v.transpose(1, 0, 2)[None, :, :, None, :], axi...  6.26 us
  transfers between devices with their start and end apart: 17, of which 15 were waited for; matrix products, arithmetic and copies ran while one was open for 2% of the time, Pallas kernels for 0%

profile of v2, /device:TPU:1, one launch (start us, length us, event | category | flops | bytes accessed | tf_op | source)
XLA Modules:
  0.0 306.3 jit_solution(5758561936089927837)
XLA Ops:
  10.9 18.7 %all_to_all.42 = f32[32,3,4,128]{3,2,1,0:T(4,128)S(1)} all-to-all(f32[32,3,4,128]{3,2,1,0:T(4,128)S(1)} %copy.123), channel_id=1, replica_groups=mesh['y'=4,'z'=8,'c'=2,'x'=4] {'y','z'}, dimensions={0} | all-to-all | bytes 393216 | tf_op jit(solution)/shard_map/all_to_all | solution.py:26
  30.5 5.5 %all-to-all-start.2 = ((bf16[32,6,2,128]{3,2,1,0:T(2,128)(2,1)}), bf16[32,6,2,128]{3,2,1,0:T(2,128)(2,1)S(1)}, u32[]{:S(2)}, u32[]{:S(2)}) async-start(bf16[32,6,2,128]{3,2,1,0:T(2,128)(2,1)} %broadcast_in_dim.27), calls=%async_computation.2 | async-start | bytes 196608 | tf_op jit(solution)/shard_map/all_to_all | solution.py:26
  36.0 9.0 %all-to-all-done.2 = bf16[32,6,2,128]{3,2,1,0:T(2,128)(2,1)S(1)} async-done(((bf16[32,6,2,128]{3,2,1,0:T(2,128)(2,1)}), bf16[32,6,2,128]{3,2,1,0:T(2,128)(2,1)S(1)}, u32[]{:S(2)}, u32[]{:S(2)}) %all-to-all-start.2) | async-done | bytes 98336 | tf_op jit(solution)/shard_map/all_to_all | solution.py:26
  45.0 4.3 %all-gather = bf16[64,6,2,128]{3,0,2,1:T(8,128)(2,1)S(1)} all-gather(bf16[32,6,2,128]{3,0,2,1:T(8,128)(2,1)S(1)} %copy.124), channel_id=2, replica_groups=mesh['y'=4,'z'=8,'c'=2,'x'=4] {'c'}, dimensions={0}, use_global_device_ids=true | all-gather | bytes 294912 | tf_op jit(solution)/shard_map/all_gather | solution.py:103
  50.3 19.0 %all_to_all.43 = f32[256,1,128]{2,1,0:T(1,128)S(1)} all-to-all(f32[256,1,128]{2,1,0:T(1,128)S(1)} %broadcast_in_dim.28), channel_id=1, replica_groups=mesh['y'=4,'z'=8,'c'=2,'x'=4] {'y','z','c','x'}, dimensions={0} | all-to-all | bytes 262144 | tf_op jit(solution)/shard_map/all_to_all | solution.py:26
  71.7 16.7 %all_to_all.44 = bf16[4,1027,128]{2,1,0:T(8,128)(2,1)S(1)} all-to-all(bf16[4,1027,128]{2,1,0:T(8,128)(2,1)S(1)} %broadcast_in_dim.29), channel_id=1, replica_groups=mesh['y'=4,'z'=8,'c'=2,'x'=4] {'x'}, dimensions={0} | all-to-all | bytes 2103296 | tf_op jit(solution)/shard_map/all_to_all | solution.py:26
  95.9 140.5 %while.11 = (s32[]{:T(128)}, f32[2,4,128]{2,1,0:T(4,128)S(1)}, f32[4,128]{1,0:T(4,128)S(1)}, bf16[2,4,2,512,128]{4,3,2,1,0:T(8,128)(2,1)S(1)}, f32[2,2,512]{2,1,0:T(2,128)}, /*index=5*/s32[]{:T(128)}, s32[]{:T(128)}, f32[]{:T(128)}) while((s32[]{:T(128)}, f32[2,4,128]{2,1,0:T(4,128)S(1)}, f32[4,128]{1,0:T(4,128)S(1)}, ...), condition=%wide.region_16.17_spmd.clone, body=%wide.region_12.16_spmd.clone.sunk | while | flops 6327811 | bytes 4987012 | solution.py:156
  102.2 9.1 %all-to-all-done = f32[32,8,128]{2,1,0:T(8,128)S(1)} async-done(((f32[32,8,128]{2,1,0:T(8,128)}), f32[32,8,128]{2,1,0:T(8,128)S(1)}, u32[]{:S(2)}, u32[]{:S(2)}) %all-to-all-start) | async-done | bytes 131104 | tf_op jit(solution)/shard_map/while/body/eval_jaxpr/all_to_all | solution.py:26
  113.9 4.5 %all-to-all-start = ((f32[32,8,128]{2,1,0:T(8,128)}), f32[32,8,128]{2,1,0:T(8,128)S(1)}, u32[]{:S(2)}, u32[]{:S(2)}) async-start(f32[32,8,128]{2,1,0:T(8,128)} %broadcast_in_dim.43), calls=%async_computation | async-start | bytes 262144 | tf_op jit(solution)/shard_map/while/body/eval_jaxpr/all_to_all | solution.py:26
  118.3 9.2 %all-to-all-done = f32[32,8,128]{2,1,0:T(8,128)S(1)} async-done(((f32[32,8,128]{2,1,0:T(8,128)}), f32[32,8,128]{2,1,0:T(8,128)S(1)}, u32[]{:S(2)}, u32[]{:S(2)}) %all-to-all-start) | async-done | bytes 131104 | tf_op jit(solution)/shard_map/while/body/eval_jaxpr/all_to_all | solution.py:26
  133.9 9.1 %all-to-all-done = f32[32,8,128]{2,1,0:T(8,128)S(1)} async-done(((f32[32,8,128]{2,1,0:T(8,128)}), f32[32,8,128]{2,1,0:T(8,128)S(1)}, u32[]{:S(2)}, u32[]{:S(2)}) %all-to-all-start) | async-done | bytes 131104 | tf_op jit(solution)/shard_map/while/body/eval_jaxpr/all_to_all | solution.py:26
  149.5 9.1 %all-to-all-done = f32[32,8,128]{2,1,0:T(8,128)S(1)} async-done(((f32[32,8,128]{2,1,0:T(8,128)}), f32[32,8,128]{2,1,0:T(8,128)S(1)}, u32[]{:S(2)}, u32[]{:S(2)}) %all-to-all-start) | async-done | bytes 131104 | tf_op jit(solution)/shard_map/while/body/eval_jaxpr/all_to_all | solution.py:26
  161.1 3.9 %all-to-all-start = ((f32[32,8,128]{2,1,0:T(8,128)}), f32[32,8,128]{2,1,0:T(8,128)S(1)}, u32[]{:S(2)}, u32[]{:S(2)}) async-start(f32[32,8,128]{2,1,0:T(8,128)} %broadcast_in_dim.43), calls=%async_computation | async-start | bytes 262144 | tf_op jit(solution)/shard_map/while/body/eval_jaxpr/all_to_all | solution.py:26
  165.0 9.1 %all-to-all-done = f32[32,8,128]{2,1,0:T(8,128)S(1)} async-done(((f32[32,8,128]{2,1,0:T(8,128)}), f32[32,8,128]{2,1,0:T(8,128)S(1)}, u32[]{:S(2)}, u32[]{:S(2)}) %all-to-all-start) | async-done | bytes 131104 | tf_op jit(solution)/shard_map/while/body/eval_jaxpr/all_to_all | solution.py:26
  180.6 9.1 %all-to-all-done = f32[32,8,128]{2,1,0:T(8,128)S(1)} async-done(((f32[32,8,128]{2,1,0:T(8,128)}), f32[32,8,128]{2,1,0:T(8,128)S(1)}, u32[]{:S(2)}, u32[]{:S(2)}) %all-to-all-start) | async-done | bytes 131104 | tf_op jit(solution)/shard_map/while/body/eval_jaxpr/all_to_all | solution.py:26
  196.1 9.1 %all-to-all-done = f32[32,8,128]{2,1,0:T(8,128)S(1)} async-done(((f32[32,8,128]{2,1,0:T(8,128)}), f32[32,8,128]{2,1,0:T(8,128)S(1)}, u32[]{:S(2)}, u32[]{:S(2)}) %all-to-all-start) | async-done | bytes 131104 | tf_op jit(solution)/shard_map/while/body/eval_jaxpr/all_to_all | solution.py:26
  211.6 9.1 %all-to-all-done = f32[32,8,128]{2,1,0:T(8,128)S(1)} async-done(((f32[32,8,128]{2,1,0:T(8,128)}), f32[32,8,128]{2,1,0:T(8,128)S(1)}, u32[]{:S(2)}, u32[]{:S(2)}) %all-to-all-start) | async-done | bytes 131104 | tf_op jit(solution)/shard_map/while/body/eval_jaxpr/all_to_all | solution.py:26
  227.2 9.1 %all-to-all-done = f32[32,8,128]{2,1,0:T(8,128)S(1)} async-done(((f32[32,8,128]{2,1,0:T(8,128)}), f32[32,8,128]{2,1,0:T(8,128)S(1)}, u32[]{:S(2)}, u32[]{:S(2)}) %all-to-all-start) | async-done | bytes 131104 | tf_op jit(solution)/shard_map/while/body/eval_jaxpr/all_to_all | solution.py:26
  243.4 11.1 %collective-permute-start.3 = (bf16[512,512]{1,0:T(8,128)(2,1)}, bf16[512,512]{1,0:T(8,128)(2,1)}, u32[]{:S(2)}, u32[]{:S(2)}) collective-permute-start(bf16[512,512]{1,0:T(8,128)(2,1)} %param.17), channel_id=1, source_target_pairs={{0,4},{4,0},{1,5},{5,1},{2,6},{6,2},{3,7},{7,3},{8,12},{12,8},{9,1... | collective-permute-start | bytes 1572872 | tf_op jit(solution)/shard_map/ppermute | solution.py:35
  258.7 9.5 %all-to-all-start.6 = ((f32[32,8,512]{2,1,0:T(8,128)}), f32[32,8,512]{2,1,0:T(8,128)S(1)}, u32[]{:S(2)}, u32[]{:S(2)}) async-start(f32[32,8,512]{2,1,0:T(8,128)} %bitcast.59), calls=%async_computation.6 | async-start | bytes 1048576 | tf_op jit(solution)/shard_map/all_to_all | solution.py:26
  268.4 11.2 %all-to-all-done.6 = f32[32,8,512]{2,1,0:T(8,128)S(1)} async-done(((f32[32,8,512]{2,1,0:T(8,128)}), f32[32,8,512]{2,1,0:T(8,128)S(1)}, u32[]{:S(2)}, u32[]{:S(2)}) %all-to-all-start.6) | async-done | bytes 524320 | tf_op jit(solution)/shard_map/all_to_all | solution.py:26
  280.4 7.0 %all-to-all-start.7 = ((bf16[32,8,512]{2,1,0:T(8,128)(2,1)}), bf16[32,8,512]{2,1,0:T(8,128)(2,1)S(1)}, u32[]{:S(2)}, u32[]{:S(2)}) async-start(bf16[32,8,512]{2,1,0:T(8,128)(2,1)} %broadcast_in_dim.39), calls=%async_computation.7 | async-start | bytes 524288 | tf_op jit(solution)/shard_map/all_to_all | solution.py:26
  289.8 7.3 %all-to-all-done.7 = bf16[32,8,512]{2,1,0:T(8,128)(2,1)S(1)} async-done(((bf16[32,8,512]{2,1,0:T(8,128)(2,1)}), bf16[32,8,512]{2,1,0:T(8,128)(2,1)S(1)}, u32[]{:S(2)}, u32[]{:S(2)}) %all-to-all-start.7) | async-done | bytes 262176 | tf_op jit(solution)/shard_map/all_to_all | solution.py:26
  297.1 8.0 %all-gather.1 = bf16[64,8,512]{2,1,0:T(8,128)(2,1)S(1)} all-gather(bf16[32,8,512]{2,1,0:T(8,128)(2,1)S(1)} %all-to-all-done.7), channel_id=3, replica_groups=mesh['y'=4,'z'=8,'c'=2,'x'=4] {'c'}, dimensions={0}, use_global_device_ids=true | all-gather | bytes 786432 | tf_op jit(solution)/shard_map/all_gather | solution.py:174
  (266 shorter events, 85.7 us)
Async XLA Ops:
  5.3 65.8 %copy-start.4 = (f32[512,128]{0,1:T(8,128)}, f32[512,128]{0,1:T(8,128)S(1)}, u32[]{:S(2)}) copy-start(f32[512,128]{0,1:T(8,128)S(1)} %copy.121) | copy-start | bytes 786436
  6.2 43.4 %copy-start.20 = (f32[128]{0:T(128)S(1)}, f32[128]{0:T(128)}, u32[]{:S(2)}) copy-start(f32[128]{0:T(128)} %param.14) | copy-start | bytes 1540
  6.4 4.4 %collective-permute-start.1 = (f32[32,3,4,128]{3,0,2,1:T(8,128)S(1)}, f32[32,3,4,128]{3,0,2,1:T(8,128)S(1)}, u32[]{:S(2)}, u32[]{:S(2)}) collective-permute-start(f32[32,3,4,128]{3,0,2,1:T(8,128)S(1)} %bitcast.259), channel_id=1, source_target_pairs={{0,4},{4,0},{1,5},{5,1},{2,6},{6,2},{3,7},{7,3},{8,12},{12,8},{9,1... | collective-permute-start | bytes 589832 | tf_op jit(solution)/shard_map/ppermute | solution.py:35
  10.8 39.1 %copy-start.9 = (bf16[512,256]{1,0:T(8,128)(2,1)S(1)}, bf16[512,256]{1,0:T(8,128)(2,1)}, u32[]{:S(2)}) copy-start(bf16[512,256]{1,0:T(8,128)(2,1)} %param.10) | copy-start | bytes 786436
  30.5 14.5 %all-to-all-start.2 = ((bf16[32,6,2,128]{3,2,1,0:T(2,128)(2,1)}), bf16[32,6,2,128]{3,2,1,0:T(2,128)(2,1)S(1)}, u32[]{:S(2)}, u32[]{:S(2)}) async-start(bf16[32,6,2,128]{3,2,1,0:T(2,128)(2,1)} %broadcast_in_dim.27), calls=%async_computation.2 | async-start | bytes 196608 | tf_op jit(solution)/shard_map/all_to_all | solution.py:26
  49.9 21.4 %copy-start.10 = (f32[512,128]{0,1:T(8,128)}, f32[512,128]{0,1:T(8,128)S(1)}, u32[]{:S(2)}) copy-start(f32[512,128]{0,1:T(8,128)S(1)} %get-tuple-element.116) | copy-start | bytes 786436
  50.2 21.5 %copy-start.12 = (f32[512,128]{0,1:T(8,128)}, f32[512,128]{0,1:T(8,128)S(1)}, u32[]{:S(2)}) copy-start(f32[512,128]{0,1:T(8,128)S(1)} %get-tuple-element.114) | copy-start | bytes 786436
  71.7 18.7 %copy-start.21 = (f32[512]{0:T(512)S(1)}, f32[512]{0:T(512)}, u32[]{:S(2)}) copy-start(f32[512]{0:T(512)} %param.16) | copy-start | bytes 6148
  88.5 4.9 %collective-permute-start.2 = (bf16[4,1024,128]{2,1,0:T(8,128)(2,1)S(1)}, bf16[4,1024,128]{2,1,0:T(8,128)(2,1)S(1)}, u32[]{:S(2)}, u32[]{:S(2)}) collective-permute-start(bf16[4,1024,128]{2,1,0:T(8,128)(2,1)S(1)} %slice.165), channel_id=1, source_target_pairs={{0,4},{4,0},{1,5},{5,1},{2,6},{6,2},{3,7},{7,3},{8,12},{12,8},{9,1... | collective-permute-start | bytes 3145736 | tf_op jit(solution)/shard_map/ppermute | solution.py:35
  90.5 2.3 collective-permute-start
  98.3 13.0 %all-to-all-start = ((f32[32,8,128]{2,1,0:T(8,128)}), f32[32,8,128]{2,1,0:T(8,128)S(1)}, u32[]{:S(2)}, u32[]{:S(2)}) async-start(f32[32,8,128]{2,1,0:T(8,128)} %broadcast_in_dim.43), calls=%async_computation | async-start | bytes 262144 | tf_op jit(solution)/shard_map/while/body/eval_jaxpr/all_to_all | solution.py:26
  113.9 13.7 %all-to-all-start = ((f32[32,8,128]{2,1,0:T(8,128)}), f32[32,8,128]{2,1,0:T(8,128)S(1)}, u32[]{:S(2)}, u32[]{:S(2)}) async-start(f32[32,8,128]{2,1,0:T(8,128)} %broadcast_in_dim.43), calls=%async_computation | async-start | bytes 262144 | tf_op jit(solution)/shard_map/while/body/eval_jaxpr/all_to_all | solution.py:26
  130.1 13.0 %all-to-all-start = ((f32[32,8,128]{2,1,0:T(8,128)}), f32[32,8,128]{2,1,0:T(8,128)S(1)}, u32[]{:S(2)}, u32[]{:S(2)}) async-start(f32[32,8,128]{2,1,0:T(8,128)} %broadcast_in_dim.43), calls=%async_computation | async-start | bytes 262144 | tf_op jit(solution)/shard_map/while/body/eval_jaxpr/all_to_all | solution.py:26
  145.6 13.0 %all-to-all-start = ((f32[32,8,128]{2,1,0:T(8,128)}), f32[32,8,128]{2,1,0:T(8,128)S(1)}, u32[]{:S(2)}, u32[]{:S(2)}) async-start(f32[32,8,128]{2,1,0:T(8,128)} %broadcast_in_dim.43), calls=%async_computation | async-start | bytes 262144 | tf_op jit(solution)/shard_map/while/body/eval_jaxpr/all_to_all | solution.py:26
  161.1 13.0 %all-to-all-start = ((f32[32,8,128]{2,1,0:T(8,128)}), f32[32,8,128]{2,1,0:T(8,128)S(1)}, u32[]{:S(2)}, u32[]{:S(2)}) async-start(f32[32,8,128]{2,1,0:T(8,128)} %broadcast_in_dim.43), calls=%async_computation | async-start | bytes 262144 | tf_op jit(solution)/shard_map/while/body/eval_jaxpr/all_to_all | solution.py:26
  176.7 13.0 %all-to-all-start = ((f32[32,8,128]{2,1,0:T(8,128)}), f32[32,8,128]{2,1,0:T(8,128)S(1)}, u32[]{:S(2)}, u32[]{:S(2)}) async-start(f32[32,8,128]{2,1,0:T(8,128)} %broadcast_in_dim.43), calls=%async_computation | async-start | bytes 262144 | tf_op jit(solution)/shard_map/while/body/eval_jaxpr/all_to_all | solution.py:26
  192.2 13.0 %all-to-all-start = ((f32[32,8,128]{2,1,0:T(8,128)}), f32[32,8,128]{2,1,0:T(8,128)S(1)}, u32[]{:S(2)}, u32[]{:S(2)}) async-start(f32[32,8,128]{2,1,0:T(8,128)} %broadcast_in_dim.43), calls=%async_computation | async-start | bytes 262144 | tf_op jit(solution)/shard_map/while/body/eval_jaxpr/all_to_all | solution.py:26
  207.8 13.0 %all-to-all-start = ((f32[32,8,128]{2,1,0:T(8,128)}), f32[32,8,128]{2,1,0:T(8,128)S(1)}, u32[]{:S(2)}, u32[]{:S(2)}) async-start(f32[32,8,128]{2,1,0:T(8,128)} %broadcast_in_dim.43), calls=%async_computation | async-start | bytes 262144 | tf_op jit(solution)/shard_map/while/body/eval_jaxpr/all_to_all | solution.py:26
  223.3 13.0 %all-to-all-start = ((f32[32,8,128]{2,1,0:T(8,128)}), f32[32,8,128]{2,1,0:T(8,128)S(1)}, u32[]{:S(2)}, u32[]{:S(2)}) async-start(f32[32,8,128]{2,1,0:T(8,128)} %broadcast_in_dim.43), calls=%async_computation | async-start | bytes 262144 | tf_op jit(solution)/shard_map/while/body/eval_jaxpr/all_to_all | solution.py:26
  239.5 15.1 %all-to-all-start.5 = ((f32[32,8,128]{2,1,0:T(8,128)}), f32[32,8,128]{2,1,0:T(8,128)S(1)}, u32[]{:S(2)}, u32[]{:S(2)}) async-start(f32[32,8,128]{2,1,0:T(8,128)} %broadcast_in_dim.38), calls=%async_computation.5 | async-start | bytes 262144 | tf_op jit(solution)/shard_map/all_to_all | solution.py:26
  243.4 13.0 %collective-permute-start.3 = (bf16[512,512]{1,0:T(8,128)(2,1)}, bf16[512,512]{1,0:T(8,128)(2,1)}, u32[]{:S(2)}, u32[]{:S(2)}) collective-permute-start(bf16[512,512]{1,0:T(8,128)(2,1)} %param.17), channel_id=1, source_target_pairs={{0,4},{4,0},{1,5},{5,1},{2,6},{6,2},{3,7},{7,3},{8,12},{12,8},{9,1... | collective-permute-start | bytes 1572872 | tf_op jit(solution)/shard_map/ppermute | solution.py:35
  258.7 21.0 %all-to-all-start.6 = ((f32[32,8,512]{2,1,0:T(8,128)}), f32[32,8,512]{2,1,0:T(8,128)S(1)}, u32[]{:S(2)}, u32[]{:S(2)}) async-start(f32[32,8,512]{2,1,0:T(8,128)} %bitcast.59), calls=%async_computation.6 | async-start | bytes 1048576 | tf_op jit(solution)/shard_map/all_to_all | solution.py:26
  268.2 21.4 %copy-start.3 = (bf16[4,1027,128]{2,1,0:T(8,128)(2,1)S(1)}, bf16[4,1027,128]{2,1,0:T(8,128)(2,1)}, u32[]{:S(2)}) copy-start(bf16[4,1027,128]{2,1,0:T(8,128)(2,1)} %copy-done.2) | copy-start | bytes 3154948
  280.4 16.7 %all-to-all-start.7 = ((bf16[32,8,512]{2,1,0:T(8,128)(2,1)}), bf16[32,8,512]{2,1,0:T(8,128)(2,1)S(1)}, u32[]{:S(2)}, u32[]{:S(2)}) async-start(bf16[32,8,512]{2,1,0:T(8,128)(2,1)} %broadcast_in_dim.39), calls=%async_computation.7 | async-start | bytes 524288 | tf_op jit(solution)/shard_map/all_to_all | solution.py:26
  (16 other events, 108.8 us)

commit v3 on v2

--- a/solution.py
+++ b/solution.py
@@ -1,6 +1,8 @@
 import jax
 import jax.numpy as jnp
 from jax import lax
+from jax.experimental import pallas as pl
+from jax.experimental.pallas import tpu as pltpu
 from jax.sharding import Mesh
 from jax.sharding import PartitionSpec as P
 
@@ -50,6 +52,86 @@
 def join3(rows):
     parts = rows.astype(F32)
     return parts[..., 0, :] + (parts[..., 1, :] + parts[..., 2, :])
+
+
+def stack3(value):
+    high = value.astype(BF16).astype(F32)
+    rest = value - high
+    middle = rest.astype(BF16).astype(F32)
+    return jnp.concatenate([high, middle, rest - middle], axis=0)
+
+
+def one_row(stacked, row, period):
+    index = lax.broadcasted_iota(jnp.int32, stacked.shape, 0) % period
+    return jnp.where(index == row, stacked, 0.0).astype(BF16)
+
+
+def new_scalings(ranks, got_ref, v_ref, log_ref):
+    t = jnp.sum(got_ref[...], axis=0)
+    passed = jnp.log(v_ref[...] * t)
+    weights = jnp.exp((log_ref[...] + passed[:ranks] + passed[ranks:]) / 3.0)
+    return jnp.concatenate([weights, weights], axis=0) / t, weights
+
+
+def send_columns(ranks, rows, v, mass_ref, own_ref, other_ref, sent_ref, u_ref):
+    v_stack = stack3(v)
+    sums = []
+    for kern_ref in (own_ref, other_ref):
+        for side in range(2):
+            total = None
+            for block in range(ranks):
+                part = lax.dot_general(
+                    one_row(v_stack, side * ranks + block, 2 * ranks),
+                    kern_ref[block, pl.ds(side * rows, rows), :],
+                    (((1,), (1,)), ((), ())),
+                    preferred_element_type=F32,
+                )
+                total = part if total is None else total + part
+            sums.append(jnp.sum(total, axis=0, keepdims=True))
+    s = jnp.concatenate(sums, axis=0)
+    u = jnp.exp(POWER * jnp.log(mass_ref[...] / s))
+    u_ref[...] = u
+    u_stack = stack3(u)
+    columns = []
+    for side in range(2):
+        picked = [one_row(u_stack, 2 * member + side, 4) for member in range(2)]
+        for block in range(ranks):
+            total = None
+            for member, kern_ref in enumerate((own_ref, other_ref)):
+                part = lax.dot_general(
+                    picked[member],
+                    kern_ref[block, pl.ds(side * rows, rows), :],
+                    (((1,), (0,)), ((), ())),
+                    preferred_element_type=F32,
+                )
+                total = part if total is None else total + part
+            columns.append(jnp.sum(total, axis=0, keepdims=True))
+    part = jnp.concatenate(columns, axis=0)
+    sent_ref[...] = jnp.broadcast_to(part[None], sent_ref.shape).astype(sent_ref.dtype)
+
+
+def first_pass(mass_ref, own_ref, other_ref, sent_ref, u_ref):
+    ranks = own_ref.shape[0]
+    rows = other_ref.shape[1] // 2
+    ones = jnp.ones((2 * ranks, own_ref.shape[2]), F32)
+    send_columns(ranks, rows, ones, mass_ref, own_ref, other_ref, sent_ref, u_ref)
+
+
+def next_pass(got_ref, v_ref, log_ref, mass_ref, own_ref, other_ref, sent_ref, u_ref, new_ref):
+    ranks = own_ref.shape[0]
+    rows = other_ref.shape[1] // 2
+    v, _ = new_scalings(ranks, got_ref, v_ref, log_ref)
+    new_ref[...] = v
+    send_columns(ranks, rows, v, mass_ref, own_ref, other_ref, sent_ref, u_ref)
+
+
+def on_chip(kernel, shapes, name):
+    return pl.pallas_call(
+        kernel,
+        out_shape=tuple(jax.ShapeDtypeStruct(shape, dtype) for shape, dtype in shapes),
+        compiler_params=pltpu.CompilerParams(vmem_limit_bytes=32 << 20),
+        name=name,
+    )
 
 
 def shards(x_emb, y_emb, q_factor, r_factor, g_weights, a_mass, b_mass, expr):
@@ -66,7 +148,7 @@
     core = lax.axis_index("c")
     other_expr = swap(expr)
     masses = jnp.stack([a_mass, b_mass])
-    masses = jnp.stack([masses, swap(masses)])
+    masses = jnp.concatenate([masses, swap(masses)])
     norms_one = jnp.sum(jnp.square(x_emb.astype(F32)), axis=1)
     norms_two = jnp.sum(jnp.square(y_emb.astype(F32)), axis=1)
     part_xq = contract_rows(x_emb, q_factor.astype(BF16)).reshape(2, others, share, width)
@@ -141,35 +223,35 @@
     log_g = jnp.log(join3(mine[:, 2 * rows :]))
     mine_q = mine[:, :rows]
     kerns = mine[:, : 2 * rows]
-    pair = jnp.stack([kerns, swap(kerns)]).reshape(2, ranks, 2, rows, width)
-    flat = jnp.ones((2, ranks, width), F32)
-
-    def one_pass(v):
-        s = jnp.sum(pair.astype(F32) * v.transpose(1, 0, 2)[None, :, :, None, :], axis=(1, 4))
-        u = (masses / s) ** POWER
-        parts = jnp.sum(pair.astype(F32) * u[:, None, :, :, None], axis=3)
-        part = (parts[0] + parts[1]).transpose(1, 0, 2).reshape(2 * ranks, width)
-        t = jnp.sum(to_all(part, CHIPS), axis=0).reshape(2, ranks, width)
-        weights = jnp.exp((log_g + jnp.log(v[0] * t[0]) + jnp.log(v[1] * t[1])) / 3.0)
-        return weights[None] / t, weights, u
-
-    v = lax.fori_loop(0, PASSES - 1, lambda step, v: one_pass(v)[0], flat)
-    (v_q, v_r), weights, u = one_pass(v)
-
-    q_new = u[0, 0][:, None] * kern_q * pick(v_q, here)[None, :]
-    r_new = u[0, 1][:, None] * kern_r * pick(v_r, here)[None, :]
+    theirs = swap(kerns)
+    sent_shape = ((others, 2 * ranks, width), F32)
+    u_shape = ((4, rows), F32)
+    v_shape = ((2 * ranks, width), F32)
+    sent, u = on_chip(first_pass, (sent_shape, u_shape), "first_pass")(masses, kerns, theirs)
+    v = jnp.ones(v_shape[0], F32)
+    for step in range(1, PASSES):
+        sent, u, v = on_chip(next_pass, (sent_shape, u_shape, v_shape), "next_pass")(
+            exchange(sent, CHIPS), v, log_g, masses, kerns, theirs
+        )
+    t = jnp.sum(exchange(sent, CHIPS), axis=0)
+    passed = jnp.log(v * t)
+    weights = jnp.exp((log_g + passed[:ranks] + passed[ranks:]) / 3.0)
+    v_q, v_r = weights / t[:ranks], weights / t[ranks:]
+
+    q_new = u[0][:, None] * kern_q * pick(v_q, here)[None, :]
+    r_new = u[1][:, None] * kern_r * pick(v_r, here)[None, :]
     s_q = jnp.sum(mine_q.astype(F32) * v_q[:, None, :], axis=(0, 2))
     scaled = (mine_q.astype(F32) * (v_q / weights)[:, None, :]).astype(BF16)
 
     half = ranks // 2
     half_v = lax.dynamic_slice_in_dim(v_r, core * half, half, 0)
 
-    def product(member, cells):
-        kern = lax.dynamic_slice_in_dim(pair[member, :, 1], core * half, half, 0)
-        right = (kern.astype(F32) * half_v[:, None, :] * u[member, 1][None, :, None]).astype(BF16)
+    def product(kern, u_cells, cells):
+        kern = lax.dynamic_slice_in_dim(kern[:, rows:], core * half, half, 0)
+        right = (kern.astype(F32) * half_v[:, None, :] * u_cells[None, :, None]).astype(BF16)
         return lax.dot_general(right, cells, (((1,), (0,)), ((), ())), preferred_element_type=F32)
 
-    part = product(0, expr) + product(1, other_expr)
+    part = product(kerns, u[1], expr) + product(theirs, u[3], other_expr)
     piece = jnp.sum(exchange(part.reshape(others, -1, genes), CHIPS), axis=0)
     profiles = lax.all_gather(to_all(piece.astype(BF16), CHIPS), "c").reshape(ranks, width, genes)
     mixed = lax.dot_general(

time: 308 us -> 291 us (0.945)
  blocking collectives: 66.7 us -> 167 us
  waiting for transfers between devices: 113 us -> 40 us
  starting transfers between devices: 77.8 us -> 48.1 us
  other arithmetic: 24.1 us -> 2.71 us
  Pallas kernels: 0 us -> 17.5 us
  local copies, waits for them, and re-layouts: 14.7 us -> 6.96 us
    all_to_all x3 -> x11, blocking collectives: 54.4 us -> 155 us  [exchange(): return lax.all_to_all(chunks, axes, 0, 0, tiled=False)]
    all_to_all x13 -> x5, waiting for transfers between devices: 110 us -> 37 us  [exchange(): return lax.all_to_all(chunks, axes, 0, 0, tiled=False)]
    all_to_all x13 -> x5, starting transfers between devices: 61.2 us -> 30.3 us  [exchange(): return lax.all_to_all(chunks, axes, 0, 0, tiled=False)]
    pallas_call x0 -> x10, Pallas kernels: none -> 17.5 us  [the longest x9 15.6 us: shards(): on_chip(next_pass, (sent_shape, u_shape, v_shape), 'next_pass')]
    reduce_sum x30 -> x1, other arithmetic: 11.6 us -> 0.04 us  [shards(): t = jnp.sum(exchange(sent, CHIPS), axis=0)]
    broadcast_in_dim x15 -> x5, local copies, waits for them, and re-layouts: 8.29 us -> 1.65 us  [to_all(): return exchange(jnp.broadcast_to(value[None], (count,) + value.shape), axes)]
    pow x10 -> x0, other arithmetic: 6.58 us -> none  [one_pass(): u = (masses / s) ** POWER]
  transfers between devices with their start and end apart: 17 -> 9, of which waited for: 15 -> 7; matrix products, arithmetic and copies ran while one was open for 2% -> 1% of each run, Pallas kernels for 0% -> 0%
where the time goes in v3:
time: 291 us; the launch traced here: 290 us
  blocking collectives  167 us (57%)
  starting transfers between devices  48.1 us (17%)
  waiting for transfers between devices  40 us (14%)
  Pallas kernels  17.5 us (6%)
  local copies, waits for them, and re-layouts  6.96 us (2%)
  matrix products  6.28 us (2%)
    all_to_all x11, blocking collectives, exchange(): return lax.all_to_all(chunks, axes, 0, 0, tiled=False)  155 us
    all_to_all x5, waiting for transfers between devices, exchange(): return lax.all_to_all(chunks, axes, 0, 0, tiled=False)  37 us
    all_to_all x5, starting transfers between devices, exchange(): return lax.all_to_all(chunks, axes, 0, 0, tiled=False)  30.3 us
    ppermute x4, starting transfers between devices, swap(): return lax.ppermute(value, 'c', [(0, 1), (1, 0)])  17.9 us
    pallas_call x9, Pallas kernels, shards(): on_chip(next_pass, (sent_shape, u_shape, v_shape), 'next_pass')  15.6 us
    all_gather x1, blocking collectives, shards(): lax.all_gather(to_all(piece.astype(BF16), CHIPS), 'c')  7.14 us
  transfers between devices with their start and end apart: 9, of which 7 were waited for; matrix products, arithmetic and copies ran while one was open for 1% of the time, Pallas kernels for 0%

profile of v3, /device:TPU:1, one launch (start us, length us, event | category | flops | bytes accessed | tf_op | source)
XLA Modules:
  0.0 290.3 jit_solution(15575587403124608681)
XLA Ops:
  4.6 3.3 %collective-permute-start.1 = (f32[32,3,4,128]{3,0,2,1:T(8,128)S(1)}, f32[32,3,4,128]{3,0,2,1:T(8,128)S(1)}, u32[]{:S(2)}, u32[]{:S(2)}) collective-permute-start(f32[32,3,4,128]{3,0,2,1:T(8,128)S(1)} %bitcast.117), channel_id=1, source_target_pairs={{0,4},{4,0},{1,5},{5,1},{2,6},{6,2},{3,7},{7,3},{8,12},{12,8},{9,1... | collective-permute-start | bytes 589832 | tf_op jit(solution)/shard_map/ppermute | solution.py:37
  9.2 18.7 %all_to_all.80 = f32[32,3,4,128]{3,2,1,0:T(4,128)S(1)} all-to-all(f32[32,3,4,128]{3,2,1,0:T(4,128)S(1)} %copy.94), channel_id=1, replica_groups=mesh['y'=4,'z'=8,'c'=2,'x'=4] {'y','z'}, dimensions={0} | all-to-all | bytes 393216 | tf_op jit(solution)/shard_map/all_to_all | solution.py:28
  28.7 5.5 %all-to-all-start.1 = ((bf16[32,6,2,128]{3,2,1,0:T(2,128)(2,1)}), bf16[32,6,2,128]{3,2,1,0:T(2,128)(2,1)S(1)}, u32[]{:S(2)}, u32[]{:S(2)}) async-start(bf16[32,6,2,128]{3,2,1,0:T(2,128)(2,1)} %broadcast_in_dim.19), calls=%async_computation.1 | async-start | bytes 196608 | tf_op jit(solution)/shard_map/all_to_all | solution.py:28
  34.2 9.0 %all-to-all-done.1 = bf16[32,6,2,128]{3,2,1,0:T(2,128)(2,1)S(1)} async-done(((bf16[32,6,2,128]{3,2,1,0:T(2,128)(2,1)}), bf16[32,6,2,128]{3,2,1,0:T(2,128)(2,1)S(1)}, u32[]{:S(2)}, u32[]{:S(2)}) %all-to-all-start.1) | async-done | bytes 98336 | tf_op jit(solution)/shard_map/all_to_all | solution.py:28
  43.3 4.3 %all-gather = bf16[64,6,2,128]{3,0,2,1:T(8,128)(2,1)S(1)} all-gather(bf16[32,6,2,128]{3,0,2,1:T(8,128)(2,1)S(1)} %copy.95), channel_id=2, replica_groups=mesh['y'=4,'z'=8,'c'=2,'x'=4] {'c'}, dimensions={0}, use_global_device_ids=true | all-gather | bytes 294912 | tf_op jit(solution)/shard_map/all_gather | solution.py:185
  48.6 19.0 %all_to_all.81 = f32[256,1,128]{2,1,0:T(1,128)S(1)} all-to-all(f32[256,1,128]{2,1,0:T(1,128)S(1)} %broadcast_in_dim.20), channel_id=1, replica_groups=mesh['y'=4,'z'=8,'c'=2,'x'=4] {'y','z','c','x'}, dimensions={0} | all-to-all | bytes 262144 | tf_op jit(solution)/shard_map/all_to_all | solution.py:28
  69.9 16.7 %all_to_all.82 = bf16[4,1027,128]{2,1,0:T(8,128)(2,1)S(1)} all-to-all(bf16[4,1027,128]{2,1,0:T(8,128)(2,1)S(1)} %broadcast_in_dim.21), channel_id=1, replica_groups=mesh['y'=4,'z'=8,'c'=2,'x'=4] {'x'}, dimensions={0} | all-to-all | bytes 2103296 | tf_op jit(solution)/shard_map/all_to_all | solution.py:28
  92.9 3.9 %all-to-all-start.4 = ((f32[32,8,128]{2,1,0:T(8,128)}), f32[32,8,128]{2,1,0:T(8,128)S(1)}, u32[]{:S(2)}, u32[]{:S(2)}) async-start(f32[32,8,128]{2,1,0:T(8,128)} %get-tuple-element.24), calls=%async_computation.4 | async-start | bytes 262144 | tf_op jit(solution)/shard_map/all_to_all | solution.py:28
  96.8 9.1 %all-to-all-done.4.got_ref = f32[32,8,128]{2,1,0:T(8,128)S(1)} async-done(((f32[32,8,128]{2,1,0:T(8,128)}), f32[32,8,128]{2,1,0:T(8,128)S(1)}, u32[]{:S(2)}, u32[]{:S(2)}) %all-to-all-start.4) | async-done | bytes 131104 | tf_op jit(solution)/shard_map/all_to_all | solution.py:28
  107.6 13.4 %all_to_all.83.got_ref = f32[32,8,128]{2,1,0:T(8,128)S(1)} all-to-all(f32[32,8,128]{2,1,0:T(8,128)S(1)} %get-tuple-element.25), channel_id=1, replica_groups=mesh['y'=4,'z'=8,'c'=2,'x'=4] {'y','z'}, dimensions={0} | all-to-all | bytes 262144 | tf_op jit(solution)/shard_map/all_to_all | solution.py:28
  122.8 12.7 %all_to_all.84.got_ref = f32[32,8,128]{2,1,0:T(8,128)S(1)} all-to-all(f32[32,8,128]{2,1,0:T(8,128)S(1)} %get-tuple-element.27), channel_id=1, replica_groups=mesh['y'=4,'z'=8,'c'=2,'x'=4] {'y','z'}, dimensions={0} | all-to-all | bytes 262144 | tf_op jit(solution)/shard_map/all_to_all | solution.py:28
  137.2 12.7 %all_to_all.85.got_ref = f32[32,8,128]{2,1,0:T(8,128)S(1)} all-to-all(f32[32,8,128]{2,1,0:T(8,128)S(1)} %get-tuple-element.29), channel_id=1, replica_groups=mesh['y'=4,'z'=8,'c'=2,'x'=4] {'y','z'}, dimensions={0} | all-to-all | bytes 262144 | tf_op jit(solution)/shard_map/all_to_all | solution.py:28
  151.6 12.6 %all_to_all.86.got_ref = f32[32,8,128]{2,1,0:T(8,128)S(1)} all-to-all(f32[32,8,128]{2,1,0:T(8,128)S(1)} %get-tuple-element.31), channel_id=1, replica_groups=mesh['y'=4,'z'=8,'c'=2,'x'=4] {'y','z'}, dimensions={0} | all-to-all | bytes 262144 | tf_op jit(solution)/shard_map/all_to_all | solution.py:28
  165.9 12.4 %all_to_all.87.got_ref = f32[32,8,128]{2,1,0:T(8,128)S(1)} all-to-all(f32[32,8,128]{2,1,0:T(8,128)S(1)} %get-tuple-element.33), channel_id=1, replica_groups=mesh['y'=4,'z'=8,'c'=2,'x'=4] {'y','z'}, dimensions={0} | all-to-all | bytes 262144 | tf_op jit(solution)/shard_map/all_to_all | solution.py:28
  180.0 12.4 %all_to_all.88.got_ref = f32[32,8,128]{2,1,0:T(8,128)S(1)} all-to-all(f32[32,8,128]{2,1,0:T(8,128)S(1)} %get-tuple-element.35), channel_id=1, replica_groups=mesh['y'=4,'z'=8,'c'=2,'x'=4] {'y','z'}, dimensions={0} | all-to-all | bytes 262144 | tf_op jit(solution)/shard_map/all_to_all | solution.py:28
  194.2 12.4 %all_to_all.89.got_ref = f32[32,8,128]{2,1,0:T(8,128)S(1)} all-to-all(f32[32,8,128]{2,1,0:T(8,128)S(1)} %get-tuple-element.37), channel_id=1, replica_groups=mesh['y'=4,'z'=8,'c'=2,'x'=4] {'y','z'}, dimensions={0} | all-to-all | bytes 262144 | tf_op jit(solution)/shard_map/all_to_all | solution.py:28
  208.3 12.4 %all_to_all.90.got_ref = f32[32,8,128]{2,1,0:T(8,128)S(1)} all-to-all(f32[32,8,128]{2,1,0:T(8,128)S(1)} %get-tuple-element.39), channel_id=1, replica_groups=mesh['y'=4,'z'=8,'c'=2,'x'=4] {'y','z'}, dimensions={0} | all-to-all | bytes 262144 | tf_op jit(solution)/shard_map/all_to_all | solution.py:28
  222.6 3.9 %all-to-all-start.13 = ((f32[32,8,128]{2,1,0:T(8,128)}), f32[32,8,128]{2,1,0:T(8,128)S(1)}, u32[]{:S(2)}, u32[]{:S(2)}) async-start(f32[32,8,128]{2,1,0:T(8,128)} %get-tuple-element.43), calls=%async_computation.13 | async-start | bytes 262144 | tf_op jit(solution)/shard_map/all_to_all | solution.py:28
  226.5 11.9 %collective-permute-start.3 = (bf16[512,512]{1,0:T(8,128)(2,1)}, bf16[512,512]{1,0:T(8,128)(2,1)}, u32[]{:S(2)}, u32[]{:S(2)}) collective-permute-start(bf16[512,512]{1,0:T(8,128)(2,1)} %param.15), channel_id=1, source_target_pairs={{0,4},{4,0},{1,5},{5,1},{2,6},{6,2},{3,7},{7,3},{8,12},{12,8},{9,1... | collective-permute-start | bytes 1572872 | tf_op jit(solution)/shard_map/ppermute | solution.py:37
  242.6 9.5 %all-to-all-start.14 = ((f32[32,8,512]{2,1,0:T(8,128)}), f32[32,8,512]{2,1,0:T(8,128)S(1)}, u32[]{:S(2)}, u32[]{:S(2)}) async-start(f32[32,8,512]{2,1,0:T(8,128)} %bitcast.37), calls=%async_computation.14 | async-start | bytes 1048576 | tf_op jit(solution)/shard_map/all_to_all | solution.py:28
  252.2 11.7 %all-to-all-done.14 = f32[32,8,512]{2,1,0:T(8,128)S(1)} async-done(((f32[32,8,512]{2,1,0:T(8,128)}), f32[32,8,512]{2,1,0:T(8,128)S(1)}, u32[]{:S(2)}, u32[]{:S(2)}) %all-to-all-start.14) | async-done | bytes 524320 | tf_op jit(solution)/shard_map/all_to_all | solution.py:28
  264.7 7.6 %all-to-all-start.15 = ((bf16[32,8,512]{2,1,0:T(8,128)(2,1)}), bf16[32,8,512]{2,1,0:T(8,128)(2,1)S(1)}, u32[]{:S(2)}, u32[]{:S(2)}) async-start(bf16[32,8,512]{2,1,0:T(8,128)(2,1)} %broadcast_in_dim.23), calls=%async_computation.15 | async-start | bytes 524288 | tf_op jit(solution)/shard_map/all_to_all | solution.py:28
  274.8 7.2 %all-to-all-done.15 = bf16[32,8,512]{2,1,0:T(8,128)(2,1)S(1)} async-done(((bf16[32,8,512]{2,1,0:T(8,128)(2,1)}), bf16[32,8,512]{2,1,0:T(8,128)(2,1)S(1)}, u32[]{:S(2)}, u32[]{:S(2)}) %all-to-all-start.15) | async-done | bytes 262176 | tf_op jit(solution)/shard_map/all_to_all | solution.py:28
  282.0 7.1 %all-gather.1 = bf16[64,8,512]{2,1,0:T(8,128)(2,1)S(1)} all-gather(bf16[32,8,512]{2,1,0:T(8,128)(2,1)S(1)} %all-to-all-done.15), channel_id=3, replica_groups=mesh['y'=4,'z'=8,'c'=2,'x'=4] {'c'}, dimensions={0}, use_global_device_ids=true | all-gather | bytes 786432 | tf_op jit(solution)/shard_map/all_gather | solution.py:256
  (132 shorter events, 39.1 us)
Async XLA Ops:
  0.6 2.6 copy-start.10
  0.6 2.8 copy-start.8
  0.7 2.9 copy-start.9
  1.8 67.6 %copy-start.3 = (f32[512,128]{0,1:T(8,128)}, f32[512,128]{0,1:T(8,128)S(1)}, u32[]{:S(2)}) copy-start(f32[512,128]{0,1:T(8,128)S(1)} %copy.99) | copy-start | bytes 786436
  3.6 65.8 %copy-start.5 = (f32[512,128]{0,1:T(8,128)}, f32[512,128]{0,1:T(8,128)S(1)}, u32[]{:S(2)}) copy-start(f32[512,128]{0,1:T(8,128)S(1)} %copy.92) | copy-start | bytes 786436
  4.6 4.4 %collective-permute-start.1 = (f32[32,3,4,128]{3,0,2,1:T(8,128)S(1)}, f32[32,3,4,128]{3,0,2,1:T(8,128)S(1)}, u32[]{:S(2)}, u32[]{:S(2)}) collective-permute-start(f32[32,3,4,128]{3,0,2,1:T(8,128)S(1)} %bitcast.117), channel_id=1, source_target_pairs={{0,4},{4,0},{1,5},{5,1},{2,6},{6,2},{3,7},{7,3},{8,12},{12,8},{9,1... | collective-permute-start | bytes 589832 | tf_op jit(solution)/shard_map/ppermute | solution.py:37
  9.2 38.6 %copy-start.18 = (f32[128]{0:T(128)S(1)}, f32[128]{0:T(128)}, u32[]{:S(2)}) copy-start(f32[128]{0:T(128)} %param.12) | copy-start | bytes 1540
  28.7 14.5 %all-to-all-start.1 = ((bf16[32,6,2,128]{3,2,1,0:T(2,128)(2,1)}), bf16[32,6,2,128]{3,2,1,0:T(2,128)(2,1)S(1)}, u32[]{:S(2)}, u32[]{:S(2)}) async-start(bf16[32,6,2,128]{3,2,1,0:T(2,128)(2,1)} %broadcast_in_dim.19), calls=%async_computation.1 | async-start | bytes 196608 | tf_op jit(solution)/shard_map/all_to_all | solution.py:28
  48.1 21.3 %copy-start.13 = (f32[512,128]{0,1:T(8,128)}, f32[512,128]{0,1:T(8,128)S(1)}, u32[]{:S(2)}) copy-start(f32[512,128]{0,1:T(8,128)S(1)} %get-tuple-element.99) | copy-start | bytes 786436
  48.4 21.0 %copy-start.11 = (f32[512,128]{0,1:T(8,128)}, f32[512,128]{0,1:T(8,128)S(1)}, u32[]{:S(2)}) copy-start(f32[512,128]{0,1:T(8,128)S(1)} %get-tuple-element.97) | copy-start | bytes 786436
  86.6 151.8 %copy-start.1 = (bf16[4,1027,128]{2,1,0:T(8,128)(2,1)}, bf16[4,1027,128]{2,1,0:T(8,128)(2,1)S(1)}, u32[]{:S(2)}) copy-start(bf16[4,1027,128]{2,1,0:T(8,128)(2,1)S(1)} %all_to_all.82) | copy-start | bytes 3154948
  86.7 4.3 %collective-permute-start.2 = (bf16[4,1024,128]{2,1,0:T(8,128)(2,1)S(1)}, bf16[4,1024,128]{2,1,0:T(8,128)(2,1)S(1)}, u32[]{:S(2)}, u32[]{:S(2)}) collective-permute-start(bf16[4,1024,128]{2,1,0:T(8,128)(2,1)S(1)} %slice.124.own_ref), channel_id=1, source_target_pairs={{0,4},{4,0},{1,5},{5,1},{2,6},{6,2},{3,7},{7,3},{8,12},{12,8},{9,1... | collective-permute-start | bytes 3145736 | tf_op jit(solution)/shard_map/ppermute | solution.py:37
  88.7 2.3 collective-permute-start
  91.0 147.4 %copy-start = (bf16[4,1024,128]{2,1,0:T(8,128)(2,1)}, bf16[4,1024,128]{2,1,0:T(8,128)(2,1)S(1)}, u32[]{:S(2)}) copy-start(bf16[4,1024,128]{2,1,0:T(8,128)(2,1)S(1)} %collective-permute-done.2.other_ref) | copy-start | bytes 3145732
  92.9 13.0 %all-to-all-start.4 = ((f32[32,8,128]{2,1,0:T(8,128)}), f32[32,8,128]{2,1,0:T(8,128)S(1)}, u32[]{:S(2)}, u32[]{:S(2)}) async-start(f32[32,8,128]{2,1,0:T(8,128)} %get-tuple-element.24), calls=%async_computation.4 | async-start | bytes 262144 | tf_op jit(solution)/shard_map/all_to_all | solution.py:28
  222.6 15.8 %all-to-all-start.13 = ((f32[32,8,128]{2,1,0:T(8,128)}), f32[32,8,128]{2,1,0:T(8,128)S(1)}, u32[]{:S(2)}, u32[]{:S(2)}) async-start(f32[32,8,128]{2,1,0:T(8,128)} %get-tuple-element.43), calls=%async_computation.13 | async-start | bytes 262144 | tf_op jit(solution)/shard_map/all_to_all | solution.py:28
  226.5 13.7 %collective-permute-start.3 = (bf16[512,512]{1,0:T(8,128)(2,1)}, bf16[512,512]{1,0:T(8,128)(2,1)}, u32[]{:S(2)}, u32[]{:S(2)}) collective-permute-start(bf16[512,512]{1,0:T(8,128)(2,1)} %param.15), channel_id=1, source_target_pairs={{0,4},{4,0},{1,5},{5,1},{2,6},{6,2},{3,7},{7,3},{8,12},{12,8},{9,1... | collective-permute-start | bytes 1572872 | tf_op jit(solution)/shard_map/ppermute | solution.py:37
  240.2 11.9 %copy-start.6 = (f32[512,128]{0,1:T(8,128)S(1)}, f32[512,128]{0,1:T(8,128)}, u32[]{:S(2)}) copy-start(f32[512,128]{0,1:T(8,128)} %copy-done.5) | copy-start | bytes 786436
  240.2 11.9 %copy-start.14 = (f32[512,128]{0,1:T(8,128)S(1)}, f32[512,128]{0,1:T(8,128)}, u32[]{:S(2)}) copy-start(f32[512,128]{0,1:T(8,128)} %copy-done.13) | copy-start | bytes 786436
  242.6 21.3 %all-to-all-start.14 = ((f32[32,8,512]{2,1,0:T(8,128)}), f32[32,8,512]{2,1,0:T(8,128)S(1)}, u32[]{:S(2)}, u32[]{:S(2)}) async-start(f32[32,8,512]{2,1,0:T(8,128)} %bitcast.37), calls=%async_computation.14 | async-start | bytes 1048576 | tf_op jit(solution)/shard_map/all_to_all | solution.py:28
  252.2 20.9 %copy-start.4 = (f32[512,128]{0,1:T(8,128)S(1)}, f32[512,128]{0,1:T(8,128)}, u32[]{:S(2)}) copy-start(f32[512,128]{0,1:T(8,128)} %copy-done.3) | copy-start | bytes 786436
  252.2 20.9 %copy-start.12 = (f32[512,128]{0,1:T(8,128)S(1)}, f32[512,128]{0,1:T(8,128)}, u32[]{:S(2)}) copy-start(f32[512,128]{0,1:T(8,128)} %copy-done.11) | copy-start | bytes 786436
  264.7 9.9 %copy-start.2 = (bf16[4,1027,128]{2,1,0:T(8,128)(2,1)S(1)}, bf16[4,1027,128]{2,1,0:T(8,128)(2,1)}, u32[]{:S(2)}) copy-start(bf16[4,1027,128]{2,1,0:T(8,128)(2,1)} %copy-done.1) | copy-start | bytes 3154948
  264.7 17.3 %all-to-all-start.15 = ((bf16[32,8,512]{2,1,0:T(8,128)(2,1)}), bf16[32,8,512]{2,1,0:T(8,128)(2,1)S(1)}, u32[]{:S(2)}, u32[]{:S(2)}) async-start(bf16[32,8,512]{2,1,0:T(8,128)(2,1)} %broadcast_in_dim.23), calls=%async_computation.15 | async-start | bytes 524288 | tf_op jit(solution)/shard_map/all_to_all | solution.py:28
  (6 other events, 10.4 us)

commit v4 on v3

v4 whole, which is shorter than its diff:
```python
import jax
import jax.numpy as jnp
from jax import lax
from jax.experimental import pallas as pl
from jax.experimental.pallas import tpu as pltpu
from jax.sharding import Mesh
from jax.sharding import PartitionSpec as P

PASSES = 10
SCALE = 0.0625
GAMMA = 10.0
POWER = 0.8

CHIPS = ("y", "z")
CELLS = ("y", "z", "c")
EVERY = ("y", "z", "c", "x")
F32 = jnp.float32
BF16 = jnp.bfloat16


def contract_rows(left, right):
    return lax.dot_general(
        left, right, (((0,), (0,)), ((), ())), preferred_element_type=F32
    )


def exchange(chunks, axes):
    return lax.all_to_all(chunks, axes, 0, 0, tiled=False)


def to_all(value, axes):
    count = lax.axis_size(axes)
    return exchange(jnp.broadcast_to(value[None], (count,) + value.shape), axes)


def swap(value):
    return lax.ppermute(value, "c", [(0, 1), (1, 0)])


def pick(value, index):
    return lax.dynamic_index_in_dim(value, index, 0, keepdims=False)


def split3(value):
    high = lax.reduce_precision(value, 8, 7)
    rest = value - high
    middle = lax.reduce_precision(rest, 8, 7)
    low = lax.reduce_precision(rest - middle, 8, 7)
    return jnp.stack([high, middle, low]).astype(BF16)


def join3(rows):
    parts = rows.astype(F32)
    return parts[..., 0, :] + (parts[..., 1, :] + parts[..., 2, :])


def stack3(value):
    high = value.astype(BF16).astype(F32)
    rest = value - high
    middle = rest.astype(BF16).astype(F32)
    return jnp.concatenate([high, middle, rest - middle], axis=0).astype(BF16)


def sum_rows(value):
    return value[0:1] + (value[1:2] + value[2:3])


def in_lanes(blocks, first, count):
    return jnp.concatenate([blocks[first + i : first + i + 1] for i in range(count)], axis=1)


def in_rows(row, count):
    width = row.shape[1] // count
    return [row[:, i * width : (i + 1) * width] for i in range(count)]


def start_kernel(x_ref, y_ref, q_ref, r_ref, xq_ref, yr_ref, vec_ref):
    rows = []
    for emb_ref, factor_ref, cross_ref in ((x_ref, q_ref, xq_ref), (y_ref, r_ref, yr_ref)):
        factor = factor_ref[...]
        cross_ref[...] = contract_rows(emb_ref[...], factor.astype(BF16))
        norms = jnp.sum(jnp.square(emb_ref[...].astype(F32)), axis=1, keepdims=True)
        rows.append(jnp.sum(norms * factor, axis=0, keepdims=True))
        rows.append(jnp.sum(factor, axis=0, keepdims=True))
    vec_ref[...] = jnp.concatenate(rows, axis=0)


def chunk_kernel(got_ref, sent_ref, vec_ref):
    summed = jnp.sum(got_ref[...], axis=0)
    xq, yr = summed[0], summed[1]
    vec_ref[...] = summed[2]
    dot = jnp.sum(xq * yr, axis=0, keepdims=True)
    high = dot.astype(BF16).astype(F32)
    rest = dot - high
    middle = rest.astype(BF16).astype(F32)
    nothing = jnp.zeros((5, dot.shape[1]), F32)
    chunk = jnp.concatenate([xq, yr, high, middle, rest - middle, nothing], axis=0)
    sent_ref[...] = jnp.broadcast_to(chunk.astype(BF16)[None], sent_ref.shape)


def new_scalings(ranks, got_ref, v_ref, log_ref):
    t = jnp.sum(got_ref[...].astype(F32), axis=0)
    passed = jnp.log(v_ref[...] * t)
    weights = jnp.exp((log_ref[...] + passed[:ranks] + passed[ranks:]) / 3.0)
    return jnp.concatenate([weights, weights], axis=0) / t, weights


def send_columns(v, mass_ref, own_ref, other_ref, sent_ref, u_ref):
    ranks = own_ref.shape[0]
    rows = other_ref.shape[1] // 2

    def kern(member, side):
        kern_ref = (own_ref, other_ref)[member]
        blocks = [kern_ref[block, pl.ds(side * rows, rows), :] for block in range(ranks)]
        return jnp.concatenate(blocks, axis=1)

    v_rows = [stack3(in_lanes(v, side * ranks, ranks)) for side in range(2)]
    sums = []
    for member in range(2):
        for side in range(2):
            part = lax.dot_general(
                v_rows[side], kern(member, side), (((1,), (1,)), ((), ())),
                preferred_element_type=F32,
            )
            sums.append(sum_rows(part))
    u = jnp.exp(POWER * jnp.log(mass_ref[...] / jnp.concatenate(sums, axis=0)))
    u_ref[...] = u
    columns = []
    for side in range(2):
        total = None
        for member in range(2):
            row = 2 * member + side
            part = jnp.dot(
                stack3(u[row : row + 1]), kern(member, side), preferred_element_type=F32
            )
            total = part if total is None else total + part
        columns += in_rows(sum_rows(total), ranks)
    part = jnp.concatenate(columns, axis=0).astype(sent_ref.dtype)
    sent_ref[...] = jnp.broadcast_to(part[None], sent_ref.shape)


def first_pass(mass_ref, own_ref, other_ref, sent_ref, u_ref):
    ones = jnp.ones((2 * own_ref.shape[0], own_ref.shape[2]), F32)
    send_columns(ones, mass_ref, own_ref, other_ref, sent_ref, u_ref)


def next_pass(got_ref, v_ref, log_ref, mass_ref, own_ref, other_ref, sent_ref, u_ref, new_ref):
    v, _ = new_scalings(own_ref.shape[0], got_ref, v_ref, log_ref)
    new_ref[...] = v
    send_columns(v, mass_ref, own_ref, other_ref, sent_ref, u_ref)


def profile_kernel(
    core_ref, got_ref, v_ref, log_ref, u_ref, own_ref, other_ref, expr_ref, more_ref,
    part_ref, new_ref, weights_ref,
):
    ranks, _, width = own_ref.shape
    rows = other_ref.shape[1] // 2
    v, weights = new_scalings(ranks, got_ref, v_ref, log_ref)
    new_ref[...] = v
    weights_ref[...] = weights
    u_columns = jnp.concatenate([u_ref[...], u_ref[...]], axis=0).T
    half = ranks // 2
    for i in range(half):
        block = core_ref[0] * half + i
        scale = new_ref[pl.ds(ranks + block, 1), :]
        total = None
        for member, (kern_ref, cells_ref) in enumerate(((own_ref, expr_ref), (other_ref, more_ref))):
            kern = kern_ref[block, pl.ds(rows, rows), :].astype(F32)
            column = u_columns[:, 2 * member + 1 : 2 * member + 2]
            part = contract_rows((kern * scale * column).astype(BF16), cells_ref[...])
            total = part if total is None else total + part
        part_ref[pl.ds(i * width, width), :] = total


def on_chip(kernel, shapes, name, scalars=0, inputs=0):
    specs = {}
    if scalars:
        specs["in_specs"] = [pl.BlockSpec(memory_space=pltpu.SMEM)] * scalars + [
            pl.BlockSpec(memory_space=pltpu.VMEM)
        ] * inputs
    return pl.pallas_call(
        kernel,
        out_shape=tuple(jax.ShapeDtypeStruct(shape, dtype) for shape, dtype in shapes),
        **specs,
        compiler_params=pltpu.CompilerParams(vmem_limit_bytes=32 << 20),
        name=name,
    )


def shards(x_emb, y_emb, q_factor, r_factor, g_weights, a_mass, b_mass, expr):
    rows, width = q_factor.shape
    dim = x_emb.shape[1]
    genes = expr.shape[1]
    others = lax.axis_size(CHIPS)
    cell_devices = 2 * others
    ranks = lax.axis_size("x")
    cells_total = rows * cell_devices
    share = dim // cell_devices

    here = lax.axis_index("x")
    core = lax.axis_index("c")
    other_expr = swap(expr)
    masses = jnp.stack([a_mass, b_mass])
    masses = jnp.concatenate([masses, swap(masses)])
    norms_one = jnp.sum(jnp.square(x_emb.astype(F32)), axis=1)
    norms_two = jnp.sum(jnp.square(y_emb.astype(F32)), axis=1)
    part_xq, part_yr, part_vec = on_chip(
        start_kernel, (((dim, width), F32), ((dim, width), F32), ((4, width), F32)), "start"
    )(x_emb, y_emb, q_factor, r_factor)
    part_cross = jnp.concatenate(
        [part.reshape(2, others, share, width) for part in (part_xq, part_yr)], axis=2
    )

    def with_vec(cross):
        return jnp.concatenate(
            [cross, jnp.broadcast_to(part_vec[None], (others, 4, width))], axis=1
        ).reshape(others, (2 * share + 4) // 4, 4, width)

    outgoing = with_vec(pick(part_cross, core)) + swap(with_vec(pick(part_cross, 1 - core)))
    chunk_rows = 2 * share + 8
    sent, vec = on_chip(
        chunk_kernel, (((others, chunk_rows, width), BF16), ((4, width), F32)), "chunk"
    )(exchange(outgoing, CHIPS))
    xq_vec, cq_vec, yr_vec, cr_vec = (vec[i] for i in range(4))
    crosses = lax.all_gather(exchange(sent, CHIPS), "c").reshape(2 * others, chunk_rows, width)
    cross_xq = crosses[:, :share].reshape(dim, width)
    cross_yr = crosses[:, share : 2 * share].reshape(dim, width)
    cross_dot = jnp.sum(join3(crosses[:, 2 * share : 2 * share + 3]), axis=0)

    grad_q = (
        SCALE
        * (
            norms_one[:, None] * cr_vec[None, :]
            + yr_vec[None, :]
            - 2.0 * jnp.dot(x_emb, cross_yr, preferred_element_type=F32)
        )
        / g_weights[None, :]
    )
    grad_r = (
        SCALE
        * (
            norms_two[:, None] * cq_vec[None, :]
            + xq_vec[None, :]
            - 2.0 * jnp.dot(y_emb, cross_xq, preferred_element_type=F32)
        )
        / g_weights[None, :]
    )
    curvature = SCALE * (xq_vec * cr_vec + cq_vec * yr_vec - 2.0 * cross_dot)
    grad_g = -curvature / jnp.square(g_weights)
    local_peak = jnp.maximum(
        jnp.max(jnp.abs(grad_q), axis=0),
        jnp.maximum(jnp.max(jnp.abs(grad_r), axis=0), jnp.abs(grad_g)),
    )
    peak = jnp.max(to_all(local_peak[None], EVERY))
    eta = GAMMA / (peak + 1e-06)
    kern_q = q_factor * jnp.exp(-eta * grad_q)
    kern_r = r_factor * jnp.exp(-eta * grad_r)
    kern_g = g_weights * jnp.exp(-eta * grad_g)

    mine = to_all(
        jnp.concatenate([kern_q.astype(BF16), kern_r.astype(BF16), split3(kern_g)], axis=0), "x"
    )
    log_g = jnp.log(join3(mine[:, 2 * rows :]))
    mine_q = mine[:, :rows]
    kerns = mine[:, : 2 * rows]
    theirs = swap(kerns)
    sent_shape = ((others, 2 * ranks, width), BF16)
    u_shape = ((4, rows), F32)
    v_shape = ((2 * ranks, width), F32)
    sent, u = on_chip(first_pass, (sent_shape, u_shape), "first_pass")(masses, kerns, theirs)
    v = jnp.ones(v_shape[0], F32)
    for step in range(1, PASSES):
        sent, u, v = on_chip(next_pass, (sent_shape, u_shape, v_shape), "next_pass")(
            exchange(sent, CHIPS), v, log_g, masses, kerns, theirs
        )
    part, v, weights = on_chip(
        profile_kernel,
        (((ranks * width // 2, genes), F32), v_shape, ((ranks, width), F32)),
        "profile",
        scalars=1,
        inputs=8,
    )(
        core.astype(jnp.int32)[None], exchange(sent, CHIPS), v, log_g, u, kerns, theirs,
        expr, other_expr,
    )
    v_q, v_r = v[:ranks], v[ranks:]
    q_new = u[0][:, None] * kern_q * pick(v_q, here)[None, :]
    r_new = u[1][:, None] * kern_r * pick(v_r, here)[None, :]
    s_q = jnp.sum(mine_q.astype(F32) * v_q[:, None, :], axis=(0, 2))
    scaled = (mine_q.astype(F32) * (v_q / weights)[:, None, :]).astype(BF16)

    piece = jnp.sum(exchange(part.reshape(others, -1, genes), CHIPS), axis=0)
    profiles = lax.all_gather(to_all(piece.astype(BF16), CHIPS), "c").reshape(ranks, width, genes)
    mixed = lax.dot_general(
        scaled, profiles, (((0, 2), (0, 1)), ((), ())), preferred_element_type=F32
    )
    predicted = (mixed / s_q[:, None]).astype(BF16)
    return (q_new, r_new, pick(weights, here) / cells_total, predicted)


def solution(mesh):
    named = Mesh(mesh.devices.reshape(4, 8, 2, 4), EVERY)
    block = P(CELLS, "x")
    return jax.shard_map(
        shards,
        mesh=named,
        in_specs=(
            P(CELLS, None),
            P(CELLS, None),
            block,
            block,
            P("x"),
            P(CELLS),
            P(CELLS),
            block,
        ),
        out_specs=(block, block, P("x"), block),
        check_vma=False,
    )
```

time: 291 us -> 283 us (0.973)
  blocking collectives: 167 us -> 121 us
  waiting for transfers between devices: 40 us -> 71.9 us
  starting transfers between devices: 48.1 us -> 55 us
  matrix products: 6.28 us -> 1.88 us
    all_to_all x11 -> x8, blocking collectives: 155 us -> 104 us  [exchange(): return lax.all_to_all(chunks, axes, 0, 0, tiled=False)]
    all_to_all x5 -> x8, waiting for transfers between devices: 37 us -> 69.2 us  [exchange(): return lax.all_to_all(chunks, axes, 0, 0, tiled=False)]
    all_to_all x5 -> x8, starting transfers between devices: 30.3 us -> 42.8 us  [exchange(): return lax.all_to_all(chunks, axes, 0, 0, tiled=False)]
    all_gather x1, blocking collectives: 7.14 us -> 13 us  [shards(): lax.all_gather(to_all(piece.astype(BF16), CHIPS), 'c')]
    ppermute x4, starting transfers between devices: 17.9 us -> 12.2 us  [swap(): return lax.ppermute(value, 'c', [(0, 1), (1, 0)])]
    dot_general x4 -> x0, matrix products: 4.39 us -> none  [the longest x2 2.74 us: product(): lax.dot_general(right, cells, (((1,), (0,)), ((), ())), preferred_element...]
  transfers between devices with their start and end apart: 9 -> 12, of which waited for: 7 -> 10; matrix products, arithmetic and copies ran while one was open for 1% -> 1% of each run, Pallas kernels for 0% -> 2%
where the time goes in v4:
time: 283 us; the launch traced here: 281 us
  blocking collectives  121 us (43%)
  waiting for transfers between devices  71.9 us (25%)
  starting transfers between devices  55 us (19%)
  Pallas kernels  18.1 us (6%)
  local copies, waits for them, and re-layouts  8.44 us (3%)
  other arithmetic  3.05 us (1%)
    all_to_all x8, blocking collectives, exchange(): return lax.all_to_all(chunks, axes, 0, 0, tiled=False)  104 us
    all_to_all x8, waiting for transfers between devices, exchange(): return lax.all_to_all(chunks, axes, 0, 0, tiled=False)  69.2 us
    all_to_all x8, starting transfers between devices, exchange(): return lax.all_to_all(chunks, axes, 0, 0, tiled=False)  42.8 us
    pallas_call x9, Pallas kernels, shards(): on_chip(next_pass, (sent_shape, u_shape, v_shape), 'next_pass')  13.6 us
    all_gather x1, blocking collectives, shards(): lax.all_gather(to_all(piece.astype(BF16), CHIPS), 'c')  13 us
    ppermute x4, starting transfers between devices, swap(): return lax.ppermute(value, 'c', [(0, 1), (1, 0)])  12.2 us
    unnamed x44, local copies, waits for them, and re-layouts  5.8 us
  transfers between devices with their start and end apart: 12, of which 10 were waited for; matrix products, arithmetic and copies ran while one was open for 1% of the time, Pallas kernels for 2%

profile of v4, /device:TPU:1, one launch (start us, length us, event | category | flops | bytes accessed | tf_op | source)
XLA Modules:
  0.0 281.5 jit_solution(969224425500301602)
XLA Ops:
  10.4 9.5 %all-to-all-start = ((f32[32,3,4,128]{3,2,1,0:T(4,128)}), f32[32,3,4,128]{3,2,1,0:T(4,128)S(1)}, u32[]{:S(2)}, u32[]{:S(2)}) async-start(f32[32,3,4,128]{3,2,1,0:T(4,128)} %copy_add_fusion), calls=%async_computation | async-start | bytes 393216 | tf_op jit(solution)/shard_map/all_to_all | solution.py:28
  20.0 9.2 %all-to-all-done.got_ref = f32[32,3,4,128]{3,2,1,0:T(4,128)S(1)} async-done(((f32[32,3,4,128]{3,2,1,0:T(4,128)}), f32[32,3,4,128]{3,2,1,0:T(4,128)S(1)}, u32[]{:S(2)}, u32[]{:S(2)}) %all-to-all-start) | async-done | bytes 196640 | tf_op jit(solution)/shard_map/all_to_all | solution.py:28
  30.0 5.5 %all-to-all-start.1 = ((bf16[32,16,128]{2,1,0:T(8,128)(2,1)}), bf16[32,16,128]{2,1,0:T(8,128)(2,1)S(1)}, u32[]{:S(2)}, u32[]{:S(2)}) async-start(bf16[32,16,128]{2,1,0:T(8,128)(2,1)} %get-tuple-element.36), calls=%async_computation.1 | async-start | bytes 262144 | tf_op jit(solution)/shard_map/all_to_all | solution.py:28
  35.6 9.0 %all-to-all-done.1 = bf16[32,16,128]{2,1,0:T(8,128)(2,1)S(1)} async-done(((bf16[32,16,128]{2,1,0:T(8,128)(2,1)}), bf16[32,16,128]{2,1,0:T(8,128)(2,1)S(1)}, u32[]{:S(2)}, u32[]{:S(2)}) %all-to-all-start.1) | async-done | bytes 131104 | tf_op jit(solution)/shard_map/all_to_all | solution.py:28
  44.6 4.5 %all-gather = bf16[64,16,128]{2,1,0:T(8,128)(2,1)S(1)} all-gather(bf16[32,16,128]{2,1,0:T(8,128)(2,1)S(1)} %all-to-all-done.1), channel_id=2, replica_groups=mesh['y'=4,'z'=8,'c'=2,'x'=4] {'c'}, dimensions={0}, use_global_device_ids=true | all-gather | bytes 393216 | tf_op jit(solution)/shard_map/all_gather | solution.py:226
  50.7 6.6 %all-to-all-start.2 = ((f32[256,1,128]{2,1,0:T(1,128)}), f32[256,1,128]{2,1,0:T(1,128)S(1)}, u32[]{:S(2)}, u32[]{:S(2)}) async-start(f32[256,1,128]{2,1,0:T(1,128)} %broadcast_in_dim.13), calls=%async_computation.2 | async-start | bytes 262144 | tf_op jit(solution)/shard_map/all_to_all | solution.py:28
  57.6 12.4 %all-to-all-done.2 = f32[256,1,128]{2,1,0:T(1,128)S(1)} async-done(((f32[256,1,128]{2,1,0:T(1,128)}), f32[256,1,128]{2,1,0:T(1,128)S(1)}, u32[]{:S(2)}, u32[]{:S(2)}) %all-to-all-start.2) | async-done | bytes 131104 | tf_op jit(solution)/shard_map/all_to_all | solution.py:28
  72.4 16.7 %all_to_all.80 = bf16[4,1027,128]{2,1,0:T(8,128)(2,1)S(1)} all-to-all(bf16[4,1027,128]{2,1,0:T(8,128)(2,1)S(1)} %broadcast_in_dim.14), channel_id=1, replica_groups=mesh['y'=4,'z'=8,'c'=2,'x'=4] {'x'}, dimensions={0} | all-to-all | bytes 2103296 | tf_op jit(solution)/shard_map/all_to_all | solution.py:28
  95.1 3.9 %all-to-all-start.4 = ((bf16[32,8,128]{2,1,0:T(8,128)(2,1)}), bf16[32,8,128]{2,1,0:T(8,128)(2,1)S(1)}, u32[]{:S(2)}, u32[]{:S(2)}) async-start(bf16[32,8,128]{2,1,0:T(8,128)(2,1)} %get-tuple-element.37), calls=%async_computation.4 | async-start | bytes 131072 | tf_op jit(solution)/shard_map/all_to_all | solution.py:28
  99.0 8.9 %all-to-all-done.4.got_ref = bf16[32,8,128]{2,1,0:T(8,128)(2,1)S(1)} async-done(((bf16[32,8,128]{2,1,0:T(8,128)(2,1)}), bf16[32,8,128]{2,1,0:T(8,128)(2,1)S(1)}, u32[]{:S(2)}, u32[]{:S(2)}) %all-to-all-start.4) | async-done | bytes 65568 | tf_op jit(solution)/shard_map/all_to_all | solution.py:28
  109.3 12.1 %all_to_all.81.got_ref = bf16[32,8,128]{2,1,0:T(8,128)(2,1)S(1)} all-to-all(bf16[32,8,128]{2,1,0:T(8,128)(2,1)S(1)} %get-tuple-element.38), channel_id=1, replica_groups=mesh['y'=4,'z'=8,'c'=2,'x'=4] {'y','z'}, dimensions={0} | all-to-all | bytes 131072 | tf_op jit(solution)/shard_map/all_to_all | solution.py:28
  122.9 11.9 %all_to_all.82.got_ref = bf16[32,8,128]{2,1,0:T(8,128)(2,1)S(1)} all-to-all(bf16[32,8,128]{2,1,0:T(8,128)(2,1)S(1)} %get-tuple-element.40), channel_id=1, replica_groups=mesh['y'=4,'z'=8,'c'=2,'x'=4] {'y','z'}, dimensions={0} | all-to-all | bytes 131072 | tf_op jit(solution)/shard_map/all_to_all | solution.py:28
  136.2 11.9 %all_to_all.83.got_ref = bf16[32,8,128]{2,1,0:T(8,128)(2,1)S(1)} all-to-all(bf16[32,8,128]{2,1,0:T(8,128)(2,1)S(1)} %get-tuple-element.42), channel_id=1, replica_groups=mesh['y'=4,'z'=8,'c'=2,'x'=4] {'y','z'}, dimensions={0} | all-to-all | bytes 131072 | tf_op jit(solution)/shard_map/all_to_all | solution.py:28
  149.6 12.0 %all_to_all.84.got_ref = bf16[32,8,128]{2,1,0:T(8,128)(2,1)S(1)} all-to-all(bf16[32,8,128]{2,1,0:T(8,128)(2,1)S(1)} %get-tuple-element.44), channel_id=1, replica_groups=mesh['y'=4,'z'=8,'c'=2,'x'=4] {'y','z'}, dimensions={0} | all-to-all | bytes 131072 | tf_op jit(solution)/shard_map/all_to_all | solution.py:28
  167.2 6.3 %collective-permute-start.3 = (bf16[512,512]{1,0:T(8,128)(2,1)S(1)}, bf16[512,512]{1,0:T(8,128)(2,1)S(1)}, u32[]{:S(2)}, u32[]{:S(2)}) collective-permute-start(bf16[512,512]{1,0:T(8,128)(2,1)S(1)} %copy-done.8), channel_id=1, source_target_pairs={{0,4},{4,0},{1,5},{5,1},{2,6},{6,2},{3,7},{7,3},{8,12},{12,8},{9,1... | collective-permute-start | bytes 1572872 | tf_op jit(solution)/shard_map/ppermute | solution.py:37
  177.5 15.6 %all_to_all.85.got_ref = bf16[32,8,128]{2,1,0:T(8,128)(2,1)S(1)} all-to-all(bf16[32,8,128]{2,1,0:T(8,128)(2,1)S(1)} %get-tuple-element.48), channel_id=1, replica_groups=mesh['y'=4,'z'=8,'c'=2,'x'=4] {'y','z'}, dimensions={0} | all-to-all | bytes 131072 | tf_op jit(solution)/shard_map/all_to_all | solution.py:28
  194.6 11.9 %all_to_all.86.got_ref = bf16[32,8,128]{2,1,0:T(8,128)(2,1)S(1)} all-to-all(bf16[32,8,128]{2,1,0:T(8,128)(2,1)S(1)} %get-tuple-element.50), channel_id=1, replica_groups=mesh['y'=4,'z'=8,'c'=2,'x'=4] {'y','z'}, dimensions={0} | all-to-all | bytes 131072 | tf_op jit(solution)/shard_map/all_to_all | solution.py:28
  207.9 11.8 %all_to_all.87.got_ref = bf16[32,8,128]{2,1,0:T(8,128)(2,1)S(1)} all-to-all(bf16[32,8,128]{2,1,0:T(8,128)(2,1)S(1)} %get-tuple-element.52), channel_id=1, replica_groups=mesh['y'=4,'z'=8,'c'=2,'x'=4] {'y','z'}, dimensions={0} | all-to-all | bytes 131072 | tf_op jit(solution)/shard_map/all_to_all | solution.py:28
  225.3 8.8 %all-to-all-done.13.got_ref = bf16[32,8,128]{2,1,0:T(8,128)(2,1)S(1)} async-done(((bf16[32,8,128]{2,1,0:T(8,128)(2,1)}), bf16[32,8,128]{2,1,0:T(8,128)(2,1)S(1)}, u32[]{:S(2)}, u32[]{:S(2)}) %all-to-all-start.13) | async-done | bytes 65568 | tf_op jit(solution)/shard_map/all_to_all | solution.py:28
  235.9 4.0 %all-to-all-start.14 = ((f32[32,8,512]{2,1,0:T(8,128)}), f32[32,8,512]{2,1,0:T(8,128)S(1)}, u32[]{:S(2)}, u32[]{:S(2)}) async-start(f32[32,8,512]{2,1,0:T(8,128)} %bitcast.27), calls=%async_computation.14 | async-start | bytes 1048576 | tf_op jit(solution)/shard_map/all_to_all | solution.py:28
  240.1 11.2 %all-to-all-done.14 = f32[32,8,512]{2,1,0:T(8,128)S(1)} async-done(((f32[32,8,512]{2,1,0:T(8,128)}), f32[32,8,512]{2,1,0:T(8,128)S(1)}, u32[]{:S(2)}, u32[]{:S(2)}) %all-to-all-start.14) | async-done | bytes 524320 | tf_op jit(solution)/shard_map/all_to_all | solution.py:28
  252.0 5.6 %all-to-all-start.15 = ((bf16[32,8,512]{2,1,0:T(8,128)(2,1)}), bf16[32,8,512]{2,1,0:T(8,128)(2,1)S(1)}, u32[]{:S(2)}, u32[]{:S(2)}) async-start(bf16[32,8,512]{2,1,0:T(8,128)(2,1)} %broadcast_in_dim.17), calls=%async_computation.15 | async-start | bytes 524288 | tf_op jit(solution)/shard_map/all_to_all | solution.py:28
  260.1 7.2 %all-to-all-done.15 = bf16[32,8,512]{2,1,0:T(8,128)(2,1)S(1)} async-done(((bf16[32,8,512]{2,1,0:T(8,128)(2,1)}), bf16[32,8,512]{2,1,0:T(8,128)(2,1)S(1)}, u32[]{:S(2)}, u32[]{:S(2)}) %all-to-all-start.15) | async-done | bytes 262176 | tf_op jit(solution)/shard_map/all_to_all | solution.py:28
  267.3 13.0 %all-gather.1 = bf16[64,8,512]{2,1,0:T(8,128)(2,1)S(1)} all-gather(bf16[32,8,512]{2,1,0:T(8,128)(2,1)S(1)} %all-to-all-done.15), channel_id=3, replica_groups=mesh['y'=4,'z'=8,'c'=2,'x'=4] {'c'}, dimensions={0}, use_global_device_ids=true | all-gather | bytes 786432 | tf_op jit(solution)/shard_map/all_gather | solution.py:294
  (111 shorter events, 50.4 us)
Async XLA Ops:
  5.0 14.9 %copy-start.1 = (bf16[512,256]{1,0:T(8,128)(2,1)S(1)}, bf16[512,256]{1,0:T(8,128)(2,1)}, u32[]{:S(2)}) copy-start(bf16[512,256]{1,0:T(8,128)(2,1)} %y_ref.1) | copy-start | bytes 786436
  5.0 30.4 %copy-start.3 = (bf16[512,256]{1,0:T(8,128)(2,1)S(1)}, bf16[512,256]{1,0:T(8,128)(2,1)}, u32[]{:S(2)}) copy-start(bf16[512,256]{1,0:T(8,128)(2,1)} %x_ref.1) | copy-start | bytes 786436
  5.2 4.4 %collective-permute-start.1 = (f32[32,3,4,128]{3,2,1,0:T(4,128)S(1)}, f32[32,3,4,128]{3,2,1,0:T(4,128)S(1)}, u32[]{:S(2)}, u32[]{:S(2)}) collective-permute-start(f32[32,3,4,128]{3,2,1,0:T(4,128)S(1)} %copy.58), channel_id=1, source_target_pairs={{0,4},{4,0},{1,5},{5,1},{2,6},{6,2},{3,7},{7,3},{8,12},{12,8},{9,1... | collective-permute-start | bytes 589832 | tf_op jit(solution)/shard_map/ppermute | solution.py:37
  10.4 18.9 %all-to-all-start = ((f32[32,3,4,128]{3,2,1,0:T(4,128)}), f32[32,3,4,128]{3,2,1,0:T(4,128)S(1)}, u32[]{:S(2)}, u32[]{:S(2)}) async-start(f32[32,3,4,128]{3,2,1,0:T(4,128)} %copy_add_fusion), calls=%async_computation | async-start | bytes 393216 | tf_op jit(solution)/shard_map/all_to_all | solution.py:28
  19.9 29.4 %copy-start.19 = (f32[128]{0:T(128)S(1)}, f32[128]{0:T(128)}, u32[]{:S(2)}) copy-start(f32[128]{0:T(128)} %param.12) | copy-start | bytes 1540
  30.0 14.6 %all-to-all-start.1 = ((bf16[32,16,128]{2,1,0:T(8,128)(2,1)}), bf16[32,16,128]{2,1,0:T(8,128)(2,1)S(1)}, u32[]{:S(2)}, u32[]{:S(2)}) async-start(bf16[32,16,128]{2,1,0:T(8,128)(2,1)} %get-tuple-element.36), calls=%async_computation.1 | async-start | bytes 262144 | tf_op jit(solution)/shard_map/all_to_all | solution.py:28
  49.6 22.2 %copy-start.15 = (f32[512,128]{0,1:T(8,128)}, f32[512,128]{0,1:T(8,128)S(1)}, u32[]{:S(2)}) copy-start(f32[512,128]{0,1:T(8,128)S(1)} %get-tuple-element.104) | copy-start | bytes 786436
  49.6 7.8 %copy-start.5 = (f32[512,128]{1,0:T(8,128)S(1)}, f32[512,128]{1,0:T(8,128)}, u32[]{:S(2)}) copy-start(f32[512,128]{1,0:T(8,128)} %r_ref.1) | copy-start | bytes 786436
  49.6 7.9 %copy-start.7 = (f32[512,128]{1,0:T(8,128)S(1)}, f32[512,128]{1,0:T(8,128)}, u32[]{:S(2)}) copy-start(f32[512,128]{1,0:T(8,128)} %q_ref.1) | copy-start | bytes 786436
  49.9 21.9 %copy-start.13 = (f32[512,128]{0,1:T(8,128)}, f32[512,128]{0,1:T(8,128)S(1)}, u32[]{:S(2)}) copy-start(f32[512,128]{0,1:T(8,128)S(1)} %get-tuple-element.102) | copy-start | bytes 786436
  50.7 19.3 %all-to-all-start.2 = ((f32[256,1,128]{2,1,0:T(1,128)}), f32[256,1,128]{2,1,0:T(1,128)S(1)}, u32[]{:S(2)}, u32[]{:S(2)}) async-start(f32[256,1,128]{2,1,0:T(1,128)} %broadcast_in_dim.13), calls=%async_computation.2 | async-start | bytes 262144 | tf_op jit(solution)/shard_map/all_to_all | solution.py:28
  57.5 14.5 %copy-start.11 = (f32[512,128]{0,1:T(8,128)}, f32[512,128]{0,1:T(8,128)S(1)}, u32[]{:S(2)}) copy-start(f32[512,128]{0,1:T(8,128)S(1)} %copy.62) | copy-start | bytes 786436
  89.0 4.4 %copy-start.9 = (bf16[4,1027,128]{2,1,0:T(8,128)(2,1)}, bf16[4,1027,128]{2,1,0:T(8,128)(2,1)S(1)}, u32[]{:S(2)}) copy-start(bf16[4,1027,128]{2,1,0:T(8,128)(2,1)S(1)} %all_to_all.80) | copy-start | bytes 3154948
  89.1 4.3 %collective-permute-start.2 = (bf16[4,1024,128]{2,1,0:T(8,128)(2,1)S(1)}, bf16[4,1024,128]{2,1,0:T(8,128)(2,1)S(1)}, u32[]{:S(2)}, u32[]{:S(2)}) collective-permute-start(bf16[4,1024,128]{2,1,0:T(8,128)(2,1)S(1)} %slice.86.own_ref), channel_id=1, source_target_pairs={{0,4},{4,0},{1,5},{5,1},{2,6},{6,2},{3,7},{7,3},{8,12},{12,8},{9,1... | collective-permute-start | bytes 3145736 | tf_op jit(solution)/shard_map/ppermute | solution.py:37
  91.1 2.3 collective-permute-start
  95.1 12.7 %all-to-all-start.4 = ((bf16[32,8,128]{2,1,0:T(8,128)(2,1)}), bf16[32,8,128]{2,1,0:T(8,128)(2,1)S(1)}, u32[]{:S(2)}, u32[]{:S(2)}) async-start(bf16[32,8,128]{2,1,0:T(8,128)(2,1)} %get-tuple-element.37), calls=%async_computation.4 | async-start | bytes 131072 | tf_op jit(solution)/shard_map/all_to_all | solution.py:28
  161.6 5.6 %copy-start.8 = (bf16[512,512]{1,0:T(8,128)(2,1)S(1)}, bf16[512,512]{1,0:T(8,128)(2,1)}, u32[]{:S(2)}) copy-start(bf16[512,512]{1,0:T(8,128)(2,1)} %expr_ref.1) | copy-start | bytes 1572868
  163.3 12.7 %all-to-all-start.9 = ((bf16[32,8,128]{2,1,0:T(8,128)(2,1)}), bf16[32,8,128]{2,1,0:T(8,128)(2,1)S(1)}, u32[]{:S(2)}, u32[]{:S(2)}) async-start(bf16[32,8,128]{2,1,0:T(8,128)(2,1)} %get-tuple-element.46), calls=%async_computation.9 | async-start | bytes 131072 | tf_op jit(solution)/shard_map/all_to_all | solution.py:28
  167.2 58.1 %collective-permute-start.3 = (bf16[512,512]{1,0:T(8,128)(2,1)S(1)}, bf16[512,512]{1,0:T(8,128)(2,1)S(1)}, u32[]{:S(2)}, u32[]{:S(2)}) collective-permute-start(bf16[512,512]{1,0:T(8,128)(2,1)S(1)} %copy-done.8), channel_id=1, source_target_pairs={{0,4},{4,0},{1,5},{5,1},{2,6},{6,2},{3,7},{7,3},{8,12},{12,8},{9,1... | collective-permute-start | bytes 1572872 | tf_op jit(solution)/shard_map/ppermute | solution.py:37
  221.5 12.7 %all-to-all-start.13 = ((bf16[32,8,128]{2,1,0:T(8,128)(2,1)}), bf16[32,8,128]{2,1,0:T(8,128)(2,1)S(1)}, u32[]{:S(2)}, u32[]{:S(2)}) async-start(bf16[32,8,128]{2,1,0:T(8,128)(2,1)} %get-tuple-element.55), calls=%async_computation.13 | async-start | bytes 131072 | tf_op jit(solution)/shard_map/all_to_all | solution.py:28
  235.9 15.4 %all-to-all-start.14 = ((f32[32,8,512]{2,1,0:T(8,128)}), f32[32,8,512]{2,1,0:T(8,128)S(1)}, u32[]{:S(2)}, u32[]{:S(2)}) async-start(f32[32,8,512]{2,1,0:T(8,128)} %bitcast.27), calls=%async_computation.14 | async-start | bytes 1048576 | tf_op jit(solution)/shard_map/all_to_all | solution.py:28
  240.0 18.5 %copy-start.14 = (f32[512,128]{0,1:T(8,128)S(1)}, f32[512,128]{0,1:T(8,128)}, u32[]{:S(2)}) copy-start(f32[512,128]{0,1:T(8,128)} %copy-done.13) | copy-start | bytes 786436
  252.0 7.9 %copy-start.10 = (bf16[4,1027,128]{2,1,0:T(8,128)(2,1)S(1)}, bf16[4,1027,128]{2,1,0:T(8,128)(2,1)}, u32[]{:S(2)}) copy-start(bf16[4,1027,128]{2,1,0:T(8,128)(2,1)} %copy-done.9) | copy-start | bytes 3154948
  252.0 15.3 %all-to-all-start.15 = ((bf16[32,8,512]{2,1,0:T(8,128)(2,1)}), bf16[32,8,512]{2,1,0:T(8,128)(2,1)S(1)}, u32[]{:S(2)}, u32[]{:S(2)}) async-start(bf16[32,8,512]{2,1,0:T(8,128)(2,1)} %broadcast_in_dim.17), calls=%async_computation.15 | async-start | bytes 524288 | tf_op jit(solution)/shard_map/all_to_all | solution.py:28
  (8 other events, 16.1 us)

commit v5 on v4

--- a/solution.py
+++ b/solution.py
@@ -85,17 +85,89 @@
     vec_ref[...] = jnp.concatenate(rows, axis=0)
 
 
-def chunk_kernel(got_ref, sent_ref, vec_ref):
+def chunk_kernel(got_ref, g_ref, sent_ref):
     summed = jnp.sum(got_ref[...], axis=0)
     xq, yr = summed[0], summed[1]
-    vec_ref[...] = summed[2]
     dot = jnp.sum(xq * yr, axis=0, keepdims=True)
+    nothing = jnp.zeros((2, dot.shape[1]), F32)
+    chunk = jnp.concatenate([xq, yr, summed[2], dot, g_ref[...], nothing], axis=0)
+    sent_ref[...] = jnp.broadcast_to(chunk[None], sent_ref.shape)
+
+
+def spread_kernel(got_ref, sent_ref, vec_ref):
+    every = jnp.concatenate([got_ref[i] for i in range(got_ref.shape[0])], axis=1)
+    dot = every[12:13]
     high = dot.astype(BF16).astype(F32)
     rest = dot - high
     middle = rest.astype(BF16).astype(F32)
     nothing = jnp.zeros((5, dot.shape[1]), F32)
-    chunk = jnp.concatenate([xq, yr, high, middle, rest - middle, nothing], axis=0)
+    chunk = jnp.concatenate([every[:8], high, middle, rest - middle, nothing], axis=0)
     sent_ref[...] = jnp.broadcast_to(chunk.astype(BF16)[None], sent_ref.shape)
+    vec_ref[...] = every[8:16]
+
+
+def grad_kernel(
+    core_ref, x_ref, y_ref, mine_ref, other_ref, vec_ref, grad_q_ref, grad_r_ref, grad_g_ref, peak_ref
+):
+    half = x_ref.shape[1] // 2
+    chunks = mine_ref.shape[0]
+    core = core_ref[0]
+    g = vec_ref[5:6]
+    scale = SCALE / g
+    place = lax.broadcasted_iota(jnp.int32, (half, chunks), 1)
+    wanted = lax.broadcasted_iota(jnp.int32, (half, chunks), 0)
+    wanted = (wanted // 4) * 16 + wanted % 4
+    place8 = lax.broadcasted_iota(jnp.int32, (8, chunks), 1) % 16
+    is_dot = jnp.where((place8 >= 8) & (place8 < 11), 1.0, 0.0).astype(BF16)
+    spread = jnp.dot(is_dot, mine_ref[...], preferred_element_type=F32) + jnp.dot(
+        is_dot, other_ref[...], preferred_element_type=F32
+    )
+    xq, cq, yr, cr = (vec_ref[i : i + 1] for i in range(4))
+    curvature = SCALE * (xq * cr + cq * yr - 2.0 * spread[0:1])
+    grad_g = -curvature / jnp.square(g)
+    grad_g_ref[...] = grad_g
+    top = jnp.abs(grad_g)
+    for emb_ref, offset, count, total, out_ref in (
+        (x_ref, 4, cr, yr, grad_q_ref),
+        (y_ref, 0, cq, xq, grad_r_ref),
+    ):
+        select = jnp.where(place == wanted + offset, 1.0, 0.0).astype(BF16)
+        product = None
+        for position, cross_ref in ((core, mine_ref), (1 - core, other_ref)):
+            rows = jnp.dot(select, cross_ref[...], preferred_element_type=F32).astype(BF16)
+            emb = emb_ref[:, pl.ds(pl.multiple_of(position * half, half), half)]
+            part = jnp.dot(emb, rows, preferred_element_type=F32)
+            product = part if product is None else product + part
+        norms = jnp.sum(jnp.square(emb_ref[...].astype(F32)), axis=1, keepdims=True)
+        grad = scale * (norms * count + total - 2.0 * product)
+        out_ref[...] = grad
+        top = jnp.maximum(top, jnp.max(jnp.abs(grad), axis=0, keepdims=True))
+    blocks = in_rows(top, top.shape[1] // peak_ref.shape[2])
+    peak = blocks[0]
+    for block in blocks[1:]:
+        peak = jnp.maximum(peak, block)
+    peak_ref[...] = jnp.broadcast_to(peak[None], peak_ref.shape)
+
+
+def kern_kernel(
+    here_ref, peak_ref, grad_q_ref, grad_r_ref, grad_g_ref, vec_ref, all_ref, q_ref, r_ref,
+    kern_ref, own_q_ref, own_r_ref, log_ref,
+):
+    ranks = all_ref.shape[0]
+    rows, width = q_ref.shape
+    peak = jnp.max(jnp.max(peak_ref[...], axis=0), axis=1, keepdims=True)
+    eta = GAMMA / (peak + 1e-06)
+    kern_g = vec_ref[5:6] * jnp.exp(-eta * grad_g_ref[...])
+    log_ref[...] = jnp.concatenate(in_rows(jnp.log(kern_g), ranks), axis=0)
+    mine = pl.ds(pl.multiple_of(here_ref[0] * width, width), width)
+    for side, (grad_ref, factor_ref, own_ref) in enumerate(
+        ((grad_q_ref, q_ref, own_q_ref), (grad_r_ref, r_ref, own_r_ref))
+    ):
+        own_ref[...] = factor_ref[...] * jnp.exp(-eta * grad_ref[:, mine])
+        for block in range(ranks):
+            lanes = pl.ds(block * width, width)
+            kern = all_ref[block, side].astype(F32) * jnp.exp(-eta * grad_ref[:, lanes])
+            kern_ref[pl.ds(side * rows, rows), lanes] = kern.astype(BF16)
 
 
 def new_scalings(ranks, got_ref, v_ref, log_ref):
@@ -106,13 +178,11 @@
 
 
 def send_columns(v, mass_ref, own_ref, other_ref, sent_ref, u_ref):
-    ranks = own_ref.shape[0]
-    rows = other_ref.shape[1] // 2
+    ranks = v.shape[0] // 2
+    rows = own_ref.shape[0] // 2
 
     def kern(member, side):
-        kern_ref = (own_ref, other_ref)[member]
-        blocks = [kern_ref[block, pl.ds(side * rows, rows), :] for block in range(ranks)]
-        return jnp.concatenate(blocks, axis=1)
+        return (own_ref, other_ref)[member][pl.ds(side * rows, rows), :]
 
     v_rows = [stack3(in_lanes(v, side * ranks, ranks)) for side in range(2)]
     sums = []
@@ -140,12 +210,12 @@
 
 
 def first_pass(mass_ref, own_ref, other_ref, sent_ref, u_ref):
-    ones = jnp.ones((2 * own_ref.shape[0], own_ref.shape[2]), F32)
+    ones = jnp.ones(sent_ref.shape[1:], F32)
     send_columns(ones, mass_ref, own_ref, other_ref, sent_ref, u_ref)
 
 
 def next_pass(got_ref, v_ref, log_ref, mass_ref, own_ref, other_ref, sent_ref, u_ref, new_ref):
-    v, _ = new_scalings(own_ref.shape[0], got_ref, v_ref, log_ref)
+    v, _ = new_scalings(log_ref.shape[0], got_ref, v_ref, log_ref)
     new_ref[...] = v
     send_columns(v, mass_ref, own_ref, other_ref, sent_ref, u_ref)
 
@@ -154,23 +224,24 @@
     core_ref, got_ref, v_ref, log_ref, u_ref, own_ref, other_ref, expr_ref, more_ref,
     part_ref, new_ref, weights_ref,
 ):
-    ranks, _, width = own_ref.shape
-    rows = other_ref.shape[1] // 2
+    ranks = log_ref.shape[0]
+    rows = own_ref.shape[0] // 2
+    half = own_ref.shape[1] // 2
     v, weights = new_scalings(ranks, got_ref, v_ref, log_ref)
     new_ref[...] = v
     weights_ref[...] = weights
     u_columns = jnp.concatenate([u_ref[...], u_ref[...]], axis=0).T
-    half = ranks // 2
-    for i in range(half):
-        block = core_ref[0] * half + i
-        scale = new_ref[pl.ds(ranks + block, 1), :]
-        total = None
-        for member, (kern_ref, cells_ref) in enumerate(((own_ref, expr_ref), (other_ref, more_ref))):
-            kern = kern_ref[block, pl.ds(rows, rows), :].astype(F32)
-            column = u_columns[:, 2 * member + 1 : 2 * member + 2]
-            part = contract_rows((kern * scale * column).astype(BF16), cells_ref[...])
-            total = part if total is None else total + part
-        part_ref[pl.ds(i * width, width), :] = total
+    core = core_ref[0]
+    blocks = [new_ref[pl.ds(ranks + core * (ranks // 2) + i, 1), :] for i in range(ranks // 2)]
+    scale = jnp.concatenate(blocks, axis=1)
+    lanes = pl.ds(pl.multiple_of(core * half, half), half)
+    total = None
+    for member, (kern_ref, cells_ref) in enumerate(((own_ref, expr_ref), (other_ref, more_ref))):
+        kern = kern_ref[pl.ds(rows, rows), lanes].astype(F32)
+        column = u_columns[:, 2 * member + 1 : 2 * member + 2]
+        part = contract_rows((kern * scale * column).astype(BF16), cells_ref[...])
+        total = part if total is None else total + part
+    part_ref[...] = total
 
 
 def on_chip(kernel, shapes, name, scalars=0, inputs=0):
@@ -203,8 +274,8 @@
     other_expr = swap(expr)
     masses = jnp.stack([a_mass, b_mass])
     masses = jnp.concatenate([masses, swap(masses)])
-    norms_one = jnp.sum(jnp.square(x_emb.astype(F32)), axis=1)
-    norms_two = jnp.sum(jnp.square(y_emb.astype(F32)), axis=1)
+    core_index = core.astype(jnp.int32)[None]
+    every = lax.all_gather(jnp.stack([q_factor, r_factor]).astype(BF16), "x")
     part_xq, part_yr, part_vec = on_chip(
         start_kernel, (((dim, width), F32), ((dim, width), F32), ((4, width), F32)), "start"
     )(x_emb, y_emb, q_factor, r_factor)
@@ -218,52 +289,32 @@
         ).reshape(others, (2 * share + 4) // 4, 4, width)
 
     outgoing = with_vec(pick(part_cross, core)) + swap(with_vec(pick(part_cross, 1 - core)))
-    chunk_rows = 2 * share + 8
+    columns = ranks * width
+    tall = ((rows, columns), F32)
+    sent = on_chip(chunk_kernel, (((ranks, 16, width), F32),), "chunk")(
+        exchange(outgoing, CHIPS), g_weights[None]
+    )[0]
     sent, vec = on_chip(
-        chunk_kernel, (((others, chunk_rows, width), BF16), ((4, width), F32)), "chunk"
-    )(exchange(outgoing, CHIPS))
-    xq_vec, cq_vec, yr_vec, cr_vec = (vec[i] for i in range(4))
-    crosses = lax.all_gather(exchange(sent, CHIPS), "c").reshape(2 * others, chunk_rows, width)
-    cross_xq = crosses[:, :share].reshape(dim, width)
-    cross_yr = crosses[:, share : 2 * share].reshape(dim, width)
-    cross_dot = jnp.sum(join3(crosses[:, 2 * share : 2 * share + 3]), axis=0)
-
-    grad_q = (
-        SCALE
-        * (
-            norms_one[:, None] * cr_vec[None, :]
-            + yr_vec[None, :]
-            - 2.0 * jnp.dot(x_emb, cross_yr, preferred_element_type=F32)
-        )
-        / g_weights[None, :]
-    )
-    grad_r = (
-        SCALE
-        * (
-            norms_two[:, None] * cq_vec[None, :]
-            + xq_vec[None, :]
-            - 2.0 * jnp.dot(y_emb, cross_xq, preferred_element_type=F32)
-        )
-        / g_weights[None, :]
-    )
-    curvature = SCALE * (xq_vec * cr_vec + cq_vec * yr_vec - 2.0 * cross_dot)
-    grad_g = -curvature / jnp.square(g_weights)
-    local_peak = jnp.maximum(
-        jnp.max(jnp.abs(grad_q), axis=0),
-        jnp.maximum(jnp.max(jnp.abs(grad_r), axis=0), jnp.abs(grad_g)),
-    )
-    peak = jnp.max(to_all(local_peak[None], EVERY))
-    eta = GAMMA / (peak + 1e-06)
-    kern_q = q_factor * jnp.exp(-eta * grad_q)
-    kern_r = r_factor * jnp.exp(-eta * grad_r)
-    kern_g = g_weights * jnp.exp(-eta * grad_g)
-
-    mine = to_all(
-        jnp.concatenate([kern_q.astype(BF16), kern_r.astype(BF16), split3(kern_g)], axis=0), "x"
-    )
-    log_g = jnp.log(join3(mine[:, 2 * rows :]))
-    mine_q = mine[:, :rows]
-    kerns = mine[:, : 2 * rows]
+        spread_kernel, (((others, 16, columns), BF16), ((8, columns), F32)), "spread"
+    )(exchange(sent, "x"))
+    crosses = exchange(sent, CHIPS).reshape(others * 16, columns)
+    grad_q, grad_r, grad_g, peak = on_chip(
+        grad_kernel,
+        (tall, tall, ((1, columns), F32), ((cell_devices, 1, width), F32)),
+        "grad",
+        scalars=1,
+        inputs=5,
+    )(core_index, x_emb, y_emb, crosses, swap(crosses), vec)
+    kerns, kern_q, kern_r, log_g = on_chip(
+        kern_kernel,
+        (((2 * rows, columns), BF16), ((rows, width), F32), ((rows, width), F32), ((ranks, width), F32)),
+        "kern",
+        scalars=1,
+        inputs=8,
+    )(
+        here.astype(jnp.int32)[None], exchange(peak, CELLS), grad_q, grad_r, grad_g, vec,
+        every, q_factor, r_factor,
+    )
     theirs = swap(kerns)
     sent_shape = ((others, 2 * ranks, width), BF16)
     u_shape = ((4, rows), F32)
@@ -281,20 +332,19 @@
         scalars=1,
         inputs=8,
     )(
-        core.astype(jnp.int32)[None], exchange(sent, CHIPS), v, log_g, u, kerns, theirs,
+        core_index, exchange(sent, CHIPS), v, log_g, u, kerns, theirs,
         expr, other_expr,
     )
     v_q, v_r = v[:ranks], v[ranks:]
     q_new = u[0][:, None] * kern_q * pick(v_q, here)[None, :]
     r_new = u[1][:, None] * kern_r * pick(v_r, here)[None, :]
-    s_q = jnp.sum(mine_q.astype(F32) * v_q[:, None, :], axis=(0, 2))
-    scaled = (mine_q.astype(F32) * (v_q / weights)[:, None, :]).astype(BF16)
+    mine_q = kerns[:rows].astype(F32)
+    s_q = jnp.sum(mine_q * v_q.reshape(1, columns), axis=1)
+    scaled = (mine_q * (v_q / weights).reshape(1, columns)).astype(BF16)
 
     piece = jnp.sum(exchange(part.reshape(others, -1, genes), CHIPS), axis=0)
-    profiles = lax.all_gather(to_all(piece.astype(BF16), CHIPS), "c").reshape(ranks, width, genes)
-    mixed = lax.dot_general(
-        scaled, profiles, (((0, 2), (0, 1)), ((), ())), preferred_element_type=F32
-    )
+    profiles = lax.all_gather(to_all(piece.astype(BF16), CHIPS), "c").reshape(columns, genes)
+    mixed = jnp.dot(scaled, profiles, preferred_element_type=F32)
     predicted = (mixed / s_q[:, None]).astype(BF16)
     return (q_new, r_new, pick(weights, here) / cells_total, predicted)
 

time: 283 us -> 290 us (1.025)
  waiting for transfers between devices: 71.9 us -> 58.7 us
  between operations: 1.81 us -> 14.3 us
  blocking collectives: 121 us -> 131 us
  starting transfers between devices: 55 us -> 49.9 us
  Pallas kernels: 18.1 us -> 21.4 us
    all_to_all x8 -> x7, waiting for transfers between devices: 69.2 us -> 52.6 us  [exchange(): return lax.all_to_all(chunks, axes, 0, 0, tiled=False)]
    all_to_all x8 -> x9, blocking collectives: 104 us -> 118 us  [exchange(): return lax.all_to_all(chunks, axes, 0, 0, tiled=False)]
    all_to_all x8 -> x7, starting transfers between devices: 42.8 us -> 33 us  [exchange(): return lax.all_to_all(chunks, axes, 0, 0, tiled=False)]
    ppermute x4 -> x5, starting transfers between devices: 12.2 us -> 16.8 us  [swap(): return lax.ppermute(value, 'c', [(0, 1), (1, 0)])]
    all_gather x1 -> x0, blocking collectives: 4.47 us -> none  [shards(): lax.all_gather(exchange(sent, CHIPS), 'c')]
    pallas_call x1 -> x4, Pallas kernels: 0.72 us -> 4.37 us  [the longest x1 2.1 us: shards(): on_chip(grad_kernel, (tall, tall, ((1, columns), F32), ((cell_devices, 1,...]
    unnamed x44 -> x34, local copies, waits for them, and re-layouts: 5.8 us -> 7.27 us
  transfers between devices with their start and end apart: 12 -> 13, of which waited for: 10 -> 11; matrix products, arithmetic and copies ran while one was open for 1% -> 1% of each run, Pallas kernels for 2% -> 3%
where the time goes in v5:
time: 290 us; the launch traced here: 288 us
  blocking collectives  131 us (45%)
  waiting for transfers between devices  58.7 us (20%)
  starting transfers between devices  49.9 us (17%)
  Pallas kernels  21.4 us (7%)
  between operations  14.3 us (5%)
  local copies, waits for them, and re-layouts  8.2 us (3%)
  other arithmetic  3.46 us (1%)
    all_to_all x9, blocking collectives, exchange(): return lax.all_to_all(chunks, axes, 0, 0, tiled=False)  118 us
    all_to_all x7, waiting for transfers between devices, exchange(): return lax.all_to_all(chunks, axes, 0, 0, tiled=False)  52.6 us
    all_to_all x7, starting transfers between devices, exchange(): return lax.all_to_all(chunks, axes, 0, 0, tiled=False)  33 us
    ppermute x5, starting transfers between devices, swap(): return lax.ppermute(value, 'c', [(0, 1), (1, 0)])  16.8 us
    pallas_call x9, Pallas kernels, shards(): on_chip(next_pass, (sent_shape, u_shape, v_shape), 'next_pass')  13.5 us
    all_gather x1, blocking collectives, shards(): lax.all_gather(to_all(piece.astype(BF16), CHIPS), 'c')  12.9 us
    unnamed x34, local copies, waits for them, and re-layouts  7.27 us
  transfers between devices with their start and end apart: 13, of which 11 were waited for; matrix products, arithmetic and copies ran while one was open for 1% of the time, Pallas kernels for 3%

profile of v5, /device:TPU:1, one launch (start us, length us, event | category | flops | bytes accessed | tf_op | source)
XLA Modules:
  0.0 288.4 jit_solution(884622065914973690)
XLA Ops:
  16.3 18.8 %all_to_all.80.got_ref = f32[32,3,4,128]{3,2,1,0:T(4,128)S(1)} all-to-all(f32[32,3,4,128]{3,2,1,0:T(4,128)S(1)} %copy_add_fusion), channel_id=1, replica_groups=mesh['y'=4,'z'=8,'c'=2,'x'=4] {'y','z'}, dimensions={0} | all-to-all | bytes 393216 | tf_op jit(solution)/shard_map/all_to_all | solution.py:28
  35.7 4.0 %all-to-all-start.1 = ((f32[4,16,128]{2,1,0:T(8,128)}), f32[4,16,128]{2,1,0:T(8,128)S(1)}, u32[]{:S(2)}, u32[]{:S(2)}) async-start(f32[4,16,128]{2,1,0:T(8,128)} %chunk.1), calls=%async_computation.1 | async-start | bytes 65536 | tf_op jit(solution)/shard_map/all_to_all | solution.py:28
  39.8 4.3 %all-to-all-done.1.got_ref = f32[4,16,128]{2,1,0:T(8,128)S(1)} async-done(((f32[4,16,128]{2,1,0:T(8,128)}), f32[4,16,128]{2,1,0:T(8,128)S(1)}, u32[]{:S(2)}, u32[]{:S(2)}) %all-to-all-start.1) | async-done | bytes 32800 | tf_op jit(solution)/shard_map/all_to_all | solution.py:28
  44.9 5.5 %all-to-all-start.2 = ((bf16[32,16,512]{2,1,0:T(8,128)(2,1)}), bf16[32,16,512]{2,1,0:T(8,128)(2,1)S(1)}, u32[]{:S(2)}, u32[]{:S(2)}) async-start(bf16[32,16,512]{2,1,0:T(8,128)(2,1)} %get-tuple-element.43), calls=%async_computation.2 | async-start | bytes 1048576 | tf_op jit(solution)/shard_map/all_to_all | solution.py:28
  51.2 11.3 %all-to-all-done.2 = bf16[32,16,512]{2,1,0:T(8,128)(2,1)S(1)} async-done(((bf16[32,16,512]{2,1,0:T(8,128)(2,1)}), bf16[32,16,512]{2,1,0:T(8,128)(2,1)S(1)}, u32[]{:S(2)}, u32[]{:S(2)}) %all-to-all-start.2) | async-done | bytes 524320 | tf_op jit(solution)/shard_map/all_to_all | solution.py:28
  62.5 5.5 %collective-permute-start.2 = (bf16[512,512]{1,0:T(8,128)(2,1)S(1)}, bf16[512,512]{1,0:T(8,128)(2,1)S(1)}, u32[]{:S(2)}, u32[]{:S(2)}) collective-permute-start(bf16[512,512]{1,0:T(8,128)(2,1)S(1)} %bitcast.34), channel_id=1, source_target_pairs={{0,4},{4,0},{1,5},{5,1},{2,6},{6,2},{3,7},{7,3},{8,12},{12,8},{9,1... | collective-permute-start | bytes 1572872 | tf_op jit(solution)/shard_map/ppermute | solution.py:37
  72.6 6.3 %all-to-all-start.3 = ((f32[64,1,128]{2,1,0:T(1,128)}), f32[64,1,128]{2,1,0:T(1,128)S(1)}, u32[]{:S(2)}, u32[]{:S(2)}) async-start(f32[64,1,128]{2,1,0:T(1,128)} %get-tuple-element.45), calls=%async_computation.3 | async-start | bytes 65536 | tf_op jit(solution)/shard_map/all_to_all | solution.py:28
  80.9 7.2 %all-to-all-done.3.peak_ref = f32[64,1,128]{2,1,0:T(1,128)S(1)} async-done(((f32[64,1,128]{2,1,0:T(1,128)}), f32[64,1,128]{2,1,0:T(1,128)S(1)}, u32[]{:S(2)}, u32[]{:S(2)}) %all-to-all-start.3) | async-done | bytes 32800 | tf_op jit(solution)/shard_map/all_to_all | solution.py:28
  95.9 12.0 %all_to_all.81.got_ref = bf16[32,8,128]{2,1,0:T(8,128)(2,1)S(1)} all-to-all(bf16[32,8,128]{2,1,0:T(8,128)(2,1)S(1)} %get-tuple-element.50), channel_id=1, replica_groups=mesh['y'=4,'z'=8,'c'=2,'x'=4] {'y','z'}, dimensions={0} | all-to-all | bytes 131072 | tf_op jit(solution)/shard_map/all_to_all | solution.py:28
  109.4 11.9 %all_to_all.82.got_ref = bf16[32,8,128]{2,1,0:T(8,128)(2,1)S(1)} all-to-all(bf16[32,8,128]{2,1,0:T(8,128)(2,1)S(1)} %get-tuple-element.52), channel_id=1, replica_groups=mesh['y'=4,'z'=8,'c'=2,'x'=4] {'y','z'}, dimensions={0} | all-to-all | bytes 131072 | tf_op jit(solution)/shard_map/all_to_all | solution.py:28
  122.7 12.0 %all_to_all.83.got_ref = bf16[32,8,128]{2,1,0:T(8,128)(2,1)S(1)} all-to-all(bf16[32,8,128]{2,1,0:T(8,128)(2,1)S(1)} %get-tuple-element.54), channel_id=1, replica_groups=mesh['y'=4,'z'=8,'c'=2,'x'=4] {'y','z'}, dimensions={0} | all-to-all | bytes 131072 | tf_op jit(solution)/shard_map/all_to_all | solution.py:28
  136.2 11.9 %all_to_all.84.got_ref = bf16[32,8,128]{2,1,0:T(8,128)(2,1)S(1)} all-to-all(bf16[32,8,128]{2,1,0:T(8,128)(2,1)S(1)} %get-tuple-element.56), channel_id=1, replica_groups=mesh['y'=4,'z'=8,'c'=2,'x'=4] {'y','z'}, dimensions={0} | all-to-all | bytes 131072 | tf_op jit(solution)/shard_map/all_to_all | solution.py:28
  149.5 12.0 %all_to_all.85.got_ref = bf16[32,8,128]{2,1,0:T(8,128)(2,1)S(1)} all-to-all(bf16[32,8,128]{2,1,0:T(8,128)(2,1)S(1)} %get-tuple-element.58), channel_id=1, replica_groups=mesh['y'=4,'z'=8,'c'=2,'x'=4] {'y','z'}, dimensions={0} | all-to-all | bytes 131072 | tf_op jit(solution)/shard_map/all_to_all | solution.py:28
  163.2 3.9 %all-to-all-start.9 = ((bf16[32,8,128]{2,1,0:T(8,128)(2,1)}), bf16[32,8,128]{2,1,0:T(8,128)(2,1)S(1)}, u32[]{:S(2)}, u32[]{:S(2)}) async-start(bf16[32,8,128]{2,1,0:T(8,128)(2,1)} %get-tuple-element.60), calls=%async_computation.9 | async-start | bytes 131072 | tf_op jit(solution)/shard_map/all_to_all | solution.py:28
  167.1 6.5 %collective-permute-start.4 = (bf16[512,512]{1,0:T(8,128)(2,1)S(1)}, bf16[512,512]{1,0:T(8,128)(2,1)S(1)}, u32[]{:S(2)}, u32[]{:S(2)}) collective-permute-start(bf16[512,512]{1,0:T(8,128)(2,1)S(1)} %copy-done.11), channel_id=1, source_target_pairs={{0,4},{4,0},{1,5},{5,1},{2,6},{6,2},{3,7},{7,3},{8,12},{12,8},{9,1... | collective-permute-start | bytes 1572872 | tf_op jit(solution)/shard_map/ppermute | solution.py:37
  177.4 15.8 %all_to_all.86.got_ref = bf16[32,8,128]{2,1,0:T(8,128)(2,1)S(1)} all-to-all(bf16[32,8,128]{2,1,0:T(8,128)(2,1)S(1)} %get-tuple-element.62), channel_id=1, replica_groups=mesh['y'=4,'z'=8,'c'=2,'x'=4] {'y','z'}, dimensions={0} | all-to-all | bytes 131072 | tf_op jit(solution)/shard_map/all_to_all | solution.py:28
  194.7 11.9 %all_to_all.87.got_ref = bf16[32,8,128]{2,1,0:T(8,128)(2,1)S(1)} all-to-all(bf16[32,8,128]{2,1,0:T(8,128)(2,1)S(1)} %get-tuple-element.64), channel_id=1, replica_groups=mesh['y'=4,'z'=8,'c'=2,'x'=4] {'y','z'}, dimensions={0} | all-to-all | bytes 131072 | tf_op jit(solution)/shard_map/all_to_all | solution.py:28
  208.1 11.8 %all_to_all.88.got_ref = bf16[32,8,128]{2,1,0:T(8,128)(2,1)S(1)} all-to-all(bf16[32,8,128]{2,1,0:T(8,128)(2,1)S(1)} %get-tuple-element.66), channel_id=1, replica_groups=mesh['y'=4,'z'=8,'c'=2,'x'=4] {'y','z'}, dimensions={0} | all-to-all | bytes 131072 | tf_op jit(solution)/shard_map/all_to_all | solution.py:28
  225.5 8.8 %all-to-all-done.13.got_ref = bf16[32,8,128]{2,1,0:T(8,128)(2,1)S(1)} async-done(((bf16[32,8,128]{2,1,0:T(8,128)(2,1)}), bf16[32,8,128]{2,1,0:T(8,128)(2,1)S(1)}, u32[]{:S(2)}, u32[]{:S(2)}) %all-to-all-start.13) | async-done | bytes 65568 | tf_op jit(solution)/shard_map/all_to_all | solution.py:28
  236.0 3.9 %all-to-all-start.14 = ((f32[32,8,512]{2,1,0:T(8,128)}), f32[32,8,512]{2,1,0:T(8,128)S(1)}, u32[]{:S(2)}, u32[]{:S(2)}) async-start(f32[32,8,512]{2,1,0:T(8,128)} %bitcast.20), calls=%async_computation.14 | async-start | bytes 1048576 | tf_op jit(solution)/shard_map/all_to_all | solution.py:28
  240.7 10.6 %all-to-all-done.14 = f32[32,8,512]{2,1,0:T(8,128)S(1)} async-done(((f32[32,8,512]{2,1,0:T(8,128)}), f32[32,8,512]{2,1,0:T(8,128)S(1)}, u32[]{:S(2)}, u32[]{:S(2)}) %all-to-all-start.14) | async-done | bytes 524320 | tf_op jit(solution)/shard_map/all_to_all | solution.py:28
  252.1 5.6 %all-to-all-start.15 = ((bf16[32,8,512]{2,1,0:T(8,128)(2,1)}), bf16[32,8,512]{2,1,0:T(8,128)(2,1)S(1)}, u32[]{:S(2)}, u32[]{:S(2)}) async-start(bf16[32,8,512]{2,1,0:T(8,128)(2,1)} %broadcast_in_dim.17), calls=%async_computation.15 | async-start | bytes 524288 | tf_op jit(solution)/shard_map/all_to_all | solution.py:28
  259.4 7.9 %all-to-all-done.15 = bf16[32,8,512]{2,1,0:T(8,128)(2,1)S(1)} async-done(((bf16[32,8,512]{2,1,0:T(8,128)(2,1)}), bf16[32,8,512]{2,1,0:T(8,128)(2,1)S(1)}, u32[]{:S(2)}, u32[]{:S(2)}) %all-to-all-start.15) | async-done | bytes 262176 | tf_op jit(solution)/shard_map/all_to_all | solution.py:28
  267.3 12.9 %all-gather = bf16[64,8,512]{2,1,0:T(8,128)(2,1)S(1)} all-gather(bf16[32,8,512]{2,1,0:T(8,128)(2,1)S(1)} %all-to-all-done.15), channel_id=2, replica_groups=mesh['y'=4,'z'=8,'c'=2,'x'=4] {'c'}, dimensions={0}, use_global_device_ids=true | all-gather | bytes 786432 | tf_op jit(solution)/shard_map/all_gather | solution.py:346
  (85 shorter events, 51.5 us)
Async XLA Ops:
  11.7 4.4 %collective-permute-start.1 = (f32[32,3,4,128]{3,2,1,0:T(4,128)S(1)}, f32[32,3,4,128]{3,2,1,0:T(4,128)S(1)}, u32[]{:S(2)}, u32[]{:S(2)}) collective-permute-start(f32[32,3,4,128]{3,2,1,0:T(4,128)S(1)} %copy.18), channel_id=1, source_target_pairs={{0,4},{4,0},{1,5},{5,1},{2,6},{6,2},{3,7},{7,3},{8,12},{12,8},{9,1... | collective-permute-start | bytes 589832 | tf_op jit(solution)/shard_map/ppermute | solution.py:37
  16.1 19.0 %copy-start.14 = (f32[128]{0:T(128)S(1)}, f32[128]{0:T(128)}, u32[]{:S(2)}) copy-start(f32[128]{0:T(128)} %param.12) | copy-start | bytes 1540
  16.2 23.5 %copy-start.1 = (f32[512,128]{1,0:T(8,128)S(1)}, f32[512,128]{1,0:T(8,128)}, u32[]{:S(2)}) copy-start(f32[512,128]{1,0:T(8,128)} %q_ref.3) | copy-start | bytes 786436
  16.2 23.5 %copy-start.3 = (f32[512,128]{1,0:T(8,128)S(1)}, f32[512,128]{1,0:T(8,128)}, u32[]{:S(2)}) copy-start(f32[512,128]{1,0:T(8,128)} %r_ref.3) | copy-start | bytes 786436
  35.7 8.3 %all-to-all-start.1 = ((f32[4,16,128]{2,1,0:T(8,128)}), f32[4,16,128]{2,1,0:T(8,128)S(1)}, u32[]{:S(2)}, u32[]{:S(2)}) async-start(f32[4,16,128]{2,1,0:T(8,128)} %chunk.1), calls=%async_computation.1 | async-start | bytes 65536 | tf_op jit(solution)/shard_map/all_to_all | solution.py:28
  44.9 17.6 %all-to-all-start.2 = ((bf16[32,16,512]{2,1,0:T(8,128)(2,1)}), bf16[32,16,512]{2,1,0:T(8,128)(2,1)S(1)}, u32[]{:S(2)}, u32[]{:S(2)}) async-start(bf16[32,16,512]{2,1,0:T(8,128)(2,1)} %get-tuple-element.43), calls=%async_computation.2 | async-start | bytes 1048576 | tf_op jit(solution)/shard_map/all_to_all | solution.py:28
  50.4 30.6 %all-gather.3.cloned.1.call-start = ((), (), s32[]{:S(2)}) async-start(), calls=%async_computation.16 | async-start | bytes 1310720 | tf_op jit(solution)/shard_map/all_gather | solution.py:278
  50.4 19.1 %copy-start.10 = (bf16[512,256]{1,0:T(8,128)(2,1)S(1)}, bf16[512,256]{1,0:T(8,128)(2,1)}, u32[]{:S(2)}) copy-start(bf16[512,256]{1,0:T(8,128)(2,1)} %y_ref.3) | copy-start | bytes 786436
  51.1 18.4 %copy-start.8 = (bf16[512,256]{1,0:T(8,128)(2,1)S(1)}, bf16[512,256]{1,0:T(8,128)(2,1)}, u32[]{:S(2)}) copy-start(bf16[512,256]{1,0:T(8,128)(2,1)} %x_ref.3) | copy-start | bytes 786436
  62.5 7.0 %collective-permute-start.2 = (bf16[512,512]{1,0:T(8,128)(2,1)S(1)}, bf16[512,512]{1,0:T(8,128)(2,1)S(1)}, u32[]{:S(2)}, u32[]{:S(2)}) collective-permute-start(bf16[512,512]{1,0:T(8,128)(2,1)S(1)} %bitcast.34), channel_id=1, source_target_pairs={{0,4},{4,0},{1,5},{5,1},{2,6},{6,2},{3,7},{7,3},{8,12},{12,8},{9,1... | collective-permute-start | bytes 1572872 | tf_op jit(solution)/shard_map/ppermute | solution.py:37
  71.6 1.0 copy-start.5
  72.6 15.6 %all-to-all-start.3 = ((f32[64,1,128]{2,1,0:T(1,128)}), f32[64,1,128]{2,1,0:T(1,128)S(1)}, u32[]{:S(2)}, u32[]{:S(2)}) async-start(f32[64,1,128]{2,1,0:T(1,128)} %get-tuple-element.45), calls=%async_computation.3 | async-start | bytes 65536 | tf_op jit(solution)/shard_map/all_to_all | solution.py:28
  88.2 1.2 copy-start.4
  89.4 1.2 copy-start.6
  91.4 4.6 %copy-start.12 = (f32[512,128]{1,0:T(8,128)}, f32[512,128]{1,0:T(8,128)S(1)}, u32[]{:S(2)}) copy-start(f32[512,128]{1,0:T(8,128)S(1)} %get-tuple-element.73) | copy-start | bytes 786436
  91.4 3.1 %collective-permute-start.3 = (bf16[1024,512]{1,0:T(8,128)(2,1)S(1)}, bf16[1024,512]{1,0:T(8,128)(2,1)S(1)}, u32[]{:S(2)}, u32[]{:S(2)}) collective-permute-start(bf16[1024,512]{1,0:T(8,128)(2,1)S(1)} %get-tuple-element.49.own_ref), channel_id=1, source_target_pairs={{0,4},{4,0},{1,5},{5,1},{2,6},{6,2},{3,7},{7,3},{8,12},{12,8},{9,1... | collective-permute-start | bytes 3145736 | tf_op jit(solution)/shard_map/ppermute | solution.py:37
  92.2 2.3 collective-permute-start
  161.5 5.6 %copy-start.11 = (bf16[512,512]{1,0:T(8,128)(2,1)S(1)}, bf16[512,512]{1,0:T(8,128)(2,1)}, u32[]{:S(2)}) copy-start(bf16[512,512]{1,0:T(8,128)(2,1)} %expr_ref.1) | copy-start | bytes 1572868
  163.2 12.7 %all-to-all-start.9 = ((bf16[32,8,128]{2,1,0:T(8,128)(2,1)}), bf16[32,8,128]{2,1,0:T(8,128)(2,1)S(1)}, u32[]{:S(2)}, u32[]{:S(2)}) async-start(bf16[32,8,128]{2,1,0:T(8,128)(2,1)} %get-tuple-element.60), calls=%async_computation.9 | async-start | bytes 131072 | tf_op jit(solution)/shard_map/all_to_all | solution.py:28
  167.1 58.3 %collective-permute-start.4 = (bf16[512,512]{1,0:T(8,128)(2,1)S(1)}, bf16[512,512]{1,0:T(8,128)(2,1)S(1)}, u32[]{:S(2)}, u32[]{:S(2)}) collective-permute-start(bf16[512,512]{1,0:T(8,128)(2,1)S(1)} %copy-done.11), channel_id=1, source_target_pairs={{0,4},{4,0},{1,5},{5,1},{2,6},{6,2},{3,7},{7,3},{8,12},{12,8},{9,1... | collective-permute-start | bytes 1572872 | tf_op jit(solution)/shard_map/ppermute | solution.py:37
  221.6 12.7 %all-to-all-start.13 = ((bf16[32,8,128]{2,1,0:T(8,128)(2,1)}), bf16[32,8,128]{2,1,0:T(8,128)(2,1)S(1)}, u32[]{:S(2)}, u32[]{:S(2)}) async-start(bf16[32,8,128]{2,1,0:T(8,128)(2,1)} %get-tuple-element.70), calls=%async_computation.13 | async-start | bytes 131072 | tf_op jit(solution)/shard_map/all_to_all | solution.py:28
  236.0 15.3 %all-to-all-start.14 = ((f32[32,8,512]{2,1,0:T(8,128)}), f32[32,8,512]{2,1,0:T(8,128)S(1)}, u32[]{:S(2)}, u32[]{:S(2)}) async-start(f32[32,8,512]{2,1,0:T(8,128)} %bitcast.20), calls=%async_computation.14 | async-start | bytes 1048576 | tf_op jit(solution)/shard_map/all_to_all | solution.py:28
  252.1 5.6 %copy-start.13 = (f32[512,128]{1,0:T(8,128)S(1)}, f32[512,128]{1,0:T(8,128)}, u32[]{:S(2)}) copy-start(f32[512,128]{1,0:T(8,128)} %copy-done.12) | copy-start | bytes 786436
  252.1 15.3 %all-to-all-start.15 = ((bf16[32,8,512]{2,1,0:T(8,128)(2,1)}), bf16[32,8,512]{2,1,0:T(8,128)(2,1)S(1)}, u32[]{:S(2)}, u32[]{:S(2)}) async-start(bf16[32,8,512]{2,1,0:T(8,128)(2,1)} %broadcast_in_dim.17), calls=%async_computation.15 | async-start | bytes 524288 | tf_op jit(solution)/shard_map/all_to_all | solution.py:28
  (6 other events, 5.4 us)
Sparse Core Ops, SparseCore 0:
  53.6 27.3 all-gather.2

commit v6 on v5

--- a/solution.py
+++ b/solution.py
@@ -10,6 +10,7 @@
 SCALE = 0.0625
 GAMMA = 10.0
 POWER = 0.8
+LIMIT = 12 << 20
 
 CHIPS = ("y", "z")
 CELLS = ("y", "z", "c")
@@ -74,11 +75,30 @@
     return [row[:, i * width : (i + 1) * width] for i in range(count)]
 
 
-def start_kernel(x_ref, y_ref, q_ref, r_ref, xq_ref, yr_ref, vec_ref):
+def start_kernel(
+    x_hbm, y_hbm, q_hbm, r_hbm, xq_ref, yr_ref, vec_ref, cast_ref, x_ref, y_ref, q_ref, r_ref, sems
+):
+    pieces = sems.shape[1]
+    copies = []
+    for i, (source, target) in enumerate(
+        ((x_hbm, x_ref), (q_hbm, q_ref), (y_hbm, y_ref), (r_hbm, r_ref))
+    ):
+        size = source.shape[0] // pieces
+        for k in range(pieces):
+            part = pl.ds(k * size, size)
+            copies.append(pltpu.make_async_copy(source.at[part], target.at[part], sems.at[i, k]))
+    for copy in copies:
+        copy.start()
     rows = []
-    for emb_ref, factor_ref, cross_ref in ((x_ref, q_ref, xq_ref), (y_ref, r_ref, yr_ref)):
+    for side, (emb_ref, factor_ref, cross_ref) in enumerate(
+        ((x_ref, q_ref, xq_ref), (y_ref, r_ref, yr_ref))
+    ):
+        for copy in copies[2 * side * pieces : 2 * (side + 1) * pieces]:
+            copy.wait()
         factor = factor_ref[...]
-        cross_ref[...] = contract_rows(emb_ref[...], factor.astype(BF16))
+        rounded = factor.astype(BF16)
+        cast_ref[side] = rounded
+        cross_ref[...] = contract_rows(emb_ref[...], rounded)
         norms = jnp.sum(jnp.square(emb_ref[...].astype(F32)), axis=1, keepdims=True)
         rows.append(jnp.sum(norms * factor, axis=0, keepdims=True))
         rows.append(jnp.sum(factor, axis=0, keepdims=True))
@@ -150,23 +170,25 @@
 
 
 def kern_kernel(
-    here_ref, peak_ref, grad_q_ref, grad_r_ref, grad_g_ref, vec_ref, all_ref, q_ref, r_ref,
-    kern_ref, own_q_ref, own_r_ref, log_ref,
+    here_ref, peak_ref, grad_q_ref, grad_r_ref, grad_g_ref, vec_ref, q_ref, r_ref, *refs
 ):
-    ranks = all_ref.shape[0]
+    from_others, (kern_ref, own_q_ref, own_r_ref, log_ref) = refs[:-4], refs[-4:]
+    ranks = len(from_others) + 1
     rows, width = q_ref.shape
     peak = jnp.max(jnp.max(peak_ref[...], axis=0), axis=1, keepdims=True)
     eta = GAMMA / (peak + 1e-06)
     kern_g = vec_ref[5:6] * jnp.exp(-eta * grad_g_ref[...])
     log_ref[...] = jnp.concatenate(in_rows(jnp.log(kern_g), ranks), axis=0)
-    mine = pl.ds(pl.multiple_of(here_ref[0] * width, width), width)
-    for side, (grad_ref, factor_ref, own_ref) in enumerate(
-        ((grad_q_ref, q_ref, own_q_ref), (grad_r_ref, r_ref, own_r_ref))
-    ):
-        own_ref[...] = factor_ref[...] * jnp.exp(-eta * grad_ref[:, mine])
-        for block in range(ranks):
-            lanes = pl.ds(block * width, width)
-            kern = all_ref[block, side].astype(F32) * jnp.exp(-eta * grad_ref[:, lanes])
+    for shift in range(ranks):
+        block = lax.rem(here_ref[0] + ranks - shift, ranks)
+        lanes = pl.ds(pl.multiple_of(block * width, width), width)
+        for side, (grad_ref, factor_ref, own_ref) in enumerate(
+            ((grad_q_ref, q_ref, own_q_ref), (grad_r_ref, r_ref, own_r_ref))
+        ):
+            factor = from_others[shift - 1][side].astype(F32) if shift else factor_ref[...]
+            kern = factor * jnp.exp(-eta * grad_ref[:, lanes])
+            if shift == 0:
+                own_ref[...] = kern
             kern_ref[pl.ds(side * rows, rows), lanes] = kern.astype(BF16)
 
 
@@ -244,17 +266,20 @@
     part_ref[...] = total
 
 
-def on_chip(kernel, shapes, name, scalars=0, inputs=0):
+def on_chip(kernel, shapes, name, scalars=0, inputs=0, off_chip=0, scratch=(), limit=LIMIT):
     specs = {}
     if scalars:
         specs["in_specs"] = [pl.BlockSpec(memory_space=pltpu.SMEM)] * scalars + [
             pl.BlockSpec(memory_space=pltpu.VMEM)
         ] * inputs
+    if off_chip:
+        specs["in_specs"] = [pl.BlockSpec(memory_space=pltpu.HBM)] * off_chip
     return pl.pallas_call(
         kernel,
         out_shape=tuple(jax.ShapeDtypeStruct(shape, dtype) for shape, dtype in shapes),
+        scratch_shapes=scratch,
         **specs,
-        compiler_params=pltpu.CompilerParams(vmem_limit_bytes=32 << 20),
+        compiler_params=pltpu.CompilerParams(vmem_limit_bytes=limit),
         name=name,
     )
 
@@ -275,10 +300,29 @@
     masses = jnp.stack([a_mass, b_mass])
     masses = jnp.concatenate([masses, swap(masses)])
     core_index = core.astype(jnp.int32)[None]
-    every = lax.all_gather(jnp.stack([q_factor, r_factor]).astype(BF16), "x")
-    part_xq, part_yr, part_vec = on_chip(
-        start_kernel, (((dim, width), F32), ((dim, width), F32), ((4, width), F32)), "start"
+    part_xq, part_yr, part_vec, rounded = on_chip(
+        start_kernel,
+        (
+            ((dim, width), F32),
+            ((dim, width), F32),
+            ((4, width), F32),
+            ((2, rows, width), BF16),
+        ),
+        "start",
+        off_chip=4,
+        limit=60 << 20,
+        scratch=[
+            pltpu.VMEM(x_emb.shape, BF16),
+            pltpu.VMEM(y_emb.shape, BF16),
+            pltpu.VMEM(q_factor.shape, F32),
+            pltpu.VMEM(r_factor.shape, F32),
+            pltpu.SemaphoreType.DMA((4, 2)),
+        ],
     )(x_emb, y_emb, q_factor, r_factor)
+    from_others = [
+        lax.ppermute(rounded, "x", [(i, (i + shift) % ranks) for i in range(ranks)])
+        for shift in range(1, ranks)
+    ]
     part_cross = jnp.concatenate(
         [part.reshape(2, others, share, width) for part in (part_xq, part_yr)], axis=2
     )
@@ -310,10 +354,10 @@
         (((2 * rows, columns), BF16), ((rows, width), F32), ((rows, width), F32), ((ranks, width), F32)),
         "kern",
         scalars=1,
-        inputs=8,
+        inputs=7 + ranks - 1,
     )(
         here.astype(jnp.int32)[None], exchange(peak, CELLS), grad_q, grad_r, grad_g, vec,
-        every, q_factor, r_factor,
+        q_factor, r_factor, *from_others,
     )
     theirs = swap(kerns)
     sent_shape = ((others, 2 * ranks, width), BF16)

time: 290 us -> 277 us (0.955)
  blocking collectives: 131 us -> 156 us
  waiting for transfers between devices: 58.7 us -> 39.7 us
  between operations: 14.3 us -> 0.9 us
  starting transfers between devices: 49.9 us -> 43.5 us
    all_to_all x9 -> x11, blocking collectives: 118 us -> 143 us  [exchange(): return lax.all_to_all(chunks, axes, 0, 0, tiled=False)]
    all_to_all x7 -> x5, waiting for transfers between devices: 52.6 us -> 34.1 us  [exchange(): return lax.all_to_all(chunks, axes, 0, 0, tiled=False)]
    all_to_all x7 -> x5, starting transfers between devices: 33 us -> 24 us  [exchange(): return lax.all_to_all(chunks, axes, 0, 0, tiled=False)]
    ppermute x0 -> x3, waiting for transfers between devices: none -> 2.96 us  [shards(): lax.ppermute(rounded, 'x', [(i, (i + shift) % ranks) for i in range(ranks)])]
    unnamed x34 -> x40, local copies, waits for them, and re-layouts: 7.27 us -> 7.41 us
  transfers between devices with their start and end apart: 13 -> 13, of which waited for: 11 -> 8; matrix products, arithmetic and copies ran while one was open for 1% -> 1% of each run, Pallas kernels for 3% -> 3%
where the time goes in v6:
time: 277 us; the launch traced here: 275 us
  blocking collectives  156 us (56%)
  starting transfers between devices  43.5 us (16%)
  waiting for transfers between devices  39.7 us (14%)
  Pallas kernels  21.9 us (8%)
  local copies, waits for them, and re-layouts  8.34 us (3%)
  other arithmetic  3.63 us (1%)
    all_to_all x11, blocking collectives, exchange(): return lax.all_to_all(chunks, axes, 0, 0, tiled=False)  143 us
    all_to_all x5, waiting for transfers between devices, exchange(): return lax.all_to_all(chunks, axes, 0, 0, tiled=False)  34.1 us
    all_to_all x5, starting transfers between devices, exchange(): return lax.all_to_all(chunks, axes, 0, 0, tiled=False)  24 us
    ppermute x5, starting transfers between devices, swap(): return lax.ppermute(value, 'c', [(0, 1), (1, 0)])  16.6 us
    pallas_call x9, Pallas kernels, shards(): on_chip(next_pass, (sent_shape, u_shape, v_shape), 'next_pass')  13.5 us
    all_gather x1, blocking collectives, shards(): lax.all_gather(to_all(piece.astype(BF16), CHIPS), 'c')  13 us
    unnamed x40, local copies, waits for them, and re-layouts  7.41 us
  transfers between devices with their start and end apart: 13, of which 8 were waited for; matrix products, arithmetic and copies ran while one was open for 1% of the time, Pallas kernels for 3%

profile of v6, /device:TPU:1, one launch (start us, length us, event | category | flops | bytes accessed | tf_op | source)
XLA Modules:
  0.0 275.5 jit_solution(1253343408086830554)
XLA Ops:
  4.9 3.3 %collective-permute-start.1 = (f32[32,3,4,128]{3,2,1,0:T(4,128)S(1)}, f32[32,3,4,128]{3,2,1,0:T(4,128)S(1)}, u32[]{:S(2)}, u32[]{:S(2)}) collective-permute-start(f32[32,3,4,128]{3,2,1,0:T(4,128)S(1)} %copy.18), channel_id=1, source_target_pairs={{0,4},{4,0},{1,5},{5,1},{2,6},{6,2},{3,7},{7,3},{8,12},{12,8},{9,1... | collective-permute-start | bytes 589832 | tf_op jit(solution)/shard_map/ppermute | solution.py:38
  9.5 18.7 %all_to_all.80.got_ref = f32[32,3,4,128]{3,2,1,0:T(4,128)S(1)} all-to-all(f32[32,3,4,128]{3,2,1,0:T(4,128)S(1)} %copy_add_fusion), channel_id=1, replica_groups=mesh['y'=4,'z'=8,'c'=2,'x'=4] {'y','z'}, dimensions={0} | all-to-all | bytes 393216 | tf_op jit(solution)/shard_map/all_to_all | solution.py:29
  28.9 8.1 %all_to_all.81.got_ref = f32[4,16,128]{2,1,0:T(8,128)S(1)} all-to-all(f32[4,16,128]{2,1,0:T(8,128)S(1)} %chunk.1), channel_id=1, replica_groups=mesh['y'=4,'z'=8,'c'=2,'x'=4] {'x'}, dimensions={0} | all-to-all | bytes 65536 | tf_op jit(solution)/shard_map/all_to_all | solution.py:29
  37.1 17.5 %all_to_all.82 = bf16[32,16,512]{2,1,0:T(8,128)(2,1)S(1)} all-to-all(bf16[32,16,512]{2,1,0:T(8,128)(2,1)S(1)} %get-tuple-element.44), channel_id=1, replica_groups=mesh['y'=4,'z'=8,'c'=2,'x'=4] {'y','z'}, dimensions={0} | all-to-all | bytes 1048576 | tf_op jit(solution)/shard_map/all_to_all | solution.py:29
  54.6 5.5 %collective-permute-start.2 = (bf16[512,512]{1,0:T(8,128)(2,1)S(1)}, bf16[512,512]{1,0:T(8,128)(2,1)S(1)}, u32[]{:S(2)}, u32[]{:S(2)}) collective-permute-start(bf16[512,512]{1,0:T(8,128)(2,1)S(1)} %bitcast.30), channel_id=1, source_target_pairs={{0,4},{4,0},{1,5},{5,1},{2,6},{6,2},{3,7},{7,3},{8,12},{12,8},{9,1... | collective-permute-start | bytes 1572872 | tf_op jit(solution)/shard_map/ppermute | solution.py:38
  65.1 6.8 %all-to-all-start.3 = ((f32[64,1,128]{2,1,0:T(1,128)}), f32[64,1,128]{2,1,0:T(1,128)S(1)}, u32[]{:S(2)}, u32[]{:S(2)}) async-start(f32[64,1,128]{2,1,0:T(1,128)} %get-tuple-element.46), calls=%async_computation.3 | async-start | bytes 65536 | tf_op jit(solution)/shard_map/all_to_all | solution.py:29
  77.0 4.2 %all-to-all-done.3.peak_ref = f32[64,1,128]{2,1,0:T(1,128)S(1)} async-done(((f32[64,1,128]{2,1,0:T(1,128)}), f32[64,1,128]{2,1,0:T(1,128)S(1)}, u32[]{:S(2)}, u32[]{:S(2)}) %all-to-all-start.3) | async-done | bytes 32800 | tf_op jit(solution)/shard_map/all_to_all | solution.py:29
  90.2 11.8 %all_to_all.83.got_ref = bf16[32,8,128]{2,1,0:T(8,128)(2,1)S(1)} all-to-all(bf16[32,8,128]{2,1,0:T(8,128)(2,1)S(1)} %get-tuple-element.52), channel_id=1, replica_groups=mesh['y'=4,'z'=8,'c'=2,'x'=4] {'y','z'}, dimensions={0} | all-to-all | bytes 131072 | tf_op jit(solution)/shard_map/all_to_all | solution.py:29
  103.5 12.1 %all_to_all.84.got_ref = bf16[32,8,128]{2,1,0:T(8,128)(2,1)S(1)} all-to-all(bf16[32,8,128]{2,1,0:T(8,128)(2,1)S(1)} %get-tuple-element.54), channel_id=1, replica_groups=mesh['y'=4,'z'=8,'c'=2,'x'=4] {'y','z'}, dimensions={0} | all-to-all | bytes 131072 | tf_op jit(solution)/shard_map/all_to_all | solution.py:29
  117.0 12.0 %all_to_all.85.got_ref = bf16[32,8,128]{2,1,0:T(8,128)(2,1)S(1)} all-to-all(bf16[32,8,128]{2,1,0:T(8,128)(2,1)S(1)} %get-tuple-element.56), channel_id=1, replica_groups=mesh['y'=4,'z'=8,'c'=2,'x'=4] {'y','z'}, dimensions={0} | all-to-all | bytes 131072 | tf_op jit(solution)/shard_map/all_to_all | solution.py:29
  130.5 11.9 %all_to_all.86.got_ref = bf16[32,8,128]{2,1,0:T(8,128)(2,1)S(1)} all-to-all(bf16[32,8,128]{2,1,0:T(8,128)(2,1)S(1)} %get-tuple-element.58), channel_id=1, replica_groups=mesh['y'=4,'z'=8,'c'=2,'x'=4] {'y','z'}, dimensions={0} | all-to-all | bytes 131072 | tf_op jit(solution)/shard_map/all_to_all | solution.py:29
  143.8 11.9 %all_to_all.87.got_ref = bf16[32,8,128]{2,1,0:T(8,128)(2,1)S(1)} all-to-all(bf16[32,8,128]{2,1,0:T(8,128)(2,1)S(1)} %get-tuple-element.60), channel_id=1, replica_groups=mesh['y'=4,'z'=8,'c'=2,'x'=4] {'y','z'}, dimensions={0} | all-to-all | bytes 131072 | tf_op jit(solution)/shard_map/all_to_all | solution.py:29
  157.5 3.9 %all-to-all-start.9 = ((bf16[32,8,128]{2,1,0:T(8,128)(2,1)}), bf16[32,8,128]{2,1,0:T(8,128)(2,1)S(1)}, u32[]{:S(2)}, u32[]{:S(2)}) async-start(bf16[32,8,128]{2,1,0:T(8,128)(2,1)} %get-tuple-element.62), calls=%async_computation.9 | async-start | bytes 131072 | tf_op jit(solution)/shard_map/all_to_all | solution.py:29
  161.3 6.3 %collective-permute-start.7 = (bf16[512,512]{1,0:T(8,128)(2,1)S(1)}, bf16[512,512]{1,0:T(8,128)(2,1)S(1)}, u32[]{:S(2)}, u32[]{:S(2)}) collective-permute-start(bf16[512,512]{1,0:T(8,128)(2,1)S(1)} %copy-done.4), channel_id=1, source_target_pairs={{0,4},{4,0},{1,5},{5,1},{2,6},{6,2},{3,7},{7,3},{8,12},{12,8},{9,1... | collective-permute-start | bytes 1572872 | tf_op jit(solution)/shard_map/ppermute | solution.py:38
  171.6 15.6 %all_to_all.88.got_ref = bf16[32,8,128]{2,1,0:T(8,128)(2,1)S(1)} all-to-all(bf16[32,8,128]{2,1,0:T(8,128)(2,1)S(1)} %get-tuple-element.64), channel_id=1, replica_groups=mesh['y'=4,'z'=8,'c'=2,'x'=4] {'y','z'}, dimensions={0} | all-to-all | bytes 131072 | tf_op jit(solution)/shard_map/all_to_all | solution.py:29
  188.7 11.9 %all_to_all.89.got_ref = bf16[32,8,128]{2,1,0:T(8,128)(2,1)S(1)} all-to-all(bf16[32,8,128]{2,1,0:T(8,128)(2,1)S(1)} %get-tuple-element.66), channel_id=1, replica_groups=mesh['y'=4,'z'=8,'c'=2,'x'=4] {'y','z'}, dimensions={0} | all-to-all | bytes 131072 | tf_op jit(solution)/shard_map/all_to_all | solution.py:29
  202.0 11.8 %all_to_all.90.got_ref = bf16[32,8,128]{2,1,0:T(8,128)(2,1)S(1)} all-to-all(bf16[32,8,128]{2,1,0:T(8,128)(2,1)S(1)} %get-tuple-element.68), channel_id=1, replica_groups=mesh['y'=4,'z'=8,'c'=2,'x'=4] {'y','z'}, dimensions={0} | all-to-all | bytes 131072 | tf_op jit(solution)/shard_map/all_to_all | solution.py:29
  215.6 3.9 %all-to-all-start.13 = ((bf16[32,8,128]{2,1,0:T(8,128)(2,1)}), bf16[32,8,128]{2,1,0:T(8,128)(2,1)S(1)}, u32[]{:S(2)}, u32[]{:S(2)}) async-start(bf16[32,8,128]{2,1,0:T(8,128)(2,1)} %get-tuple-element.72), calls=%async_computation.13 | async-start | bytes 131072 | tf_op jit(solution)/shard_map/all_to_all | solution.py:29
  219.4 8.8 %all-to-all-done.13.got_ref = bf16[32,8,128]{2,1,0:T(8,128)(2,1)S(1)} async-done(((bf16[32,8,128]{2,1,0:T(8,128)(2,1)}), bf16[32,8,128]{2,1,0:T(8,128)(2,1)S(1)}, u32[]{:S(2)}, u32[]{:S(2)}) %all-to-all-start.13) | async-done | bytes 65568 | tf_op jit(solution)/shard_map/all_to_all | solution.py:29
  230.0 3.9 %all-to-all-start.14 = ((f32[32,8,512]{2,1,0:T(8,128)}), f32[32,8,512]{2,1,0:T(8,128)S(1)}, u32[]{:S(2)}, u32[]{:S(2)}) async-start(f32[32,8,512]{2,1,0:T(8,128)} %bitcast.18), calls=%async_computation.14 | async-start | bytes 1048576 | tf_op jit(solution)/shard_map/all_to_all | solution.py:29
  234.6 10.6 %all-to-all-done.14 = f32[32,8,512]{2,1,0:T(8,128)S(1)} async-done(((f32[32,8,512]{2,1,0:T(8,128)}), f32[32,8,512]{2,1,0:T(8,128)S(1)}, u32[]{:S(2)}, u32[]{:S(2)}) %all-to-all-start.14) | async-done | bytes 524320 | tf_op jit(solution)/shard_map/all_to_all | solution.py:29
  246.0 5.6 %all-to-all-start.15 = ((bf16[32,8,512]{2,1,0:T(8,128)(2,1)}), bf16[32,8,512]{2,1,0:T(8,128)(2,1)S(1)}, u32[]{:S(2)}, u32[]{:S(2)}) async-start(bf16[32,8,512]{2,1,0:T(8,128)(2,1)} %broadcast_in_dim.17), calls=%async_computation.15 | async-start | bytes 524288 | tf_op jit(solution)/shard_map/all_to_all | solution.py:29
  253.5 7.8 %all-to-all-done.15 = bf16[32,8,512]{2,1,0:T(8,128)(2,1)S(1)} async-done(((bf16[32,8,512]{2,1,0:T(8,128)(2,1)}), bf16[32,8,512]{2,1,0:T(8,128)(2,1)S(1)}, u32[]{:S(2)}, u32[]{:S(2)}) %all-to-all-start.15) | async-done | bytes 262176 | tf_op jit(solution)/shard_map/all_to_all | solution.py:29
  261.3 13.0 %all-gather = bf16[64,8,512]{2,1,0:T(8,128)(2,1)S(1)} all-gather(bf16[32,8,512]{2,1,0:T(8,128)(2,1)S(1)} %all-to-all-done.15), channel_id=2, replica_groups=mesh['y'=4,'z'=8,'c'=2,'x'=4] {'c'}, dimensions={0}, use_global_device_ids=true | all-gather | bytes 786432 | tf_op jit(solution)/shard_map/all_gather | solution.py:390
  (90 shorter events, 47.6 us)
Async XLA Ops:
  4.9 4.4 %collective-permute-start.1 = (f32[32,3,4,128]{3,2,1,0:T(4,128)S(1)}, f32[32,3,4,128]{3,2,1,0:T(4,128)S(1)}, u32[]{:S(2)}, u32[]{:S(2)}) collective-permute-start(f32[32,3,4,128]{3,2,1,0:T(4,128)S(1)} %copy.18), channel_id=1, source_target_pairs={{0,4},{4,0},{1,5},{5,1},{2,6},{6,2},{3,7},{7,3},{8,12},{12,8},{9,1... | collective-permute-start | bytes 589832 | tf_op jit(solution)/shard_map/ppermute | solution.py:38
  37.0 23.1 %copy-start.19 = (bf16[2,512,128]{2,1,0:T(8,128)(2,1)S(1)}, bf16[2,512,128]{2,1,0:T(8,128)(2,1)}, u32[]{:S(2)}) copy-start(bf16[2,512,128]{2,1,0:T(8,128)(2,1)} %get-tuple-element.50) | copy-start | bytes 786436
  37.0 25.9 %copy-start.2 = (bf16[512,256]{1,0:T(8,128)(2,1)S(1)}, bf16[512,256]{1,0:T(8,128)(2,1)}, u32[]{:S(2)}) copy-start(bf16[512,256]{1,0:T(8,128)(2,1)} %x_ref.1) | copy-start | bytes 786436
  37.1 25.9 %copy-start.3 = (bf16[512,256]{1,0:T(8,128)(2,1)S(1)}, bf16[512,256]{1,0:T(8,128)(2,1)}, u32[]{:S(2)}) copy-start(bf16[512,256]{1,0:T(8,128)(2,1)} %y_ref.1) | copy-start | bytes 786436
  54.6 8.4 %collective-permute-start.2 = (bf16[512,512]{1,0:T(8,128)(2,1)S(1)}, bf16[512,512]{1,0:T(8,128)(2,1)S(1)}, u32[]{:S(2)}, u32[]{:S(2)}) collective-permute-start(bf16[512,512]{1,0:T(8,128)(2,1)S(1)} %bitcast.30), channel_id=1, source_target_pairs={{0,4},{4,0},{1,5},{5,1},{2,6},{6,2},{3,7},{7,3},{8,12},{12,8},{9,1... | collective-permute-start | bytes 1572872 | tf_op jit(solution)/shard_map/ppermute | solution.py:38
  60.1 14.8 %collective-permute-start.3 = (bf16[2,512,128]{2,1,0:T(8,128)(2,1)S(1)}, bf16[2,512,128]{2,1,0:T(8,128)(2,1)S(1)}, u32[]{:S(2)}, u32[]{:S(2)}) collective-permute-start(bf16[2,512,128]{2,1,0:T(8,128)(2,1)S(1)} %copy-done.19), channel_id=1, source_target_pairs={{0,1},{1,2},{2,3},{3,0},{4,5},{5,6},{6,7},{7,4},{8,9},{9,10},{10,1... | collective-permute-start | bytes 786440 | tf_op jit(solution)/shard_map/ppermute | solution.py:323
  60.4 15.2 %collective-permute-start.4 = (bf16[2,512,128]{2,1,0:T(8,128)(2,1)S(1)}, bf16[2,512,128]{2,1,0:T(8,128)(2,1)S(1)}, u32[]{:S(2)}, u32[]{:S(2)}) collective-permute-start(bf16[2,512,128]{2,1,0:T(8,128)(2,1)S(1)} %copy-done.19), channel_id=1, source_target_pairs={{0,2},{1,3},{2,0},{3,1},{4,6},{5,7},{6,4},{7,5},{8,10},{9,11},{10,... | collective-permute-start | bytes 786440 | tf_op jit(solution)/shard_map/ppermute | solution.py:323
  62.2 14.1 %collective-permute-start.5 = (bf16[2,512,128]{2,1,0:T(8,128)(2,1)S(1)}, bf16[2,512,128]{2,1,0:T(8,128)(2,1)S(1)}, u32[]{:S(2)}, u32[]{:S(2)}) collective-permute-start(bf16[2,512,128]{2,1,0:T(8,128)(2,1)S(1)} %copy-done.19), channel_id=1, source_target_pairs={{0,3},{1,0},{2,1},{3,2},{4,7},{5,4},{6,5},{7,6},{8,11},{9,8},{10,9... | collective-permute-start | bytes 786440 | tf_op jit(solution)/shard_map/ppermute | solution.py:323
  63.0 18.2 %copy-start = (f32[512,128]{1,0:T(8,128)S(1)}, f32[512,128]{1,0:T(8,128)}, u32[]{:S(2)}) copy-start(f32[512,128]{1,0:T(8,128)} %q_ref.1) | copy-start | bytes 786436
  65.1 16.1 %all-to-all-start.3 = ((f32[64,1,128]{2,1,0:T(1,128)}), f32[64,1,128]{2,1,0:T(1,128)S(1)}, u32[]{:S(2)}, u32[]{:S(2)}) async-start(f32[64,1,128]{2,1,0:T(1,128)} %get-tuple-element.46), calls=%async_computation.3 | async-start | bytes 65536 | tf_op jit(solution)/shard_map/all_to_all | solution.py:29
  81.2 1.0 copy-start.1
  82.2 0.9 copy-start.6
  85.6 4.6 %copy-start.11 = (f32[512,128]{1,0:T(8,128)}, f32[512,128]{1,0:T(8,128)S(1)}, u32[]{:S(2)}) copy-start(f32[512,128]{1,0:T(8,128)S(1)} %get-tuple-element.71) | copy-start | bytes 786436
  85.6 4.5 %copy-start.13 = (f32[512,128]{1,0:T(8,128)}, f32[512,128]{1,0:T(8,128)S(1)}, u32[]{:S(2)}) copy-start(f32[512,128]{1,0:T(8,128)S(1)} %get-tuple-element.75) | copy-start | bytes 786436
  85.7 3.1 %collective-permute-start.6 = (bf16[1024,512]{1,0:T(8,128)(2,1)S(1)}, bf16[1024,512]{1,0:T(8,128)(2,1)S(1)}, u32[]{:S(2)}, u32[]{:S(2)}) collective-permute-start(bf16[1024,512]{1,0:T(8,128)(2,1)S(1)} %get-tuple-element.51.own_ref), channel_id=1, source_target_pairs={{0,4},{4,0},{1,5},{5,1},{2,6},{6,2},{3,7},{7,3},{8,12},{12,8},{9,1... | collective-permute-start | bytes 3145736 | tf_op jit(solution)/shard_map/ppermute | solution.py:38
  86.5 2.3 collective-permute-start
  155.8 5.6 %copy-start.4 = (bf16[512,512]{1,0:T(8,128)(2,1)S(1)}, bf16[512,512]{1,0:T(8,128)(2,1)}, u32[]{:S(2)}) copy-start(bf16[512,512]{1,0:T(8,128)(2,1)} %expr_ref.1) | copy-start | bytes 1572868
  157.5 12.7 %all-to-all-start.9 = ((bf16[32,8,128]{2,1,0:T(8,128)(2,1)}), bf16[32,8,128]{2,1,0:T(8,128)(2,1)S(1)}, u32[]{:S(2)}, u32[]{:S(2)}) async-start(bf16[32,8,128]{2,1,0:T(8,128)(2,1)} %get-tuple-element.62), calls=%async_computation.9 | async-start | bytes 131072 | tf_op jit(solution)/shard_map/all_to_all | solution.py:29
  161.3 58.1 %collective-permute-start.7 = (bf16[512,512]{1,0:T(8,128)(2,1)S(1)}, bf16[512,512]{1,0:T(8,128)(2,1)S(1)}, u32[]{:S(2)}, u32[]{:S(2)}) collective-permute-start(bf16[512,512]{1,0:T(8,128)(2,1)S(1)} %copy-done.4), channel_id=1, source_target_pairs={{0,4},{4,0},{1,5},{5,1},{2,6},{6,2},{3,7},{7,3},{8,12},{12,8},{9,1... | collective-permute-start | bytes 1572872 | tf_op jit(solution)/shard_map/ppermute | solution.py:38
  215.6 12.7 %all-to-all-start.13 = ((bf16[32,8,128]{2,1,0:T(8,128)(2,1)}), bf16[32,8,128]{2,1,0:T(8,128)(2,1)S(1)}, u32[]{:S(2)}, u32[]{:S(2)}) async-start(bf16[32,8,128]{2,1,0:T(8,128)(2,1)} %get-tuple-element.72), calls=%async_computation.13 | async-start | bytes 131072 | tf_op jit(solution)/shard_map/all_to_all | solution.py:29
  230.0 15.3 %all-to-all-start.14 = ((f32[32,8,512]{2,1,0:T(8,128)}), f32[32,8,512]{2,1,0:T(8,128)S(1)}, u32[]{:S(2)}, u32[]{:S(2)}) async-start(f32[32,8,512]{2,1,0:T(8,128)} %bitcast.18), calls=%async_computation.14 | async-start | bytes 1048576 | tf_op jit(solution)/shard_map/all_to_all | solution.py:29
  246.0 5.6 %copy-start.14 = (f32[512,128]{1,0:T(8,128)S(1)}, f32[512,128]{1,0:T(8,128)}, u32[]{:S(2)}) copy-start(f32[512,128]{1,0:T(8,128)} %copy-done.13) | copy-start | bytes 786436
  246.0 15.3 %all-to-all-start.15 = ((bf16[32,8,512]{2,1,0:T(8,128)(2,1)}), bf16[32,8,512]{2,1,0:T(8,128)(2,1)S(1)}, u32[]{:S(2)}, u32[]{:S(2)}) async-start(bf16[32,8,512]{2,1,0:T(8,128)(2,1)} %broadcast_in_dim.17), calls=%async_computation.15 | async-start | bytes 524288 | tf_op jit(solution)/shard_map/all_to_all | solution.py:29
  251.7 1.0 copy-start.12
  (9 other events, 6.9 us)

commit v7 on v6

--- a/solution.py
+++ b/solution.py
@@ -127,8 +127,21 @@
 
 
 def grad_kernel(
-    core_ref, x_ref, y_ref, mine_ref, other_ref, vec_ref, grad_q_ref, grad_r_ref, grad_g_ref, peak_ref
+    core_ref, here_ref, x_ref, y_ref, mine_ref, other_ref, vec_ref, mass_ref, mass2_ref, *refs
 ):
+    factors = refs[:-8]
+    grad_q_ref, grad_r_ref, grad_g_ref, peak_ref, all_ref, own_q_ref, own_r_ref, masses_ref = refs[-8:]
+    masses_ref[...] = jnp.concatenate([mass_ref[...], mass2_ref[...]], axis=0)
+    ranks = len(factors)
+    rows, width = factors[0].shape[1:]
+
+    def lanes_of(block):
+        return pl.ds(pl.multiple_of(block * width, width), width)
+
+    for shift, factor_ref in enumerate(factors):
+        lanes = lanes_of(lax.rem(here_ref[0] + ranks - shift, ranks))
+        for side in range(2):
+            all_ref[pl.ds(side * rows, rows), lanes] = factor_ref[side]
     half = x_ref.shape[1] // 2
     chunks = mine_ref.shape[0]
     core = core_ref[0]
@@ -147,9 +160,9 @@
     grad_g = -curvature / jnp.square(g)
     grad_g_ref[...] = grad_g
     top = jnp.abs(grad_g)
-    for emb_ref, offset, count, total, out_ref in (
-        (x_ref, 4, cr, yr, grad_q_ref),
-        (y_ref, 0, cq, xq, grad_r_ref),
+    for emb_ref, offset, count, total, out_ref, own_ref in (
+        (x_ref, 4, cr, yr, grad_q_ref, own_q_ref),
+        (y_ref, 0, cq, xq, grad_r_ref, own_r_ref),
     ):
         select = jnp.where(place == wanted + offset, 1.0, 0.0).astype(BF16)
         product = None
@@ -161,6 +174,7 @@
         norms = jnp.sum(jnp.square(emb_ref[...].astype(F32)), axis=1, keepdims=True)
         grad = scale * (norms * count + total - 2.0 * product)
         out_ref[...] = grad
+        own_ref[...] = out_ref[:, lanes_of(here_ref[0])]
         top = jnp.maximum(top, jnp.max(jnp.abs(grad), axis=0, keepdims=True))
     blocks = in_rows(top, top.shape[1] // peak_ref.shape[2])
     peak = blocks[0]
@@ -170,26 +184,18 @@
 
 
 def kern_kernel(
-    here_ref, peak_ref, grad_q_ref, grad_r_ref, grad_g_ref, vec_ref, q_ref, r_ref, *refs
+    peak_ref, grad_q_ref, grad_r_ref, grad_g_ref, vec_ref, all_ref, kern_ref, log_ref, eta_ref
 ):
-    from_others, (kern_ref, own_q_ref, own_r_ref, log_ref) = refs[:-4], refs[-4:]
-    ranks = len(from_others) + 1
-    rows, width = q_ref.shape
+    rows = grad_q_ref.shape[0]
     peak = jnp.max(jnp.max(peak_ref[...], axis=0), axis=1, keepdims=True)
     eta = GAMMA / (peak + 1e-06)
+    eta_ref[...] = jnp.broadcast_to(eta, eta_ref.shape)
     kern_g = vec_ref[5:6] * jnp.exp(-eta * grad_g_ref[...])
-    log_ref[...] = jnp.concatenate(in_rows(jnp.log(kern_g), ranks), axis=0)
-    for shift in range(ranks):
-        block = lax.rem(here_ref[0] + ranks - shift, ranks)
-        lanes = pl.ds(pl.multiple_of(block * width, width), width)
-        for side, (grad_ref, factor_ref, own_ref) in enumerate(
-            ((grad_q_ref, q_ref, own_q_ref), (grad_r_ref, r_ref, own_r_ref))
-        ):
-            factor = from_others[shift - 1][side].astype(F32) if shift else factor_ref[...]
-            kern = factor * jnp.exp(-eta * grad_ref[:, lanes])
-            if shift == 0:
-                own_ref[...] = kern
-            kern_ref[pl.ds(side * rows, rows), lanes] = kern.astype(BF16)
+    log_ref[...] = jnp.concatenate(in_rows(jnp.log(kern_g), log_ref.shape[0]), axis=0)
+    for side, grad_ref in enumerate((grad_q_ref, grad_r_ref)):
+        part = pl.ds(side * rows, rows)
+        kern = all_ref[part, :].astype(F32) * jnp.exp(-eta * grad_ref[...])
+        kern_ref[part, :] = kern.astype(BF16)
 
 
 def new_scalings(ranks, got_ref, v_ref, log_ref):
@@ -297,8 +303,6 @@
     here = lax.axis_index("x")
     core = lax.axis_index("c")
     other_expr = swap(expr)
-    masses = jnp.stack([a_mass, b_mass])
-    masses = jnp.concatenate([masses, swap(masses)])
     core_index = core.astype(jnp.int32)[None]
     part_xq, part_yr, part_vec, rounded = on_chip(
         start_kernel,
@@ -341,24 +345,30 @@
     sent, vec = on_chip(
         spread_kernel, (((others, 16, columns), BF16), ((8, columns), F32)), "spread"
     )(exchange(sent, "x"))
-    crosses = exchange(sent, CHIPS).reshape(others * 16, columns)
-    grad_q, grad_r, grad_g, peak = on_chip(
+    masses = jnp.stack([a_mass, b_mass])
+    crosses, from_others, their_masses = lax.optimization_barrier(
+        (exchange(sent, CHIPS), from_others, swap(masses))
+    )
+    crosses = crosses.reshape(others * 16, columns)
+    own_grad = ((rows, width), F32)
+    grad_q, grad_r, grad_g, peak, factors, own_grad_q, own_grad_r, masses = on_chip(
         grad_kernel,
-        (tall, tall, ((1, columns), F32), ((cell_devices, 1, width), F32)),
+        (
+            tall, tall, ((1, columns), F32), ((cell_devices, 1, width), F32),
+            ((2 * rows, columns), BF16), own_grad, own_grad, ((4, rows), F32),
+        ),
         "grad",
-        scalars=1,
-        inputs=5,
-    )(core_index, x_emb, y_emb, crosses, swap(crosses), vec)
-    kerns, kern_q, kern_r, log_g = on_chip(
+        scalars=2,
+        inputs=7 + ranks,
+    )(
+        core_index, here.astype(jnp.int32)[None], x_emb, y_emb, crosses, swap(crosses), vec,
+        masses, their_masses, rounded, *from_others,
+    )
+    kerns, log_g, eta = on_chip(
         kern_kernel,
-        (((2 * rows, columns), BF16), ((rows, width), F32), ((rows, width), F32), ((ranks, width), F32)),
+        (((2 * rows, columns), BF16), ((ranks, width), F32), ((1, width), F32)),
         "kern",
-        scalars=1,
-        inputs=7 + ranks - 1,
-    )(
-        here.astype(jnp.int32)[None], exchange(peak, CELLS), grad_q, grad_r, grad_g, vec,
-        q_factor, r_factor, *from_others,
-    )
+    )(exchange(peak, CELLS), grad_q, grad_r, grad_g, vec, factors)
     theirs = swap(kerns)
     sent_shape = ((others, 2 * ranks, width), BF16)
     u_shape = ((4, rows), F32)
@@ -380,6 +390,8 @@
         expr, other_expr,
     )
     v_q, v_r = v[:ranks], v[ranks:]
+    kern_q = q_factor * jnp.exp(-eta * own_grad_q)
+    kern_r = r_factor * jnp.exp(-eta * own_grad_r)
     q_new = u[0][:, None] * kern_q * pick(v_q, here)[None, :]
     r_new = u[1][:, None] * kern_r * pick(v_r, here)[None, :]
     mine_q = kerns[:rows].astype(F32)
@@ -387,8 +399,15 @@
     scaled = (mine_q * (v_q / weights).reshape(1, columns)).astype(BF16)
 
     piece = jnp.sum(exchange(part.reshape(others, -1, genes), CHIPS), axis=0)
-    profiles = lax.all_gather(to_all(piece.astype(BF16), CHIPS), "c").reshape(columns, genes)
-    mixed = jnp.dot(scaled, profiles, preferred_element_type=F32)
+    mine = to_all(piece.astype(BF16), CHIPS).reshape(columns // 2, genes)
+    half = columns // 2
+    mixed = jnp.dot(
+        lax.dynamic_slice_in_dim(scaled, core * half, half, 1), mine, preferred_element_type=F32
+    ) + jnp.dot(
+        lax.dynamic_slice_in_dim(scaled, (1 - core) * half, half, 1),
+        swap(mine),
+        preferred_element_type=F32,
+    )
     predicted = (mixed / s_q[:, None]).astype(BF16)
     return (q_new, r_new, pick(weights, here) / cells_total, predicted)
 

time: 277 us -> 274 us (0.989)
  blocking collectives: 156 us -> 144 us
  starting transfers between devices: 43.5 us -> 55.2 us
  local copies, waits for them, and re-layouts: 8.34 us -> 3.85 us
    ppermute x5 -> x6, starting transfers between devices: 16.6 us -> 29.6 us  [swap(): return lax.ppermute(value, 'c', [(0, 1), (1, 0)])]
    all_gather x1 -> x0, blocking collectives: 13 us -> none  [shards(): lax.all_gather(to_all(piece.astype(BF16), CHIPS), 'c')]
    unnamed x40 -> x24, local copies, waits for them, and re-layouts: 7.41 us -> 2.91 us
    all_to_all x5, waiting for transfers between devices: 34.1 us -> 30.2 us  [exchange(): return lax.all_to_all(chunks, axes, 0, 0, tiled=False)]
    ppermute x5 -> x6, waiting for transfers between devices: 2.6 us -> 6.07 us  [swap(): return lax.ppermute(value, 'c', [(0, 1), (1, 0)])]
    ppermute x3, waiting for transfers between devices: 2.96 us -> 5.79 us  [shards(): lax.ppermute(rounded, 'x', [(i, (i + shift) % ranks) for i in range(ranks)])]
  transfers between devices with their start and end apart: 13 -> 14, of which waited for: 8 -> 12; matrix products, arithmetic and copies ran while one was open for 1% -> 1% of each run, Pallas kernels for 3% -> 2%
where the time goes in v7:
time: 274 us; the launch traced here: 273 us
  blocking collectives  144 us (53%)
  starting transfers between devices  55.2 us (20%)
  waiting for transfers between devices  42.1 us (15%)
  Pallas kernels  22.4 us (8%)
  local copies, waits for them, and re-layouts  3.85 us (1%)
  other arithmetic  3 us (1%)
    all_to_all x11, blocking collectives, exchange(): return lax.all_to_all(chunks, axes, 0, 0, tiled=False)  144 us
    all_to_all x5, waiting for transfers between devices, exchange(): return lax.all_to_all(chunks, axes, 0, 0, tiled=False)  30.2 us
    ppermute x6, starting transfers between devices, swap(): return lax.ppermute(value, 'c', [(0, 1), (1, 0)])  29.6 us
    all_to_all x5, starting transfers between devices, exchange(): return lax.all_to_all(chunks, axes, 0, 0, tiled=False)  22.7 us
    pallas_call x9, Pallas kernels, shards(): on_chip(next_pass, (sent_shape, u_shape, v_shape), 'next_pass')  13.5 us
    ppermute x6, waiting for transfers between devices, swap(): return lax.ppermute(value, 'c', [(0, 1), (1, 0)])  6.07 us
    ppermute x3, waiting for transfers between devices, shards(): lax.ppermute(rounded, 'x', [(i, (i + shift) % ranks) for i in range(ranks)])  5.79 us
  transfers between devices with their start and end apart: 14, of which 12 were waited for; matrix products, arithmetic and copies ran while one was open for 1% of the time, Pallas kernels for 2%

profile of v7, /device:TPU:1, one launch (start us, length us, event | category | flops | bytes accessed | tf_op | source)
XLA Modules:
  0.0 272.6 jit_solution(7097015987994243627)
XLA Ops:
  4.9 3.3 %collective-permute-start = (f32[32,3,4,128]{3,2,1,0:T(4,128)S(1)}, f32[32,3,4,128]{3,2,1,0:T(4,128)S(1)}, u32[]{:S(2)}, u32[]{:S(2)}) collective-permute-start(f32[32,3,4,128]{3,2,1,0:T(4,128)S(1)} %copy.14), channel_id=1, source_target_pairs={{0,4},{4,0},{1,5},{5,1},{2,6},{6,2},{3,7},{7,3},{8,12},{12,8},{9,1... | collective-permute-start | bytes 589832 | tf_op jit(solution)/shard_map/ppermute | solution.py:38
  9.5 18.7 %all_to_all.80.got_ref = f32[32,3,4,128]{3,2,1,0:T(4,128)S(1)} all-to-all(f32[32,3,4,128]{3,2,1,0:T(4,128)S(1)} %copy_add_fusion), channel_id=1, replica_groups=mesh['y'=4,'z'=8,'c'=2,'x'=4] {'y','z'}, dimensions={0} | all-to-all | bytes 393216 | tf_op jit(solution)/shard_map/all_to_all | solution.py:29
  28.9 8.1 %all_to_all.81.got_ref = f32[4,16,128]{2,1,0:T(8,128)S(1)} all-to-all(f32[4,16,128]{2,1,0:T(8,128)S(1)} %chunk.1), channel_id=1, replica_groups=mesh['y'=4,'z'=8,'c'=2,'x'=4] {'x'}, dimensions={0} | all-to-all | bytes 65536 | tf_op jit(solution)/shard_map/all_to_all | solution.py:29
  37.8 5.6 %all-to-all-start.2 = ((bf16[32,16,512]{2,1,0:T(8,128)(2,1)}), bf16[32,16,512]{2,1,0:T(8,128)(2,1)S(1)}, u32[]{:S(2)}, u32[]{:S(2)}) async-start(bf16[32,16,512]{2,1,0:T(8,128)(2,1)} %get-tuple-element.52), calls=%async_computation.2 | async-start | bytes 1048576 | tf_op jit(solution)/shard_map/all_to_all | solution.py:29
  46.4 3.9 %collective-permute-start.4 = (f32[2,512]{1,0:T(2,128)S(1)}, f32[2,512]{1,0:T(2,128)S(1)}, u32[]{:S(2)}, u32[]{:S(2)}) collective-permute-start(f32[2,512]{1,0:T(2,128)S(1)} %pad_maximum_fusion.2.mass_ref), channel_id=1, source_target_pairs={{0,4},{4,0},{1,5},{5,1},{2,6},{6,2},{3,7},{7,3},{8,12},{12,8},{9,1... | collective-permute-start | bytes 12296 | tf_op jit(solution)/shard_map/ppermute | solution.py:38
  57.0 4.1 %collective-permute-start.5 = (bf16[512,512]{1,0:T(8,128)(2,1)S(1)}, bf16[512,512]{1,0:T(8,128)(2,1)S(1)}, u32[]{:S(2)}, u32[]{:S(2)}) collective-permute-start(bf16[512,512]{1,0:T(8,128)(2,1)S(1)} %bitcast.33), channel_id=1, source_target_pairs={{0,4},{4,0},{1,5},{5,1},{2,6},{6,2},{3,7},{7,3},{8,12},{12,8},{9,1... | collective-permute-start | bytes 1572872 | tf_op jit(solution)/shard_map/ppermute | solution.py:38
  65.0 17.8 %all_to_all.82.peak_ref = f32[64,1,128]{2,1,0:T(1,128)S(1)} all-to-all(f32[64,1,128]{2,1,0:T(1,128)S(1)} %get-tuple-element.61), channel_id=1, replica_groups=mesh['y'=4,'z'=8,'c'=2,'x'=4] {'y','z','c'}, dimensions={0} | all-to-all | bytes 65536 | tf_op jit(solution)/shard_map/all_to_all | solution.py:29
  88.0 11.8 %all_to_all.83.got_ref = bf16[32,8,128]{2,1,0:T(8,128)(2,1)S(1)} all-to-all(bf16[32,8,128]{2,1,0:T(8,128)(2,1)S(1)} %get-tuple-element.67), channel_id=1, replica_groups=mesh['y'=4,'z'=8,'c'=2,'x'=4] {'y','z'}, dimensions={0} | all-to-all | bytes 131072 | tf_op jit(solution)/shard_map/all_to_all | solution.py:29
  101.3 12.1 %all_to_all.84.got_ref = bf16[32,8,128]{2,1,0:T(8,128)(2,1)S(1)} all-to-all(bf16[32,8,128]{2,1,0:T(8,128)(2,1)S(1)} %get-tuple-element.69), channel_id=1, replica_groups=mesh['y'=4,'z'=8,'c'=2,'x'=4] {'y','z'}, dimensions={0} | all-to-all | bytes 131072 | tf_op jit(solution)/shard_map/all_to_all | solution.py:29
  114.8 12.1 %all_to_all.85.got_ref = bf16[32,8,128]{2,1,0:T(8,128)(2,1)S(1)} all-to-all(bf16[32,8,128]{2,1,0:T(8,128)(2,1)S(1)} %get-tuple-element.71), channel_id=1, replica_groups=mesh['y'=4,'z'=8,'c'=2,'x'=4] {'y','z'}, dimensions={0} | all-to-all | bytes 131072 | tf_op jit(solution)/shard_map/all_to_all | solution.py:29
  128.4 11.9 %all_to_all.86.got_ref = bf16[32,8,128]{2,1,0:T(8,128)(2,1)S(1)} all-to-all(bf16[32,8,128]{2,1,0:T(8,128)(2,1)S(1)} %get-tuple-element.73), channel_id=1, replica_groups=mesh['y'=4,'z'=8,'c'=2,'x'=4] {'y','z'}, dimensions={0} | all-to-all | bytes 131072 | tf_op jit(solution)/shard_map/all_to_all | solution.py:29
  141.7 11.9 %all_to_all.87.got_ref = bf16[32,8,128]{2,1,0:T(8,128)(2,1)S(1)} all-to-all(bf16[32,8,128]{2,1,0:T(8,128)(2,1)S(1)} %get-tuple-element.75), channel_id=1, replica_groups=mesh['y'=4,'z'=8,'c'=2,'x'=4] {'y','z'}, dimensions={0} | all-to-all | bytes 131072 | tf_op jit(solution)/shard_map/all_to_all | solution.py:29
  155.4 3.9 %all-to-all-start.9 = ((bf16[32,8,128]{2,1,0:T(8,128)(2,1)}), bf16[32,8,128]{2,1,0:T(8,128)(2,1)S(1)}, u32[]{:S(2)}, u32[]{:S(2)}) async-start(bf16[32,8,128]{2,1,0:T(8,128)(2,1)} %get-tuple-element.77), calls=%async_computation.9 | async-start | bytes 131072 | tf_op jit(solution)/shard_map/all_to_all | solution.py:29
  159.2 6.3 %collective-permute-start.7 = (bf16[512,512]{1,0:T(8,128)(2,1)S(1)}, bf16[512,512]{1,0:T(8,128)(2,1)S(1)}, u32[]{:S(2)}, u32[]{:S(2)}) collective-permute-start(bf16[512,512]{1,0:T(8,128)(2,1)S(1)} %copy-done.2), channel_id=1, source_target_pairs={{0,4},{4,0},{1,5},{5,1},{2,6},{6,2},{3,7},{7,3},{8,12},{12,8},{9,1... | collective-permute-start | bytes 1572872 | tf_op jit(solution)/shard_map/ppermute | solution.py:38
  169.5 15.6 %all_to_all.88.got_ref = bf16[32,8,128]{2,1,0:T(8,128)(2,1)S(1)} all-to-all(bf16[32,8,128]{2,1,0:T(8,128)(2,1)S(1)} %get-tuple-element.79), channel_id=1, replica_groups=mesh['y'=4,'z'=8,'c'=2,'x'=4] {'y','z'}, dimensions={0} | all-to-all | bytes 131072 | tf_op jit(solution)/shard_map/all_to_all | solution.py:29
  186.6 11.9 %all_to_all.89.got_ref = bf16[32,8,128]{2,1,0:T(8,128)(2,1)S(1)} all-to-all(bf16[32,8,128]{2,1,0:T(8,128)(2,1)S(1)} %get-tuple-element.81), channel_id=1, replica_groups=mesh['y'=4,'z'=8,'c'=2,'x'=4] {'y','z'}, dimensions={0} | all-to-all | bytes 131072 | tf_op jit(solution)/shard_map/all_to_all | solution.py:29
  200.0 11.8 %all_to_all.90.got_ref = bf16[32,8,128]{2,1,0:T(8,128)(2,1)S(1)} all-to-all(bf16[32,8,128]{2,1,0:T(8,128)(2,1)S(1)} %get-tuple-element.83), channel_id=1, replica_groups=mesh['y'=4,'z'=8,'c'=2,'x'=4] {'y','z'}, dimensions={0} | all-to-all | bytes 131072 | tf_op jit(solution)/shard_map/all_to_all | solution.py:29
  213.5 3.9 %all-to-all-start.13 = ((bf16[32,8,128]{2,1,0:T(8,128)(2,1)}), bf16[32,8,128]{2,1,0:T(8,128)(2,1)S(1)}, u32[]{:S(2)}, u32[]{:S(2)}) async-start(bf16[32,8,128]{2,1,0:T(8,128)(2,1)} %get-tuple-element.88), calls=%async_computation.13 | async-start | bytes 131072 | tf_op jit(solution)/shard_map/all_to_all | solution.py:29
  217.4 8.8 %all-to-all-done.13.got_ref = bf16[32,8,128]{2,1,0:T(8,128)(2,1)S(1)} async-done(((bf16[32,8,128]{2,1,0:T(8,128)(2,1)}), bf16[32,8,128]{2,1,0:T(8,128)(2,1)S(1)}, u32[]{:S(2)}, u32[]{:S(2)}) %all-to-all-start.13) | async-done | bytes 65568 | tf_op jit(solution)/shard_map/all_to_all | solution.py:29
  228.0 3.9 %all-to-all-start.14 = ((f32[32,8,512]{2,1,0:T(8,128)}), f32[32,8,512]{2,1,0:T(8,128)S(1)}, u32[]{:S(2)}, u32[]{:S(2)}) async-start(f32[32,8,512]{2,1,0:T(8,128)} %bitcast.19), calls=%async_computation.14 | async-start | bytes 1048576 | tf_op jit(solution)/shard_map/all_to_all | solution.py:29
  231.9 11.3 %all-to-all-done.14 = f32[32,8,512]{2,1,0:T(8,128)S(1)} async-done(((f32[32,8,512]{2,1,0:T(8,128)}), f32[32,8,512]{2,1,0:T(8,128)S(1)}, u32[]{:S(2)}, u32[]{:S(2)}) %all-to-all-start.14) | async-done | bytes 524320 | tf_op jit(solution)/shard_map/all_to_all | solution.py:29
  244.0 5.5 %all-to-all-start.15 = ((bf16[32,8,512]{2,1,0:T(8,128)(2,1)}), bf16[32,8,512]{2,1,0:T(8,128)(2,1)S(1)}, u32[]{:S(2)}, u32[]{:S(2)}) async-start(bf16[32,8,512]{2,1,0:T(8,128)(2,1)} %broadcast_in_dim.17), calls=%async_computation.15 | async-start | bytes 524288 | tf_op jit(solution)/shard_map/all_to_all | solution.py:29
  251.6 7.5 %all-to-all-done.15 = bf16[32,8,512]{2,1,0:T(8,128)(2,1)S(1)} async-done(((bf16[32,8,512]{2,1,0:T(8,128)(2,1)}), bf16[32,8,512]{2,1,0:T(8,128)(2,1)S(1)}, u32[]{:S(2)}, u32[]{:S(2)}) %all-to-all-start.15) | async-done | bytes 262176 | tf_op jit(solution)/shard_map/all_to_all | solution.py:29
  259.1 11.2 %collective-permute-start.8 = (bf16[256,512]{1,0:T(8,128)(2,1)S(1)}, bf16[256,512]{1,0:T(8,128)(2,1)S(1)}, u32[]{:S(2)}, u32[]{:S(2)}) collective-permute-start(bf16[256,512]{1,0:T(8,128)(2,1)S(1)} %bitcast.36), channel_id=1, source_target_pairs={{0,4},{4,0},{1,5},{5,1},{2,6},{6,2},{3,7},{7,3},{8,12},{12,8},{9,1... | collective-permute-start | bytes 786440 | tf_op jit(solution)/shard_map/ppermute | solution.py:38
  (75 shorter events, 48.7 us)
Async XLA Ops:
  4.9 4.4 %collective-permute-start = (f32[32,3,4,128]{3,2,1,0:T(4,128)S(1)}, f32[32,3,4,128]{3,2,1,0:T(4,128)S(1)}, u32[]{:S(2)}, u32[]{:S(2)}) collective-permute-start(f32[32,3,4,128]{3,2,1,0:T(4,128)S(1)} %copy.14), channel_id=1, source_target_pairs={{0,4},{4,0},{1,5},{5,1},{2,6},{6,2},{3,7},{7,3},{8,12},{12,8},{9,1... | collective-permute-start | bytes 589832 | tf_op jit(solution)/shard_map/ppermute | solution.py:38
  37.8 5.6 %copy-start.5 = (bf16[2,512,128]{2,1,0:T(8,128)(2,1)S(1)}, bf16[2,512,128]{2,1,0:T(8,128)(2,1)}, u32[]{:S(2)}) copy-start(bf16[2,512,128]{2,1,0:T(8,128)(2,1)} %get-tuple-element.53.refs_0_) | copy-start | bytes 786436
  37.8 24.8 %copy-start = (bf16[512,256]{1,0:T(8,128)(2,1)S(1)}, bf16[512,256]{1,0:T(8,128)(2,1)}, u32[]{:S(2)}) copy-start(bf16[512,256]{1,0:T(8,128)(2,1)} %x_ref.1) | copy-start | bytes 786436
  37.8 24.8 %copy-start.1 = (bf16[512,256]{1,0:T(8,128)(2,1)S(1)}, bf16[512,256]{1,0:T(8,128)(2,1)}, u32[]{:S(2)}) copy-start(bf16[512,256]{1,0:T(8,128)(2,1)} %y_ref.1) | copy-start | bytes 786436
  37.8 19.1 %all-to-all-start.2 = ((bf16[32,16,512]{2,1,0:T(8,128)(2,1)}), bf16[32,16,512]{2,1,0:T(8,128)(2,1)S(1)}, u32[]{:S(2)}, u32[]{:S(2)}) async-start(bf16[32,16,512]{2,1,0:T(8,128)(2,1)} %get-tuple-element.52), calls=%async_computation.2 | async-start | bytes 1048576 | tf_op jit(solution)/shard_map/all_to_all | solution.py:29
  43.4 3.0 %copy-start.11 = (f32[512]{0:T(512)S(1)}, f32[512]{0:T(512)}, u32[]{:S(2)}) copy-start(f32[512]{0:T(512)} %param.13) | copy-start | bytes 6148
  43.5 3.0 %copy-start.10 = (f32[512]{0:T(512)S(1)}, f32[512]{0:T(512)}, u32[]{:S(2)}) copy-start(f32[512]{0:T(512)} %param.14) | copy-start | bytes 6148
  43.5 8.6 %collective-permute-start.1 = (bf16[2,512,128]{2,1,0:T(8,128)(2,1)S(1)}, bf16[2,512,128]{2,1,0:T(8,128)(2,1)S(1)}, u32[]{:S(2)}, u32[]{:S(2)}) collective-permute-start(bf16[2,512,128]{2,1,0:T(8,128)(2,1)S(1)} %copy-done.5), channel_id=1, source_target_pairs={{0,1},{1,2},{2,3},{3,0},{4,5},{5,6},{6,7},{7,4},{8,9},{9,10},{10,1... | collective-permute-start | bytes 786440 | tf_op jit(solution)/shard_map/ppermute | solution.py:327
  43.8 10.8 %collective-permute-start.2 = (bf16[2,512,128]{2,1,0:T(8,128)(2,1)S(1)}, bf16[2,512,128]{2,1,0:T(8,128)(2,1)S(1)}, u32[]{:S(2)}, u32[]{:S(2)}) collective-permute-start(bf16[2,512,128]{2,1,0:T(8,128)(2,1)S(1)} %copy-done.5), channel_id=1, source_target_pairs={{0,2},{1,3},{2,0},{3,1},{4,6},{5,7},{6,4},{7,5},{8,10},{9,11},{10,... | collective-permute-start | bytes 786440 | tf_op jit(solution)/shard_map/ppermute | solution.py:327
  45.6 11.3 %collective-permute-start.3 = (bf16[2,512,128]{2,1,0:T(8,128)(2,1)S(1)}, bf16[2,512,128]{2,1,0:T(8,128)(2,1)S(1)}, u32[]{:S(2)}, u32[]{:S(2)}) collective-permute-start(bf16[2,512,128]{2,1,0:T(8,128)(2,1)S(1)} %copy-done.5), channel_id=1, source_target_pairs={{0,3},{1,0},{2,1},{3,2},{4,7},{5,4},{6,5},{7,6},{8,11},{9,8},{10,9... | collective-permute-start | bytes 786440 | tf_op jit(solution)/shard_map/ppermute | solution.py:327
  46.4 4.7 %collective-permute-start.4 = (f32[2,512]{1,0:T(2,128)S(1)}, f32[2,512]{1,0:T(2,128)S(1)}, u32[]{:S(2)}, u32[]{:S(2)}) collective-permute-start(f32[2,512]{1,0:T(2,128)S(1)} %pad_maximum_fusion.2.mass_ref), channel_id=1, source_target_pairs={{0,4},{4,0},{1,5},{5,1},{2,6},{6,2},{3,7},{7,3},{8,12},{12,8},{9,1... | collective-permute-start | bytes 12296 | tf_op jit(solution)/shard_map/ppermute | solution.py:38
  57.0 5.6 %collective-permute-start.5 = (bf16[512,512]{1,0:T(8,128)(2,1)S(1)}, bf16[512,512]{1,0:T(8,128)(2,1)S(1)}, u32[]{:S(2)}, u32[]{:S(2)}) collective-permute-start(bf16[512,512]{1,0:T(8,128)(2,1)S(1)} %bitcast.33), channel_id=1, source_target_pairs={{0,4},{4,0},{1,5},{5,1},{2,6},{6,2},{3,7},{7,3},{8,12},{12,8},{9,1... | collective-permute-start | bytes 1572872 | tf_op jit(solution)/shard_map/ppermute | solution.py:38
  64.3 0.7 copy-start.3
  83.5 3.0 %collective-permute-start.6 = (bf16[1024,512]{1,0:T(8,128)(2,1)S(1)}, bf16[1024,512]{1,0:T(8,128)(2,1)S(1)}, u32[]{:S(2)}, u32[]{:S(2)}) collective-permute-start(bf16[1024,512]{1,0:T(8,128)(2,1)S(1)} %get-tuple-element.66.own_ref), channel_id=1, source_target_pairs={{0,4},{4,0},{1,5},{5,1},{2,6},{6,2},{3,7},{7,3},{8,12},{12,8},{9,1... | collective-permute-start | bytes 3145736 | tf_op jit(solution)/shard_map/ppermute | solution.py:38
  153.7 5.6 %copy-start.2 = (bf16[512,512]{1,0:T(8,128)(2,1)S(1)}, bf16[512,512]{1,0:T(8,128)(2,1)}, u32[]{:S(2)}) copy-start(bf16[512,512]{1,0:T(8,128)(2,1)} %expr_ref.1) | copy-start | bytes 1572868
  155.4 12.7 %all-to-all-start.9 = ((bf16[32,8,128]{2,1,0:T(8,128)(2,1)}), bf16[32,8,128]{2,1,0:T(8,128)(2,1)S(1)}, u32[]{:S(2)}, u32[]{:S(2)}) async-start(bf16[32,8,128]{2,1,0:T(8,128)(2,1)} %get-tuple-element.77), calls=%async_computation.9 | async-start | bytes 131072 | tf_op jit(solution)/shard_map/all_to_all | solution.py:29
  159.2 58.1 %collective-permute-start.7 = (bf16[512,512]{1,0:T(8,128)(2,1)S(1)}, bf16[512,512]{1,0:T(8,128)(2,1)S(1)}, u32[]{:S(2)}, u32[]{:S(2)}) collective-permute-start(bf16[512,512]{1,0:T(8,128)(2,1)S(1)} %copy-done.2), channel_id=1, source_target_pairs={{0,4},{4,0},{1,5},{5,1},{2,6},{6,2},{3,7},{7,3},{8,12},{12,8},{9,1... | collective-permute-start | bytes 1572872 | tf_op jit(solution)/shard_map/ppermute | solution.py:38
  213.5 12.7 %all-to-all-start.13 = ((bf16[32,8,128]{2,1,0:T(8,128)(2,1)}), bf16[32,8,128]{2,1,0:T(8,128)(2,1)S(1)}, u32[]{:S(2)}, u32[]{:S(2)}) async-start(bf16[32,8,128]{2,1,0:T(8,128)(2,1)} %get-tuple-element.88), calls=%async_computation.13 | async-start | bytes 131072 | tf_op jit(solution)/shard_map/all_to_all | solution.py:29
  228.0 15.3 %all-to-all-start.14 = ((f32[32,8,512]{2,1,0:T(8,128)}), f32[32,8,512]{2,1,0:T(8,128)S(1)}, u32[]{:S(2)}, u32[]{:S(2)}) async-start(f32[32,8,512]{2,1,0:T(8,128)} %bitcast.19), calls=%async_computation.14 | async-start | bytes 1048576 | tf_op jit(solution)/shard_map/all_to_all | solution.py:29
  244.0 15.1 %all-to-all-start.15 = ((bf16[32,8,512]{2,1,0:T(8,128)(2,1)}), bf16[32,8,512]{2,1,0:T(8,128)(2,1)S(1)}, u32[]{:S(2)}, u32[]{:S(2)}) async-start(bf16[32,8,512]{2,1,0:T(8,128)(2,1)} %broadcast_in_dim.17), calls=%async_computation.15 | async-start | bytes 524288 | tf_op jit(solution)/shard_map/all_to_all | solution.py:29
  249.5 1.0 copy-start.4
  249.5 1.0 copy-start.7
  249.5 1.1 copy-start.8
  259.1 12.3 %collective-permute-start.8 = (bf16[256,512]{1,0:T(8,128)(2,1)S(1)}, bf16[256,512]{1,0:T(8,128)(2,1)S(1)}, u32[]{:S(2)}, u32[]{:S(2)}) collective-permute-start(bf16[256,512]{1,0:T(8,128)(2,1)S(1)} %bitcast.36), channel_id=1, source_target_pairs={{0,4},{4,0},{1,5},{5,1},{2,6},{6,2},{3,7},{7,3},{8,12},{12,8},{9,1... | collective-permute-start | bytes 786440 | tf_op jit(solution)/shard_map/ppermute | solution.py:38
  (2 other events, 1.3 us)

commit v8 on v7

--- a/solution.py
+++ b/solution.py
@@ -76,7 +76,8 @@
 
 
 def start_kernel(
-    x_hbm, y_hbm, q_hbm, r_hbm, xq_ref, yr_ref, vec_ref, cast_ref, x_ref, y_ref, q_ref, r_ref, sems
+    core_ref, x_hbm, y_hbm, q_hbm, r_hbm, keep_ref, give_ref, cast_ref,
+    x_ref, y_ref, q_ref, r_ref, sems,
 ):
     pieces = sems.shape[1]
     copies = []
@@ -89,20 +90,26 @@
             copies.append(pltpu.make_async_copy(source.at[part], target.at[part], sems.at[i, k]))
     for copy in copies:
         copy.start()
+    chunks, _, share, width = keep_ref.shape
+    half = x_ref.shape[1] // 2
     rows = []
-    for side, (emb_ref, factor_ref, cross_ref) in enumerate(
-        ((x_ref, q_ref, xq_ref), (y_ref, r_ref, yr_ref))
-    ):
+    for side, (emb_ref, factor_ref) in enumerate(((x_ref, q_ref), (y_ref, r_ref))):
         for copy in copies[2 * side * pieces : 2 * (side + 1) * pieces]:
             copy.wait()
         factor = factor_ref[...]
         rounded = factor.astype(BF16)
         cast_ref[side] = rounded
-        cross_ref[...] = contract_rows(emb_ref[...], rounded)
+        for position, out_ref in ((core_ref[0], keep_ref), (1 - core_ref[0], give_ref)):
+            emb = emb_ref[:, pl.ds(pl.multiple_of(position * half, half), half)]
+            cross = contract_rows(emb, rounded)
+            for chunk in range(chunks):
+                out_ref[chunk, side] = cross[chunk * share : (chunk + 1) * share]
         norms = jnp.sum(jnp.square(emb_ref[...].astype(F32)), axis=1, keepdims=True)
         rows.append(jnp.sum(norms * factor, axis=0, keepdims=True))
         rows.append(jnp.sum(factor, axis=0, keepdims=True))
-    vec_ref[...] = jnp.concatenate(rows, axis=0)
+    vec = jnp.concatenate(rows, axis=0)
+    for out_ref in (keep_ref, give_ref):
+        out_ref[:, 2] = jnp.broadcast_to(vec[None], (chunks, 4, width))
 
 
 def chunk_kernel(got_ref, g_ref, sent_ref):
@@ -129,8 +136,8 @@
 def grad_kernel(
     core_ref, here_ref, x_ref, y_ref, mine_ref, other_ref, vec_ref, mass_ref, mass2_ref, *refs
 ):
-    factors = refs[:-8]
-    grad_q_ref, grad_r_ref, grad_g_ref, peak_ref, all_ref, own_q_ref, own_r_ref, masses_ref = refs[-8:]
+    factors = refs[:-6]
+    grad_q_ref, grad_r_ref, grad_g_ref, peak_ref, all_ref, masses_ref = refs[-6:]
     masses_ref[...] = jnp.concatenate([mass_ref[...], mass2_ref[...]], axis=0)
     ranks = len(factors)
     rows, width = factors[0].shape[1:]
@@ -160,9 +167,9 @@
     grad_g = -curvature / jnp.square(g)
     grad_g_ref[...] = grad_g
     top = jnp.abs(grad_g)
-    for emb_ref, offset, count, total, out_ref, own_ref in (
-        (x_ref, 4, cr, yr, grad_q_ref, own_q_ref),
-        (y_ref, 0, cq, xq, grad_r_ref, own_r_ref),
+    for emb_ref, offset, count, total, out_ref in (
+        (x_ref, 4, cr, yr, grad_q_ref),
+        (y_ref, 0, cq, xq, grad_r_ref),
     ):
         select = jnp.where(place == wanted + offset, 1.0, 0.0).astype(BF16)
         product = None
@@ -174,7 +181,6 @@
         norms = jnp.sum(jnp.square(emb_ref[...].astype(F32)), axis=1, keepdims=True)
         grad = scale * (norms * count + total - 2.0 * product)
         out_ref[...] = grad
-        own_ref[...] = out_ref[:, lanes_of(here_ref[0])]
         top = jnp.maximum(top, jnp.max(jnp.abs(grad), axis=0, keepdims=True))
     blocks = in_rows(top, top.shape[1] // peak_ref.shape[2])
     peak = blocks[0]
@@ -184,9 +190,14 @@
 
 
 def kern_kernel(
-    peak_ref, grad_q_ref, grad_r_ref, grad_g_ref, vec_ref, all_ref, kern_ref, log_ref, eta_ref
+    here_ref, peak_ref, grad_q_ref, grad_r_ref, grad_g_ref, vec_ref, all_ref,
+    kern_ref, log_ref, eta_ref, own_q_ref, own_r_ref,
 ):
     rows = grad_q_ref.shape[0]
+    width = own_q_ref.shape[1]
+    mine = pl.ds(pl.multiple_of(here_ref[0] * width, width), width)
+    own_q_ref[...] = grad_q_ref[:, mine]
+    own_r_ref[...] = grad_r_ref[:, mine]
     peak = jnp.max(jnp.max(peak_ref[...], axis=0), axis=1, keepdims=True)
     eta = GAMMA / (peak + 1e-06)
     eta_ref[...] = jnp.broadcast_to(eta, eta_ref.shape)
@@ -275,11 +286,11 @@
 def on_chip(kernel, shapes, name, scalars=0, inputs=0, off_chip=0, scratch=(), limit=LIMIT):
     specs = {}
     if scalars:
-        specs["in_specs"] = [pl.BlockSpec(memory_space=pltpu.SMEM)] * scalars + [
-            pl.BlockSpec(memory_space=pltpu.VMEM)
-        ] * inputs
-    if off_chip:
-        specs["in_specs"] = [pl.BlockSpec(memory_space=pltpu.HBM)] * off_chip
+        specs["in_specs"] = (
+            [pl.BlockSpec(memory_space=pltpu.SMEM)] * scalars
+            + [pl.BlockSpec(memory_space=pltpu.VMEM)] * inputs
+            + [pl.BlockSpec(memory_space=pltpu.HBM)] * off_chip
+        )
     return pl.pallas_call(
         kernel,
         out_shape=tuple(jax.ShapeDtypeStruct(shape, dtype) for shape, dtype in shapes),
@@ -304,15 +315,12 @@
     core = lax.axis_index("c")
     other_expr = swap(expr)
     core_index = core.astype(jnp.int32)[None]
-    part_xq, part_yr, part_vec, rounded = on_chip(
+    chunk_shape = ((others, 3, share, width), F32)
+    keep, give, rounded = on_chip(
         start_kernel,
-        (
-            ((dim, width), F32),
-            ((dim, width), F32),
-            ((4, width), F32),
-            ((2, rows, width), BF16),
-        ),
+        (chunk_shape, chunk_shape, ((2, rows, width), BF16)),
         "start",
+        scalars=1,
         off_chip=4,
         limit=60 << 20,
         scratch=[
@@ -322,53 +330,48 @@
             pltpu.VMEM(r_factor.shape, F32),
             pltpu.SemaphoreType.DMA((4, 2)),
         ],
-    )(x_emb, y_emb, q_factor, r_factor)
-    from_others = [
-        lax.ppermute(rounded, "x", [(i, (i + shift) % ranks) for i in range(ranks)])
-        for shift in range(1, ranks)
-    ]
-    part_cross = jnp.concatenate(
-        [part.reshape(2, others, share, width) for part in (part_xq, part_yr)], axis=2
-    )
-
-    def with_vec(cross):
-        return jnp.concatenate(
-            [cross, jnp.broadcast_to(part_vec[None], (others, 4, width))], axis=1
-        ).reshape(others, (2 * share + 4) // 4, 4, width)
-
-    outgoing = with_vec(pick(part_cross, core)) + swap(with_vec(pick(part_cross, 1 - core)))
+    )(core_index, x_emb, y_emb, q_factor, r_factor)
+
+    def from_shift(shift):
+        return lax.ppermute(rounded, "x", [(i, (i + shift) % ranks) for i in range(ranks)])
+
+    outgoing = keep + swap(give)
     columns = ranks * width
     tall = ((rows, columns), F32)
-    sent = on_chip(chunk_kernel, (((ranks, 16, width), F32),), "chunk")(
-        exchange(outgoing, CHIPS), g_weights[None]
-    )[0]
+    got, second = lax.optimization_barrier((exchange(outgoing, CHIPS), from_shift(2)))
+    sent = on_chip(chunk_kernel, (((ranks, 16, width), F32),), "chunk")(got, g_weights[None])[0]
+    got, first = lax.optimization_barrier((exchange(sent, "x"), from_shift(1)))
     sent, vec = on_chip(
         spread_kernel, (((others, 16, columns), BF16), ((8, columns), F32)), "spread"
-    )(exchange(sent, "x"))
+    )(got)
     masses = jnp.stack([a_mass, b_mass])
-    crosses, from_others, their_masses = lax.optimization_barrier(
-        (exchange(sent, CHIPS), from_others, swap(masses))
+    crosses, third, their_masses = lax.optimization_barrier(
+        (exchange(sent, CHIPS), from_shift(3), swap(masses))
     )
     crosses = crosses.reshape(others * 16, columns)
     own_grad = ((rows, width), F32)
-    grad_q, grad_r, grad_g, peak, factors, own_grad_q, own_grad_r, masses = on_chip(
+    grad_q, grad_r, grad_g, peak, factors, masses = on_chip(
         grad_kernel,
         (
             tall, tall, ((1, columns), F32), ((cell_devices, 1, width), F32),
-            ((2 * rows, columns), BF16), own_grad, own_grad, ((4, rows), F32),
+            ((2 * rows, columns), BF16), ((4, rows), F32),
         ),
         "grad",
         scalars=2,
         inputs=7 + ranks,
     )(
         core_index, here.astype(jnp.int32)[None], x_emb, y_emb, crosses, swap(crosses), vec,
-        masses, their_masses, rounded, *from_others,
-    )
-    kerns, log_g, eta = on_chip(
+        masses, their_masses, rounded, first, second, third,
+    )
+    kerns, log_g, eta, own_grad_q, own_grad_r = on_chip(
         kern_kernel,
-        (((2 * rows, columns), BF16), ((ranks, width), F32), ((1, width), F32)),
+        (((2 * rows, columns), BF16), ((ranks, width), F32), ((1, width), F32), own_grad, own_grad),
         "kern",
-    )(exchange(peak, CELLS), grad_q, grad_r, grad_g, vec, factors)
+        scalars=1,
+        inputs=6,
+    )(
+        here.astype(jnp.int32)[None], exchange(peak, CELLS), grad_q, grad_r, grad_g, vec, factors
+    )
     theirs = swap(kerns)
     sent_shape = ((others, 2 * ranks, width), BF16)
     u_shape = ((4, rows), F32)

time: 274 us -> 274 us (level)
  blocking collectives: 144 us -> 113 us
  starting transfers between devices: 55.2 us -> 78.3 us
  waiting for transfers between devices: 42.1 us -> 51.4 us
    all_to_all x11 -> x9, blocking collectives: 144 us -> 113 us  [exchange(): return lax.all_to_all(chunks, axes, 0, 0, tiled=False)]
    all_to_all x5 -> x7, starting transfers between devices: 22.7 us -> 39.2 us  [exchange(): return lax.all_to_all(chunks, axes, 0, 0, tiled=False)]
    all_to_all x5 -> x7, waiting for transfers between devices: 30.2 us -> 38 us  [exchange(): return lax.all_to_all(chunks, axes, 0, 0, tiled=False)]
    ppermute x6, starting transfers between devices: 29.6 us -> 35 us  [swap(): return lax.ppermute(value, 'c', [(0, 1), (1, 0)])]
  transfers between devices with their start and end apart: 14 -> 16, of which waited for: 12 -> 14; matrix products, arithmetic and copies ran while one was open for 1% -> 1% of each run, Pallas kernels for 2% -> 2%
where the time goes in v8:
time: 274 us; the launch traced here: 273 us
  blocking collectives  113 us (41%)
  starting transfers between devices  78.3 us (29%)
  waiting for transfers between devices  51.4 us (19%)
  Pallas kernels  23.2 us (8%)
  other arithmetic  3.47 us (1%)
    all_to_all x9, blocking collectives, exchange(): return lax.all_to_all(chunks, axes, 0, 0, tiled=False)  113 us
    all_to_all x7, starting transfers between devices, exchange(): return lax.all_to_all(chunks, axes, 0, 0, tiled=False)  39.2 us
    all_to_all x7, waiting for transfers between devices, exchange(): return lax.all_to_all(chunks, axes, 0, 0, tiled=False)  38 us
    ppermute x6, starting transfers between devices, swap(): return lax.ppermute(value, 'c', [(0, 1), (1, 0)])  35 us
    pallas_call x9, Pallas kernels, shards(): on_chip(next_pass, (sent_shape, u_shape, v_shape), 'next_pass')  13.5 us
    ppermute x3, waiting for transfers between devices, from_shift(): lax.ppermute(rounded, 'x', [(i, (i + shift) % ranks) for i in range(ranks)])  7.08 us
    ppermute x6, waiting for transfers between devices, swap(): return lax.ppermute(value, 'c', [(0, 1), (1, 0)])  6.29 us
  transfers between devices with their start and end apart: 16, of which 14 were waited for; matrix products, arithmetic and copies ran while one was open for 1% of the time, Pallas kernels for 2%

profile of v8, /device:TPU:1, one launch (start us, length us, event | category | flops | bytes accessed | tf_op | source)
XLA Modules:
  0.0 272.9 jit_solution(1037860144872112632)
XLA Ops:
  9.5 9.6 %all-to-all-start = ((f32[32,3,4,128]{3,2,1,0:T(4,128)}), f32[32,3,4,128]{3,2,1,0:T(4,128)S(1)}, u32[]{:S(2)}, u32[]{:S(2)}) async-start(f32[32,3,4,128]{3,2,1,0:T(4,128)} %add.18), calls=%async_computation | async-start | bytes 393216 | tf_op jit(solution)/shard_map/all_to_all | solution.py:29
  22.2 5.7 %collective-permute-done.1.refs_2_ = bf16[2,512,128]{2,1,0:T(8,128)(2,1)S(1)} collective-permute-done((bf16[2,512,128]{2,1,0:T(8,128)(2,1)S(1)}, bf16[2,512,128]{2,1,0:T(8,128)(2,1)S(1)}, u32[]{:S(2)}, u32[]{:S(2)}) %collective-permute-start.1) | collective-permute-done | bytes 262176 | tf_op jit(solution)/shard_map/ppermute | solution.py:336
  29.1 4.0 %all-to-all-start.1 = ((f32[4,16,128]{2,1,0:T(8,128)}), f32[4,16,128]{2,1,0:T(8,128)S(1)}, u32[]{:S(2)}, u32[]{:S(2)}) async-start(f32[4,16,128]{2,1,0:T(8,128)} %chunk.1), calls=%async_computation.1 | async-start | bytes 65536 | tf_op jit(solution)/shard_map/all_to_all | solution.py:29
  38.3 8.5 %all-to-all-start.2 = ((bf16[32,16,512]{2,1,0:T(8,128)(2,1)}), bf16[32,16,512]{2,1,0:T(8,128)(2,1)S(1)}, u32[]{:S(2)}, u32[]{:S(2)}) async-start(bf16[32,16,512]{2,1,0:T(8,128)(2,1)} %get-tuple-element.55), calls=%async_computation.2 | async-start | bytes 1048576 | tf_op jit(solution)/shard_map/all_to_all | solution.py:29
  47.9 5.3 %collective-permute-start.4 = (f32[2,512]{1,0:T(2,128)S(1)}, f32[2,512]{1,0:T(2,128)S(1)}, u32[]{:S(2)}, u32[]{:S(2)}) collective-permute-start(f32[2,512]{1,0:T(2,128)S(1)} %pad_maximum_fusion.mass_ref), channel_id=1, source_target_pairs={{0,4},{4,0},{1,5},{5,1},{2,6},{6,2},{3,7},{7,3},{8,12},{12,8},{9,1... | collective-permute-start | bytes 12296 | tf_op jit(solution)/shard_map/ppermute | solution.py:38
  54.0 4.4 %all-to-all-done.2 = bf16[32,16,512]{2,1,0:T(8,128)(2,1)S(1)} async-done(((bf16[32,16,512]{2,1,0:T(8,128)(2,1)}), bf16[32,16,512]{2,1,0:T(8,128)(2,1)S(1)}, u32[]{:S(2)}, u32[]{:S(2)}) %all-to-all-start.2) | async-done | bytes 524320 | tf_op jit(solution)/shard_map/all_to_all | solution.py:29
  58.4 8.1 %collective-permute-start.5 = (bf16[512,512]{1,0:T(8,128)(2,1)S(1)}, bf16[512,512]{1,0:T(8,128)(2,1)S(1)}, u32[]{:S(2)}, u32[]{:S(2)}) collective-permute-start(bf16[512,512]{1,0:T(8,128)(2,1)S(1)} %bitcast.25), channel_id=1, source_target_pairs={{0,4},{4,0},{1,5},{5,1},{2,6},{6,2},{3,7},{7,3},{8,12},{12,8},{9,1... | collective-permute-start | bytes 1572872 | tf_op jit(solution)/shard_map/ppermute | solution.py:38
  69.7 13.6 %all_to_all.80.peak_ref = f32[64,1,128]{2,1,0:T(1,128)S(1)} all-to-all(f32[64,1,128]{2,1,0:T(1,128)S(1)} %get-tuple-element.63), channel_id=1, replica_groups=mesh['y'=4,'z'=8,'c'=2,'x'=4] {'y','z','c'}, dimensions={0} | all-to-all | bytes 65536 | tf_op jit(solution)/shard_map/all_to_all | solution.py:29
  88.5 11.8 %all_to_all.81.got_ref = bf16[32,8,128]{2,1,0:T(8,128)(2,1)S(1)} all-to-all(bf16[32,8,128]{2,1,0:T(8,128)(2,1)S(1)} %get-tuple-element.69), channel_id=1, replica_groups=mesh['y'=4,'z'=8,'c'=2,'x'=4] {'y','z'}, dimensions={0} | all-to-all | bytes 131072 | tf_op jit(solution)/shard_map/all_to_all | solution.py:29
  101.8 12.1 %all_to_all.82.got_ref = bf16[32,8,128]{2,1,0:T(8,128)(2,1)S(1)} all-to-all(bf16[32,8,128]{2,1,0:T(8,128)(2,1)S(1)} %get-tuple-element.71), channel_id=1, replica_groups=mesh['y'=4,'z'=8,'c'=2,'x'=4] {'y','z'}, dimensions={0} | all-to-all | bytes 131072 | tf_op jit(solution)/shard_map/all_to_all | solution.py:29
  115.4 11.9 %all_to_all.83.got_ref = bf16[32,8,128]{2,1,0:T(8,128)(2,1)S(1)} all-to-all(bf16[32,8,128]{2,1,0:T(8,128)(2,1)S(1)} %get-tuple-element.73), channel_id=1, replica_groups=mesh['y'=4,'z'=8,'c'=2,'x'=4] {'y','z'}, dimensions={0} | all-to-all | bytes 131072 | tf_op jit(solution)/shard_map/all_to_all | solution.py:29
  128.7 11.9 %all_to_all.84.got_ref = bf16[32,8,128]{2,1,0:T(8,128)(2,1)S(1)} all-to-all(bf16[32,8,128]{2,1,0:T(8,128)(2,1)S(1)} %get-tuple-element.75), channel_id=1, replica_groups=mesh['y'=4,'z'=8,'c'=2,'x'=4] {'y','z'}, dimensions={0} | all-to-all | bytes 131072 | tf_op jit(solution)/shard_map/all_to_all | solution.py:29
  142.1 11.9 %all_to_all.85.got_ref = bf16[32,8,128]{2,1,0:T(8,128)(2,1)S(1)} all-to-all(bf16[32,8,128]{2,1,0:T(8,128)(2,1)S(1)} %get-tuple-element.77), channel_id=1, replica_groups=mesh['y'=4,'z'=8,'c'=2,'x'=4] {'y','z'}, dimensions={0} | all-to-all | bytes 131072 | tf_op jit(solution)/shard_map/all_to_all | solution.py:29
  155.7 3.9 %all-to-all-start.9 = ((bf16[32,8,128]{2,1,0:T(8,128)(2,1)}), bf16[32,8,128]{2,1,0:T(8,128)(2,1)S(1)}, u32[]{:S(2)}, u32[]{:S(2)}) async-start(bf16[32,8,128]{2,1,0:T(8,128)(2,1)} %get-tuple-element.79), calls=%async_computation.9 | async-start | bytes 131072 | tf_op jit(solution)/shard_map/all_to_all | solution.py:29
  159.6 6.3 %collective-permute-start.7 = (bf16[512,512]{1,0:T(8,128)(2,1)S(1)}, bf16[512,512]{1,0:T(8,128)(2,1)S(1)}, u32[]{:S(2)}, u32[]{:S(2)}) collective-permute-start(bf16[512,512]{1,0:T(8,128)(2,1)S(1)} %copy-done.2), channel_id=1, source_target_pairs={{0,4},{4,0},{1,5},{5,1},{2,6},{6,2},{3,7},{7,3},{8,12},{12,8},{9,1... | collective-permute-start | bytes 1572872 | tf_op jit(solution)/shard_map/ppermute | solution.py:38
  169.9 15.6 %all_to_all.86.got_ref = bf16[32,8,128]{2,1,0:T(8,128)(2,1)S(1)} all-to-all(bf16[32,8,128]{2,1,0:T(8,128)(2,1)S(1)} %get-tuple-element.81), channel_id=1, replica_groups=mesh['y'=4,'z'=8,'c'=2,'x'=4] {'y','z'}, dimensions={0} | all-to-all | bytes 131072 | tf_op jit(solution)/shard_map/all_to_all | solution.py:29
  187.0 11.9 %all_to_all.87.got_ref = bf16[32,8,128]{2,1,0:T(8,128)(2,1)S(1)} all-to-all(bf16[32,8,128]{2,1,0:T(8,128)(2,1)S(1)} %get-tuple-element.83), channel_id=1, replica_groups=mesh['y'=4,'z'=8,'c'=2,'x'=4] {'y','z'}, dimensions={0} | all-to-all | bytes 131072 | tf_op jit(solution)/shard_map/all_to_all | solution.py:29
  200.4 11.8 %all_to_all.88.got_ref = bf16[32,8,128]{2,1,0:T(8,128)(2,1)S(1)} all-to-all(bf16[32,8,128]{2,1,0:T(8,128)(2,1)S(1)} %get-tuple-element.85), channel_id=1, replica_groups=mesh['y'=4,'z'=8,'c'=2,'x'=4] {'y','z'}, dimensions={0} | all-to-all | bytes 131072 | tf_op jit(solution)/shard_map/all_to_all | solution.py:29
  217.8 8.8 %all-to-all-done.13.got_ref = bf16[32,8,128]{2,1,0:T(8,128)(2,1)S(1)} async-done(((bf16[32,8,128]{2,1,0:T(8,128)(2,1)}), bf16[32,8,128]{2,1,0:T(8,128)(2,1)S(1)}, u32[]{:S(2)}, u32[]{:S(2)}) %all-to-all-start.13) | async-done | bytes 65568 | tf_op jit(solution)/shard_map/all_to_all | solution.py:29
  228.3 3.9 %all-to-all-start.14 = ((f32[32,8,512]{2,1,0:T(8,128)}), f32[32,8,512]{2,1,0:T(8,128)S(1)}, u32[]{:S(2)}, u32[]{:S(2)}) async-start(f32[32,8,512]{2,1,0:T(8,128)} %bitcast.13), calls=%async_computation.14 | async-start | bytes 1048576 | tf_op jit(solution)/shard_map/all_to_all | solution.py:29
  232.3 11.3 %all-to-all-done.14 = f32[32,8,512]{2,1,0:T(8,128)S(1)} async-done(((f32[32,8,512]{2,1,0:T(8,128)}), f32[32,8,512]{2,1,0:T(8,128)S(1)}, u32[]{:S(2)}, u32[]{:S(2)}) %all-to-all-start.14) | async-done | bytes 524320 | tf_op jit(solution)/shard_map/all_to_all | solution.py:29
  244.4 5.5 %all-to-all-start.15 = ((bf16[32,8,512]{2,1,0:T(8,128)(2,1)}), bf16[32,8,512]{2,1,0:T(8,128)(2,1)S(1)}, u32[]{:S(2)}, u32[]{:S(2)}) async-start(bf16[32,8,512]{2,1,0:T(8,128)(2,1)} %broadcast_in_dim.26), calls=%async_computation.15 | async-start | bytes 524288 | tf_op jit(solution)/shard_map/all_to_all | solution.py:29
  252.0 7.5 %all-to-all-done.15 = bf16[32,8,512]{2,1,0:T(8,128)(2,1)S(1)} async-done(((bf16[32,8,512]{2,1,0:T(8,128)(2,1)}), bf16[32,8,512]{2,1,0:T(8,128)(2,1)S(1)}, u32[]{:S(2)}, u32[]{:S(2)}) %all-to-all-start.15) | async-done | bytes 262176 | tf_op jit(solution)/shard_map/all_to_all | solution.py:29
  259.5 11.2 %collective-permute-start.8 = (bf16[256,512]{1,0:T(8,128)(2,1)S(1)}, bf16[256,512]{1,0:T(8,128)(2,1)S(1)}, u32[]{:S(2)}, u32[]{:S(2)}) collective-permute-start(bf16[256,512]{1,0:T(8,128)(2,1)S(1)} %bitcast.28), channel_id=1, source_target_pairs={{0,4},{4,0},{1,5},{5,1},{2,6},{6,2},{3,7},{7,3},{8,12},{12,8},{9,1... | collective-permute-start | bytes 786440 | tf_op jit(solution)/shard_map/ppermute | solution.py:38
  (69 shorter events, 55.4 us)
Async XLA Ops:
  3.2 4.6 %collective-permute-start = (f32[32,3,4,128]{3,2,1,0:T(4,128)}, f32[32,3,4,128]{3,2,1,0:T(4,128)S(1)}, u32[]{:S(2)}, u32[]{:S(2)}) collective-permute-start(f32[32,3,4,128]{3,2,1,0:T(4,128)} %get-tuple-element.51), channel_id=1, source_target_pairs={{0,4},{4,0},{1,5},{5,1},{2,6},{6,2},{3,7},{7,3},{8,12},{12,8},{9,1... | collective-permute-start | bytes 589832 | tf_op jit(solution)/shard_map/ppermute | solution.py:38
  9.5 9.6 %copy-start.5 = (bf16[2,512,128]{2,1,0:T(8,128)(2,1)S(1)}, bf16[2,512,128]{2,1,0:T(8,128)(2,1)}, u32[]{:S(2)}) copy-start(bf16[2,512,128]{2,1,0:T(8,128)(2,1)} %get-tuple-element.52.refs_0_) | copy-start | bytes 786436
  9.5 19.0 %all-to-all-start = ((f32[32,3,4,128]{3,2,1,0:T(4,128)}), f32[32,3,4,128]{3,2,1,0:T(4,128)S(1)}, u32[]{:S(2)}, u32[]{:S(2)}) async-start(f32[32,3,4,128]{3,2,1,0:T(4,128)} %add.18), calls=%async_computation | async-start | bytes 393216 | tf_op jit(solution)/shard_map/all_to_all | solution.py:29
  19.1 9.4 %copy-start.6 = (f32[128]{0:T(128)S(1)}, f32[128]{0:T(128)}, u32[]{:S(2)}) copy-start(f32[128]{0:T(128)} %param.12) | copy-start | bytes 1540
  19.1 8.8 %collective-permute-start.1 = (bf16[2,512,128]{2,1,0:T(8,128)(2,1)S(1)}, bf16[2,512,128]{2,1,0:T(8,128)(2,1)S(1)}, u32[]{:S(2)}, u32[]{:S(2)}) collective-permute-start(bf16[2,512,128]{2,1,0:T(8,128)(2,1)S(1)} %copy-done.5), channel_id=1, source_target_pairs={{0,2},{1,3},{2,0},{3,1},{4,6},{5,7},{6,4},{7,5},{8,10},{9,11},{10,... | collective-permute-start | bytes 786440 | tf_op jit(solution)/shard_map/ppermute | solution.py:336
  21.9 12.6 %collective-permute-start.2 = (bf16[2,512,128]{2,1,0:T(8,128)(2,1)S(1)}, bf16[2,512,128]{2,1,0:T(8,128)(2,1)S(1)}, u32[]{:S(2)}, u32[]{:S(2)}) collective-permute-start(bf16[2,512,128]{2,1,0:T(8,128)(2,1)S(1)} %copy-done.5), channel_id=1, source_target_pairs={{0,1},{1,2},{2,3},{3,0},{4,5},{5,6},{6,7},{7,4},{8,9},{9,10},{10,1... | collective-permute-start | bytes 786440 | tf_op jit(solution)/shard_map/ppermute | solution.py:336
  29.1 8.3 %all-to-all-start.1 = ((f32[4,16,128]{2,1,0:T(8,128)}), f32[4,16,128]{2,1,0:T(8,128)S(1)}, u32[]{:S(2)}, u32[]{:S(2)}) async-start(f32[4,16,128]{2,1,0:T(8,128)} %chunk.1), calls=%async_computation.1 | async-start | bytes 65536 | tf_op jit(solution)/shard_map/all_to_all | solution.py:29
  38.3 9.5 %copy-start.10 = (f32[512]{0:T(512)S(1)}, f32[512]{0:T(512)}, u32[]{:S(2)}) copy-start(f32[512]{0:T(512)} %param.13) | copy-start | bytes 6148
  38.3 29.7 %copy-start = (bf16[512,256]{1,0:T(8,128)(2,1)S(1)}, bf16[512,256]{1,0:T(8,128)(2,1)}, u32[]{:S(2)}) copy-start(bf16[512,256]{1,0:T(8,128)(2,1)} %x_ref.1) | copy-start | bytes 786436
  38.3 29.7 %copy-start.1 = (bf16[512,256]{1,0:T(8,128)(2,1)S(1)}, bf16[512,256]{1,0:T(8,128)(2,1)}, u32[]{:S(2)}) copy-start(bf16[512,256]{1,0:T(8,128)(2,1)} %y_ref.1) | copy-start | bytes 786436
  38.3 20.0 %all-to-all-start.2 = ((bf16[32,16,512]{2,1,0:T(8,128)(2,1)}), bf16[32,16,512]{2,1,0:T(8,128)(2,1)S(1)}, u32[]{:S(2)}, u32[]{:S(2)}) async-start(bf16[32,16,512]{2,1,0:T(8,128)(2,1)} %get-tuple-element.55), calls=%async_computation.2 | async-start | bytes 1048576 | tf_op jit(solution)/shard_map/all_to_all | solution.py:29
  46.9 7.1 %collective-permute-start.3 = (bf16[2,512,128]{2,1,0:T(8,128)(2,1)S(1)}, bf16[2,512,128]{2,1,0:T(8,128)(2,1)S(1)}, u32[]{:S(2)}, u32[]{:S(2)}) collective-permute-start(bf16[2,512,128]{2,1,0:T(8,128)(2,1)S(1)} %copy-done.5), channel_id=1, source_target_pairs={{0,3},{1,0},{2,1},{3,2},{4,7},{5,4},{6,5},{7,6},{8,11},{9,8},{10,9... | collective-permute-start | bytes 786440 | tf_op jit(solution)/shard_map/ppermute | solution.py:336
  47.9 6.1 %collective-permute-start.4 = (f32[2,512]{1,0:T(2,128)S(1)}, f32[2,512]{1,0:T(2,128)S(1)}, u32[]{:S(2)}, u32[]{:S(2)}) collective-permute-start(f32[2,512]{1,0:T(2,128)S(1)} %pad_maximum_fusion.mass_ref), channel_id=1, source_target_pairs={{0,4},{4,0},{1,5},{5,1},{2,6},{6,2},{3,7},{7,3},{8,12},{12,8},{9,1... | collective-permute-start | bytes 12296 | tf_op jit(solution)/shard_map/ppermute | solution.py:38
  58.4 9.7 %collective-permute-start.5 = (bf16[512,512]{1,0:T(8,128)(2,1)S(1)}, bf16[512,512]{1,0:T(8,128)(2,1)S(1)}, u32[]{:S(2)}, u32[]{:S(2)}) collective-permute-start(bf16[512,512]{1,0:T(8,128)(2,1)S(1)} %bitcast.25), channel_id=1, source_target_pairs={{0,4},{4,0},{1,5},{5,1},{2,6},{6,2},{3,7},{7,3},{8,12},{12,8},{9,1... | collective-permute-start | bytes 1572872 | tf_op jit(solution)/shard_map/ppermute | solution.py:38
  84.0 4.5 %copy-start.3 = (f32[512,128]{1,0:T(8,128)}, f32[512,128]{1,0:T(8,128)S(1)}, u32[]{:S(2)}) copy-start(f32[512,128]{1,0:T(8,128)S(1)} %get-tuple-element.93) | copy-start | bytes 786436
  84.1 3.0 %collective-permute-start.6 = (bf16[1024,512]{1,0:T(8,128)(2,1)S(1)}, bf16[1024,512]{1,0:T(8,128)(2,1)S(1)}, u32[]{:S(2)}, u32[]{:S(2)}) collective-permute-start(bf16[1024,512]{1,0:T(8,128)(2,1)S(1)} %get-tuple-element.68.own_ref), channel_id=1, source_target_pairs={{0,4},{4,0},{1,5},{5,1},{2,6},{6,2},{3,7},{7,3},{8,12},{12,8},{9,1... | collective-permute-start | bytes 3145736 | tf_op jit(solution)/shard_map/ppermute | solution.py:38
  154.0 5.6 %copy-start.2 = (bf16[512,512]{1,0:T(8,128)(2,1)S(1)}, bf16[512,512]{1,0:T(8,128)(2,1)}, u32[]{:S(2)}) copy-start(bf16[512,512]{1,0:T(8,128)(2,1)} %expr_ref.1) | copy-start | bytes 1572868
  155.7 12.7 %all-to-all-start.9 = ((bf16[32,8,128]{2,1,0:T(8,128)(2,1)}), bf16[32,8,128]{2,1,0:T(8,128)(2,1)S(1)}, u32[]{:S(2)}, u32[]{:S(2)}) async-start(bf16[32,8,128]{2,1,0:T(8,128)(2,1)} %get-tuple-element.79), calls=%async_computation.9 | async-start | bytes 131072 | tf_op jit(solution)/shard_map/all_to_all | solution.py:29
  159.6 58.1 %collective-permute-start.7 = (bf16[512,512]{1,0:T(8,128)(2,1)S(1)}, bf16[512,512]{1,0:T(8,128)(2,1)S(1)}, u32[]{:S(2)}, u32[]{:S(2)}) collective-permute-start(bf16[512,512]{1,0:T(8,128)(2,1)S(1)} %copy-done.2), channel_id=1, source_target_pairs={{0,4},{4,0},{1,5},{5,1},{2,6},{6,2},{3,7},{7,3},{8,12},{12,8},{9,1... | collective-permute-start | bytes 1572872 | tf_op jit(solution)/shard_map/ppermute | solution.py:38
  213.9 12.7 %all-to-all-start.13 = ((bf16[32,8,128]{2,1,0:T(8,128)(2,1)}), bf16[32,8,128]{2,1,0:T(8,128)(2,1)S(1)}, u32[]{:S(2)}, u32[]{:S(2)}) async-start(bf16[32,8,128]{2,1,0:T(8,128)(2,1)} %get-tuple-element.90), calls=%async_computation.13 | async-start | bytes 131072 | tf_op jit(solution)/shard_map/all_to_all | solution.py:29
  228.3 15.3 %all-to-all-start.14 = ((f32[32,8,512]{2,1,0:T(8,128)}), f32[32,8,512]{2,1,0:T(8,128)S(1)}, u32[]{:S(2)}, u32[]{:S(2)}) async-start(f32[32,8,512]{2,1,0:T(8,128)} %bitcast.13), calls=%async_computation.14 | async-start | bytes 1048576 | tf_op jit(solution)/shard_map/all_to_all | solution.py:29
  244.4 15.1 %all-to-all-start.15 = ((bf16[32,8,512]{2,1,0:T(8,128)(2,1)}), bf16[32,8,512]{2,1,0:T(8,128)(2,1)S(1)}, u32[]{:S(2)}, u32[]{:S(2)}) async-start(bf16[32,8,512]{2,1,0:T(8,128)(2,1)} %broadcast_in_dim.26), calls=%async_computation.15 | async-start | bytes 524288 | tf_op jit(solution)/shard_map/all_to_all | solution.py:29
  249.9 1.1 copy-start.8
  259.5 12.3 %collective-permute-start.8 = (bf16[256,512]{1,0:T(8,128)(2,1)S(1)}, bf16[256,512]{1,0:T(8,128)(2,1)S(1)}, u32[]{:S(2)}, u32[]{:S(2)}) collective-permute-start(bf16[256,512]{1,0:T(8,128)(2,1)S(1)} %bitcast.28), channel_id=1, source_target_pairs={{0,4},{4,0},{1,5},{5,1},{2,6},{6,2},{3,7},{7,3},{8,12},{12,8},{9,1... | collective-permute-start | bytes 786440 | tf_op jit(solution)/shard_map/ppermute | solution.py:38
  (3 other events, 3.0 us)

commit v9 on v8

--- a/solution.py
+++ b/solution.py
@@ -313,7 +313,6 @@
 
     here = lax.axis_index("x")
     core = lax.axis_index("c")
-    other_expr = swap(expr)
     core_index = core.astype(jnp.int32)[None]
     chunk_shape = ((others, 3, share, width), F32)
     keep, give, rounded = on_chip(
@@ -338,16 +337,17 @@
     outgoing = keep + swap(give)
     columns = ranks * width
     tall = ((rows, columns), F32)
-    got, second = lax.optimization_barrier((exchange(outgoing, CHIPS), from_shift(2)))
-    sent = on_chip(chunk_kernel, (((ranks, 16, width), F32),), "chunk")(got, g_weights[None])[0]
-    got, first = lax.optimization_barrier((exchange(sent, "x"), from_shift(1)))
+    sent = on_chip(chunk_kernel, (((ranks, 16, width), F32),), "chunk")(
+        exchange(outgoing, CHIPS), g_weights[None]
+    )[0]
+    masses = jnp.stack([a_mass, b_mass])
+    got, first, second, third, their_masses = lax.optimization_barrier(
+        (exchange(sent, "x"), from_shift(1), from_shift(2), from_shift(3), swap(masses))
+    )
     sent, vec = on_chip(
         spread_kernel, (((others, 16, columns), BF16), ((8, columns), F32)), "spread"
     )(got)
-    masses = jnp.stack([a_mass, b_mass])
-    crosses, third, their_masses = lax.optimization_barrier(
-        (exchange(sent, CHIPS), from_shift(3), swap(masses))
-    )
+    crosses, other_expr = lax.optimization_barrier((exchange(sent, CHIPS), swap(expr)))
     crosses = crosses.reshape(others * 16, columns)
     own_grad = ((rows, width), F32)
     grad_q, grad_r, grad_g, peak, factors, masses = on_chip(

time: 274 us -> 273 us (level)
  blocking collectives: 113 us -> 134 us
  starting transfers between devices: 78.3 us -> 63.8 us
  waiting for transfers between devices: 51.4 us -> 41.7 us
    all_to_all x9 -> x11, blocking collectives: 113 us -> 134 us  [exchange(): return lax.all_to_all(chunks, axes, 0, 0, tiled=False)]
    all_to_all x7 -> x5, starting transfers between devices: 39.2 us -> 28 us  [exchange(): return lax.all_to_all(chunks, axes, 0, 0, tiled=False)]
    ppermute x3, waiting for transfers between devices: 7.08 us -> 0.01 us  [from_shift(): lax.ppermute(rounded, 'x', [(i, (i + shift) % ranks) for i in range(ranks)])]
    all_to_all x7 -> x5, waiting for transfers between devices: 38 us -> 33.9 us  [exchange(): return lax.all_to_all(chunks, axes, 0, 0, tiled=False)]
    ppermute x6, starting transfers between devices: 35 us -> 30.9 us  [swap(): return lax.ppermute(value, 'c', [(0, 1), (1, 0)])]
  transfers between devices with their start and end apart: 16 -> 14, of which waited for: 14 -> 10; matrix products, arithmetic and copies ran while one was open for 1% -> 1% of each run, Pallas kernels for 2% -> 0%
where the time goes in v9:
time: 273 us; the launch traced here: 271 us
  blocking collectives  134 us (49%)
  starting transfers between devices  63.8 us (23%)
  waiting for transfers between devices  41.7 us (15%)
  Pallas kernels  22.3 us (8%)
  local copies, waits for them, and re-layouts  3.88 us (1%)
  other arithmetic  3.46 us (1%)
    all_to_all x11, blocking collectives, exchange(): return lax.all_to_all(chunks, axes, 0, 0, tiled=False)  134 us
    all_to_all x5, waiting for transfers between devices, exchange(): return lax.all_to_all(chunks, axes, 0, 0, tiled=False)  33.9 us
    ppermute x6, starting transfers between devices, swap(): return lax.ppermute(value, 'c', [(0, 1), (1, 0)])  30.9 us
    all_to_all x5, starting transfers between devices, exchange(): return lax.all_to_all(chunks, axes, 0, 0, tiled=False)  28 us
    pallas_call x9, Pallas kernels, shards(): on_chip(next_pass, (sent_shape, u_shape, v_shape), 'next_pass')  12.7 us
    ppermute x6, waiting for transfers between devices, swap(): return lax.ppermute(value, 'c', [(0, 1), (1, 0)])  7.82 us
  transfers between devices with their start and end apart: 14, of which 10 were waited for; matrix products, arithmetic and copies ran while one was open for 1% of the time, Pallas kernels for 0%

profile of v9, /device:TPU:1, one launch (start us, length us, event | category | flops | bytes accessed | tf_op | source)
XLA Modules:
  0.0 271.4 jit_solution(17815022920350819683)
XLA Ops:
  3.2 3.3 %collective-permute-start = (f32[32,3,4,128]{3,2,1,0:T(4,128)}, f32[32,3,4,128]{3,2,1,0:T(4,128)S(1)}, u32[]{:S(2)}, u32[]{:S(2)}) collective-permute-start(f32[32,3,4,128]{3,2,1,0:T(4,128)} %get-tuple-element.51), channel_id=1, source_target_pairs={{0,4},{4,0},{1,5},{5,1},{2,6},{6,2},{3,7},{7,3},{8,12},{12,8},{9,1... | collective-permute-start | bytes 589832 | tf_op jit(solution)/shard_map/ppermute | solution.py:38
  9.5 9.6 %all-to-all-start = ((f32[32,3,4,128]{3,2,1,0:T(4,128)}), f32[32,3,4,128]{3,2,1,0:T(4,128)S(1)}, u32[]{:S(2)}, u32[]{:S(2)}) async-start(f32[32,3,4,128]{3,2,1,0:T(4,128)} %add.18), calls=%async_computation | async-start | bytes 393216 | tf_op jit(solution)/shard_map/all_to_all | solution.py:29
  24.0 4.5 %all-to-all-done.got_ref = f32[32,3,4,128]{3,2,1,0:T(4,128)S(1)} async-done(((f32[32,3,4,128]{3,2,1,0:T(4,128)}), f32[32,3,4,128]{3,2,1,0:T(4,128)S(1)}, u32[]{:S(2)}, u32[]{:S(2)}) %all-to-all-start) | async-done | bytes 196640 | tf_op jit(solution)/shard_map/all_to_all | solution.py:29
  29.1 4.1 %all-to-all-start.1 = ((f32[4,16,128]{2,1,0:T(8,128)}), f32[4,16,128]{2,1,0:T(8,128)S(1)}, u32[]{:S(2)}, u32[]{:S(2)}) async-start(f32[4,16,128]{2,1,0:T(8,128)} %chunk.1), calls=%async_computation.1 | async-start | bytes 65536 | tf_op jit(solution)/shard_map/all_to_all | solution.py:29
  34.0 3.3 %collective-permute-start.4 = (f32[2,512]{1,0:T(2,128)S(1)}, f32[2,512]{1,0:T(2,128)S(1)}, u32[]{:S(2)}, u32[]{:S(2)}) collective-permute-start(f32[2,512]{1,0:T(2,128)S(1)} %pad_maximum_fusion.mass_ref), channel_id=1, source_target_pairs={{0,4},{4,0},{1,5},{5,1},{2,6},{6,2},{3,7},{7,3},{8,12},{12,8},{9,1... | collective-permute-start | bytes 12296 | tf_op jit(solution)/shard_map/ppermute | solution.py:38
  39.7 5.1 %all-to-all-start.2 = ((bf16[32,16,512]{2,1,0:T(8,128)(2,1)}), bf16[32,16,512]{2,1,0:T(8,128)(2,1)S(1)}, u32[]{:S(2)}, u32[]{:S(2)}) async-start(bf16[32,16,512]{2,1,0:T(8,128)(2,1)} %get-tuple-element.54), calls=%async_computation.2 | async-start | bytes 1048576 | tf_op jit(solution)/shard_map/all_to_all | solution.py:29
  48.7 8.8 %all-to-all-done.2 = bf16[32,16,512]{2,1,0:T(8,128)(2,1)S(1)} async-done(((bf16[32,16,512]{2,1,0:T(8,128)(2,1)}), bf16[32,16,512]{2,1,0:T(8,128)(2,1)S(1)}, u32[]{:S(2)}, u32[]{:S(2)}) %all-to-all-start.2) | async-done | bytes 524320 | tf_op jit(solution)/shard_map/all_to_all | solution.py:29
  57.6 5.1 %collective-permute-start.6 = (bf16[512,512]{1,0:T(8,128)(2,1)S(1)}, bf16[512,512]{1,0:T(8,128)(2,1)S(1)}, u32[]{:S(2)}, u32[]{:S(2)}) collective-permute-start(bf16[512,512]{1,0:T(8,128)(2,1)S(1)} %bitcast.25), channel_id=1, source_target_pairs={{0,4},{4,0},{1,5},{5,1},{2,6},{6,2},{3,7},{7,3},{8,12},{12,8},{9,1... | collective-permute-start | bytes 1572872 | tf_op jit(solution)/shard_map/ppermute | solution.py:38
  66.9 15.2 %all_to_all.80.peak_ref = f32[64,1,128]{2,1,0:T(1,128)S(1)} all-to-all(f32[64,1,128]{2,1,0:T(1,128)S(1)} %get-tuple-element.62), channel_id=1, replica_groups=mesh['y'=4,'z'=8,'c'=2,'x'=4] {'y','z','c'}, dimensions={0} | all-to-all | bytes 65536 | tf_op jit(solution)/shard_map/all_to_all | solution.py:29
  87.3 11.8 %all_to_all.81.got_ref = bf16[32,8,128]{2,1,0:T(8,128)(2,1)S(1)} all-to-all(bf16[32,8,128]{2,1,0:T(8,128)(2,1)S(1)} %get-tuple-element.68), channel_id=1, replica_groups=mesh['y'=4,'z'=8,'c'=2,'x'=4] {'y','z'}, dimensions={0} | all-to-all | bytes 131072 | tf_op jit(solution)/shard_map/all_to_all | solution.py:29
  100.6 12.1 %all_to_all.82.got_ref = bf16[32,8,128]{2,1,0:T(8,128)(2,1)S(1)} all-to-all(bf16[32,8,128]{2,1,0:T(8,128)(2,1)S(1)} %get-tuple-element.70), channel_id=1, replica_groups=mesh['y'=4,'z'=8,'c'=2,'x'=4] {'y','z'}, dimensions={0} | all-to-all | bytes 131072 | tf_op jit(solution)/shard_map/all_to_all | solution.py:29
  114.1 11.9 %all_to_all.83.got_ref = bf16[32,8,128]{2,1,0:T(8,128)(2,1)S(1)} all-to-all(bf16[32,8,128]{2,1,0:T(8,128)(2,1)S(1)} %get-tuple-element.72), channel_id=1, replica_groups=mesh['y'=4,'z'=8,'c'=2,'x'=4] {'y','z'}, dimensions={0} | all-to-all | bytes 131072 | tf_op jit(solution)/shard_map/all_to_all | solution.py:29
  127.5 11.9 %all_to_all.84.got_ref = bf16[32,8,128]{2,1,0:T(8,128)(2,1)S(1)} all-to-all(bf16[32,8,128]{2,1,0:T(8,128)(2,1)S(1)} %get-tuple-element.74), channel_id=1, replica_groups=mesh['y'=4,'z'=8,'c'=2,'x'=4] {'y','z'}, dimensions={0} | all-to-all | bytes 131072 | tf_op jit(solution)/shard_map/all_to_all | solution.py:29
  140.8 11.9 %all_to_all.85.got_ref = bf16[32,8,128]{2,1,0:T(8,128)(2,1)S(1)} all-to-all(bf16[32,8,128]{2,1,0:T(8,128)(2,1)S(1)} %get-tuple-element.76), channel_id=1, replica_groups=mesh['y'=4,'z'=8,'c'=2,'x'=4] {'y','z'}, dimensions={0} | all-to-all | bytes 131072 | tf_op jit(solution)/shard_map/all_to_all | solution.py:29
  154.2 11.8 %all_to_all.86.got_ref = bf16[32,8,128]{2,1,0:T(8,128)(2,1)S(1)} all-to-all(bf16[32,8,128]{2,1,0:T(8,128)(2,1)S(1)} %get-tuple-element.78), channel_id=1, replica_groups=mesh['y'=4,'z'=8,'c'=2,'x'=4] {'y','z'}, dimensions={0} | all-to-all | bytes 131072 | tf_op jit(solution)/shard_map/all_to_all | solution.py:29
  167.5 11.8 %all_to_all.87.got_ref = bf16[32,8,128]{2,1,0:T(8,128)(2,1)S(1)} all-to-all(bf16[32,8,128]{2,1,0:T(8,128)(2,1)S(1)} %get-tuple-element.80), channel_id=1, replica_groups=mesh['y'=4,'z'=8,'c'=2,'x'=4] {'y','z'}, dimensions={0} | all-to-all | bytes 131072 | tf_op jit(solution)/shard_map/all_to_all | solution.py:29
  180.8 11.8 %all_to_all.88.got_ref = bf16[32,8,128]{2,1,0:T(8,128)(2,1)S(1)} all-to-all(bf16[32,8,128]{2,1,0:T(8,128)(2,1)S(1)} %get-tuple-element.82), channel_id=1, replica_groups=mesh['y'=4,'z'=8,'c'=2,'x'=4] {'y','z'}, dimensions={0} | all-to-all | bytes 131072 | tf_op jit(solution)/shard_map/all_to_all | solution.py:29
  194.0 11.8 %all_to_all.89.got_ref = bf16[32,8,128]{2,1,0:T(8,128)(2,1)S(1)} all-to-all(bf16[32,8,128]{2,1,0:T(8,128)(2,1)S(1)} %get-tuple-element.84), channel_id=1, replica_groups=mesh['y'=4,'z'=8,'c'=2,'x'=4] {'y','z'}, dimensions={0} | all-to-all | bytes 131072 | tf_op jit(solution)/shard_map/all_to_all | solution.py:29
  206.9 11.8 %all_to_all.90.got_ref = bf16[32,8,128]{2,1,0:T(8,128)(2,1)S(1)} all-to-all(bf16[32,8,128]{2,1,0:T(8,128)(2,1)S(1)} %get-tuple-element.89), channel_id=1, replica_groups=mesh['y'=4,'z'=8,'c'=2,'x'=4] {'y','z'}, dimensions={0} | all-to-all | bytes 131072 | tf_op jit(solution)/shard_map/all_to_all | solution.py:29
  220.4 3.9 %all-to-all-start.14 = ((f32[32,8,512]{2,1,0:T(8,128)}), f32[32,8,512]{2,1,0:T(8,128)S(1)}, u32[]{:S(2)}, u32[]{:S(2)}) async-start(f32[32,8,512]{2,1,0:T(8,128)} %bitcast.13), calls=%async_computation.14 | async-start | bytes 1048576 | tf_op jit(solution)/shard_map/all_to_all | solution.py:29
  224.4 11.5 %all-to-all-done.14 = f32[32,8,512]{2,1,0:T(8,128)S(1)} async-done(((f32[32,8,512]{2,1,0:T(8,128)}), f32[32,8,512]{2,1,0:T(8,128)S(1)}, u32[]{:S(2)}, u32[]{:S(2)}) %all-to-all-start.14) | async-done | bytes 524320 | tf_op jit(solution)/shard_map/all_to_all | solution.py:29
  236.7 5.3 %all-to-all-start.15 = ((bf16[32,8,512]{2,1,0:T(8,128)(2,1)}), bf16[32,8,512]{2,1,0:T(8,128)(2,1)S(1)}, u32[]{:S(2)}, u32[]{:S(2)}) async-start(bf16[32,8,512]{2,1,0:T(8,128)(2,1)} %broadcast_in_dim.26), calls=%async_computation.15 | async-start | bytes 524288 | tf_op jit(solution)/shard_map/all_to_all | solution.py:29
  244.0 9.1 %all-to-all-done.15 = bf16[32,8,512]{2,1,0:T(8,128)(2,1)S(1)} async-done(((bf16[32,8,512]{2,1,0:T(8,128)(2,1)}), bf16[32,8,512]{2,1,0:T(8,128)(2,1)S(1)}, u32[]{:S(2)}, u32[]{:S(2)}) %all-to-all-start.15) | async-done | bytes 262176 | tf_op jit(solution)/shard_map/all_to_all | solution.py:29
  253.1 16.1 %collective-permute-start.8 = (bf16[256,512]{1,0:T(8,128)(2,1)S(1)}, bf16[256,512]{1,0:T(8,128)(2,1)S(1)}, u32[]{:S(2)}, u32[]{:S(2)}) collective-permute-start(bf16[256,512]{1,0:T(8,128)(2,1)S(1)} %bitcast.28), channel_id=1, source_target_pairs={{0,4},{4,0},{1,5},{5,1},{2,6},{6,2},{3,7},{7,3},{8,12},{12,8},{9,1... | collective-permute-start | bytes 786440 | tf_op jit(solution)/shard_map/ppermute | solution.py:38
  (67 shorter events, 46.9 us)
Async XLA Ops:
  3.2 4.6 %collective-permute-start = (f32[32,3,4,128]{3,2,1,0:T(4,128)}, f32[32,3,4,128]{3,2,1,0:T(4,128)S(1)}, u32[]{:S(2)}, u32[]{:S(2)}) collective-permute-start(f32[32,3,4,128]{3,2,1,0:T(4,128)} %get-tuple-element.51), channel_id=1, source_target_pairs={{0,4},{4,0},{1,5},{5,1},{2,6},{6,2},{3,7},{7,3},{8,12},{12,8},{9,1... | collective-permute-start | bytes 589832 | tf_op jit(solution)/shard_map/ppermute | solution.py:38
  9.5 9.6 %copy-start.3 = (bf16[2,512,128]{2,1,0:T(8,128)(2,1)S(1)}, bf16[2,512,128]{2,1,0:T(8,128)(2,1)}, u32[]{:S(2)}) copy-start(bf16[2,512,128]{2,1,0:T(8,128)(2,1)} %get-tuple-element.52.refs_0_) | copy-start | bytes 786436
  9.5 19.0 %all-to-all-start = ((f32[32,3,4,128]{3,2,1,0:T(4,128)}), f32[32,3,4,128]{3,2,1,0:T(4,128)S(1)}, u32[]{:S(2)}, u32[]{:S(2)}) async-start(f32[32,3,4,128]{3,2,1,0:T(4,128)} %add.18), calls=%async_computation | async-start | bytes 393216 | tf_op jit(solution)/shard_map/all_to_all | solution.py:29
  19.1 9.4 %copy-start.6 = (f32[128]{0:T(128)S(1)}, f32[128]{0:T(128)}, u32[]{:S(2)}) copy-start(f32[128]{0:T(128)} %param.12) | copy-start | bytes 1540
  19.1 19.0 %collective-permute-start.1 = (bf16[2,512,128]{2,1,0:T(8,128)(2,1)S(1)}, bf16[2,512,128]{2,1,0:T(8,128)(2,1)S(1)}, u32[]{:S(2)}, u32[]{:S(2)}) collective-permute-start(bf16[2,512,128]{2,1,0:T(8,128)(2,1)S(1)} %copy-done.3), channel_id=1, source_target_pairs={{0,1},{1,2},{2,3},{3,0},{4,5},{5,6},{6,7},{7,4},{8,9},{9,10},{10,1... | collective-permute-start | bytes 786440 | tf_op jit(solution)/shard_map/ppermute | solution.py:335
  20.4 17.7 %collective-permute-start.2 = (bf16[2,512,128]{2,1,0:T(8,128)(2,1)S(1)}, bf16[2,512,128]{2,1,0:T(8,128)(2,1)S(1)}, u32[]{:S(2)}, u32[]{:S(2)}) collective-permute-start(bf16[2,512,128]{2,1,0:T(8,128)(2,1)S(1)} %copy-done.3), channel_id=1, source_target_pairs={{0,2},{1,3},{2,0},{3,1},{4,6},{5,7},{6,4},{7,5},{8,10},{9,11},{10,... | collective-permute-start | bytes 786440 | tf_op jit(solution)/shard_map/ppermute | solution.py:335
  22.8 15.3 %collective-permute-start.3 = (bf16[2,512,128]{2,1,0:T(8,128)(2,1)S(1)}, bf16[2,512,128]{2,1,0:T(8,128)(2,1)S(1)}, u32[]{:S(2)}, u32[]{:S(2)}) collective-permute-start(bf16[2,512,128]{2,1,0:T(8,128)(2,1)S(1)} %copy-done.3), channel_id=1, source_target_pairs={{0,3},{1,0},{2,1},{3,2},{4,7},{5,4},{6,5},{7,6},{8,11},{9,8},{10,9... | collective-permute-start | bytes 786440 | tf_op jit(solution)/shard_map/ppermute | solution.py:335
  29.1 4.2 %copy-start.10 = (f32[512]{0:T(512)S(1)}, f32[512]{0:T(512)}, u32[]{:S(2)}) copy-start(f32[512]{0:T(512)} %param.13) | copy-start | bytes 6148
  29.1 9.7 %all-to-all-start.1 = ((f32[4,16,128]{2,1,0:T(8,128)}), f32[4,16,128]{2,1,0:T(8,128)S(1)}, u32[]{:S(2)}, u32[]{:S(2)}) async-start(f32[4,16,128]{2,1,0:T(8,128)} %chunk.1), calls=%async_computation.1 | async-start | bytes 65536 | tf_op jit(solution)/shard_map/all_to_all | solution.py:29
  34.0 4.1 %collective-permute-start.4 = (f32[2,512]{1,0:T(2,128)S(1)}, f32[2,512]{1,0:T(2,128)S(1)}, u32[]{:S(2)}, u32[]{:S(2)}) collective-permute-start(f32[2,512]{1,0:T(2,128)S(1)} %pad_maximum_fusion.mass_ref), channel_id=1, source_target_pairs={{0,4},{4,0},{1,5},{5,1},{2,6},{6,2},{3,7},{7,3},{8,12},{12,8},{9,1... | collective-permute-start | bytes 12296 | tf_op jit(solution)/shard_map/ppermute | solution.py:38
  38.1 0.7 copy-start.4
  39.7 5.1 %copy-start.2 = (bf16[512,512]{1,0:T(8,128)(2,1)S(1)}, bf16[512,512]{1,0:T(8,128)(2,1)}, u32[]{:S(2)}) copy-start(bf16[512,512]{1,0:T(8,128)(2,1)} %expr_ref.1) | copy-start | bytes 1572868
  39.7 24.6 %copy-start = (bf16[512,256]{1,0:T(8,128)(2,1)S(1)}, bf16[512,256]{1,0:T(8,128)(2,1)}, u32[]{:S(2)}) copy-start(bf16[512,256]{1,0:T(8,128)(2,1)} %x_ref.1) | copy-start | bytes 786436
  39.7 24.6 %copy-start.1 = (bf16[512,256]{1,0:T(8,128)(2,1)S(1)}, bf16[512,256]{1,0:T(8,128)(2,1)}, u32[]{:S(2)}) copy-start(bf16[512,256]{1,0:T(8,128)(2,1)} %y_ref.1) | copy-start | bytes 786436
  39.7 17.9 %all-to-all-start.2 = ((bf16[32,16,512]{2,1,0:T(8,128)(2,1)}), bf16[32,16,512]{2,1,0:T(8,128)(2,1)S(1)}, u32[]{:S(2)}, u32[]{:S(2)}) async-start(bf16[32,16,512]{2,1,0:T(8,128)(2,1)} %get-tuple-element.54), calls=%async_computation.2 | async-start | bytes 1048576 | tf_op jit(solution)/shard_map/all_to_all | solution.py:29
  44.8 3.9 %collective-permute-start.5 = (bf16[512,512]{1,0:T(8,128)(2,1)S(1)}, bf16[512,512]{1,0:T(8,128)(2,1)S(1)}, u32[]{:S(2)}, u32[]{:S(2)}) collective-permute-start(bf16[512,512]{1,0:T(8,128)(2,1)S(1)} %copy-done.2), channel_id=1, source_target_pairs={{0,4},{4,0},{1,5},{5,1},{2,6},{6,2},{3,7},{7,3},{8,12},{12,8},{9,1... | collective-permute-start | bytes 1572872 | tf_op jit(solution)/shard_map/ppermute | solution.py:38
  57.6 6.7 %collective-permute-start.6 = (bf16[512,512]{1,0:T(8,128)(2,1)S(1)}, bf16[512,512]{1,0:T(8,128)(2,1)S(1)}, u32[]{:S(2)}, u32[]{:S(2)}) collective-permute-start(bf16[512,512]{1,0:T(8,128)(2,1)S(1)} %bitcast.25), channel_id=1, source_target_pairs={{0,4},{4,0},{1,5},{5,1},{2,6},{6,2},{3,7},{7,3},{8,12},{12,8},{9,1... | collective-permute-start | bytes 1572872 | tf_op jit(solution)/shard_map/ppermute | solution.py:38
  64.2 1.0 copy-start.5
  82.8 3.0 %collective-permute-start.7 = (bf16[1024,512]{1,0:T(8,128)(2,1)S(1)}, bf16[1024,512]{1,0:T(8,128)(2,1)S(1)}, u32[]{:S(2)}, u32[]{:S(2)}) collective-permute-start(bf16[1024,512]{1,0:T(8,128)(2,1)S(1)} %get-tuple-element.67.own_ref), channel_id=1, source_target_pairs={{0,4},{4,0},{1,5},{5,1},{2,6},{6,2},{3,7},{7,3},{8,12},{12,8},{9,1... | collective-permute-start | bytes 3145736 | tf_op jit(solution)/shard_map/ppermute | solution.py:38
  220.4 15.5 %all-to-all-start.14 = ((f32[32,8,512]{2,1,0:T(8,128)}), f32[32,8,512]{2,1,0:T(8,128)S(1)}, u32[]{:S(2)}, u32[]{:S(2)}) async-start(f32[32,8,512]{2,1,0:T(8,128)} %bitcast.13), calls=%async_computation.14 | async-start | bytes 1048576 | tf_op jit(solution)/shard_map/all_to_all | solution.py:29
  236.7 16.4 %all-to-all-start.15 = ((bf16[32,8,512]{2,1,0:T(8,128)(2,1)}), bf16[32,8,512]{2,1,0:T(8,128)(2,1)S(1)}, u32[]{:S(2)}, u32[]{:S(2)}) async-start(bf16[32,8,512]{2,1,0:T(8,128)(2,1)} %broadcast_in_dim.26), calls=%async_computation.15 | async-start | bytes 524288 | tf_op jit(solution)/shard_map/all_to_all | solution.py:29
  242.0 1.0 copy-start.7
  242.0 1.0 copy-start.8
  253.1 17.2 %collective-permute-start.8 = (bf16[256,512]{1,0:T(8,128)(2,1)S(1)}, bf16[256,512]{1,0:T(8,128)(2,1)S(1)}, u32[]{:S(2)}, u32[]{:S(2)}) collective-permute-start(bf16[256,512]{1,0:T(8,128)(2,1)S(1)} %bitcast.28), channel_id=1, source_target_pairs={{0,4},{4,0},{1,5},{5,1},{2,6},{6,2},{3,7},{7,3},{8,12},{12,8},{9,1... | collective-permute-start | bytes 786440 | tf_op jit(solution)/shard_map/ppermute | solution.py:38
  (1 other events, 0.7 us)

commit v10 on v9

--- a/solution.py
+++ b/solution.py
@@ -216,7 +216,7 @@
     return jnp.concatenate([weights, weights], axis=0) / t, weights
 
 
-def send_columns(v, mass_ref, own_ref, other_ref, sent_ref, u_ref):
+def send_columns(v, mass_ref, own_ref, other_ref, sent_ref, u_ref=None):
     ranks = v.shape[0] // 2
     rows = own_ref.shape[0] // 2
 
@@ -233,7 +233,8 @@
             )
             sums.append(sum_rows(part))
     u = jnp.exp(POWER * jnp.log(mass_ref[...] / jnp.concatenate(sums, axis=0)))
-    u_ref[...] = u
+    if u_ref is not None:
+        u_ref[...] = u
     columns = []
     for side in range(2):
         total = None
@@ -248,12 +249,14 @@
     sent_ref[...] = jnp.broadcast_to(part[None], sent_ref.shape)
 
 
-def first_pass(mass_ref, own_ref, other_ref, sent_ref, u_ref):
+def first_pass(mass_ref, own_ref, other_ref, sent_ref):
     ones = jnp.ones(sent_ref.shape[1:], F32)
-    send_columns(ones, mass_ref, own_ref, other_ref, sent_ref, u_ref)
-
-
-def next_pass(got_ref, v_ref, log_ref, mass_ref, own_ref, other_ref, sent_ref, u_ref, new_ref):
+    send_columns(ones, mass_ref, own_ref, other_ref, sent_ref)
+
+
+def next_pass(
+    got_ref, v_ref, log_ref, mass_ref, own_ref, other_ref, sent_ref, new_ref, u_ref=None
+):
     v, _ = new_scalings(log_ref.shape[0], got_ref, v_ref, log_ref)
     new_ref[...] = v
     send_columns(v, mass_ref, own_ref, other_ref, sent_ref, u_ref)
@@ -376,12 +379,14 @@
     sent_shape = ((others, 2 * ranks, width), BF16)
     u_shape = ((4, rows), F32)
     v_shape = ((2 * ranks, width), F32)
-    sent, u = on_chip(first_pass, (sent_shape, u_shape), "first_pass")(masses, kerns, theirs)
+    sent = on_chip(first_pass, (sent_shape,), "first_pass")(masses, kerns, theirs)[0]
     v = jnp.ones(v_shape[0], F32)
     for step in range(1, PASSES):
-        sent, u, v = on_chip(next_pass, (sent_shape, u_shape, v_shape), "next_pass")(
+        last = (u_shape,) if step == PASSES - 1 else ()
+        sent, v, *u = on_chip(next_pass, (sent_shape, v_shape) + last, "next_pass")(
             exchange(sent, CHIPS), v, log_g, masses, kerns, theirs
         )
+    (u,) = u
     part, v, weights = on_chip(
         profile_kernel,
         (((ranks * width // 2, genes), F32), v_shape, ((ranks, width), F32)),

time: 273 us -> 269 us (0.985)
  Pallas kernels: 22.3 us -> 18.9 us
    pallas_call x10, Pallas kernels: 14.1 us -> 10.7 us  [the longest x9 9.6 us: shards(): on_chip(next_pass, (sent_shape, v_shape) + last, 'next_pass')]
where the time goes in v10:
time: 269 us; the launch traced here: 268 us
  blocking collectives  134 us (50%)
  starting transfers between devices  64 us (24%)
  waiting for transfers between devices  41.6 us (15%)
  Pallas kernels  18.9 us (7%)
  local copies, waits for them, and re-layouts  3.88 us (1%)
  other arithmetic  3.46 us (1%)
    all_to_all x11, blocking collectives, exchange(): return lax.all_to_all(chunks, axes, 0, 0, tiled=False)  134 us
    all_to_all x5, waiting for transfers between devices, exchange(): return lax.all_to_all(chunks, axes, 0, 0, tiled=False)  33.7 us
    ppermute x6, starting transfers between devices, swap(): return lax.ppermute(value, 'c', [(0, 1), (1, 0)])  30.9 us
    all_to_all x5, starting transfers between devices, exchange(): return lax.all_to_all(chunks, axes, 0, 0, tiled=False)  28.2 us
    pallas_call x9, Pallas kernels, shards(): on_chip(next_pass, (sent_shape, v_shape) + last, 'next_pass')  9.6 us
    ppermute x6, waiting for transfers between devices, swap(): return lax.ppermute(value, 'c', [(0, 1), (1, 0)])  7.82 us
  transfers between devices with their start and end apart: 14, of which 10 were waited for; matrix products, arithmetic and copies ran while one was open for 1% of the time, Pallas kernels for 0%

profile of v10, /device:TPU:1, one launch (start us, length us, event | category | flops | bytes accessed | tf_op | source)
XLA Modules:
  0.0 268.2 jit_solution(1492316848313840879)
XLA Ops:
  3.2 3.3 %collective-permute-start = (f32[32,3,4,128]{3,2,1,0:T(4,128)}, f32[32,3,4,128]{3,2,1,0:T(4,128)S(1)}, u32[]{:S(2)}, u32[]{:S(2)}) collective-permute-start(f32[32,3,4,128]{3,2,1,0:T(4,128)} %get-tuple-element.50), channel_id=1, source_target_pairs={{0,4},{4,0},{1,5},{5,1},{2,6},{6,2},{3,7},{7,3},{8,12},{12,8},{9,1... | collective-permute-start | bytes 589832 | tf_op jit(solution)/shard_map/ppermute | solution.py:38
  9.5 9.6 %all-to-all-start = ((f32[32,3,4,128]{3,2,1,0:T(4,128)}), f32[32,3,4,128]{3,2,1,0:T(4,128)S(1)}, u32[]{:S(2)}, u32[]{:S(2)}) async-start(f32[32,3,4,128]{3,2,1,0:T(4,128)} %add.18), calls=%async_computation | async-start | bytes 393216 | tf_op jit(solution)/shard_map/all_to_all | solution.py:29
  24.0 4.5 %all-to-all-done.got_ref = f32[32,3,4,128]{3,2,1,0:T(4,128)S(1)} async-done(((f32[32,3,4,128]{3,2,1,0:T(4,128)}), f32[32,3,4,128]{3,2,1,0:T(4,128)S(1)}, u32[]{:S(2)}, u32[]{:S(2)}) %all-to-all-start) | async-done | bytes 196640 | tf_op jit(solution)/shard_map/all_to_all | solution.py:29
  29.1 4.1 %all-to-all-start.1 = ((f32[4,16,128]{2,1,0:T(8,128)}), f32[4,16,128]{2,1,0:T(8,128)S(1)}, u32[]{:S(2)}, u32[]{:S(2)}) async-start(f32[4,16,128]{2,1,0:T(8,128)} %chunk.1), calls=%async_computation.1 | async-start | bytes 65536 | tf_op jit(solution)/shard_map/all_to_all | solution.py:29
  34.0 3.3 %collective-permute-start.4 = (f32[2,512]{1,0:T(2,128)S(1)}, f32[2,512]{1,0:T(2,128)S(1)}, u32[]{:S(2)}, u32[]{:S(2)}) collective-permute-start(f32[2,512]{1,0:T(2,128)S(1)} %pad_maximum_fusion.mass_ref), channel_id=1, source_target_pairs={{0,4},{4,0},{1,5},{5,1},{2,6},{6,2},{3,7},{7,3},{8,12},{12,8},{9,1... | collective-permute-start | bytes 12296 | tf_op jit(solution)/shard_map/ppermute | solution.py:38
  39.7 5.1 %all-to-all-start.2 = ((bf16[32,16,512]{2,1,0:T(8,128)(2,1)}), bf16[32,16,512]{2,1,0:T(8,128)(2,1)S(1)}, u32[]{:S(2)}, u32[]{:S(2)}) async-start(bf16[32,16,512]{2,1,0:T(8,128)(2,1)} %get-tuple-element.53), calls=%async_computation.2 | async-start | bytes 1048576 | tf_op jit(solution)/shard_map/all_to_all | solution.py:29
  48.7 8.8 %all-to-all-done.2 = bf16[32,16,512]{2,1,0:T(8,128)(2,1)S(1)} async-done(((bf16[32,16,512]{2,1,0:T(8,128)(2,1)}), bf16[32,16,512]{2,1,0:T(8,128)(2,1)S(1)}, u32[]{:S(2)}, u32[]{:S(2)}) %all-to-all-start.2) | async-done | bytes 524320 | tf_op jit(solution)/shard_map/all_to_all | solution.py:29
  57.6 5.1 %collective-permute-start.6 = (bf16[512,512]{1,0:T(8,128)(2,1)S(1)}, bf16[512,512]{1,0:T(8,128)(2,1)S(1)}, u32[]{:S(2)}, u32[]{:S(2)}) collective-permute-start(bf16[512,512]{1,0:T(8,128)(2,1)S(1)} %bitcast.25), channel_id=1, source_target_pairs={{0,4},{4,0},{1,5},{5,1},{2,6},{6,2},{3,7},{7,3},{8,12},{12,8},{9,1... | collective-permute-start | bytes 1572872 | tf_op jit(solution)/shard_map/ppermute | solution.py:38
  66.9 15.2 %all_to_all.80.peak_ref = f32[64,1,128]{2,1,0:T(1,128)S(1)} all-to-all(f32[64,1,128]{2,1,0:T(1,128)S(1)} %get-tuple-element.61), channel_id=1, replica_groups=mesh['y'=4,'z'=8,'c'=2,'x'=4] {'y','z','c'}, dimensions={0} | all-to-all | bytes 65536 | tf_op jit(solution)/shard_map/all_to_all | solution.py:29
  86.9 11.8 %all_to_all.81.got_ref = bf16[32,8,128]{2,1,0:T(8,128)(2,1)S(1)} all-to-all(bf16[32,8,128]{2,1,0:T(8,128)(2,1)S(1)} %first_pass.1), channel_id=1, replica_groups=mesh['y'=4,'z'=8,'c'=2,'x'=4] {'y','z'}, dimensions={0} | all-to-all | bytes 131072 | tf_op jit(solution)/shard_map/all_to_all | solution.py:29
  99.8 12.1 %all_to_all.82.got_ref = bf16[32,8,128]{2,1,0:T(8,128)(2,1)S(1)} all-to-all(bf16[32,8,128]{2,1,0:T(8,128)(2,1)S(1)} %get-tuple-element.68), channel_id=1, replica_groups=mesh['y'=4,'z'=8,'c'=2,'x'=4] {'y','z'}, dimensions={0} | all-to-all | bytes 131072 | tf_op jit(solution)/shard_map/all_to_all | solution.py:29
  113.0 11.9 %all_to_all.83.got_ref = bf16[32,8,128]{2,1,0:T(8,128)(2,1)S(1)} all-to-all(bf16[32,8,128]{2,1,0:T(8,128)(2,1)S(1)} %get-tuple-element.70), channel_id=1, replica_groups=mesh['y'=4,'z'=8,'c'=2,'x'=4] {'y','z'}, dimensions={0} | all-to-all | bytes 131072 | tf_op jit(solution)/shard_map/all_to_all | solution.py:29
  126.0 11.9 %all_to_all.84.got_ref = bf16[32,8,128]{2,1,0:T(8,128)(2,1)S(1)} all-to-all(bf16[32,8,128]{2,1,0:T(8,128)(2,1)S(1)} %get-tuple-element.72), channel_id=1, replica_groups=mesh['y'=4,'z'=8,'c'=2,'x'=4] {'y','z'}, dimensions={0} | all-to-all | bytes 131072 | tf_op jit(solution)/shard_map/all_to_all | solution.py:29
  139.0 11.9 %all_to_all.85.got_ref = bf16[32,8,128]{2,1,0:T(8,128)(2,1)S(1)} all-to-all(bf16[32,8,128]{2,1,0:T(8,128)(2,1)S(1)} %get-tuple-element.74), channel_id=1, replica_groups=mesh['y'=4,'z'=8,'c'=2,'x'=4] {'y','z'}, dimensions={0} | all-to-all | bytes 131072 | tf_op jit(solution)/shard_map/all_to_all | solution.py:29
  152.0 11.8 %all_to_all.86.got_ref = bf16[32,8,128]{2,1,0:T(8,128)(2,1)S(1)} all-to-all(bf16[32,8,128]{2,1,0:T(8,128)(2,1)S(1)} %get-tuple-element.76), channel_id=1, replica_groups=mesh['y'=4,'z'=8,'c'=2,'x'=4] {'y','z'}, dimensions={0} | all-to-all | bytes 131072 | tf_op jit(solution)/shard_map/all_to_all | solution.py:29
  164.9 11.8 %all_to_all.87.got_ref = bf16[32,8,128]{2,1,0:T(8,128)(2,1)S(1)} all-to-all(bf16[32,8,128]{2,1,0:T(8,128)(2,1)S(1)} %get-tuple-element.78), channel_id=1, replica_groups=mesh['y'=4,'z'=8,'c'=2,'x'=4] {'y','z'}, dimensions={0} | all-to-all | bytes 131072 | tf_op jit(solution)/shard_map/all_to_all | solution.py:29
  177.8 11.8 %all_to_all.88.got_ref = bf16[32,8,128]{2,1,0:T(8,128)(2,1)S(1)} all-to-all(bf16[32,8,128]{2,1,0:T(8,128)(2,1)S(1)} %get-tuple-element.80), channel_id=1, replica_groups=mesh['y'=4,'z'=8,'c'=2,'x'=4] {'y','z'}, dimensions={0} | all-to-all | bytes 131072 | tf_op jit(solution)/shard_map/all_to_all | solution.py:29
  190.7 11.8 %all_to_all.89.got_ref = bf16[32,8,128]{2,1,0:T(8,128)(2,1)S(1)} all-to-all(bf16[32,8,128]{2,1,0:T(8,128)(2,1)S(1)} %get-tuple-element.82), channel_id=1, replica_groups=mesh['y'=4,'z'=8,'c'=2,'x'=4] {'y','z'}, dimensions={0} | all-to-all | bytes 131072 | tf_op jit(solution)/shard_map/all_to_all | solution.py:29
  203.7 11.8 %all_to_all.90.got_ref = bf16[32,8,128]{2,1,0:T(8,128)(2,1)S(1)} all-to-all(bf16[32,8,128]{2,1,0:T(8,128)(2,1)S(1)} %get-tuple-element.87), channel_id=1, replica_groups=mesh['y'=4,'z'=8,'c'=2,'x'=4] {'y','z'}, dimensions={0} | all-to-all | bytes 131072 | tf_op jit(solution)/shard_map/all_to_all | solution.py:29
  217.2 3.9 %all-to-all-start.14 = ((f32[32,8,512]{2,1,0:T(8,128)}), f32[32,8,512]{2,1,0:T(8,128)S(1)}, u32[]{:S(2)}, u32[]{:S(2)}) async-start(f32[32,8,512]{2,1,0:T(8,128)} %bitcast.13), calls=%async_computation.14 | async-start | bytes 1048576 | tf_op jit(solution)/shard_map/all_to_all | solution.py:29
  221.2 11.4 %all-to-all-done.14 = f32[32,8,512]{2,1,0:T(8,128)S(1)} async-done(((f32[32,8,512]{2,1,0:T(8,128)}), f32[32,8,512]{2,1,0:T(8,128)S(1)}, u32[]{:S(2)}, u32[]{:S(2)}) %all-to-all-start.14) | async-done | bytes 524320 | tf_op jit(solution)/shard_map/all_to_all | solution.py:29
  233.3 5.4 %all-to-all-start.15 = ((bf16[32,8,512]{2,1,0:T(8,128)(2,1)}), bf16[32,8,512]{2,1,0:T(8,128)(2,1)S(1)}, u32[]{:S(2)}, u32[]{:S(2)}) async-start(bf16[32,8,512]{2,1,0:T(8,128)(2,1)} %broadcast_in_dim.26), calls=%async_computation.15 | async-start | bytes 524288 | tf_op jit(solution)/shard_map/all_to_all | solution.py:29
  240.8 9.1 %all-to-all-done.15 = bf16[32,8,512]{2,1,0:T(8,128)(2,1)S(1)} async-done(((bf16[32,8,512]{2,1,0:T(8,128)(2,1)}), bf16[32,8,512]{2,1,0:T(8,128)(2,1)S(1)}, u32[]{:S(2)}, u32[]{:S(2)}) %all-to-all-start.15) | async-done | bytes 262176 | tf_op jit(solution)/shard_map/all_to_all | solution.py:29
  249.8 16.1 %collective-permute-start.8 = (bf16[256,512]{1,0:T(8,128)(2,1)S(1)}, bf16[256,512]{1,0:T(8,128)(2,1)S(1)}, u32[]{:S(2)}, u32[]{:S(2)}) collective-permute-start(bf16[256,512]{1,0:T(8,128)(2,1)S(1)} %bitcast.28), channel_id=1, source_target_pairs={{0,4},{4,0},{1,5},{5,1},{2,6},{6,2},{3,7},{7,3},{8,12},{12,8},{9,1... | collective-permute-start | bytes 786440 | tf_op jit(solution)/shard_map/ppermute | solution.py:38
  (67 shorter events, 43.5 us)
Async XLA Ops:
  3.2 4.6 %collective-permute-start = (f32[32,3,4,128]{3,2,1,0:T(4,128)}, f32[32,3,4,128]{3,2,1,0:T(4,128)S(1)}, u32[]{:S(2)}, u32[]{:S(2)}) collective-permute-start(f32[32,3,4,128]{3,2,1,0:T(4,128)} %get-tuple-element.50), channel_id=1, source_target_pairs={{0,4},{4,0},{1,5},{5,1},{2,6},{6,2},{3,7},{7,3},{8,12},{12,8},{9,1... | collective-permute-start | bytes 589832 | tf_op jit(solution)/shard_map/ppermute | solution.py:38
  9.5 9.6 %copy-start.3 = (bf16[2,512,128]{2,1,0:T(8,128)(2,1)S(1)}, bf16[2,512,128]{2,1,0:T(8,128)(2,1)}, u32[]{:S(2)}) copy-start(bf16[2,512,128]{2,1,0:T(8,128)(2,1)} %get-tuple-element.51.refs_0_) | copy-start | bytes 786436
  9.5 19.0 %all-to-all-start = ((f32[32,3,4,128]{3,2,1,0:T(4,128)}), f32[32,3,4,128]{3,2,1,0:T(4,128)S(1)}, u32[]{:S(2)}, u32[]{:S(2)}) async-start(f32[32,3,4,128]{3,2,1,0:T(4,128)} %add.18), calls=%async_computation | async-start | bytes 393216 | tf_op jit(solution)/shard_map/all_to_all | solution.py:29
  19.1 9.4 %copy-start.6 = (f32[128]{0:T(128)S(1)}, f32[128]{0:T(128)}, u32[]{:S(2)}) copy-start(f32[128]{0:T(128)} %param.12) | copy-start | bytes 1540
  19.1 19.0 %collective-permute-start.1 = (bf16[2,512,128]{2,1,0:T(8,128)(2,1)S(1)}, bf16[2,512,128]{2,1,0:T(8,128)(2,1)S(1)}, u32[]{:S(2)}, u32[]{:S(2)}) collective-permute-start(bf16[2,512,128]{2,1,0:T(8,128)(2,1)S(1)} %copy-done.3), channel_id=1, source_target_pairs={{0,1},{1,2},{2,3},{3,0},{4,5},{5,6},{6,7},{7,4},{8,9},{9,10},{10,1... | collective-permute-start | bytes 786440 | tf_op jit(solution)/shard_map/ppermute | solution.py:338
  20.4 17.7 %collective-permute-start.2 = (bf16[2,512,128]{2,1,0:T(8,128)(2,1)S(1)}, bf16[2,512,128]{2,1,0:T(8,128)(2,1)S(1)}, u32[]{:S(2)}, u32[]{:S(2)}) collective-permute-start(bf16[2,512,128]{2,1,0:T(8,128)(2,1)S(1)} %copy-done.3), channel_id=1, source_target_pairs={{0,2},{1,3},{2,0},{3,1},{4,6},{5,7},{6,4},{7,5},{8,10},{9,11},{10,... | collective-permute-start | bytes 786440 | tf_op jit(solution)/shard_map/ppermute | solution.py:338
  22.8 15.3 %collective-permute-start.3 = (bf16[2,512,128]{2,1,0:T(8,128)(2,1)S(1)}, bf16[2,512,128]{2,1,0:T(8,128)(2,1)S(1)}, u32[]{:S(2)}, u32[]{:S(2)}) collective-permute-start(bf16[2,512,128]{2,1,0:T(8,128)(2,1)S(1)} %copy-done.3), channel_id=1, source_target_pairs={{0,3},{1,0},{2,1},{3,2},{4,7},{5,4},{6,5},{7,6},{8,11},{9,8},{10,9... | collective-permute-start | bytes 786440 | tf_op jit(solution)/shard_map/ppermute | solution.py:338
  29.1 4.2 %copy-start.10 = (f32[512]{0:T(512)S(1)}, f32[512]{0:T(512)}, u32[]{:S(2)}) copy-start(f32[512]{0:T(512)} %param.13) | copy-start | bytes 6148
  29.1 9.7 %all-to-all-start.1 = ((f32[4,16,128]{2,1,0:T(8,128)}), f32[4,16,128]{2,1,0:T(8,128)S(1)}, u32[]{:S(2)}, u32[]{:S(2)}) async-start(f32[4,16,128]{2,1,0:T(8,128)} %chunk.1), calls=%async_computation.1 | async-start | bytes 65536 | tf_op jit(solution)/shard_map/all_to_all | solution.py:29
  34.0 4.1 %collective-permute-start.4 = (f32[2,512]{1,0:T(2,128)S(1)}, f32[2,512]{1,0:T(2,128)S(1)}, u32[]{:S(2)}, u32[]{:S(2)}) collective-permute-start(f32[2,512]{1,0:T(2,128)S(1)} %pad_maximum_fusion.mass_ref), channel_id=1, source_target_pairs={{0,4},{4,0},{1,5},{5,1},{2,6},{6,2},{3,7},{7,3},{8,12},{12,8},{9,1... | collective-permute-start | bytes 12296 | tf_op jit(solution)/shard_map/ppermute | solution.py:38
  38.1 0.7 copy-start.4
  39.7 5.1 %copy-start.2 = (bf16[512,512]{1,0:T(8,128)(2,1)S(1)}, bf16[512,512]{1,0:T(8,128)(2,1)}, u32[]{:S(2)}) copy-start(bf16[512,512]{1,0:T(8,128)(2,1)} %expr_ref.1) | copy-start | bytes 1572868
  39.7 24.6 %copy-start = (bf16[512,256]{1,0:T(8,128)(2,1)S(1)}, bf16[512,256]{1,0:T(8,128)(2,1)}, u32[]{:S(2)}) copy-start(bf16[512,256]{1,0:T(8,128)(2,1)} %x_ref.1) | copy-start | bytes 786436
  39.7 24.6 %copy-start.1 = (bf16[512,256]{1,0:T(8,128)(2,1)S(1)}, bf16[512,256]{1,0:T(8,128)(2,1)}, u32[]{:S(2)}) copy-start(bf16[512,256]{1,0:T(8,128)(2,1)} %y_ref.1) | copy-start | bytes 786436
  39.7 17.9 %all-to-all-start.2 = ((bf16[32,16,512]{2,1,0:T(8,128)(2,1)}), bf16[32,16,512]{2,1,0:T(8,128)(2,1)S(1)}, u32[]{:S(2)}, u32[]{:S(2)}) async-start(bf16[32,16,512]{2,1,0:T(8,128)(2,1)} %get-tuple-element.53), calls=%async_computation.2 | async-start | bytes 1048576 | tf_op jit(solution)/shard_map/all_to_all | solution.py:29
  44.8 3.9 %collective-permute-start.5 = (bf16[512,512]{1,0:T(8,128)(2,1)S(1)}, bf16[512,512]{1,0:T(8,128)(2,1)S(1)}, u32[]{:S(2)}, u32[]{:S(2)}) collective-permute-start(bf16[512,512]{1,0:T(8,128)(2,1)S(1)} %copy-done.2), channel_id=1, source_target_pairs={{0,4},{4,0},{1,5},{5,1},{2,6},{6,2},{3,7},{7,3},{8,12},{12,8},{9,1... | collective-permute-start | bytes 1572872 | tf_op jit(solution)/shard_map/ppermute | solution.py:38
  57.6 6.7 %collective-permute-start.6 = (bf16[512,512]{1,0:T(8,128)(2,1)S(1)}, bf16[512,512]{1,0:T(8,128)(2,1)S(1)}, u32[]{:S(2)}, u32[]{:S(2)}) collective-permute-start(bf16[512,512]{1,0:T(8,128)(2,1)S(1)} %bitcast.25), channel_id=1, source_target_pairs={{0,4},{4,0},{1,5},{5,1},{2,6},{6,2},{3,7},{7,3},{8,12},{12,8},{9,1... | collective-permute-start | bytes 1572872 | tf_op jit(solution)/shard_map/ppermute | solution.py:38
  64.2 1.0 copy-start.5
  82.8 3.0 %collective-permute-start.7 = (bf16[1024,512]{1,0:T(8,128)(2,1)S(1)}, bf16[1024,512]{1,0:T(8,128)(2,1)S(1)}, u32[]{:S(2)}, u32[]{:S(2)}) collective-permute-start(bf16[1024,512]{1,0:T(8,128)(2,1)S(1)} %get-tuple-element.66.own_ref), channel_id=1, source_target_pairs={{0,4},{4,0},{1,5},{5,1},{2,6},{6,2},{3,7},{7,3},{8,12},{12,8},{9,1... | collective-permute-start | bytes 3145736 | tf_op jit(solution)/shard_map/ppermute | solution.py:38
  217.2 15.3 %all-to-all-start.14 = ((f32[32,8,512]{2,1,0:T(8,128)}), f32[32,8,512]{2,1,0:T(8,128)S(1)}, u32[]{:S(2)}, u32[]{:S(2)}) async-start(f32[32,8,512]{2,1,0:T(8,128)} %bitcast.13), calls=%async_computation.14 | async-start | bytes 1048576 | tf_op jit(solution)/shard_map/all_to_all | solution.py:29
  233.3 16.5 %all-to-all-start.15 = ((bf16[32,8,512]{2,1,0:T(8,128)(2,1)}), bf16[32,8,512]{2,1,0:T(8,128)(2,1)S(1)}, u32[]{:S(2)}, u32[]{:S(2)}) async-start(bf16[32,8,512]{2,1,0:T(8,128)(2,1)} %broadcast_in_dim.26), calls=%async_computation.15 | async-start | bytes 524288 | tf_op jit(solution)/shard_map/all_to_all | solution.py:29
  238.7 1.0 copy-start.7
  238.7 1.0 copy-start.8
  249.8 17.2 %collective-permute-start.8 = (bf16[256,512]{1,0:T(8,128)(2,1)S(1)}, bf16[256,512]{1,0:T(8,128)(2,1)S(1)}, u32[]{:S(2)}, u32[]{:S(2)}) collective-permute-start(bf16[256,512]{1,0:T(8,128)(2,1)S(1)} %bitcast.28), channel_id=1, source_target_pairs={{0,4},{4,0},{1,5},{5,1},{2,6},{6,2},{3,7},{7,3},{8,12},{12,8},{9,1... | collective-permute-start | bytes 786440 | tf_op jit(solution)/shard_map/ppermute | solution.py:38
  (1 other events, 0.7 us)

commit v11 on v10

--- a/solution.py
+++ b/solution.py
@@ -121,23 +121,20 @@
     sent_ref[...] = jnp.broadcast_to(chunk[None], sent_ref.shape)
 
 
-def spread_kernel(got_ref, sent_ref, vec_ref):
-    every = jnp.concatenate([got_ref[i] for i in range(got_ref.shape[0])], axis=1)
-    dot = every[12:13]
-    high = dot.astype(BF16).astype(F32)
-    rest = dot - high
-    middle = rest.astype(BF16).astype(F32)
-    nothing = jnp.zeros((5, dot.shape[1]), F32)
-    chunk = jnp.concatenate([every[:8], high, middle, rest - middle, nothing], axis=0)
-    sent_ref[...] = jnp.broadcast_to(chunk.astype(BF16)[None], sent_ref.shape)
+def spread_kernel(got_ref, sent_ref, vec_ref, dot_ref):
+    ranks = got_ref.shape[0]
+    every = jnp.concatenate([got_ref[i] for i in range(ranks)], axis=1)
+    sent_ref[...] = jnp.broadcast_to(every[:8].astype(BF16)[None], sent_ref.shape)
     vec_ref[...] = every[8:16]
+    dot_ref[...] = jnp.concatenate([got_ref[i, 12:13] for i in range(ranks)], axis=0)
 
 
 def grad_kernel(
-    core_ref, here_ref, x_ref, y_ref, mine_ref, other_ref, vec_ref, mass_ref, mass2_ref, *refs
+    core_ref, here_ref, x_ref, y_ref, mine_ref, other_ref, vec_ref, dot_ref, mass_ref, mass2_ref,
+    *refs
 ):
-    factors = refs[:-6]
-    grad_q_ref, grad_r_ref, grad_g_ref, peak_ref, all_ref, masses_ref = refs[-6:]
+    factors = refs[:-5]
+    grad_q_ref, grad_r_ref, peak_ref, all_ref, masses_ref = refs[-5:]
     masses_ref[...] = jnp.concatenate([mass_ref[...], mass2_ref[...]], axis=0)
     ranks = len(factors)
     rows, width = factors[0].shape[1:]
@@ -156,17 +153,9 @@
     scale = SCALE / g
     place = lax.broadcasted_iota(jnp.int32, (half, chunks), 1)
     wanted = lax.broadcasted_iota(jnp.int32, (half, chunks), 0)
-    wanted = (wanted // 4) * 16 + wanted % 4
-    place8 = lax.broadcasted_iota(jnp.int32, (8, chunks), 1) % 16
-    is_dot = jnp.where((place8 >= 8) & (place8 < 11), 1.0, 0.0).astype(BF16)
-    spread = jnp.dot(is_dot, mine_ref[...], preferred_element_type=F32) + jnp.dot(
-        is_dot, other_ref[...], preferred_element_type=F32
-    )
+    wanted = (wanted // 4) * 8 + wanted % 4
     xq, cq, yr, cr = (vec_ref[i : i + 1] for i in range(4))
-    curvature = SCALE * (xq * cr + cq * yr - 2.0 * spread[0:1])
-    grad_g = -curvature / jnp.square(g)
-    grad_g_ref[...] = grad_g
-    top = jnp.abs(grad_g)
+    top = None
     for emb_ref, offset, count, total, out_ref in (
         (x_ref, 4, cr, yr, grad_q_ref),
         (y_ref, 0, cq, xq, grad_r_ref),
@@ -181,16 +170,21 @@
         norms = jnp.sum(jnp.square(emb_ref[...].astype(F32)), axis=1, keepdims=True)
         grad = scale * (norms * count + total - 2.0 * product)
         out_ref[...] = grad
-        top = jnp.maximum(top, jnp.max(jnp.abs(grad), axis=0, keepdims=True))
-    blocks = in_rows(top, top.shape[1] // peak_ref.shape[2])
+        here = jnp.max(jnp.abs(grad), axis=0, keepdims=True)
+        top = here if top is None else jnp.maximum(top, here)
+    blocks = in_rows(top, dot_ref.shape[0])
     peak = blocks[0]
     for block in blocks[1:]:
         peak = jnp.maximum(peak, block)
-    peak_ref[...] = jnp.broadcast_to(peak[None], peak_ref.shape)
+    count = peak_ref.shape[0]
+    peak_ref[:, 0] = jnp.broadcast_to(peak[None], (count,) + peak.shape)
+    for i in range(dot_ref.shape[0]):
+        row = dot_ref[i : i + 1]
+        peak_ref[:, 1 + i] = jnp.broadcast_to(row[None], (count,) + row.shape)
 
 
 def kern_kernel(
-    here_ref, peak_ref, grad_q_ref, grad_r_ref, grad_g_ref, vec_ref, all_ref,
+    here_ref, peak_ref, grad_q_ref, grad_r_ref, vec_ref, all_ref,
     kern_ref, log_ref, eta_ref, own_q_ref, own_r_ref,
 ):
     rows = grad_q_ref.shape[0]
@@ -198,10 +192,18 @@
     mine = pl.ds(pl.multiple_of(here_ref[0] * width, width), width)
     own_q_ref[...] = grad_q_ref[:, mine]
     own_r_ref[...] = grad_r_ref[:, mine]
-    peak = jnp.max(jnp.max(peak_ref[...], axis=0), axis=1, keepdims=True)
+    xq, cq, yr, cr = (vec_ref[i : i + 1] for i in range(4))
+    g = vec_ref[5:6]
+    dots = [jnp.sum(peak_ref[:, 1 + i], axis=0) for i in range(log_ref.shape[0])]
+    dot = jnp.concatenate(dots, axis=1)
+    grad_g = -(SCALE * (xq * cr + cq * yr - 2.0 * dot)) / jnp.square(g)
+    peak = jnp.maximum(
+        jnp.max(jnp.max(peak_ref[:, 0], axis=0), axis=1, keepdims=True),
+        jnp.max(jnp.abs(grad_g), axis=1, keepdims=True),
+    )
     eta = GAMMA / (peak + 1e-06)
     eta_ref[...] = jnp.broadcast_to(eta, eta_ref.shape)
-    kern_g = vec_ref[5:6] * jnp.exp(-eta * grad_g_ref[...])
+    kern_g = g * jnp.exp(-eta * grad_g)
     log_ref[...] = jnp.concatenate(in_rows(jnp.log(kern_g), log_ref.shape[0]), axis=0)
     for side, grad_ref in enumerate((grad_q_ref, grad_r_ref)):
         part = pl.ds(side * rows, rows)
@@ -347,33 +349,35 @@
     got, first, second, third, their_masses = lax.optimization_barrier(
         (exchange(sent, "x"), from_shift(1), from_shift(2), from_shift(3), swap(masses))
     )
-    sent, vec = on_chip(
-        spread_kernel, (((others, 16, columns), BF16), ((8, columns), F32)), "spread"
+    sent, vec, dot = on_chip(
+        spread_kernel,
+        (((others, 8, columns), BF16), ((8, columns), F32), ((ranks, width), F32)),
+        "spread",
     )(got)
     crosses, other_expr = lax.optimization_barrier((exchange(sent, CHIPS), swap(expr)))
-    crosses = crosses.reshape(others * 16, columns)
+    crosses = crosses.reshape(others * 8, columns)
     own_grad = ((rows, width), F32)
-    grad_q, grad_r, grad_g, peak, factors, masses = on_chip(
+    grad_q, grad_r, peak, factors, masses = on_chip(
         grad_kernel,
         (
-            tall, tall, ((1, columns), F32), ((cell_devices, 1, width), F32),
+            tall, tall, ((cell_devices, 1 + ranks, 1, width), F32),
             ((2 * rows, columns), BF16), ((4, rows), F32),
         ),
         "grad",
         scalars=2,
-        inputs=7 + ranks,
+        inputs=8 + ranks,
     )(
         core_index, here.astype(jnp.int32)[None], x_emb, y_emb, crosses, swap(crosses), vec,
-        masses, their_masses, rounded, first, second, third,
+        dot, masses, their_masses, rounded, first, second, third,
     )
     kerns, log_g, eta, own_grad_q, own_grad_r = on_chip(
         kern_kernel,
         (((2 * rows, columns), BF16), ((ranks, width), F32), ((1, width), F32), own_grad, own_grad),
         "kern",
         scalars=1,
-        inputs=6,
+        inputs=5,
     )(
-        here.astype(jnp.int32)[None], exchange(peak, CELLS), grad_q, grad_r, grad_g, vec, factors
+        here.astype(jnp.int32)[None], exchange(peak, CELLS), grad_q, grad_r, vec, factors
     )
     theirs = swap(kerns)
     sent_shape = ((others, 2 * ranks, width), BF16)

time: 269 us -> 265 us (0.985)
  transfers between devices with their start and end apart: 14 -> 14, of which waited for: 10 -> 9; matrix products, arithmetic and copies ran while one was open for 1% -> 1% of each run, Pallas kernels for 0% -> 1%
where the time goes in v11:
time: 265 us; the launch traced here: 264 us
  blocking collectives  135 us (51%)
  starting transfers between devices  62.4 us (24%)
  waiting for transfers between devices  39.7 us (15%)
  Pallas kernels  18.5 us (7%)
  other arithmetic  3.46 us (1%)
    all_to_all x11, blocking collectives, exchange(): return lax.all_to_all(chunks, axes, 0, 0, tiled=False)  135 us
    all_to_all x5, waiting for transfers between devices, exchange(): return lax.all_to_all(chunks, axes, 0, 0, tiled=False)  33.7 us
    all_to_all x5, starting transfers between devices, exchange(): return lax.all_to_all(chunks, axes, 0, 0, tiled=False)  28.7 us
    ppermute x6, starting transfers between devices, swap(): return lax.ppermute(value, 'c', [(0, 1), (1, 0)])  28.7 us
    pallas_call x9, Pallas kernels, shards(): on_chip(next_pass, (sent_shape, v_shape) + last, 'next_pass')  9.6 us
    ppermute x6, waiting for transfers between devices, swap(): return lax.ppermute(value, 'c', [(0, 1), (1, 0)])  5.91 us
  transfers between devices with their start and end apart: 14, of which 9 were waited for; matrix products, arithmetic and copies ran while one was open for 1% of the time, Pallas kernels for 1%

profile of v11, /device:TPU:1, one launch (start us, length us, event | category | flops | bytes accessed | tf_op | source)
XLA Modules:
  0.0 264.0 jit_solution(18127045078140297736)
XLA Ops:
  3.2 3.3 %collective-permute-start = (f32[32,3,4,128]{3,2,1,0:T(4,128)}, f32[32,3,4,128]{3,2,1,0:T(4,128)S(1)}, u32[]{:S(2)}, u32[]{:S(2)}) collective-permute-start(f32[32,3,4,128]{3,2,1,0:T(4,128)} %get-tuple-element.50), channel_id=1, source_target_pairs={{0,4},{4,0},{1,5},{5,1},{2,6},{6,2},{3,7},{7,3},{8,12},{12,8},{9,1... | collective-permute-start | bytes 589832 | tf_op jit(solution)/shard_map/ppermute | solution.py:38
  9.5 9.6 %all-to-all-start = ((f32[32,3,4,128]{3,2,1,0:T(4,128)}), f32[32,3,4,128]{3,2,1,0:T(4,128)S(1)}, u32[]{:S(2)}, u32[]{:S(2)}) async-start(f32[32,3,4,128]{3,2,1,0:T(4,128)} %add.18), calls=%async_computation | async-start | bytes 393216 | tf_op jit(solution)/shard_map/all_to_all | solution.py:29
  25.5 3.0 %all-to-all-done.got_ref = f32[32,3,4,128]{3,2,1,0:T(4,128)S(1)} async-done(((f32[32,3,4,128]{3,2,1,0:T(4,128)}), f32[32,3,4,128]{3,2,1,0:T(4,128)S(1)}, u32[]{:S(2)}, u32[]{:S(2)}) %all-to-all-start) | async-done | bytes 196640 | tf_op jit(solution)/shard_map/all_to_all | solution.py:29
  29.2 4.1 %all-to-all-start.1 = ((f32[4,16,128]{2,1,0:T(8,128)}), f32[4,16,128]{2,1,0:T(8,128)S(1)}, u32[]{:S(2)}, u32[]{:S(2)}) async-start(f32[4,16,128]{2,1,0:T(8,128)} %chunk.1), calls=%async_computation.1 | async-start | bytes 65536 | tf_op jit(solution)/shard_map/all_to_all | solution.py:29
  34.0 3.3 %collective-permute-start.4 = (f32[2,512]{1,0:T(2,128)S(1)}, f32[2,512]{1,0:T(2,128)S(1)}, u32[]{:S(2)}, u32[]{:S(2)}) collective-permute-start(f32[2,512]{1,0:T(2,128)S(1)} %pad_maximum_fusion.mass_ref), channel_id=1, source_target_pairs={{0,4},{4,0},{1,5},{5,1},{2,6},{6,2},{3,7},{7,3},{8,12},{12,8},{9,1... | collective-permute-start | bytes 12296 | tf_op jit(solution)/shard_map/ppermute | solution.py:38
  38.9 5.9 %all-to-all-start.2 = ((bf16[32,8,512]{2,1,0:T(8,128)(2,1)}), bf16[32,8,512]{2,1,0:T(8,128)(2,1)S(1)}, u32[]{:S(2)}, u32[]{:S(2)}) async-start(bf16[32,8,512]{2,1,0:T(8,128)(2,1)} %get-tuple-element.53), calls=%async_computation.2 | async-start | bytes 524288 | tf_op jit(solution)/shard_map/all_to_all | solution.py:29
  44.8 9.7 %all-to-all-done.2 = bf16[32,8,512]{2,1,0:T(8,128)(2,1)S(1)} async-done(((bf16[32,8,512]{2,1,0:T(8,128)(2,1)}), bf16[32,8,512]{2,1,0:T(8,128)(2,1)S(1)}, u32[]{:S(2)}, u32[]{:S(2)}) %all-to-all-start.2) | async-done | bytes 262176 | tf_op jit(solution)/shard_map/all_to_all | solution.py:29
  54.4 3.7 %collective-permute-start.6 = (bf16[256,512]{1,0:T(8,128)(2,1)S(1)}, bf16[256,512]{1,0:T(8,128)(2,1)S(1)}, u32[]{:S(2)}, u32[]{:S(2)}) collective-permute-start(bf16[256,512]{1,0:T(8,128)(2,1)S(1)} %bitcast.25), channel_id=1, source_target_pairs={{0,4},{4,0},{1,5},{5,1},{2,6},{6,2},{3,7},{7,3},{8,12},{12,8},{9,1... | collective-permute-start | bytes 786440 | tf_op jit(solution)/shard_map/ppermute | solution.py:38
  60.8 15.3 %all_to_all.80.peak_ref = f32[64,5,1,128]{3,2,1,0:T(1,128)S(1)} all-to-all(f32[64,5,1,128]{3,2,1,0:T(1,128)S(1)} %get-tuple-element.62), channel_id=1, replica_groups=mesh['y'=4,'z'=8,'c'=2,'x'=4] {'y','z','c'}, dimensions={0} | all-to-all | bytes 327680 | tf_op jit(solution)/shard_map/all_to_all | solution.py:29
  80.7 13.3 %all_to_all.81.got_ref = bf16[32,8,128]{2,1,0:T(8,128)(2,1)S(1)} all-to-all(bf16[32,8,128]{2,1,0:T(8,128)(2,1)S(1)} %first_pass.1), channel_id=1, replica_groups=mesh['y'=4,'z'=8,'c'=2,'x'=4] {'y','z'}, dimensions={0} | all-to-all | bytes 131072 | tf_op jit(solution)/shard_map/all_to_all | solution.py:29
  95.1 11.9 %all_to_all.82.got_ref = bf16[32,8,128]{2,1,0:T(8,128)(2,1)S(1)} all-to-all(bf16[32,8,128]{2,1,0:T(8,128)(2,1)S(1)} %get-tuple-element.68), channel_id=1, replica_groups=mesh['y'=4,'z'=8,'c'=2,'x'=4] {'y','z'}, dimensions={0} | all-to-all | bytes 131072 | tf_op jit(solution)/shard_map/all_to_all | solution.py:29
  108.1 12.0 %all_to_all.83.got_ref = bf16[32,8,128]{2,1,0:T(8,128)(2,1)S(1)} all-to-all(bf16[32,8,128]{2,1,0:T(8,128)(2,1)S(1)} %get-tuple-element.70), channel_id=1, replica_groups=mesh['y'=4,'z'=8,'c'=2,'x'=4] {'y','z'}, dimensions={0} | all-to-all | bytes 131072 | tf_op jit(solution)/shard_map/all_to_all | solution.py:29
  121.1 11.9 %all_to_all.84.got_ref = bf16[32,8,128]{2,1,0:T(8,128)(2,1)S(1)} all-to-all(bf16[32,8,128]{2,1,0:T(8,128)(2,1)S(1)} %get-tuple-element.72), channel_id=1, replica_groups=mesh['y'=4,'z'=8,'c'=2,'x'=4] {'y','z'}, dimensions={0} | all-to-all | bytes 131072 | tf_op jit(solution)/shard_map/all_to_all | solution.py:29
  134.2 11.8 %all_to_all.85.got_ref = bf16[32,8,128]{2,1,0:T(8,128)(2,1)S(1)} all-to-all(bf16[32,8,128]{2,1,0:T(8,128)(2,1)S(1)} %get-tuple-element.74), channel_id=1, replica_groups=mesh['y'=4,'z'=8,'c'=2,'x'=4] {'y','z'}, dimensions={0} | all-to-all | bytes 131072 | tf_op jit(solution)/shard_map/all_to_all | solution.py:29
  147.1 11.8 %all_to_all.86.got_ref = bf16[32,8,128]{2,1,0:T(8,128)(2,1)S(1)} all-to-all(bf16[32,8,128]{2,1,0:T(8,128)(2,1)S(1)} %get-tuple-element.76), channel_id=1, replica_groups=mesh['y'=4,'z'=8,'c'=2,'x'=4] {'y','z'}, dimensions={0} | all-to-all | bytes 131072 | tf_op jit(solution)/shard_map/all_to_all | solution.py:29
  160.0 11.8 %all_to_all.87.got_ref = bf16[32,8,128]{2,1,0:T(8,128)(2,1)S(1)} all-to-all(bf16[32,8,128]{2,1,0:T(8,128)(2,1)S(1)} %get-tuple-element.78), channel_id=1, replica_groups=mesh['y'=4,'z'=8,'c'=2,'x'=4] {'y','z'}, dimensions={0} | all-to-all | bytes 131072 | tf_op jit(solution)/shard_map/all_to_all | solution.py:29
  172.9 11.8 %all_to_all.88.got_ref = bf16[32,8,128]{2,1,0:T(8,128)(2,1)S(1)} all-to-all(bf16[32,8,128]{2,1,0:T(8,128)(2,1)S(1)} %get-tuple-element.80), channel_id=1, replica_groups=mesh['y'=4,'z'=8,'c'=2,'x'=4] {'y','z'}, dimensions={0} | all-to-all | bytes 131072 | tf_op jit(solution)/shard_map/all_to_all | solution.py:29
  185.8 11.9 %all_to_all.89.got_ref = bf16[32,8,128]{2,1,0:T(8,128)(2,1)S(1)} all-to-all(bf16[32,8,128]{2,1,0:T(8,128)(2,1)S(1)} %get-tuple-element.82), channel_id=1, replica_groups=mesh['y'=4,'z'=8,'c'=2,'x'=4] {'y','z'}, dimensions={0} | all-to-all | bytes 131072 | tf_op jit(solution)/shard_map/all_to_all | solution.py:29
  198.7 11.8 %all_to_all.90.got_ref = bf16[32,8,128]{2,1,0:T(8,128)(2,1)S(1)} all-to-all(bf16[32,8,128]{2,1,0:T(8,128)(2,1)S(1)} %get-tuple-element.87), channel_id=1, replica_groups=mesh['y'=4,'z'=8,'c'=2,'x'=4] {'y','z'}, dimensions={0} | all-to-all | bytes 131072 | tf_op jit(solution)/shard_map/all_to_all | solution.py:29
  212.3 3.9 %all-to-all-start.14 = ((f32[32,8,512]{2,1,0:T(8,128)}), f32[32,8,512]{2,1,0:T(8,128)S(1)}, u32[]{:S(2)}, u32[]{:S(2)}) async-start(f32[32,8,512]{2,1,0:T(8,128)} %bitcast.13), calls=%async_computation.14 | async-start | bytes 1048576 | tf_op jit(solution)/shard_map/all_to_all | solution.py:29
  216.2 11.6 %all-to-all-done.14 = f32[32,8,512]{2,1,0:T(8,128)S(1)} async-done(((f32[32,8,512]{2,1,0:T(8,128)}), f32[32,8,512]{2,1,0:T(8,128)S(1)}, u32[]{:S(2)}, u32[]{:S(2)}) %all-to-all-start.14) | async-done | bytes 524320 | tf_op jit(solution)/shard_map/all_to_all | solution.py:29
  228.6 5.2 %all-to-all-start.15 = ((bf16[32,8,512]{2,1,0:T(8,128)(2,1)}), bf16[32,8,512]{2,1,0:T(8,128)(2,1)S(1)}, u32[]{:S(2)}, u32[]{:S(2)}) async-start(bf16[32,8,512]{2,1,0:T(8,128)(2,1)} %broadcast_in_dim.26), calls=%async_computation.15 | async-start | bytes 524288 | tf_op jit(solution)/shard_map/all_to_all | solution.py:29
  235.8 9.5 %all-to-all-done.15 = bf16[32,8,512]{2,1,0:T(8,128)(2,1)S(1)} async-done(((bf16[32,8,512]{2,1,0:T(8,128)(2,1)}), bf16[32,8,512]{2,1,0:T(8,128)(2,1)S(1)}, u32[]{:S(2)}, u32[]{:S(2)}) %all-to-all-start.15) | async-done | bytes 262176 | tf_op jit(solution)/shard_map/all_to_all | solution.py:29
  245.3 16.4 %collective-permute-start.8 = (bf16[256,512]{1,0:T(8,128)(2,1)S(1)}, bf16[256,512]{1,0:T(8,128)(2,1)S(1)}, u32[]{:S(2)}, u32[]{:S(2)}) collective-permute-start(bf16[256,512]{1,0:T(8,128)(2,1)S(1)} %bitcast.28), channel_id=1, source_target_pairs={{0,4},{4,0},{1,5},{5,1},{2,6},{6,2},{3,7},{7,3},{8,12},{12,8},{9,1... | collective-permute-start | bytes 786440 | tf_op jit(solution)/shard_map/ppermute | solution.py:38
  (63 shorter events, 38.4 us)
Async XLA Ops:
  3.2 20.8 %copy-start.2 = (bf16[512,512]{1,0:T(8,128)(2,1)S(1)}, bf16[512,512]{1,0:T(8,128)(2,1)}, u32[]{:S(2)}) copy-start(bf16[512,512]{1,0:T(8,128)(2,1)} %expr_ref.1) | copy-start | bytes 1572868
  3.2 4.6 %collective-permute-start = (f32[32,3,4,128]{3,2,1,0:T(4,128)}, f32[32,3,4,128]{3,2,1,0:T(4,128)S(1)}, u32[]{:S(2)}, u32[]{:S(2)}) collective-permute-start(f32[32,3,4,128]{3,2,1,0:T(4,128)} %get-tuple-element.50), channel_id=1, source_target_pairs={{0,4},{4,0},{1,5},{5,1},{2,6},{6,2},{3,7},{7,3},{8,12},{12,8},{9,1... | collective-permute-start | bytes 589832 | tf_op jit(solution)/shard_map/ppermute | solution.py:38
  9.5 9.6 %copy-start.3 = (bf16[2,512,128]{2,1,0:T(8,128)(2,1)S(1)}, bf16[2,512,128]{2,1,0:T(8,128)(2,1)}, u32[]{:S(2)}) copy-start(bf16[2,512,128]{2,1,0:T(8,128)(2,1)} %get-tuple-element.51.refs_0_) | copy-start | bytes 786436
  9.5 19.0 %all-to-all-start = ((f32[32,3,4,128]{3,2,1,0:T(4,128)}), f32[32,3,4,128]{3,2,1,0:T(4,128)S(1)}, u32[]{:S(2)}, u32[]{:S(2)}) async-start(f32[32,3,4,128]{3,2,1,0:T(4,128)} %add.18), calls=%async_computation | async-start | bytes 393216 | tf_op jit(solution)/shard_map/all_to_all | solution.py:29
  19.1 9.4 %copy-start.4 = (f32[128]{0:T(128)S(1)}, f32[128]{0:T(128)}, u32[]{:S(2)}) copy-start(f32[128]{0:T(128)} %param.12) | copy-start | bytes 1540
  19.1 19.0 %collective-permute-start.1 = (bf16[2,512,128]{2,1,0:T(8,128)(2,1)S(1)}, bf16[2,512,128]{2,1,0:T(8,128)(2,1)S(1)}, u32[]{:S(2)}, u32[]{:S(2)}) collective-permute-start(bf16[2,512,128]{2,1,0:T(8,128)(2,1)S(1)} %copy-done.3), channel_id=1, source_target_pairs={{0,1},{1,2},{2,3},{3,0},{4,5},{5,6},{6,7},{7,4},{8,9},{9,10},{10,1... | collective-permute-start | bytes 786440 | tf_op jit(solution)/shard_map/ppermute | solution.py:340
  20.4 17.7 %collective-permute-start.2 = (bf16[2,512,128]{2,1,0:T(8,128)(2,1)S(1)}, bf16[2,512,128]{2,1,0:T(8,128)(2,1)S(1)}, u32[]{:S(2)}, u32[]{:S(2)}) collective-permute-start(bf16[2,512,128]{2,1,0:T(8,128)(2,1)S(1)} %copy-done.3), channel_id=1, source_target_pairs={{0,2},{1,3},{2,0},{3,1},{4,6},{5,7},{6,4},{7,5},{8,10},{9,11},{10,... | collective-permute-start | bytes 786440 | tf_op jit(solution)/shard_map/ppermute | solution.py:340
  22.9 15.3 %collective-permute-start.3 = (bf16[2,512,128]{2,1,0:T(8,128)(2,1)S(1)}, bf16[2,512,128]{2,1,0:T(8,128)(2,1)S(1)}, u32[]{:S(2)}, u32[]{:S(2)}) collective-permute-start(bf16[2,512,128]{2,1,0:T(8,128)(2,1)S(1)} %copy-done.3), channel_id=1, source_target_pairs={{0,3},{1,0},{2,1},{3,2},{4,7},{5,4},{6,5},{7,6},{8,11},{9,8},{10,9... | collective-permute-start | bytes 786440 | tf_op jit(solution)/shard_map/ppermute | solution.py:340
  24.0 20.7 %collective-permute-start.5 = (bf16[512,512]{1,0:T(8,128)(2,1)S(1)}, bf16[512,512]{1,0:T(8,128)(2,1)S(1)}, u32[]{:S(2)}, u32[]{:S(2)}) collective-permute-start(bf16[512,512]{1,0:T(8,128)(2,1)S(1)} %copy-done.2), channel_id=1, source_target_pairs={{0,4},{4,0},{1,5},{5,1},{2,6},{6,2},{3,7},{7,3},{8,12},{12,8},{9,1... | collective-permute-start | bytes 1572872 | tf_op jit(solution)/shard_map/ppermute | solution.py:38
  29.2 4.2 %copy-start.8 = (f32[512]{0:T(512)S(1)}, f32[512]{0:T(512)}, u32[]{:S(2)}) copy-start(f32[512]{0:T(512)} %param.13) | copy-start | bytes 6148
  29.2 9.0 %all-to-all-start.1 = ((f32[4,16,128]{2,1,0:T(8,128)}), f32[4,16,128]{2,1,0:T(8,128)S(1)}, u32[]{:S(2)}, u32[]{:S(2)}) async-start(f32[4,16,128]{2,1,0:T(8,128)} %chunk.1), calls=%async_computation.1 | async-start | bytes 65536 | tf_op jit(solution)/shard_map/all_to_all | solution.py:29
  33.3 0.7 copy-start.7
  34.0 4.1 %collective-permute-start.4 = (f32[2,512]{1,0:T(2,128)S(1)}, f32[2,512]{1,0:T(2,128)S(1)}, u32[]{:S(2)}, u32[]{:S(2)}) collective-permute-start(f32[2,512]{1,0:T(2,128)S(1)} %pad_maximum_fusion.mass_ref), channel_id=1, source_target_pairs={{0,4},{4,0},{1,5},{5,1},{2,6},{6,2},{3,7},{7,3},{8,12},{12,8},{9,1... | collective-permute-start | bytes 12296 | tf_op jit(solution)/shard_map/ppermute | solution.py:38
  38.8 20.5 %copy-start = (bf16[512,256]{1,0:T(8,128)(2,1)S(1)}, bf16[512,256]{1,0:T(8,128)(2,1)}, u32[]{:S(2)}) copy-start(bf16[512,256]{1,0:T(8,128)(2,1)} %x_ref.1) | copy-start | bytes 786436
  38.9 20.5 %copy-start.1 = (bf16[512,256]{1,0:T(8,128)(2,1)S(1)}, bf16[512,256]{1,0:T(8,128)(2,1)}, u32[]{:S(2)}) copy-start(bf16[512,256]{1,0:T(8,128)(2,1)} %y_ref.1) | copy-start | bytes 786436
  38.9 15.6 %all-to-all-start.2 = ((bf16[32,8,512]{2,1,0:T(8,128)(2,1)}), bf16[32,8,512]{2,1,0:T(8,128)(2,1)S(1)}, u32[]{:S(2)}, u32[]{:S(2)}) async-start(bf16[32,8,512]{2,1,0:T(8,128)(2,1)} %get-tuple-element.53), calls=%async_computation.2 | async-start | bytes 524288 | tf_op jit(solution)/shard_map/all_to_all | solution.py:29
  54.4 4.9 %collective-permute-start.6 = (bf16[256,512]{1,0:T(8,128)(2,1)S(1)}, bf16[256,512]{1,0:T(8,128)(2,1)S(1)}, u32[]{:S(2)}, u32[]{:S(2)}) collective-permute-start(bf16[256,512]{1,0:T(8,128)(2,1)S(1)} %bitcast.25), channel_id=1, source_target_pairs={{0,4},{4,0},{1,5},{5,1},{2,6},{6,2},{3,7},{7,3},{8,12},{12,8},{9,1... | collective-permute-start | bytes 786440 | tf_op jit(solution)/shard_map/ppermute | solution.py:38
  76.9 2.8 %collective-permute-start.7 = (bf16[1024,512]{1,0:T(8,128)(2,1)S(1)}, bf16[1024,512]{1,0:T(8,128)(2,1)S(1)}, u32[]{:S(2)}, u32[]{:S(2)}) collective-permute-start(bf16[1024,512]{1,0:T(8,128)(2,1)S(1)} %get-tuple-element.66.own_ref), channel_id=1, source_target_pairs={{0,4},{4,0},{1,5},{5,1},{2,6},{6,2},{3,7},{7,3},{8,12},{12,8},{9,1... | collective-permute-start | bytes 3145736 | tf_op jit(solution)/shard_map/ppermute | solution.py:38
  212.3 15.5 %all-to-all-start.14 = ((f32[32,8,512]{2,1,0:T(8,128)}), f32[32,8,512]{2,1,0:T(8,128)S(1)}, u32[]{:S(2)}, u32[]{:S(2)}) async-start(f32[32,8,512]{2,1,0:T(8,128)} %bitcast.13), calls=%async_computation.14 | async-start | bytes 1048576 | tf_op jit(solution)/shard_map/all_to_all | solution.py:29
  228.6 16.8 %all-to-all-start.15 = ((bf16[32,8,512]{2,1,0:T(8,128)(2,1)}), bf16[32,8,512]{2,1,0:T(8,128)(2,1)S(1)}, u32[]{:S(2)}, u32[]{:S(2)}) async-start(bf16[32,8,512]{2,1,0:T(8,128)(2,1)} %broadcast_in_dim.26), calls=%async_computation.15 | async-start | bytes 524288 | tf_op jit(solution)/shard_map/all_to_all | solution.py:29
  233.8 1.0 copy-start.5
  233.8 1.0 copy-start.6
  245.3 17.6 %collective-permute-start.8 = (bf16[256,512]{1,0:T(8,128)(2,1)S(1)}, bf16[256,512]{1,0:T(8,128)(2,1)S(1)}, u32[]{:S(2)}, u32[]{:S(2)}) collective-permute-start(bf16[256,512]{1,0:T(8,128)(2,1)S(1)} %bitcast.28), channel_id=1, source_target_pairs={{0,4},{4,0},{1,5},{5,1},{2,6},{6,2},{3,7},{7,3},{8,12},{12,8},{9,1... | collective-permute-start | bytes 786440 | tf_op jit(solution)/shard_map/ppermute | solution.py:38

commit v12 on v11

--- a/solution.py
+++ b/solution.py
@@ -326,7 +326,7 @@
         "start",
         scalars=1,
         off_chip=4,
-        limit=60 << 20,
+        limit=107 << 19,
         scratch=[
             pltpu.VMEM(x_emb.shape, BF16),
             pltpu.VMEM(y_emb.shape, BF16),

time: 265 us -> 264 us (level)
  no operation moved by 1% of the time
where the time goes in v12:
time: 264 us; the launch traced here: 262 us
  blocking collectives  135 us (51%)
  starting transfers between devices  62.4 us (24%)
  waiting for transfers between devices  39.4 us (15%)
  Pallas kernels  18.2 us (7%)
    all_to_all x11, blocking collectives, exchange(): return lax.all_to_all(chunks, axes, 0, 0, tiled=False)  135 us
    all_to_all x5, waiting for transfers between devices, exchange(): return lax.all_to_all(chunks, axes, 0, 0, tiled=False)  33.7 us
    all_to_all x5, starting transfers between devices, exchange(): return lax.all_to_all(chunks, axes, 0, 0, tiled=False)  28.7 us
    ppermute x6, starting transfers between devices, swap(): return lax.ppermute(value, 'c', [(0, 1), (1, 0)])  28.7 us
    pallas_call x9, Pallas kernels, shards(): on_chip(next_pass, (sent_shape, v_shape) + last, 'next_pass')  9.6 us
    ppermute x6, waiting for transfers between devices, swap(): return lax.ppermute(value, 'c', [(0, 1), (1, 0)])  5.69 us
  transfers between devices with their start and end apart: 14, of which 9 were waited for; matrix products, arithmetic and copies ran while one was open for 1% of the time, Pallas kernels for 1%

profile of v12, /device:TPU:1, one launch (start us, length us, event | category | flops | bytes accessed | tf_op | source)
XLA Modules:
  0.0 262.5 jit_solution(16459765735214407091)
XLA Ops:
  2.9 3.3 %collective-permute-start = (f32[32,3,4,128]{3,2,1,0:T(4,128)S(1)}, f32[32,3,4,128]{3,2,1,0:T(4,128)S(1)}, u32[]{:S(2)}, u32[]{:S(2)}) collective-permute-start(f32[32,3,4,128]{3,2,1,0:T(4,128)S(1)} %get-tuple-element.50), channel_id=1, source_target_pairs={{0,4},{4,0},{1,5},{5,1},{2,6},{6,2},{3,7},{7,3},{8,12},{12,8},{9,1... | collective-permute-start | bytes 589832 | tf_op jit(solution)/shard_map/ppermute | solution.py:38
  8.0 9.6 %all-to-all-start = ((f32[32,3,4,128]{3,2,1,0:T(4,128)}), f32[32,3,4,128]{3,2,1,0:T(4,128)S(1)}, u32[]{:S(2)}, u32[]{:S(2)}) async-start(f32[32,3,4,128]{3,2,1,0:T(4,128)} %add.18), calls=%async_computation | async-start | bytes 393216 | tf_op jit(solution)/shard_map/all_to_all | solution.py:29
  24.0 3.0 %all-to-all-done.got_ref = f32[32,3,4,128]{3,2,1,0:T(4,128)S(1)} async-done(((f32[32,3,4,128]{3,2,1,0:T(4,128)}), f32[32,3,4,128]{3,2,1,0:T(4,128)S(1)}, u32[]{:S(2)}, u32[]{:S(2)}) %all-to-all-start) | async-done | bytes 196640 | tf_op jit(solution)/shard_map/all_to_all | solution.py:29
  27.7 4.1 %all-to-all-start.1 = ((f32[4,16,128]{2,1,0:T(8,128)}), f32[4,16,128]{2,1,0:T(8,128)S(1)}, u32[]{:S(2)}, u32[]{:S(2)}) async-start(f32[4,16,128]{2,1,0:T(8,128)} %chunk.1), calls=%async_computation.1 | async-start | bytes 65536 | tf_op jit(solution)/shard_map/all_to_all | solution.py:29
  32.5 3.3 %collective-permute-start.4 = (f32[2,512]{1,0:T(2,128)S(1)}, f32[2,512]{1,0:T(2,128)S(1)}, u32[]{:S(2)}, u32[]{:S(2)}) collective-permute-start(f32[2,512]{1,0:T(2,128)S(1)} %pad_maximum_fusion.mass_ref), channel_id=1, source_target_pairs={{0,4},{4,0},{1,5},{5,1},{2,6},{6,2},{3,7},{7,3},{8,12},{12,8},{9,1... | collective-permute-start | bytes 12296 | tf_op jit(solution)/shard_map/ppermute | solution.py:38
  37.3 5.9 %all-to-all-start.2 = ((bf16[32,8,512]{2,1,0:T(8,128)(2,1)}), bf16[32,8,512]{2,1,0:T(8,128)(2,1)S(1)}, u32[]{:S(2)}, u32[]{:S(2)}) async-start(bf16[32,8,512]{2,1,0:T(8,128)(2,1)} %get-tuple-element.53), calls=%async_computation.2 | async-start | bytes 524288 | tf_op jit(solution)/shard_map/all_to_all | solution.py:29
  43.3 9.7 %all-to-all-done.2 = bf16[32,8,512]{2,1,0:T(8,128)(2,1)S(1)} async-done(((bf16[32,8,512]{2,1,0:T(8,128)(2,1)}), bf16[32,8,512]{2,1,0:T(8,128)(2,1)S(1)}, u32[]{:S(2)}, u32[]{:S(2)}) %all-to-all-start.2) | async-done | bytes 262176 | tf_op jit(solution)/shard_map/all_to_all | solution.py:29
  52.9 3.7 %collective-permute-start.6 = (bf16[256,512]{1,0:T(8,128)(2,1)S(1)}, bf16[256,512]{1,0:T(8,128)(2,1)S(1)}, u32[]{:S(2)}, u32[]{:S(2)}) collective-permute-start(bf16[256,512]{1,0:T(8,128)(2,1)S(1)} %bitcast.25), channel_id=1, source_target_pairs={{0,4},{4,0},{1,5},{5,1},{2,6},{6,2},{3,7},{7,3},{8,12},{12,8},{9,1... | collective-permute-start | bytes 786440 | tf_op jit(solution)/shard_map/ppermute | solution.py:38
  59.3 15.3 %all_to_all.80.peak_ref = f32[64,5,1,128]{3,2,1,0:T(1,128)S(1)} all-to-all(f32[64,5,1,128]{3,2,1,0:T(1,128)S(1)} %get-tuple-element.62), channel_id=1, replica_groups=mesh['y'=4,'z'=8,'c'=2,'x'=4] {'y','z','c'}, dimensions={0} | all-to-all | bytes 327680 | tf_op jit(solution)/shard_map/all_to_all | solution.py:29
  79.2 13.3 %all_to_all.81.got_ref = bf16[32,8,128]{2,1,0:T(8,128)(2,1)S(1)} all-to-all(bf16[32,8,128]{2,1,0:T(8,128)(2,1)S(1)} %first_pass.1), channel_id=1, replica_groups=mesh['y'=4,'z'=8,'c'=2,'x'=4] {'y','z'}, dimensions={0} | all-to-all | bytes 131072 | tf_op jit(solution)/shard_map/all_to_all | solution.py:29
  93.6 11.9 %all_to_all.82.got_ref = bf16[32,8,128]{2,1,0:T(8,128)(2,1)S(1)} all-to-all(bf16[32,8,128]{2,1,0:T(8,128)(2,1)S(1)} %get-tuple-element.68), channel_id=1, replica_groups=mesh['y'=4,'z'=8,'c'=2,'x'=4] {'y','z'}, dimensions={0} | all-to-all | bytes 131072 | tf_op jit(solution)/shard_map/all_to_all | solution.py:29
  106.5 12.0 %all_to_all.83.got_ref = bf16[32,8,128]{2,1,0:T(8,128)(2,1)S(1)} all-to-all(bf16[32,8,128]{2,1,0:T(8,128)(2,1)S(1)} %get-tuple-element.70), channel_id=1, replica_groups=mesh['y'=4,'z'=8,'c'=2,'x'=4] {'y','z'}, dimensions={0} | all-to-all | bytes 131072 | tf_op jit(solution)/shard_map/all_to_all | solution.py:29
  119.6 11.9 %all_to_all.84.got_ref = bf16[32,8,128]{2,1,0:T(8,128)(2,1)S(1)} all-to-all(bf16[32,8,128]{2,1,0:T(8,128)(2,1)S(1)} %get-tuple-element.72), channel_id=1, replica_groups=mesh['y'=4,'z'=8,'c'=2,'x'=4] {'y','z'}, dimensions={0} | all-to-all | bytes 131072 | tf_op jit(solution)/shard_map/all_to_all | solution.py:29
  132.6 11.8 %all_to_all.85.got_ref = bf16[32,8,128]{2,1,0:T(8,128)(2,1)S(1)} all-to-all(bf16[32,8,128]{2,1,0:T(8,128)(2,1)S(1)} %get-tuple-element.74), channel_id=1, replica_groups=mesh['y'=4,'z'=8,'c'=2,'x'=4] {'y','z'}, dimensions={0} | all-to-all | bytes 131072 | tf_op jit(solution)/shard_map/all_to_all | solution.py:29
  145.5 11.8 %all_to_all.86.got_ref = bf16[32,8,128]{2,1,0:T(8,128)(2,1)S(1)} all-to-all(bf16[32,8,128]{2,1,0:T(8,128)(2,1)S(1)} %get-tuple-element.76), channel_id=1, replica_groups=mesh['y'=4,'z'=8,'c'=2,'x'=4] {'y','z'}, dimensions={0} | all-to-all | bytes 131072 | tf_op jit(solution)/shard_map/all_to_all | solution.py:29
  158.4 11.8 %all_to_all.87.got_ref = bf16[32,8,128]{2,1,0:T(8,128)(2,1)S(1)} all-to-all(bf16[32,8,128]{2,1,0:T(8,128)(2,1)S(1)} %get-tuple-element.78), channel_id=1, replica_groups=mesh['y'=4,'z'=8,'c'=2,'x'=4] {'y','z'}, dimensions={0} | all-to-all | bytes 131072 | tf_op jit(solution)/shard_map/all_to_all | solution.py:29
  171.3 11.8 %all_to_all.88.got_ref = bf16[32,8,128]{2,1,0:T(8,128)(2,1)S(1)} all-to-all(bf16[32,8,128]{2,1,0:T(8,128)(2,1)S(1)} %get-tuple-element.80), channel_id=1, replica_groups=mesh['y'=4,'z'=8,'c'=2,'x'=4] {'y','z'}, dimensions={0} | all-to-all | bytes 131072 | tf_op jit(solution)/shard_map/all_to_all | solution.py:29
  184.2 11.9 %all_to_all.89.got_ref = bf16[32,8,128]{2,1,0:T(8,128)(2,1)S(1)} all-to-all(bf16[32,8,128]{2,1,0:T(8,128)(2,1)S(1)} %get-tuple-element.82), channel_id=1, replica_groups=mesh['y'=4,'z'=8,'c'=2,'x'=4] {'y','z'}, dimensions={0} | all-to-all | bytes 131072 | tf_op jit(solution)/shard_map/all_to_all | solution.py:29
  197.2 11.8 %all_to_all.90.got_ref = bf16[32,8,128]{2,1,0:T(8,128)(2,1)S(1)} all-to-all(bf16[32,8,128]{2,1,0:T(8,128)(2,1)S(1)} %get-tuple-element.87), channel_id=1, replica_groups=mesh['y'=4,'z'=8,'c'=2,'x'=4] {'y','z'}, dimensions={0} | all-to-all | bytes 131072 | tf_op jit(solution)/shard_map/all_to_all | solution.py:29
  210.8 3.9 %all-to-all-start.14 = ((f32[32,8,512]{2,1,0:T(8,128)}), f32[32,8,512]{2,1,0:T(8,128)S(1)}, u32[]{:S(2)}, u32[]{:S(2)}) async-start(f32[32,8,512]{2,1,0:T(8,128)} %bitcast.13), calls=%async_computation.14 | async-start | bytes 1048576 | tf_op jit(solution)/shard_map/all_to_all | solution.py:29
  214.7 11.6 %all-to-all-done.14 = f32[32,8,512]{2,1,0:T(8,128)S(1)} async-done(((f32[32,8,512]{2,1,0:T(8,128)}), f32[32,8,512]{2,1,0:T(8,128)S(1)}, u32[]{:S(2)}, u32[]{:S(2)}) %all-to-all-start.14) | async-done | bytes 524320 | tf_op jit(solution)/shard_map/all_to_all | solution.py:29
  227.1 5.2 %all-to-all-start.15 = ((bf16[32,8,512]{2,1,0:T(8,128)(2,1)}), bf16[32,8,512]{2,1,0:T(8,128)(2,1)S(1)}, u32[]{:S(2)}, u32[]{:S(2)}) async-start(bf16[32,8,512]{2,1,0:T(8,128)(2,1)} %broadcast_in_dim.26), calls=%async_computation.15 | async-start | bytes 524288 | tf_op jit(solution)/shard_map/all_to_all | solution.py:29
  234.3 9.5 %all-to-all-done.15 = bf16[32,8,512]{2,1,0:T(8,128)(2,1)S(1)} async-done(((bf16[32,8,512]{2,1,0:T(8,128)(2,1)}), bf16[32,8,512]{2,1,0:T(8,128)(2,1)S(1)}, u32[]{:S(2)}, u32[]{:S(2)}) %all-to-all-start.15) | async-done | bytes 262176 | tf_op jit(solution)/shard_map/all_to_all | solution.py:29
  243.8 16.4 %collective-permute-start.8 = (bf16[256,512]{1,0:T(8,128)(2,1)S(1)}, bf16[256,512]{1,0:T(8,128)(2,1)S(1)}, u32[]{:S(2)}, u32[]{:S(2)}) collective-permute-start(bf16[256,512]{1,0:T(8,128)(2,1)S(1)} %bitcast.28), channel_id=1, source_target_pairs={{0,4},{4,0},{1,5},{5,1},{2,6},{6,2},{3,7},{7,3},{8,12},{12,8},{9,1... | collective-permute-start | bytes 786440 | tf_op jit(solution)/shard_map/ppermute | solution.py:38
  (63 shorter events, 36.9 us)
Async XLA Ops:
  2.8 19.7 %copy-start.2 = (bf16[512,512]{1,0:T(8,128)(2,1)S(1)}, bf16[512,512]{1,0:T(8,128)(2,1)}, u32[]{:S(2)}) copy-start(bf16[512,512]{1,0:T(8,128)(2,1)} %expr_ref.1) | copy-start | bytes 1572868
  2.9 4.4 %collective-permute-start = (f32[32,3,4,128]{3,2,1,0:T(4,128)S(1)}, f32[32,3,4,128]{3,2,1,0:T(4,128)S(1)}, u32[]{:S(2)}, u32[]{:S(2)}) collective-permute-start(f32[32,3,4,128]{3,2,1,0:T(4,128)S(1)} %get-tuple-element.50), channel_id=1, source_target_pairs={{0,4},{4,0},{1,5},{5,1},{2,6},{6,2},{3,7},{7,3},{8,12},{12,8},{9,1... | collective-permute-start | bytes 589832 | tf_op jit(solution)/shard_map/ppermute | solution.py:38
  8.0 9.6 %copy-start.3 = (bf16[2,512,128]{2,1,0:T(8,128)(2,1)S(1)}, bf16[2,512,128]{2,1,0:T(8,128)(2,1)}, u32[]{:S(2)}) copy-start(bf16[2,512,128]{2,1,0:T(8,128)(2,1)} %get-tuple-element.51.refs_0_) | copy-start | bytes 786436
  8.0 19.0 %all-to-all-start = ((f32[32,3,4,128]{3,2,1,0:T(4,128)}), f32[32,3,4,128]{3,2,1,0:T(4,128)S(1)}, u32[]{:S(2)}, u32[]{:S(2)}) async-start(f32[32,3,4,128]{3,2,1,0:T(4,128)} %add.18), calls=%async_computation | async-start | bytes 393216 | tf_op jit(solution)/shard_map/all_to_all | solution.py:29
  17.6 9.4 %copy-start.4 = (f32[128]{0:T(128)S(1)}, f32[128]{0:T(128)}, u32[]{:S(2)}) copy-start(f32[128]{0:T(128)} %param.12) | copy-start | bytes 1540
  17.6 19.0 %collective-permute-start.1 = (bf16[2,512,128]{2,1,0:T(8,128)(2,1)S(1)}, bf16[2,512,128]{2,1,0:T(8,128)(2,1)S(1)}, u32[]{:S(2)}, u32[]{:S(2)}) collective-permute-start(bf16[2,512,128]{2,1,0:T(8,128)(2,1)S(1)} %copy-done.3), channel_id=1, source_target_pairs={{0,1},{1,2},{2,3},{3,0},{4,5},{5,6},{6,7},{7,4},{8,9},{9,10},{10,1... | collective-permute-start | bytes 786440 | tf_op jit(solution)/shard_map/ppermute | solution.py:340
  18.9 17.7 %collective-permute-start.2 = (bf16[2,512,128]{2,1,0:T(8,128)(2,1)S(1)}, bf16[2,512,128]{2,1,0:T(8,128)(2,1)S(1)}, u32[]{:S(2)}, u32[]{:S(2)}) collective-permute-start(bf16[2,512,128]{2,1,0:T(8,128)(2,1)S(1)} %copy-done.3), channel_id=1, source_target_pairs={{0,2},{1,3},{2,0},{3,1},{4,6},{5,7},{6,4},{7,5},{8,10},{9,11},{10,... | collective-permute-start | bytes 786440 | tf_op jit(solution)/shard_map/ppermute | solution.py:340
  21.4 15.3 %collective-permute-start.3 = (bf16[2,512,128]{2,1,0:T(8,128)(2,1)S(1)}, bf16[2,512,128]{2,1,0:T(8,128)(2,1)S(1)}, u32[]{:S(2)}, u32[]{:S(2)}) collective-permute-start(bf16[2,512,128]{2,1,0:T(8,128)(2,1)S(1)} %copy-done.3), channel_id=1, source_target_pairs={{0,3},{1,0},{2,1},{3,2},{4,7},{5,4},{6,5},{7,6},{8,11},{9,8},{10,9... | collective-permute-start | bytes 786440 | tf_op jit(solution)/shard_map/ppermute | solution.py:340
  22.5 20.7 %collective-permute-start.5 = (bf16[512,512]{1,0:T(8,128)(2,1)S(1)}, bf16[512,512]{1,0:T(8,128)(2,1)S(1)}, u32[]{:S(2)}, u32[]{:S(2)}) collective-permute-start(bf16[512,512]{1,0:T(8,128)(2,1)S(1)} %copy-done.2), channel_id=1, source_target_pairs={{0,4},{4,0},{1,5},{5,1},{2,6},{6,2},{3,7},{7,3},{8,12},{12,8},{9,1... | collective-permute-start | bytes 1572872 | tf_op jit(solution)/shard_map/ppermute | solution.py:38
  27.7 4.2 %copy-start.8 = (f32[512]{0:T(512)S(1)}, f32[512]{0:T(512)}, u32[]{:S(2)}) copy-start(f32[512]{0:T(512)} %param.13) | copy-start | bytes 6148
  27.7 9.0 %all-to-all-start.1 = ((f32[4,16,128]{2,1,0:T(8,128)}), f32[4,16,128]{2,1,0:T(8,128)S(1)}, u32[]{:S(2)}, u32[]{:S(2)}) async-start(f32[4,16,128]{2,1,0:T(8,128)} %chunk.1), calls=%async_computation.1 | async-start | bytes 65536 | tf_op jit(solution)/shard_map/all_to_all | solution.py:29
  31.8 0.7 copy-start.7
  32.5 4.1 %collective-permute-start.4 = (f32[2,512]{1,0:T(2,128)S(1)}, f32[2,512]{1,0:T(2,128)S(1)}, u32[]{:S(2)}, u32[]{:S(2)}) collective-permute-start(f32[2,512]{1,0:T(2,128)S(1)} %pad_maximum_fusion.mass_ref), channel_id=1, source_target_pairs={{0,4},{4,0},{1,5},{5,1},{2,6},{6,2},{3,7},{7,3},{8,12},{12,8},{9,1... | collective-permute-start | bytes 12296 | tf_op jit(solution)/shard_map/ppermute | solution.py:38
  37.3 20.5 %copy-start = (bf16[512,256]{1,0:T(8,128)(2,1)S(1)}, bf16[512,256]{1,0:T(8,128)(2,1)}, u32[]{:S(2)}) copy-start(bf16[512,256]{1,0:T(8,128)(2,1)} %x_ref.1) | copy-start | bytes 786436
  37.3 20.5 %copy-start.1 = (bf16[512,256]{1,0:T(8,128)(2,1)S(1)}, bf16[512,256]{1,0:T(8,128)(2,1)}, u32[]{:S(2)}) copy-start(bf16[512,256]{1,0:T(8,128)(2,1)} %y_ref.1) | copy-start | bytes 786436
  37.3 15.6 %all-to-all-start.2 = ((bf16[32,8,512]{2,1,0:T(8,128)(2,1)}), bf16[32,8,512]{2,1,0:T(8,128)(2,1)S(1)}, u32[]{:S(2)}, u32[]{:S(2)}) async-start(bf16[32,8,512]{2,1,0:T(8,128)(2,1)} %get-tuple-element.53), calls=%async_computation.2 | async-start | bytes 524288 | tf_op jit(solution)/shard_map/all_to_all | solution.py:29
  52.9 4.9 %collective-permute-start.6 = (bf16[256,512]{1,0:T(8,128)(2,1)S(1)}, bf16[256,512]{1,0:T(8,128)(2,1)S(1)}, u32[]{:S(2)}, u32[]{:S(2)}) collective-permute-start(bf16[256,512]{1,0:T(8,128)(2,1)S(1)} %bitcast.25), channel_id=1, source_target_pairs={{0,4},{4,0},{1,5},{5,1},{2,6},{6,2},{3,7},{7,3},{8,12},{12,8},{9,1... | collective-permute-start | bytes 786440 | tf_op jit(solution)/shard_map/ppermute | solution.py:38
  75.4 2.8 %collective-permute-start.7 = (bf16[1024,512]{1,0:T(8,128)(2,1)S(1)}, bf16[1024,512]{1,0:T(8,128)(2,1)S(1)}, u32[]{:S(2)}, u32[]{:S(2)}) collective-permute-start(bf16[1024,512]{1,0:T(8,128)(2,1)S(1)} %get-tuple-element.66.own_ref), channel_id=1, source_target_pairs={{0,4},{4,0},{1,5},{5,1},{2,6},{6,2},{3,7},{7,3},{8,12},{12,8},{9,1... | collective-permute-start | bytes 3145736 | tf_op jit(solution)/shard_map/ppermute | solution.py:38
  210.8 15.5 %all-to-all-start.14 = ((f32[32,8,512]{2,1,0:T(8,128)}), f32[32,8,512]{2,1,0:T(8,128)S(1)}, u32[]{:S(2)}, u32[]{:S(2)}) async-start(f32[32,8,512]{2,1,0:T(8,128)} %bitcast.13), calls=%async_computation.14 | async-start | bytes 1048576 | tf_op jit(solution)/shard_map/all_to_all | solution.py:29
  227.1 16.8 %all-to-all-start.15 = ((bf16[32,8,512]{2,1,0:T(8,128)(2,1)}), bf16[32,8,512]{2,1,0:T(8,128)(2,1)S(1)}, u32[]{:S(2)}, u32[]{:S(2)}) async-start(bf16[32,8,512]{2,1,0:T(8,128)(2,1)} %broadcast_in_dim.26), calls=%async_computation.15 | async-start | bytes 524288 | tf_op jit(solution)/shard_map/all_to_all | solution.py:29
  232.3 1.0 copy-start.5
  232.3 1.0 copy-start.6
  243.8 17.6 %collective-permute-start.8 = (bf16[256,512]{1,0:T(8,128)(2,1)S(1)}, bf16[256,512]{1,0:T(8,128)(2,1)S(1)}, u32[]{:S(2)}, u32[]{:S(2)}) collective-permute-start(bf16[256,512]{1,0:T(8,128)(2,1)S(1)} %bitcast.28), channel_id=1, source_target_pairs={{0,4},{4,0},{1,5},{5,1},{2,6},{6,2},{3,7},{7,3},{8,12},{12,8},{9,1... | collective-permute-start | bytes 786440 | tf_op jit(solution)/shard_map/ppermute | solution.py:38

commit v13 on v12

--- a/solution.py
+++ b/solution.py
@@ -401,6 +401,9 @@
         core_index, exchange(sent, CHIPS), v, log_g, u, kerns, theirs,
         expr, other_expr,
     )
+    part, v, weights, u, eta, core, here = lax.optimization_barrier(
+        (part, v, weights, u, eta, core, here)
+    )
     v_q, v_r = v[:ranks], v[ranks:]
     kern_q = q_factor * jnp.exp(-eta * own_grad_q)
     kern_r = r_factor * jnp.exp(-eta * own_grad_r)
@@ -410,18 +413,23 @@
     s_q = jnp.sum(mine_q * v_q.reshape(1, columns), axis=1)
     scaled = (mine_q * (v_q / weights).reshape(1, columns)).astype(BF16)
 
-    piece = jnp.sum(exchange(part.reshape(others, -1, genes), CHIPS), axis=0)
-    mine = to_all(piece.astype(BF16), CHIPS).reshape(columns // 2, genes)
     half = columns // 2
-    mixed = jnp.dot(
-        lax.dynamic_slice_in_dim(scaled, core * half, half, 1), mine, preferred_element_type=F32
-    ) + jnp.dot(
-        lax.dynamic_slice_in_dim(scaled, (1 - core) * half, half, 1),
-        swap(mine),
-        preferred_element_type=F32,
+    mine_scaled = lax.dynamic_slice_in_dim(scaled, core * half, half, 1)
+    other_scaled = lax.dynamic_slice_in_dim(scaled, (1 - core) * half, half, 1)
+    rank_share = pick(weights, here) / cells_total
+    got, q_new, r_new, rank_share, s_q, mine_scaled, other_scaled = lax.optimization_barrier(
+        (
+            exchange(part.reshape(others, -1, genes), CHIPS),
+            q_new, r_new, rank_share, s_q, mine_scaled, other_scaled,
+        )
+    )
+    piece = jnp.sum(got, axis=0)
+    mine = to_all(piece.astype(BF16), CHIPS).reshape(half, genes)
+    mixed = jnp.dot(mine_scaled, mine, preferred_element_type=F32) + jnp.dot(
+        other_scaled, swap(mine), preferred_element_type=F32
     )
     predicted = (mixed / s_q[:, None]).astype(BF16)
-    return (q_new, r_new, pick(weights, here) / cells_total, predicted)
+    return (q_new, r_new, rank_share, predicted)
 
 
 def solution(mesh):

time: 264 us -> 263 us (level)
  blocking collectives: 135 us -> 152 us
  waiting for transfers between devices: 39.4 us -> 28.2 us
  starting transfers between devices: 62.4 us -> 57.1 us
    all_to_all x11 -> x12, blocking collectives: 135 us -> 152 us  [exchange(): return lax.all_to_all(chunks, axes, 0, 0, tiled=False)]
    all_to_all x5 -> x4, waiting for transfers between devices: 33.7 us -> 22 us  [exchange(): return lax.all_to_all(chunks, axes, 0, 0, tiled=False)]
    all_to_all x5 -> x4, starting transfers between devices: 28.7 us -> 23.5 us  [exchange(): return lax.all_to_all(chunks, axes, 0, 0, tiled=False)]
  transfers between devices with their start and end apart: 14 -> 13, of which waited for: 9 -> 8; matrix products, arithmetic and copies ran while one was open for 1% -> 1% of each run, Pallas kernels for 1% -> 1%
where the time goes in v13:
time: 263 us; the launch traced here: 262 us
  blocking collectives  152 us (58%)
  starting transfers between devices  57.1 us (22%)
  waiting for transfers between devices  28.2 us (11%)
  Pallas kernels  18.2 us (7%)
    all_to_all x12, blocking collectives, exchange(): return lax.all_to_all(chunks, axes, 0, 0, tiled=False)  152 us
    ppermute x6, starting transfers between devices, swap(): return lax.ppermute(value, 'c', [(0, 1), (1, 0)])  28.6 us
    all_to_all x4, starting transfers between devices, exchange(): return lax.all_to_all(chunks, axes, 0, 0, tiled=False)  23.5 us
    all_to_all x4, waiting for transfers between devices, exchange(): return lax.all_to_all(chunks, axes, 0, 0, tiled=False)  22 us
    pallas_call x9, Pallas kernels, shards(): on_chip(next_pass, (sent_shape, v_shape) + last, 'next_pass')  9.6 us
    ppermute x6, waiting for transfers between devices, swap(): return lax.ppermute(value, 'c', [(0, 1), (1, 0)])  6.21 us
  transfers between devices with their start and end apart: 13, of which 8 were waited for; matrix products, arithmetic and copies ran while one was open for 1% of the time, Pallas kernels for 1%

profile of v13, /device:TPU:1, one launch (start us, length us, event | category | flops | bytes accessed | tf_op | source)
XLA Modules:
  0.0 261.9 jit_solution(6720024455718522213)
XLA Ops:
  2.9 3.3 %collective-permute-start = (f32[32,3,4,128]{3,2,1,0:T(4,128)S(1)}, f32[32,3,4,128]{3,2,1,0:T(4,128)S(1)}, u32[]{:S(2)}, u32[]{:S(2)}) collective-permute-start(f32[32,3,4,128]{3,2,1,0:T(4,128)S(1)} %get-tuple-element.64), channel_id=1, source_target_pairs={{0,4},{4,0},{1,5},{5,1},{2,6},{6,2},{3,7},{7,3},{8,12},{12,8},{9,1... | collective-permute-start | bytes 589832 | tf_op jit(solution)/shard_map/ppermute | solution.py:38
  8.0 9.6 %all-to-all-start = ((f32[32,3,4,128]{3,2,1,0:T(4,128)}), f32[32,3,4,128]{3,2,1,0:T(4,128)S(1)}, u32[]{:S(2)}, u32[]{:S(2)}) async-start(f32[32,3,4,128]{3,2,1,0:T(4,128)} %add.18), calls=%async_computation | async-start | bytes 393216 | tf_op jit(solution)/shard_map/all_to_all | solution.py:29
  18.9 2.4 collective-permute-start.2
  24.0 3.0 %all-to-all-done.got_ref = f32[32,3,4,128]{3,2,1,0:T(4,128)S(1)} async-done(((f32[32,3,4,128]{3,2,1,0:T(4,128)}), f32[32,3,4,128]{3,2,1,0:T(4,128)S(1)}, u32[]{:S(2)}, u32[]{:S(2)}) %all-to-all-start) | async-done | bytes 196640 | tf_op jit(solution)/shard_map/all_to_all | solution.py:29
  27.7 4.1 %all-to-all-start.1 = ((f32[4,16,128]{2,1,0:T(8,128)}), f32[4,16,128]{2,1,0:T(8,128)S(1)}, u32[]{:S(2)}, u32[]{:S(2)}) async-start(f32[4,16,128]{2,1,0:T(8,128)} %chunk.1), calls=%async_computation.1 | async-start | bytes 65536 | tf_op jit(solution)/shard_map/all_to_all | solution.py:29
  32.5 3.3 %collective-permute-start.4 = (f32[2,512]{1,0:T(2,128)S(1)}, f32[2,512]{1,0:T(2,128)S(1)}, u32[]{:S(2)}, u32[]{:S(2)}) collective-permute-start(f32[2,512]{1,0:T(2,128)S(1)} %pad_maximum_fusion.mass_ref), channel_id=1, source_target_pairs={{0,4},{4,0},{1,5},{5,1},{2,6},{6,2},{3,7},{7,3},{8,12},{12,8},{9,1... | collective-permute-start | bytes 12296 | tf_op jit(solution)/shard_map/ppermute | solution.py:38
  37.4 5.9 %all-to-all-start.2 = ((bf16[32,8,512]{2,1,0:T(8,128)(2,1)}), bf16[32,8,512]{2,1,0:T(8,128)(2,1)S(1)}, u32[]{:S(2)}, u32[]{:S(2)}) async-start(bf16[32,8,512]{2,1,0:T(8,128)(2,1)} %get-tuple-element.67), calls=%async_computation.2 | async-start | bytes 524288 | tf_op jit(solution)/shard_map/all_to_all | solution.py:29
  43.3 9.7 %all-to-all-done.2 = bf16[32,8,512]{2,1,0:T(8,128)(2,1)S(1)} async-done(((bf16[32,8,512]{2,1,0:T(8,128)(2,1)}), bf16[32,8,512]{2,1,0:T(8,128)(2,1)S(1)}, u32[]{:S(2)}, u32[]{:S(2)}) %all-to-all-start.2) | async-done | bytes 262176 | tf_op jit(solution)/shard_map/all_to_all | solution.py:29
  52.9 3.7 %collective-permute-start.6 = (bf16[256,512]{1,0:T(8,128)(2,1)S(1)}, bf16[256,512]{1,0:T(8,128)(2,1)S(1)}, u32[]{:S(2)}, u32[]{:S(2)}) collective-permute-start(bf16[256,512]{1,0:T(8,128)(2,1)S(1)} %bitcast.27), channel_id=1, source_target_pairs={{0,4},{4,0},{1,5},{5,1},{2,6},{6,2},{3,7},{7,3},{8,12},{12,8},{9,1... | collective-permute-start | bytes 786440 | tf_op jit(solution)/shard_map/ppermute | solution.py:38
  59.3 15.3 %all_to_all.80.peak_ref = f32[64,5,1,128]{3,2,1,0:T(1,128)S(1)} all-to-all(f32[64,5,1,128]{3,2,1,0:T(1,128)S(1)} %get-tuple-element.76), channel_id=1, replica_groups=mesh['y'=4,'z'=8,'c'=2,'x'=4] {'y','z','c'}, dimensions={0} | all-to-all | bytes 327680 | tf_op jit(solution)/shard_map/all_to_all | solution.py:29
  79.2 13.3 %all_to_all.81.got_ref = bf16[32,8,128]{2,1,0:T(8,128)(2,1)S(1)} all-to-all(bf16[32,8,128]{2,1,0:T(8,128)(2,1)S(1)} %first_pass.1), channel_id=1, replica_groups=mesh['y'=4,'z'=8,'c'=2,'x'=4] {'y','z'}, dimensions={0} | all-to-all | bytes 131072 | tf_op jit(solution)/shard_map/all_to_all | solution.py:29
  93.6 11.9 %all_to_all.82.got_ref = bf16[32,8,128]{2,1,0:T(8,128)(2,1)S(1)} all-to-all(bf16[32,8,128]{2,1,0:T(8,128)(2,1)S(1)} %get-tuple-element.82), channel_id=1, replica_groups=mesh['y'=4,'z'=8,'c'=2,'x'=4] {'y','z'}, dimensions={0} | all-to-all | bytes 131072 | tf_op jit(solution)/shard_map/all_to_all | solution.py:29
  106.6 12.0 %all_to_all.83.got_ref = bf16[32,8,128]{2,1,0:T(8,128)(2,1)S(1)} all-to-all(bf16[32,8,128]{2,1,0:T(8,128)(2,1)S(1)} %get-tuple-element.84), channel_id=1, replica_groups=mesh['y'=4,'z'=8,'c'=2,'x'=4] {'y','z'}, dimensions={0} | all-to-all | bytes 131072 | tf_op jit(solution)/shard_map/all_to_all | solution.py:29
  119.6 11.9 %all_to_all.84.got_ref = bf16[32,8,128]{2,1,0:T(8,128)(2,1)S(1)} all-to-all(bf16[32,8,128]{2,1,0:T(8,128)(2,1)S(1)} %get-tuple-element.86), channel_id=1, replica_groups=mesh['y'=4,'z'=8,'c'=2,'x'=4] {'y','z'}, dimensions={0} | all-to-all | bytes 131072 | tf_op jit(solution)/shard_map/all_to_all | solution.py:29
  132.7 11.8 %all_to_all.85.got_ref = bf16[32,8,128]{2,1,0:T(8,128)(2,1)S(1)} all-to-all(bf16[32,8,128]{2,1,0:T(8,128)(2,1)S(1)} %get-tuple-element.88), channel_id=1, replica_groups=mesh['y'=4,'z'=8,'c'=2,'x'=4] {'y','z'}, dimensions={0} | all-to-all | bytes 131072 | tf_op jit(solution)/shard_map/all_to_all | solution.py:29
  145.6 11.8 %all_to_all.86.got_ref = bf16[32,8,128]{2,1,0:T(8,128)(2,1)S(1)} all-to-all(bf16[32,8,128]{2,1,0:T(8,128)(2,1)S(1)} %get-tuple-element.90), channel_id=1, replica_groups=mesh['y'=4,'z'=8,'c'=2,'x'=4] {'y','z'}, dimensions={0} | all-to-all | bytes 131072 | tf_op jit(solution)/shard_map/all_to_all | solution.py:29
  158.4 11.8 %all_to_all.87.got_ref = bf16[32,8,128]{2,1,0:T(8,128)(2,1)S(1)} all-to-all(bf16[32,8,128]{2,1,0:T(8,128)(2,1)S(1)} %get-tuple-element.92), channel_id=1, replica_groups=mesh['y'=4,'z'=8,'c'=2,'x'=4] {'y','z'}, dimensions={0} | all-to-all | bytes 131072 | tf_op jit(solution)/shard_map/all_to_all | solution.py:29
  171.3 11.8 %all_to_all.88.got_ref = bf16[32,8,128]{2,1,0:T(8,128)(2,1)S(1)} all-to-all(bf16[32,8,128]{2,1,0:T(8,128)(2,1)S(1)} %get-tuple-element.94), channel_id=1, replica_groups=mesh['y'=4,'z'=8,'c'=2,'x'=4] {'y','z'}, dimensions={0} | all-to-all | bytes 131072 | tf_op jit(solution)/shard_map/all_to_all | solution.py:29
  184.2 11.9 %all_to_all.89.got_ref = bf16[32,8,128]{2,1,0:T(8,128)(2,1)S(1)} all-to-all(bf16[32,8,128]{2,1,0:T(8,128)(2,1)S(1)} %get-tuple-element.96), channel_id=1, replica_groups=mesh['y'=4,'z'=8,'c'=2,'x'=4] {'y','z'}, dimensions={0} | all-to-all | bytes 131072 | tf_op jit(solution)/shard_map/all_to_all | solution.py:29
  197.2 11.8 %all_to_all.90.got_ref = bf16[32,8,128]{2,1,0:T(8,128)(2,1)S(1)} all-to-all(bf16[32,8,128]{2,1,0:T(8,128)(2,1)S(1)} %get-tuple-element.98), channel_id=1, replica_groups=mesh['y'=4,'z'=8,'c'=2,'x'=4] {'y','z'}, dimensions={0} | all-to-all | bytes 131072 | tf_op jit(solution)/shard_map/all_to_all | solution.py:29
  210.8 3.9 %all-to-all-start.14 = ((f32[32,8,512]{2,1,0:T(8,128)}), f32[32,8,512]{2,1,0:T(8,128)S(1)}, u32[]{:S(2)}, u32[]{:S(2)}) async-start(f32[32,8,512]{2,1,0:T(8,128)} %bitcast.6), calls=%async_computation.14 | async-start | bytes 1048576 | tf_op jit(solution)/shard_map/all_to_all | solution.py:29
  217.0 9.3 %all-to-all-done.14 = f32[32,8,512]{2,1,0:T(8,128)S(1)} async-done(((f32[32,8,512]{2,1,0:T(8,128)}), f32[32,8,512]{2,1,0:T(8,128)S(1)}, u32[]{:S(2)}, u32[]{:S(2)}) %all-to-all-start.14) | async-done | bytes 524320 | tf_op jit(solution)/shard_map/all_to_all | solution.py:29
  226.4 17.0 %all_to_all.91 = bf16[32,8,512]{2,1,0:T(8,128)(2,1)S(1)} all-to-all(bf16[32,8,512]{2,1,0:T(8,128)(2,1)S(1)} %broadcast_in_dim.26), channel_id=1, replica_groups=mesh['y'=4,'z'=8,'c'=2,'x'=4] {'y','z'}, dimensions={0} | all-to-all | bytes 524288 | tf_op jit(solution)/shard_map/all_to_all | solution.py:29
  243.3 16.3 %collective-permute-start.8 = (bf16[256,512]{1,0:T(8,128)(2,1)S(1)}, bf16[256,512]{1,0:T(8,128)(2,1)S(1)}, u32[]{:S(2)}, u32[]{:S(2)}) collective-permute-start(bf16[256,512]{1,0:T(8,128)(2,1)S(1)} %bitcast.30), channel_id=1, source_target_pairs={{0,4},{4,0},{1,5},{5,1},{2,6},{6,2},{3,7},{7,3},{8,12},{12,8},{9,1... | collective-permute-start | bytes 786440 | tf_op jit(solution)/shard_map/ppermute | solution.py:38
  (62 shorter events, 34.0 us)
Async XLA Ops:
  2.8 19.7 %copy-start.2 = (bf16[512,512]{1,0:T(8,128)(2,1)S(1)}, bf16[512,512]{1,0:T(8,128)(2,1)}, u32[]{:S(2)}) copy-start(bf16[512,512]{1,0:T(8,128)(2,1)} %expr_ref.1) | copy-start | bytes 1572868
  2.9 4.4 %collective-permute-start = (f32[32,3,4,128]{3,2,1,0:T(4,128)S(1)}, f32[32,3,4,128]{3,2,1,0:T(4,128)S(1)}, u32[]{:S(2)}, u32[]{:S(2)}) collective-permute-start(f32[32,3,4,128]{3,2,1,0:T(4,128)S(1)} %get-tuple-element.64), channel_id=1, source_target_pairs={{0,4},{4,0},{1,5},{5,1},{2,6},{6,2},{3,7},{7,3},{8,12},{12,8},{9,1... | collective-permute-start | bytes 589832 | tf_op jit(solution)/shard_map/ppermute | solution.py:38
  8.0 9.6 %copy-start.3 = (bf16[2,512,128]{2,1,0:T(8,128)(2,1)S(1)}, bf16[2,512,128]{2,1,0:T(8,128)(2,1)}, u32[]{:S(2)}) copy-start(bf16[2,512,128]{2,1,0:T(8,128)(2,1)} %get-tuple-element.65.refs_0_) | copy-start | bytes 786436
  8.0 19.0 %all-to-all-start = ((f32[32,3,4,128]{3,2,1,0:T(4,128)}), f32[32,3,4,128]{3,2,1,0:T(4,128)S(1)}, u32[]{:S(2)}, u32[]{:S(2)}) async-start(f32[32,3,4,128]{3,2,1,0:T(4,128)} %add.18), calls=%async_computation | async-start | bytes 393216 | tf_op jit(solution)/shard_map/all_to_all | solution.py:29
  17.6 9.4 %copy-start.4 = (f32[128]{0:T(128)S(1)}, f32[128]{0:T(128)}, u32[]{:S(2)}) copy-start(f32[128]{0:T(128)} %param.12) | copy-start | bytes 1540
  17.6 19.0 %collective-permute-start.1 = (bf16[2,512,128]{2,1,0:T(8,128)(2,1)S(1)}, bf16[2,512,128]{2,1,0:T(8,128)(2,1)S(1)}, u32[]{:S(2)}, u32[]{:S(2)}) collective-permute-start(bf16[2,512,128]{2,1,0:T(8,128)(2,1)S(1)} %copy-done.3), channel_id=1, source_target_pairs={{0,1},{1,2},{2,3},{3,0},{4,5},{5,6},{6,7},{7,4},{8,9},{9,10},{10,1... | collective-permute-start | bytes 786440 | tf_op jit(solution)/shard_map/ppermute | solution.py:340
  18.9 17.7 %collective-permute-start.2 = (bf16[2,512,128]{2,1,0:T(8,128)(2,1)S(1)}, bf16[2,512,128]{2,1,0:T(8,128)(2,1)S(1)}, u32[]{:S(2)}, u32[]{:S(2)}) collective-permute-start(bf16[2,512,128]{2,1,0:T(8,128)(2,1)S(1)} %copy-done.3), channel_id=1, source_target_pairs={{0,2},{1,3},{2,0},{3,1},{4,6},{5,7},{6,4},{7,5},{8,10},{9,11},{10,... | collective-permute-start | bytes 786440 | tf_op jit(solution)/shard_map/ppermute | solution.py:340
  21.4 15.3 %collective-permute-start.3 = (bf16[2,512,128]{2,1,0:T(8,128)(2,1)S(1)}, bf16[2,512,128]{2,1,0:T(8,128)(2,1)S(1)}, u32[]{:S(2)}, u32[]{:S(2)}) collective-permute-start(bf16[2,512,128]{2,1,0:T(8,128)(2,1)S(1)} %copy-done.3), channel_id=1, source_target_pairs={{0,3},{1,0},{2,1},{3,2},{4,7},{5,4},{6,5},{7,6},{8,11},{9,8},{10,9... | collective-permute-start | bytes 786440 | tf_op jit(solution)/shard_map/ppermute | solution.py:340
  22.5 20.7 %collective-permute-start.5 = (bf16[512,512]{1,0:T(8,128)(2,1)S(1)}, bf16[512,512]{1,0:T(8,128)(2,1)S(1)}, u32[]{:S(2)}, u32[]{:S(2)}) collective-permute-start(bf16[512,512]{1,0:T(8,128)(2,1)S(1)} %copy-done.2), channel_id=1, source_target_pairs={{0,4},{4,0},{1,5},{5,1},{2,6},{6,2},{3,7},{7,3},{8,12},{12,8},{9,1... | collective-permute-start | bytes 1572872 | tf_op jit(solution)/shard_map/ppermute | solution.py:38
  27.7 4.2 %copy-start.8 = (f32[512]{0:T(512)S(1)}, f32[512]{0:T(512)}, u32[]{:S(2)}) copy-start(f32[512]{0:T(512)} %param.13) | copy-start | bytes 6148
  27.7 9.0 %all-to-all-start.1 = ((f32[4,16,128]{2,1,0:T(8,128)}), f32[4,16,128]{2,1,0:T(8,128)S(1)}, u32[]{:S(2)}, u32[]{:S(2)}) async-start(f32[4,16,128]{2,1,0:T(8,128)} %chunk.1), calls=%async_computation.1 | async-start | bytes 65536 | tf_op jit(solution)/shard_map/all_to_all | solution.py:29
  31.8 0.7 copy-start.7
  32.5 4.1 %collective-permute-start.4 = (f32[2,512]{1,0:T(2,128)S(1)}, f32[2,512]{1,0:T(2,128)S(1)}, u32[]{:S(2)}, u32[]{:S(2)}) collective-permute-start(f32[2,512]{1,0:T(2,128)S(1)} %pad_maximum_fusion.mass_ref), channel_id=1, source_target_pairs={{0,4},{4,0},{1,5},{5,1},{2,6},{6,2},{3,7},{7,3},{8,12},{12,8},{9,1... | collective-permute-start | bytes 12296 | tf_op jit(solution)/shard_map/ppermute | solution.py:38
  37.3 20.5 %copy-start = (bf16[512,256]{1,0:T(8,128)(2,1)S(1)}, bf16[512,256]{1,0:T(8,128)(2,1)}, u32[]{:S(2)}) copy-start(bf16[512,256]{1,0:T(8,128)(2,1)} %x_ref.1) | copy-start | bytes 786436
  37.3 20.5 %copy-start.1 = (bf16[512,256]{1,0:T(8,128)(2,1)S(1)}, bf16[512,256]{1,0:T(8,128)(2,1)}, u32[]{:S(2)}) copy-start(bf16[512,256]{1,0:T(8,128)(2,1)} %y_ref.1) | copy-start | bytes 786436
  37.4 15.6 %all-to-all-start.2 = ((bf16[32,8,512]{2,1,0:T(8,128)(2,1)}), bf16[32,8,512]{2,1,0:T(8,128)(2,1)S(1)}, u32[]{:S(2)}, u32[]{:S(2)}) async-start(bf16[32,8,512]{2,1,0:T(8,128)(2,1)} %get-tuple-element.67), calls=%async_computation.2 | async-start | bytes 524288 | tf_op jit(solution)/shard_map/all_to_all | solution.py:29
  52.9 4.9 %collective-permute-start.6 = (bf16[256,512]{1,0:T(8,128)(2,1)S(1)}, bf16[256,512]{1,0:T(8,128)(2,1)S(1)}, u32[]{:S(2)}, u32[]{:S(2)}) collective-permute-start(bf16[256,512]{1,0:T(8,128)(2,1)S(1)} %bitcast.27), channel_id=1, source_target_pairs={{0,4},{4,0},{1,5},{5,1},{2,6},{6,2},{3,7},{7,3},{8,12},{12,8},{9,1... | collective-permute-start | bytes 786440 | tf_op jit(solution)/shard_map/ppermute | solution.py:38
  75.4 2.8 %collective-permute-start.7 = (bf16[1024,512]{1,0:T(8,128)(2,1)S(1)}, bf16[1024,512]{1,0:T(8,128)(2,1)S(1)}, u32[]{:S(2)}, u32[]{:S(2)}) collective-permute-start(bf16[1024,512]{1,0:T(8,128)(2,1)S(1)} %get-tuple-element.80.own_ref), channel_id=1, source_target_pairs={{0,4},{4,0},{1,5},{5,1},{2,6},{6,2},{3,7},{7,3},{8,12},{12,8},{9,1... | collective-permute-start | bytes 3145736 | tf_op jit(solution)/shard_map/ppermute | solution.py:38
  210.8 15.5 %all-to-all-start.14 = ((f32[32,8,512]{2,1,0:T(8,128)}), f32[32,8,512]{2,1,0:T(8,128)S(1)}, u32[]{:S(2)}, u32[]{:S(2)}) async-start(f32[32,8,512]{2,1,0:T(8,128)} %bitcast.6), calls=%async_computation.14 | async-start | bytes 1048576 | tf_op jit(solution)/shard_map/all_to_all | solution.py:29
  214.9 1.0 copy-start.5
  214.9 1.0 copy-start.6
  243.3 17.5 %collective-permute-start.8 = (bf16[256,512]{1,0:T(8,128)(2,1)S(1)}, bf16[256,512]{1,0:T(8,128)(2,1)S(1)}, u32[]{:S(2)}, u32[]{:S(2)}) collective-permute-start(bf16[256,512]{1,0:T(8,128)(2,1)S(1)} %bitcast.30), channel_id=1, source_target_pairs={{0,4},{4,0},{1,5},{5,1},{2,6},{6,2},{3,7},{7,3},{8,12},{12,8},{9,1... | collective-permute-start | bytes 786440 | tf_op jit(solution)/shard_map/ppermute | solution.py:38

commit v14 on v13

--- a/solution.py
+++ b/solution.py
@@ -130,8 +130,8 @@
 
 
 def grad_kernel(
-    core_ref, here_ref, x_ref, y_ref, mine_ref, other_ref, vec_ref, dot_ref, mass_ref, mass2_ref,
-    *refs
+    core_ref, here_ref, x_ref, y_ref, mine_ref, other_ref, vec_ref, dot_ref, dot2_ref, mass_ref,
+    mass2_ref, *refs
 ):
     factors = refs[:-5]
     grad_q_ref, grad_r_ref, peak_ref, all_ref, masses_ref = refs[-5:]
@@ -178,8 +178,10 @@
         peak = jnp.maximum(peak, block)
     count = peak_ref.shape[0]
     peak_ref[:, 0] = jnp.broadcast_to(peak[None], (count,) + peak.shape)
-    for i in range(dot_ref.shape[0]):
-        row = dot_ref[i : i + 1]
+    dots = dot_ref[...] + dot2_ref[...]
+    kept = peak_ref.shape[1] - 1
+    for i in range(kept):
+        row = jnp.where(core == 0, dots[i : i + 1], dots[kept + i : kept + i + 1])
         peak_ref[:, 1 + i] = jnp.broadcast_to(row[None], (count,) + row.shape)
 
 
@@ -194,8 +196,11 @@
     own_r_ref[...] = grad_r_ref[:, mine]
     xq, cq, yr, cr = (vec_ref[i : i + 1] for i in range(4))
     g = vec_ref[5:6]
-    dots = [jnp.sum(peak_ref[:, 1 + i], axis=0) for i in range(log_ref.shape[0])]
-    dot = jnp.concatenate(dots, axis=1)
+    kept = peak_ref.shape[1] - 1
+    got = peak_ref[...].reshape((peak_ref.shape[0] // 2, 2) + peak_ref.shape[1:])
+    dot = jnp.concatenate(
+        [jnp.sum(got[:, member, 1 + i], axis=0) for member in range(2) for i in range(kept)], axis=1
+    )
     grad_g = -(SCALE * (xq * cr + cq * yr - 2.0 * dot)) / jnp.square(g)
     peak = jnp.maximum(
         jnp.max(jnp.max(peak_ref[:, 0], axis=0), axis=1, keepdims=True),
@@ -332,7 +337,7 @@
             pltpu.VMEM(y_emb.shape, BF16),
             pltpu.VMEM(q_factor.shape, F32),
             pltpu.VMEM(r_factor.shape, F32),
-            pltpu.SemaphoreType.DMA((4, 2)),
+            pltpu.SemaphoreType.DMA((4, 4)),
         ],
     )(core_index, x_emb, y_emb, q_factor, r_factor)
 
@@ -354,21 +359,23 @@
         (((others, 8, columns), BF16), ((8, columns), F32), ((ranks, width), F32)),
         "spread",
     )(got)
-    crosses, other_expr = lax.optimization_barrier((exchange(sent, CHIPS), swap(expr)))
+    crosses, other_expr, their_dot = lax.optimization_barrier(
+        (exchange(sent, CHIPS), swap(expr), swap(dot))
+    )
     crosses = crosses.reshape(others * 8, columns)
     own_grad = ((rows, width), F32)
     grad_q, grad_r, peak, factors, masses = on_chip(
         grad_kernel,
         (
-            tall, tall, ((cell_devices, 1 + ranks, 1, width), F32),
+            tall, tall, ((cell_devices, 1 + ranks // 2, 1, width), F32),
             ((2 * rows, columns), BF16), ((4, rows), F32),
         ),
         "grad",
         scalars=2,
-        inputs=8 + ranks,
+        inputs=9 + ranks,
     )(
         core_index, here.astype(jnp.int32)[None], x_emb, y_emb, crosses, swap(crosses), vec,
-        dot, masses, their_masses, rounded, first, second, third,
+        dot, their_dot, masses, their_masses, rounded, first, second, third,
     )
     kerns, log_g, eta, own_grad_q, own_grad_r = on_chip(
         kern_kernel,

time: 263 us -> 261 us (level)
    all_to_all x4, waiting for transfers between devices: 22 us -> 18.9 us  [exchange(): return lax.all_to_all(chunks, axes, 0, 0, tiled=False)]
    ppermute x6 -> x7, starting transfers between devices: 28.6 us -> 30.9 us  [swap(): return lax.ppermute(value, 'c', [(0, 1), (1, 0)])]
    ppermute x6 -> x7, waiting for transfers between devices: 6.21 us -> 7.03 us  [swap(): return lax.ppermute(value, 'c', [(0, 1), (1, 0)])]
  transfers between devices with their start and end apart: 13 -> 14, of which waited for: 8 -> 9; matrix products, arithmetic and copies ran while one was open for 1% -> 1% of each run, Pallas kernels for 1% -> 1%
where the time goes in v14:
time: 261 us; the launch traced here: 260 us
  blocking collectives  151 us (58%)
  starting transfers between devices  59.3 us (23%)
  waiting for transfers between devices  26 us (10%)
  Pallas kernels  18.1 us (7%)
    all_to_all x12, blocking collectives, exchange(): return lax.all_to_all(chunks, axes, 0, 0, tiled=False)  151 us
    ppermute x7, starting transfers between devices, swap(): return lax.ppermute(value, 'c', [(0, 1), (1, 0)])  30.9 us
    all_to_all x4, starting transfers between devices, exchange(): return lax.all_to_all(chunks, axes, 0, 0, tiled=False)  23.5 us
    all_to_all x4, waiting for transfers between devices, exchange(): return lax.all_to_all(chunks, axes, 0, 0, tiled=False)  18.9 us
    pallas_call x9, Pallas kernels, shards(): on_chip(next_pass, (sent_shape, v_shape) + last, 'next_pass')  9.6 us
    ppermute x7, waiting for transfers between devices, swap(): return lax.ppermute(value, 'c', [(0, 1), (1, 0)])  7.03 us
  transfers between devices with their start and end apart: 14, of which 9 were waited for; matrix products, arithmetic and copies ran while one was open for 1% of the time, Pallas kernels for 1%

profile of v14, /device:TPU:1, one launch (start us, length us, event | category | flops | bytes accessed | tf_op | source)
XLA Modules:
  0.0 260.4 jit_solution(9416413256503449495)
XLA Ops:
  2.9 3.3 %collective-permute-start = (f32[32,3,4,128]{3,2,1,0:T(4,128)S(1)}, f32[32,3,4,128]{3,2,1,0:T(4,128)S(1)}, u32[]{:S(2)}, u32[]{:S(2)}) collective-permute-start(f32[32,3,4,128]{3,2,1,0:T(4,128)S(1)} %get-tuple-element.65), channel_id=1, source_target_pairs={{0,4},{4,0},{1,5},{5,1},{2,6},{6,2},{3,7},{7,3},{8,12},{12,8},{9,1... | collective-permute-start | bytes 589832 | tf_op jit(solution)/shard_map/ppermute | solution.py:38
  8.0 9.6 %all-to-all-start = ((f32[32,3,4,128]{3,2,1,0:T(4,128)}), f32[32,3,4,128]{3,2,1,0:T(4,128)S(1)}, u32[]{:S(2)}, u32[]{:S(2)}) async-start(f32[32,3,4,128]{3,2,1,0:T(4,128)} %add.18), calls=%async_computation | async-start | bytes 393216 | tf_op jit(solution)/shard_map/all_to_all | solution.py:29
  19.0 2.4 collective-permute-start.2
  24.1 3.0 %all-to-all-done.got_ref = f32[32,3,4,128]{3,2,1,0:T(4,128)S(1)} async-done(((f32[32,3,4,128]{3,2,1,0:T(4,128)}), f32[32,3,4,128]{3,2,1,0:T(4,128)S(1)}, u32[]{:S(2)}, u32[]{:S(2)}) %all-to-all-start) | async-done | bytes 196640 | tf_op jit(solution)/shard_map/all_to_all | solution.py:29
  27.7 4.1 %all-to-all-start.1 = ((f32[4,16,128]{2,1,0:T(8,128)}), f32[4,16,128]{2,1,0:T(8,128)S(1)}, u32[]{:S(2)}, u32[]{:S(2)}) async-start(f32[4,16,128]{2,1,0:T(8,128)} %chunk.1), calls=%async_computation.1 | async-start | bytes 65536 | tf_op jit(solution)/shard_map/all_to_all | solution.py:29
  32.5 3.3 %collective-permute-start.4 = (f32[2,512]{1,0:T(2,128)S(1)}, f32[2,512]{1,0:T(2,128)S(1)}, u32[]{:S(2)}, u32[]{:S(2)}) collective-permute-start(f32[2,512]{1,0:T(2,128)S(1)} %pad_maximum_fusion.mass_ref), channel_id=1, source_target_pairs={{0,4},{4,0},{1,5},{5,1},{2,6},{6,2},{3,7},{7,3},{8,12},{12,8},{9,1... | collective-permute-start | bytes 12296 | tf_op jit(solution)/shard_map/ppermute | solution.py:38
  37.4 5.9 %all-to-all-start.2 = ((bf16[32,8,512]{2,1,0:T(8,128)(2,1)}), bf16[32,8,512]{2,1,0:T(8,128)(2,1)S(1)}, u32[]{:S(2)}, u32[]{:S(2)}) async-start(bf16[32,8,512]{2,1,0:T(8,128)(2,1)} %get-tuple-element.68), calls=%async_computation.2 | async-start | bytes 524288 | tf_op jit(solution)/shard_map/all_to_all | solution.py:29
  46.4 6.6 %all-to-all-done.2 = bf16[32,8,512]{2,1,0:T(8,128)(2,1)S(1)} async-done(((bf16[32,8,512]{2,1,0:T(8,128)(2,1)}), bf16[32,8,512]{2,1,0:T(8,128)(2,1)S(1)}, u32[]{:S(2)}, u32[]{:S(2)}) %all-to-all-start.2) | async-done | bytes 262176 | tf_op jit(solution)/shard_map/all_to_all | solution.py:29
  53.0 3.7 %collective-permute-start.7 = (bf16[256,512]{1,0:T(8,128)(2,1)S(1)}, bf16[256,512]{1,0:T(8,128)(2,1)S(1)}, u32[]{:S(2)}, u32[]{:S(2)}) collective-permute-start(bf16[256,512]{1,0:T(8,128)(2,1)S(1)} %bitcast.27), channel_id=1, source_target_pairs={{0,4},{4,0},{1,5},{5,1},{2,6},{6,2},{3,7},{7,3},{8,12},{12,8},{9,1... | collective-permute-start | bytes 786440 | tf_op jit(solution)/shard_map/ppermute | solution.py:38
  59.3 14.9 %all_to_all.80.peak_ref = f32[64,3,1,128]{3,2,1,0:T(1,128)S(1)} all-to-all(f32[64,3,1,128]{3,2,1,0:T(1,128)S(1)} %get-tuple-element.78), channel_id=1, replica_groups=mesh['y'=4,'z'=8,'c'=2,'x'=4] {'y','z','c'}, dimensions={0} | all-to-all | bytes 196608 | tf_op jit(solution)/shard_map/all_to_all | solution.py:29
  78.7 12.3 %all_to_all.81.got_ref = bf16[32,8,128]{2,1,0:T(8,128)(2,1)S(1)} all-to-all(bf16[32,8,128]{2,1,0:T(8,128)(2,1)S(1)} %first_pass.1), channel_id=1, replica_groups=mesh['y'=4,'z'=8,'c'=2,'x'=4] {'y','z'}, dimensions={0} | all-to-all | bytes 131072 | tf_op jit(solution)/shard_map/all_to_all | solution.py:29
  92.1 12.0 %all_to_all.82.got_ref = bf16[32,8,128]{2,1,0:T(8,128)(2,1)S(1)} all-to-all(bf16[32,8,128]{2,1,0:T(8,128)(2,1)S(1)} %get-tuple-element.84), channel_id=1, replica_groups=mesh['y'=4,'z'=8,'c'=2,'x'=4] {'y','z'}, dimensions={0} | all-to-all | bytes 131072 | tf_op jit(solution)/shard_map/all_to_all | solution.py:29
  105.2 12.0 %all_to_all.83.got_ref = bf16[32,8,128]{2,1,0:T(8,128)(2,1)S(1)} all-to-all(bf16[32,8,128]{2,1,0:T(8,128)(2,1)S(1)} %get-tuple-element.86), channel_id=1, replica_groups=mesh['y'=4,'z'=8,'c'=2,'x'=4] {'y','z'}, dimensions={0} | all-to-all | bytes 131072 | tf_op jit(solution)/shard_map/all_to_all | solution.py:29
  118.2 11.9 %all_to_all.84.got_ref = bf16[32,8,128]{2,1,0:T(8,128)(2,1)S(1)} all-to-all(bf16[32,8,128]{2,1,0:T(8,128)(2,1)S(1)} %get-tuple-element.88), channel_id=1, replica_groups=mesh['y'=4,'z'=8,'c'=2,'x'=4] {'y','z'}, dimensions={0} | all-to-all | bytes 131072 | tf_op jit(solution)/shard_map/all_to_all | solution.py:29
  131.2 11.8 %all_to_all.85.got_ref = bf16[32,8,128]{2,1,0:T(8,128)(2,1)S(1)} all-to-all(bf16[32,8,128]{2,1,0:T(8,128)(2,1)S(1)} %get-tuple-element.90), channel_id=1, replica_groups=mesh['y'=4,'z'=8,'c'=2,'x'=4] {'y','z'}, dimensions={0} | all-to-all | bytes 131072 | tf_op jit(solution)/shard_map/all_to_all | solution.py:29
  144.1 11.8 %all_to_all.86.got_ref = bf16[32,8,128]{2,1,0:T(8,128)(2,1)S(1)} all-to-all(bf16[32,8,128]{2,1,0:T(8,128)(2,1)S(1)} %get-tuple-element.92), channel_id=1, replica_groups=mesh['y'=4,'z'=8,'c'=2,'x'=4] {'y','z'}, dimensions={0} | all-to-all | bytes 131072 | tf_op jit(solution)/shard_map/all_to_all | solution.py:29
  157.0 11.8 %all_to_all.87.got_ref = bf16[32,8,128]{2,1,0:T(8,128)(2,1)S(1)} all-to-all(bf16[32,8,128]{2,1,0:T(8,128)(2,1)S(1)} %get-tuple-element.94), channel_id=1, replica_groups=mesh['y'=4,'z'=8,'c'=2,'x'=4] {'y','z'}, dimensions={0} | all-to-all | bytes 131072 | tf_op jit(solution)/shard_map/all_to_all | solution.py:29
  169.9 11.8 %all_to_all.88.got_ref = bf16[32,8,128]{2,1,0:T(8,128)(2,1)S(1)} all-to-all(bf16[32,8,128]{2,1,0:T(8,128)(2,1)S(1)} %get-tuple-element.96), channel_id=1, replica_groups=mesh['y'=4,'z'=8,'c'=2,'x'=4] {'y','z'}, dimensions={0} | all-to-all | bytes 131072 | tf_op jit(solution)/shard_map/all_to_all | solution.py:29
  182.8 11.9 %all_to_all.89.got_ref = bf16[32,8,128]{2,1,0:T(8,128)(2,1)S(1)} all-to-all(bf16[32,8,128]{2,1,0:T(8,128)(2,1)S(1)} %get-tuple-element.98), channel_id=1, replica_groups=mesh['y'=4,'z'=8,'c'=2,'x'=4] {'y','z'}, dimensions={0} | all-to-all | bytes 131072 | tf_op jit(solution)/shard_map/all_to_all | solution.py:29
  195.8 11.8 %all_to_all.90.got_ref = bf16[32,8,128]{2,1,0:T(8,128)(2,1)S(1)} all-to-all(bf16[32,8,128]{2,1,0:T(8,128)(2,1)S(1)} %get-tuple-element.100), channel_id=1, replica_groups=mesh['y'=4,'z'=8,'c'=2,'x'=4] {'y','z'}, dimensions={0} | all-to-all | bytes 131072 | tf_op jit(solution)/shard_map/all_to_all | solution.py:29
  209.3 3.9 %all-to-all-start.14 = ((f32[32,8,512]{2,1,0:T(8,128)}), f32[32,8,512]{2,1,0:T(8,128)S(1)}, u32[]{:S(2)}, u32[]{:S(2)}) async-start(f32[32,8,512]{2,1,0:T(8,128)} %bitcast.6), calls=%async_computation.14 | async-start | bytes 1048576 | tf_op jit(solution)/shard_map/all_to_all | solution.py:29
  215.5 9.3 %all-to-all-done.14 = f32[32,8,512]{2,1,0:T(8,128)S(1)} async-done(((f32[32,8,512]{2,1,0:T(8,128)}), f32[32,8,512]{2,1,0:T(8,128)S(1)}, u32[]{:S(2)}, u32[]{:S(2)}) %all-to-all-start.14) | async-done | bytes 524320 | tf_op jit(solution)/shard_map/all_to_all | solution.py:29
  224.9 16.9 %all_to_all.91 = bf16[32,8,512]{2,1,0:T(8,128)(2,1)S(1)} all-to-all(bf16[32,8,512]{2,1,0:T(8,128)(2,1)S(1)} %broadcast_in_dim.26), channel_id=1, replica_groups=mesh['y'=4,'z'=8,'c'=2,'x'=4] {'y','z'}, dimensions={0} | all-to-all | bytes 524288 | tf_op jit(solution)/shard_map/all_to_all | solution.py:29
  241.8 16.3 %collective-permute-start.9 = (bf16[256,512]{1,0:T(8,128)(2,1)S(1)}, bf16[256,512]{1,0:T(8,128)(2,1)S(1)}, u32[]{:S(2)}, u32[]{:S(2)}) collective-permute-start(bf16[256,512]{1,0:T(8,128)(2,1)S(1)} %bitcast.30), channel_id=1, source_target_pairs={{0,4},{4,0},{1,5},{5,1},{2,6},{6,2},{3,7},{7,3},{8,12},{12,8},{9,1... | collective-permute-start | bytes 786440 | tf_op jit(solution)/shard_map/ppermute | solution.py:38
  (64 shorter events, 37.0 us)
Async XLA Ops:
  2.9 19.7 %copy-start.2 = (bf16[512,512]{1,0:T(8,128)(2,1)S(1)}, bf16[512,512]{1,0:T(8,128)(2,1)}, u32[]{:S(2)}) copy-start(bf16[512,512]{1,0:T(8,128)(2,1)} %expr_ref.1) | copy-start | bytes 1572868
  2.9 4.4 %collective-permute-start = (f32[32,3,4,128]{3,2,1,0:T(4,128)S(1)}, f32[32,3,4,128]{3,2,1,0:T(4,128)S(1)}, u32[]{:S(2)}, u32[]{:S(2)}) collective-permute-start(f32[32,3,4,128]{3,2,1,0:T(4,128)S(1)} %get-tuple-element.65), channel_id=1, source_target_pairs={{0,4},{4,0},{1,5},{5,1},{2,6},{6,2},{3,7},{7,3},{8,12},{12,8},{9,1... | collective-permute-start | bytes 589832 | tf_op jit(solution)/shard_map/ppermute | solution.py:38
  8.0 9.6 %copy-start.3 = (bf16[2,512,128]{2,1,0:T(8,128)(2,1)S(1)}, bf16[2,512,128]{2,1,0:T(8,128)(2,1)}, u32[]{:S(2)}) copy-start(bf16[2,512,128]{2,1,0:T(8,128)(2,1)} %get-tuple-element.66.refs_0_) | copy-start | bytes 786436
  8.0 19.0 %all-to-all-start = ((f32[32,3,4,128]{3,2,1,0:T(4,128)}), f32[32,3,4,128]{3,2,1,0:T(4,128)S(1)}, u32[]{:S(2)}, u32[]{:S(2)}) async-start(f32[32,3,4,128]{3,2,1,0:T(4,128)} %add.18), calls=%async_computation | async-start | bytes 393216 | tf_op jit(solution)/shard_map/all_to_all | solution.py:29
  17.6 9.4 %copy-start.4 = (f32[128]{0:T(128)S(1)}, f32[128]{0:T(128)}, u32[]{:S(2)}) copy-start(f32[128]{0:T(128)} %param.12) | copy-start | bytes 1540
  17.7 19.0 %collective-permute-start.1 = (bf16[2,512,128]{2,1,0:T(8,128)(2,1)S(1)}, bf16[2,512,128]{2,1,0:T(8,128)(2,1)S(1)}, u32[]{:S(2)}, u32[]{:S(2)}) collective-permute-start(bf16[2,512,128]{2,1,0:T(8,128)(2,1)S(1)} %copy-done.3), channel_id=1, source_target_pairs={{0,1},{1,2},{2,3},{3,0},{4,5},{5,6},{6,7},{7,4},{8,9},{9,10},{10,1... | collective-permute-start | bytes 786440 | tf_op jit(solution)/shard_map/ppermute | solution.py:345
  19.0 17.7 %collective-permute-start.2 = (bf16[2,512,128]{2,1,0:T(8,128)(2,1)S(1)}, bf16[2,512,128]{2,1,0:T(8,128)(2,1)S(1)}, u32[]{:S(2)}, u32[]{:S(2)}) collective-permute-start(bf16[2,512,128]{2,1,0:T(8,128)(2,1)S(1)} %copy-done.3), channel_id=1, source_target_pairs={{0,2},{1,3},{2,0},{3,1},{4,6},{5,7},{6,4},{7,5},{8,10},{9,11},{10,... | collective-permute-start | bytes 786440 | tf_op jit(solution)/shard_map/ppermute | solution.py:345
  21.4 15.3 %collective-permute-start.3 = (bf16[2,512,128]{2,1,0:T(8,128)(2,1)S(1)}, bf16[2,512,128]{2,1,0:T(8,128)(2,1)S(1)}, u32[]{:S(2)}, u32[]{:S(2)}) collective-permute-start(bf16[2,512,128]{2,1,0:T(8,128)(2,1)S(1)} %copy-done.3), channel_id=1, source_target_pairs={{0,3},{1,0},{2,1},{3,2},{4,7},{5,4},{6,5},{7,6},{8,11},{9,8},{10,9... | collective-permute-start | bytes 786440 | tf_op jit(solution)/shard_map/ppermute | solution.py:345
  22.6 23.0 %collective-permute-start.5 = (bf16[512,512]{1,0:T(8,128)(2,1)S(1)}, bf16[512,512]{1,0:T(8,128)(2,1)S(1)}, u32[]{:S(2)}, u32[]{:S(2)}) collective-permute-start(bf16[512,512]{1,0:T(8,128)(2,1)S(1)} %copy-done.2), channel_id=1, source_target_pairs={{0,4},{4,0},{1,5},{5,1},{2,6},{6,2},{3,7},{7,3},{8,12},{12,8},{9,1... | collective-permute-start | bytes 1572872 | tf_op jit(solution)/shard_map/ppermute | solution.py:38
  27.7 4.2 %copy-start.8 = (f32[512]{0:T(512)S(1)}, f32[512]{0:T(512)}, u32[]{:S(2)}) copy-start(f32[512]{0:T(512)} %param.13) | copy-start | bytes 6148
  27.7 9.0 %all-to-all-start.1 = ((f32[4,16,128]{2,1,0:T(8,128)}), f32[4,16,128]{2,1,0:T(8,128)S(1)}, u32[]{:S(2)}, u32[]{:S(2)}) async-start(f32[4,16,128]{2,1,0:T(8,128)} %chunk.1), calls=%async_computation.1 | async-start | bytes 65536 | tf_op jit(solution)/shard_map/all_to_all | solution.py:29
  31.8 0.7 copy-start.7
  32.5 4.1 %collective-permute-start.4 = (f32[2,512]{1,0:T(2,128)S(1)}, f32[2,512]{1,0:T(2,128)S(1)}, u32[]{:S(2)}, u32[]{:S(2)}) collective-permute-start(f32[2,512]{1,0:T(2,128)S(1)} %pad_maximum_fusion.mass_ref), channel_id=1, source_target_pairs={{0,4},{4,0},{1,5},{5,1},{2,6},{6,2},{3,7},{7,3},{8,12},{12,8},{9,1... | collective-permute-start | bytes 12296 | tf_op jit(solution)/shard_map/ppermute | solution.py:38
  37.4 20.5 %copy-start = (bf16[512,256]{1,0:T(8,128)(2,1)S(1)}, bf16[512,256]{1,0:T(8,128)(2,1)}, u32[]{:S(2)}) copy-start(bf16[512,256]{1,0:T(8,128)(2,1)} %x_ref.1) | copy-start | bytes 786436
  37.4 20.5 %copy-start.1 = (bf16[512,256]{1,0:T(8,128)(2,1)S(1)}, bf16[512,256]{1,0:T(8,128)(2,1)}, u32[]{:S(2)}) copy-start(bf16[512,256]{1,0:T(8,128)(2,1)} %y_ref.1) | copy-start | bytes 786436
  37.4 15.6 %all-to-all-start.2 = ((bf16[32,8,512]{2,1,0:T(8,128)(2,1)}), bf16[32,8,512]{2,1,0:T(8,128)(2,1)S(1)}, u32[]{:S(2)}, u32[]{:S(2)}) async-start(bf16[32,8,512]{2,1,0:T(8,128)(2,1)} %get-tuple-element.68), calls=%async_computation.2 | async-start | bytes 524288 | tf_op jit(solution)/shard_map/all_to_all | solution.py:29
  43.3 3.1 %collective-permute-start.6 = (f32[4,128]{1,0:T(4,128)S(1)}, f32[4,128]{1,0:T(4,128)S(1)}, u32[]{:S(2)}, u32[]{:S(2)}) collective-permute-start(f32[4,128]{1,0:T(4,128)S(1)} %get-tuple-element.69.dot_ref), channel_id=1, source_target_pairs={{0,4},{4,0},{1,5},{5,1},{2,6},{6,2},{3,7},{7,3},{8,12},{12,8},{9,1... | collective-permute-start | bytes 6152 | tf_op jit(solution)/shard_map/ppermute | solution.py:38
  53.0 4.9 %collective-permute-start.7 = (bf16[256,512]{1,0:T(8,128)(2,1)S(1)}, bf16[256,512]{1,0:T(8,128)(2,1)S(1)}, u32[]{:S(2)}, u32[]{:S(2)}) collective-permute-start(bf16[256,512]{1,0:T(8,128)(2,1)S(1)} %bitcast.27), channel_id=1, source_target_pairs={{0,4},{4,0},{1,5},{5,1},{2,6},{6,2},{3,7},{7,3},{8,12},{12,8},{9,1... | collective-permute-start | bytes 786440 | tf_op jit(solution)/shard_map/ppermute | solution.py:38
  74.9 2.8 %collective-permute-start.8 = (bf16[1024,512]{1,0:T(8,128)(2,1)S(1)}, bf16[1024,512]{1,0:T(8,128)(2,1)S(1)}, u32[]{:S(2)}, u32[]{:S(2)}) collective-permute-start(bf16[1024,512]{1,0:T(8,128)(2,1)S(1)} %get-tuple-element.82.own_ref), channel_id=1, source_target_pairs={{0,4},{4,0},{1,5},{5,1},{2,6},{6,2},{3,7},{7,3},{8,12},{12,8},{9,1... | collective-permute-start | bytes 3145736 | tf_op jit(solution)/shard_map/ppermute | solution.py:38
  209.3 15.5 %all-to-all-start.14 = ((f32[32,8,512]{2,1,0:T(8,128)}), f32[32,8,512]{2,1,0:T(8,128)S(1)}, u32[]{:S(2)}, u32[]{:S(2)}) async-start(f32[32,8,512]{2,1,0:T(8,128)} %bitcast.6), calls=%async_computation.14 | async-start | bytes 1048576 | tf_op jit(solution)/shard_map/all_to_all | solution.py:29
  213.5 1.0 copy-start.5
  213.5 1.0 copy-start.6
  241.8 17.5 %collective-permute-start.9 = (bf16[256,512]{1,0:T(8,128)(2,1)S(1)}, bf16[256,512]{1,0:T(8,128)(2,1)S(1)}, u32[]{:S(2)}, u32[]{:S(2)}) collective-permute-start(bf16[256,512]{1,0:T(8,128)(2,1)S(1)} %bitcast.30), channel_id=1, source_target_pairs={{0,4},{4,0},{1,5},{5,1},{2,6},{6,2},{3,7},{7,3},{8,12},{12,8},{9,1... | collective-permute-start | bytes 786440 | tf_op jit(solution)/shard_map/ppermute | solution.py:38

commit v15 on v14

--- a/solution.py
+++ b/solution.py
@@ -256,9 +256,27 @@
     sent_ref[...] = jnp.broadcast_to(part[None], sent_ref.shape)
 
 
-def first_pass(mass_ref, own_ref, other_ref, sent_ref):
-    ones = jnp.ones(sent_ref.shape[1:], F32)
-    send_columns(ones, mass_ref, own_ref, other_ref, sent_ref)
+def first_columns(member, mass_ref, kern_ref):
+    rows, columns = kern_ref.shape[0] // 2, kern_ref.shape[1]
+    ones = jnp.ones((1, columns), BF16)
+    parts = []
+    for side in range(2):
+        kern = kern_ref[pl.ds(side * rows, rows), :]
+        s = lax.dot_general(ones, kern, (((1,), (1,)), ((), ())), preferred_element_type=F32)
+        row = 2 * member + side
+        u = jnp.exp(POWER * jnp.log(mass_ref[row : row + 1] / s))
+        part = sum_rows(jnp.dot(stack3(u), kern, preferred_element_type=F32))
+        parts += in_rows(part, columns // 128)
+    return jnp.concatenate(parts, axis=0)
+
+
+def first_own(mass_ref, kern_ref, part_ref):
+    part_ref[...] = first_columns(0, mass_ref, kern_ref)
+
+
+def first_other(mass_ref, kern_ref, part_ref, sent_ref):
+    part = (part_ref[...] + first_columns(1, mass_ref, kern_ref)).astype(sent_ref.dtype)
+    sent_ref[...] = jnp.broadcast_to(part[None], sent_ref.shape)
 
 
 def next_pass(
@@ -390,7 +408,8 @@
     sent_shape = ((others, 2 * ranks, width), BF16)
     u_shape = ((4, rows), F32)
     v_shape = ((2 * ranks, width), F32)
-    sent = on_chip(first_pass, (sent_shape,), "first_pass")(masses, kerns, theirs)[0]
+    part = on_chip(first_own, (v_shape,), "first_own")(masses, kerns)[0]
+    sent = on_chip(first_other, (sent_shape,), "first_other")(masses, theirs, part)[0]
     v = jnp.ones(v_shape[0], F32)
     for step in range(1, PASSES):
         last = (u_shape,) if step == PASSES - 1 else ()

time: 261 us -> 261 us (level)
  no operation moved by 1% of the time
where the time goes in v15:
time: 261 us; the launch traced here: 260 us
  blocking collectives  151 us (58%)
  starting transfers between devices  59.3 us (23%)
  waiting for transfers between devices  25.2 us (10%)
  Pallas kernels  18.6 us (7%)
    all_to_all x12, blocking collectives, exchange(): return lax.all_to_all(chunks, axes, 0, 0, tiled=False)  151 us
    ppermute x7, starting transfers between devices, swap(): return lax.ppermute(value, 'c', [(0, 1), (1, 0)])  30.9 us
    all_to_all x4, starting transfers between devices, exchange(): return lax.all_to_all(chunks, axes, 0, 0, tiled=False)  23.5 us
    all_to_all x4, waiting for transfers between devices, exchange(): return lax.all_to_all(chunks, axes, 0, 0, tiled=False)  18.9 us
    pallas_call x9, Pallas kernels, shards(): on_chip(next_pass, (sent_shape, v_shape) + last, 'next_pass')  9.6 us
    ppermute x7, waiting for transfers between devices, swap(): return lax.ppermute(value, 'c', [(0, 1), (1, 0)])  6.27 us
  transfers between devices with their start and end apart: 14, of which 9 were waited for; matrix products, arithmetic and copies ran while one was open for 1% of the time, Pallas kernels for 1%

profile of v15, /device:TPU:1, one launch (start us, length us, event | category | flops | bytes accessed | tf_op | source)
XLA Modules:
  0.0 260.1 jit_solution(4907483406161515017)
XLA Ops:
  2.9 3.3 %collective-permute-start = (f32[32,3,4,128]{3,2,1,0:T(4,128)S(1)}, f32[32,3,4,128]{3,2,1,0:T(4,128)S(1)}, u32[]{:S(2)}, u32[]{:S(2)}) collective-permute-start(f32[32,3,4,128]{3,2,1,0:T(4,128)S(1)} %get-tuple-element.65), channel_id=1, source_target_pairs={{0,4},{4,0},{1,5},{5,1},{2,6},{6,2},{3,7},{7,3},{8,12},{12,8},{9,1... | collective-permute-start | bytes 589832 | tf_op jit(solution)/shard_map/ppermute | solution.py:38
  8.0 9.6 %all-to-all-start = ((f32[32,3,4,128]{3,2,1,0:T(4,128)}), f32[32,3,4,128]{3,2,1,0:T(4,128)S(1)}, u32[]{:S(2)}, u32[]{:S(2)}) async-start(f32[32,3,4,128]{3,2,1,0:T(4,128)} %add.18), calls=%async_computation | async-start | bytes 393216 | tf_op jit(solution)/shard_map/all_to_all | solution.py:29
  19.0 2.4 collective-permute-start.2
  24.1 3.0 %all-to-all-done.got_ref = f32[32,3,4,128]{3,2,1,0:T(4,128)S(1)} async-done(((f32[32,3,4,128]{3,2,1,0:T(4,128)}), f32[32,3,4,128]{3,2,1,0:T(4,128)S(1)}, u32[]{:S(2)}, u32[]{:S(2)}) %all-to-all-start) | async-done | bytes 196640 | tf_op jit(solution)/shard_map/all_to_all | solution.py:29
  27.7 4.1 %all-to-all-start.1 = ((f32[4,16,128]{2,1,0:T(8,128)}), f32[4,16,128]{2,1,0:T(8,128)S(1)}, u32[]{:S(2)}, u32[]{:S(2)}) async-start(f32[4,16,128]{2,1,0:T(8,128)} %chunk.1), calls=%async_computation.1 | async-start | bytes 65536 | tf_op jit(solution)/shard_map/all_to_all | solution.py:29
  32.5 3.3 %collective-permute-start.4 = (f32[2,512]{1,0:T(2,128)S(1)}, f32[2,512]{1,0:T(2,128)S(1)}, u32[]{:S(2)}, u32[]{:S(2)}) collective-permute-start(f32[2,512]{1,0:T(2,128)S(1)} %pad_maximum_fusion.mass_ref), channel_id=1, source_target_pairs={{0,4},{4,0},{1,5},{5,1},{2,6},{6,2},{3,7},{7,3},{8,12},{12,8},{9,1... | collective-permute-start | bytes 12296 | tf_op jit(solution)/shard_map/ppermute | solution.py:38
  37.4 5.9 %all-to-all-start.2 = ((bf16[32,8,512]{2,1,0:T(8,128)(2,1)}), bf16[32,8,512]{2,1,0:T(8,128)(2,1)S(1)}, u32[]{:S(2)}, u32[]{:S(2)}) async-start(bf16[32,8,512]{2,1,0:T(8,128)(2,1)} %get-tuple-element.68), calls=%async_computation.2 | async-start | bytes 524288 | tf_op jit(solution)/shard_map/all_to_all | solution.py:29
  46.4 6.6 %all-to-all-done.2 = bf16[32,8,512]{2,1,0:T(8,128)(2,1)S(1)} async-done(((bf16[32,8,512]{2,1,0:T(8,128)(2,1)}), bf16[32,8,512]{2,1,0:T(8,128)(2,1)S(1)}, u32[]{:S(2)}, u32[]{:S(2)}) %all-to-all-start.2) | async-done | bytes 262176 | tf_op jit(solution)/shard_map/all_to_all | solution.py:29
  53.0 3.7 %collective-permute-start.7 = (bf16[256,512]{1,0:T(8,128)(2,1)S(1)}, bf16[256,512]{1,0:T(8,128)(2,1)S(1)}, u32[]{:S(2)}, u32[]{:S(2)}) collective-permute-start(bf16[256,512]{1,0:T(8,128)(2,1)S(1)} %bitcast.27), channel_id=1, source_target_pairs={{0,4},{4,0},{1,5},{5,1},{2,6},{6,2},{3,7},{7,3},{8,12},{12,8},{9,1... | collective-permute-start | bytes 786440 | tf_op jit(solution)/shard_map/ppermute | solution.py:38
  59.3 14.9 %all_to_all.80.peak_ref = f32[64,3,1,128]{3,2,1,0:T(1,128)S(1)} all-to-all(f32[64,3,1,128]{3,2,1,0:T(1,128)S(1)} %get-tuple-element.78), channel_id=1, replica_groups=mesh['y'=4,'z'=8,'c'=2,'x'=4] {'y','z','c'}, dimensions={0} | all-to-all | bytes 196608 | tf_op jit(solution)/shard_map/all_to_all | solution.py:29
  78.5 12.3 %all_to_all.81.got_ref = bf16[32,8,128]{2,1,0:T(8,128)(2,1)S(1)} all-to-all(bf16[32,8,128]{2,1,0:T(8,128)(2,1)S(1)} %first_other.1), channel_id=1, replica_groups=mesh['y'=4,'z'=8,'c'=2,'x'=4] {'y','z'}, dimensions={0} | all-to-all | bytes 131072 | tf_op jit(solution)/shard_map/all_to_all | solution.py:29
  91.8 12.0 %all_to_all.82.got_ref = bf16[32,8,128]{2,1,0:T(8,128)(2,1)S(1)} all-to-all(bf16[32,8,128]{2,1,0:T(8,128)(2,1)S(1)} %get-tuple-element.84), channel_id=1, replica_groups=mesh['y'=4,'z'=8,'c'=2,'x'=4] {'y','z'}, dimensions={0} | all-to-all | bytes 131072 | tf_op jit(solution)/shard_map/all_to_all | solution.py:29
  104.9 12.0 %all_to_all.83.got_ref = bf16[32,8,128]{2,1,0:T(8,128)(2,1)S(1)} all-to-all(bf16[32,8,128]{2,1,0:T(8,128)(2,1)S(1)} %get-tuple-element.86), channel_id=1, replica_groups=mesh['y'=4,'z'=8,'c'=2,'x'=4] {'y','z'}, dimensions={0} | all-to-all | bytes 131072 | tf_op jit(solution)/shard_map/all_to_all | solution.py:29
  117.9 11.9 %all_to_all.84.got_ref = bf16[32,8,128]{2,1,0:T(8,128)(2,1)S(1)} all-to-all(bf16[32,8,128]{2,1,0:T(8,128)(2,1)S(1)} %get-tuple-element.88), channel_id=1, replica_groups=mesh['y'=4,'z'=8,'c'=2,'x'=4] {'y','z'}, dimensions={0} | all-to-all | bytes 131072 | tf_op jit(solution)/shard_map/all_to_all | solution.py:29
  131.0 11.8 %all_to_all.85.got_ref = bf16[32,8,128]{2,1,0:T(8,128)(2,1)S(1)} all-to-all(bf16[32,8,128]{2,1,0:T(8,128)(2,1)S(1)} %get-tuple-element.90), channel_id=1, replica_groups=mesh['y'=4,'z'=8,'c'=2,'x'=4] {'y','z'}, dimensions={0} | all-to-all | bytes 131072 | tf_op jit(solution)/shard_map/all_to_all | solution.py:29
  143.9 11.8 %all_to_all.86.got_ref = bf16[32,8,128]{2,1,0:T(8,128)(2,1)S(1)} all-to-all(bf16[32,8,128]{2,1,0:T(8,128)(2,1)S(1)} %get-tuple-element.92), channel_id=1, replica_groups=mesh['y'=4,'z'=8,'c'=2,'x'=4] {'y','z'}, dimensions={0} | all-to-all | bytes 131072 | tf_op jit(solution)/shard_map/all_to_all | solution.py:29
  156.8 11.8 %all_to_all.87.got_ref = bf16[32,8,128]{2,1,0:T(8,128)(2,1)S(1)} all-to-all(bf16[32,8,128]{2,1,0:T(8,128)(2,1)S(1)} %get-tuple-element.94), channel_id=1, replica_groups=mesh['y'=4,'z'=8,'c'=2,'x'=4] {'y','z'}, dimensions={0} | all-to-all | bytes 131072 | tf_op jit(solution)/shard_map/all_to_all | solution.py:29
  169.7 11.8 %all_to_all.88.got_ref = bf16[32,8,128]{2,1,0:T(8,128)(2,1)S(1)} all-to-all(bf16[32,8,128]{2,1,0:T(8,128)(2,1)S(1)} %get-tuple-element.96), channel_id=1, replica_groups=mesh['y'=4,'z'=8,'c'=2,'x'=4] {'y','z'}, dimensions={0} | all-to-all | bytes 131072 | tf_op jit(solution)/shard_map/all_to_all | solution.py:29
  182.6 11.9 %all_to_all.89.got_ref = bf16[32,8,128]{2,1,0:T(8,128)(2,1)S(1)} all-to-all(bf16[32,8,128]{2,1,0:T(8,128)(2,1)S(1)} %get-tuple-element.98), channel_id=1, replica_groups=mesh['y'=4,'z'=8,'c'=2,'x'=4] {'y','z'}, dimensions={0} | all-to-all | bytes 131072 | tf_op jit(solution)/shard_map/all_to_all | solution.py:29
  195.5 11.8 %all_to_all.90.got_ref = bf16[32,8,128]{2,1,0:T(8,128)(2,1)S(1)} all-to-all(bf16[32,8,128]{2,1,0:T(8,128)(2,1)S(1)} %get-tuple-element.100), channel_id=1, replica_groups=mesh['y'=4,'z'=8,'c'=2,'x'=4] {'y','z'}, dimensions={0} | all-to-all | bytes 131072 | tf_op jit(solution)/shard_map/all_to_all | solution.py:29
  209.1 3.9 %all-to-all-start.14 = ((f32[32,8,512]{2,1,0:T(8,128)}), f32[32,8,512]{2,1,0:T(8,128)S(1)}, u32[]{:S(2)}, u32[]{:S(2)}) async-start(f32[32,8,512]{2,1,0:T(8,128)} %bitcast.6), calls=%async_computation.14 | async-start | bytes 1048576 | tf_op jit(solution)/shard_map/all_to_all | solution.py:29
  215.3 9.3 %all-to-all-done.14 = f32[32,8,512]{2,1,0:T(8,128)S(1)} async-done(((f32[32,8,512]{2,1,0:T(8,128)}), f32[32,8,512]{2,1,0:T(8,128)S(1)}, u32[]{:S(2)}, u32[]{:S(2)}) %all-to-all-start.14) | async-done | bytes 524320 | tf_op jit(solution)/shard_map/all_to_all | solution.py:29
  224.7 16.9 %all_to_all.91 = bf16[32,8,512]{2,1,0:T(8,128)(2,1)S(1)} all-to-all(bf16[32,8,512]{2,1,0:T(8,128)(2,1)S(1)} %broadcast_in_dim.26), channel_id=1, replica_groups=mesh['y'=4,'z'=8,'c'=2,'x'=4] {'y','z'}, dimensions={0} | all-to-all | bytes 524288 | tf_op jit(solution)/shard_map/all_to_all | solution.py:29
  241.5 16.3 %collective-permute-start.9 = (bf16[256,512]{1,0:T(8,128)(2,1)S(1)}, bf16[256,512]{1,0:T(8,128)(2,1)S(1)}, u32[]{:S(2)}, u32[]{:S(2)}) collective-permute-start(bf16[256,512]{1,0:T(8,128)(2,1)S(1)} %bitcast.30), channel_id=1, source_target_pairs={{0,4},{4,0},{1,5},{5,1},{2,6},{6,2},{3,7},{7,3},{8,12},{12,8},{9,1... | collective-permute-start | bytes 786440 | tf_op jit(solution)/shard_map/ppermute | solution.py:38
  (65 shorter events, 36.7 us)
Async XLA Ops:
  2.9 19.7 %copy-start.2 = (bf16[512,512]{1,0:T(8,128)(2,1)S(1)}, bf16[512,512]{1,0:T(8,128)(2,1)}, u32[]{:S(2)}) copy-start(bf16[512,512]{1,0:T(8,128)(2,1)} %expr_ref.1) | copy-start | bytes 1572868
  2.9 4.4 %collective-permute-start = (f32[32,3,4,128]{3,2,1,0:T(4,128)S(1)}, f32[32,3,4,128]{3,2,1,0:T(4,128)S(1)}, u32[]{:S(2)}, u32[]{:S(2)}) collective-permute-start(f32[32,3,4,128]{3,2,1,0:T(4,128)S(1)} %get-tuple-element.65), channel_id=1, source_target_pairs={{0,4},{4,0},{1,5},{5,1},{2,6},{6,2},{3,7},{7,3},{8,12},{12,8},{9,1... | collective-permute-start | bytes 589832 | tf_op jit(solution)/shard_map/ppermute | solution.py:38
  8.0 9.6 %copy-start.3 = (bf16[2,512,128]{2,1,0:T(8,128)(2,1)S(1)}, bf16[2,512,128]{2,1,0:T(8,128)(2,1)}, u32[]{:S(2)}) copy-start(bf16[2,512,128]{2,1,0:T(8,128)(2,1)} %get-tuple-element.66.refs_0_) | copy-start | bytes 786436
  8.0 19.0 %all-to-all-start = ((f32[32,3,4,128]{3,2,1,0:T(4,128)}), f32[32,3,4,128]{3,2,1,0:T(4,128)S(1)}, u32[]{:S(2)}, u32[]{:S(2)}) async-start(f32[32,3,4,128]{3,2,1,0:T(4,128)} %add.18), calls=%async_computation | async-start | bytes 393216 | tf_op jit(solution)/shard_map/all_to_all | solution.py:29
  17.6 9.4 %copy-start.4 = (f32[128]{0:T(128)S(1)}, f32[128]{0:T(128)}, u32[]{:S(2)}) copy-start(f32[128]{0:T(128)} %param.12) | copy-start | bytes 1540
  17.7 19.0 %collective-permute-start.1 = (bf16[2,512,128]{2,1,0:T(8,128)(2,1)S(1)}, bf16[2,512,128]{2,1,0:T(8,128)(2,1)S(1)}, u32[]{:S(2)}, u32[]{:S(2)}) collective-permute-start(bf16[2,512,128]{2,1,0:T(8,128)(2,1)S(1)} %copy-done.3), channel_id=1, source_target_pairs={{0,1},{1,2},{2,3},{3,0},{4,5},{5,6},{6,7},{7,4},{8,9},{9,10},{10,1... | collective-permute-start | bytes 786440 | tf_op jit(solution)/shard_map/ppermute | solution.py:363
  19.0 17.7 %collective-permute-start.2 = (bf16[2,512,128]{2,1,0:T(8,128)(2,1)S(1)}, bf16[2,512,128]{2,1,0:T(8,128)(2,1)S(1)}, u32[]{:S(2)}, u32[]{:S(2)}) collective-permute-start(bf16[2,512,128]{2,1,0:T(8,128)(2,1)S(1)} %copy-done.3), channel_id=1, source_target_pairs={{0,2},{1,3},{2,0},{3,1},{4,6},{5,7},{6,4},{7,5},{8,10},{9,11},{10,... | collective-permute-start | bytes 786440 | tf_op jit(solution)/shard_map/ppermute | solution.py:363
  21.4 15.3 %collective-permute-start.3 = (bf16[2,512,128]{2,1,0:T(8,128)(2,1)S(1)}, bf16[2,512,128]{2,1,0:T(8,128)(2,1)S(1)}, u32[]{:S(2)}, u32[]{:S(2)}) collective-permute-start(bf16[2,512,128]{2,1,0:T(8,128)(2,1)S(1)} %copy-done.3), channel_id=1, source_target_pairs={{0,3},{1,0},{2,1},{3,2},{4,7},{5,4},{6,5},{7,6},{8,11},{9,8},{10,9... | collective-permute-start | bytes 786440 | tf_op jit(solution)/shard_map/ppermute | solution.py:363
  22.6 23.0 %collective-permute-start.5 = (bf16[512,512]{1,0:T(8,128)(2,1)S(1)}, bf16[512,512]{1,0:T(8,128)(2,1)S(1)}, u32[]{:S(2)}, u32[]{:S(2)}) collective-permute-start(bf16[512,512]{1,0:T(8,128)(2,1)S(1)} %copy-done.2), channel_id=1, source_target_pairs={{0,4},{4,0},{1,5},{5,1},{2,6},{6,2},{3,7},{7,3},{8,12},{12,8},{9,1... | collective-permute-start | bytes 1572872 | tf_op jit(solution)/shard_map/ppermute | solution.py:38
  27.7 4.2 %copy-start.8 = (f32[512]{0:T(512)S(1)}, f32[512]{0:T(512)}, u32[]{:S(2)}) copy-start(f32[512]{0:T(512)} %param.13) | copy-start | bytes 6148
  27.7 9.0 %all-to-all-start.1 = ((f32[4,16,128]{2,1,0:T(8,128)}), f32[4,16,128]{2,1,0:T(8,128)S(1)}, u32[]{:S(2)}, u32[]{:S(2)}) async-start(f32[4,16,128]{2,1,0:T(8,128)} %chunk.1), calls=%async_computation.1 | async-start | bytes 65536 | tf_op jit(solution)/shard_map/all_to_all | solution.py:29
  31.8 0.7 copy-start.7
  32.5 4.1 %collective-permute-start.4 = (f32[2,512]{1,0:T(2,128)S(1)}, f32[2,512]{1,0:T(2,128)S(1)}, u32[]{:S(2)}, u32[]{:S(2)}) collective-permute-start(f32[2,512]{1,0:T(2,128)S(1)} %pad_maximum_fusion.mass_ref), channel_id=1, source_target_pairs={{0,4},{4,0},{1,5},{5,1},{2,6},{6,2},{3,7},{7,3},{8,12},{12,8},{9,1... | collective-permute-start | bytes 12296 | tf_op jit(solution)/shard_map/ppermute | solution.py:38
  37.4 20.5 %copy-start = (bf16[512,256]{1,0:T(8,128)(2,1)S(1)}, bf16[512,256]{1,0:T(8,128)(2,1)}, u32[]{:S(2)}) copy-start(bf16[512,256]{1,0:T(8,128)(2,1)} %x_ref.1) | copy-start | bytes 786436
  37.4 20.5 %copy-start.1 = (bf16[512,256]{1,0:T(8,128)(2,1)S(1)}, bf16[512,256]{1,0:T(8,128)(2,1)}, u32[]{:S(2)}) copy-start(bf16[512,256]{1,0:T(8,128)(2,1)} %y_ref.1) | copy-start | bytes 786436
  37.4 15.6 %all-to-all-start.2 = ((bf16[32,8,512]{2,1,0:T(8,128)(2,1)}), bf16[32,8,512]{2,1,0:T(8,128)(2,1)S(1)}, u32[]{:S(2)}, u32[]{:S(2)}) async-start(bf16[32,8,512]{2,1,0:T(8,128)(2,1)} %get-tuple-element.68), calls=%async_computation.2 | async-start | bytes 524288 | tf_op jit(solution)/shard_map/all_to_all | solution.py:29
  43.3 3.1 %collective-permute-start.6 = (f32[4,128]{1,0:T(4,128)S(1)}, f32[4,128]{1,0:T(4,128)S(1)}, u32[]{:S(2)}, u32[]{:S(2)}) collective-permute-start(f32[4,128]{1,0:T(4,128)S(1)} %get-tuple-element.69.dot_ref), channel_id=1, source_target_pairs={{0,4},{4,0},{1,5},{5,1},{2,6},{6,2},{3,7},{7,3},{8,12},{12,8},{9,1... | collective-permute-start | bytes 6152 | tf_op jit(solution)/shard_map/ppermute | solution.py:38
  53.0 4.9 %collective-permute-start.7 = (bf16[256,512]{1,0:T(8,128)(2,1)S(1)}, bf16[256,512]{1,0:T(8,128)(2,1)S(1)}, u32[]{:S(2)}, u32[]{:S(2)}) collective-permute-start(bf16[256,512]{1,0:T(8,128)(2,1)S(1)} %bitcast.27), channel_id=1, source_target_pairs={{0,4},{4,0},{1,5},{5,1},{2,6},{6,2},{3,7},{7,3},{8,12},{12,8},{9,1... | collective-permute-start | bytes 786440 | tf_op jit(solution)/shard_map/ppermute | solution.py:38
  74.9 2.8 %collective-permute-start.8 = (bf16[1024,512]{1,0:T(8,128)(2,1)S(1)}, bf16[1024,512]{1,0:T(8,128)(2,1)S(1)}, u32[]{:S(2)}, u32[]{:S(2)}) collective-permute-start(bf16[1024,512]{1,0:T(8,128)(2,1)S(1)} %get-tuple-element.82.kern_ref.own_ref), channel_id=1, source_target_pairs={{0,4},{4,0},{1,5},{5,1},{2,6},{6,2},{3,7},{7,3},{8,12},{12,8},{9,1... | collective-permute-start | bytes 3145736 | tf_op jit(solution)/shard_map/ppermute | solution.py:38
  209.1 15.5 %all-to-all-start.14 = ((f32[32,8,512]{2,1,0:T(8,128)}), f32[32,8,512]{2,1,0:T(8,128)S(1)}, u32[]{:S(2)}, u32[]{:S(2)}) async-start(f32[32,8,512]{2,1,0:T(8,128)} %bitcast.6), calls=%async_computation.14 | async-start | bytes 1048576 | tf_op jit(solution)/shard_map/all_to_all | solution.py:29
  213.2 1.0 copy-start.5
  213.3 1.0 copy-start.6
  241.5 17.5 %collective-permute-start.9 = (bf16[256,512]{1,0:T(8,128)(2,1)S(1)}, bf16[256,512]{1,0:T(8,128)(2,1)S(1)}, u32[]{:S(2)}, u32[]{:S(2)}) collective-permute-start(bf16[256,512]{1,0:T(8,128)(2,1)S(1)} %bitcast.30), channel_id=1, source_target_pairs={{0,4},{4,0},{1,5},{5,1},{2,6},{6,2},{3,7},{7,3},{8,12},{12,8},{9,1... | collective-permute-start | bytes 786440 | tf_op jit(solution)/shard_map/ppermute | solution.py:38

commit v16 on v15

--- a/solution.py
+++ b/solution.py
@@ -369,16 +369,16 @@
         exchange(outgoing, CHIPS), g_weights[None]
     )[0]
     masses = jnp.stack([a_mass, b_mass])
-    got, first, second, third, their_masses = lax.optimization_barrier(
-        (exchange(sent, "x"), from_shift(1), from_shift(2), from_shift(3), swap(masses))
+    got, first, second, third = lax.optimization_barrier(
+        (exchange(sent, "x"), from_shift(1), from_shift(2), from_shift(3))
     )
     sent, vec, dot = on_chip(
         spread_kernel,
         (((others, 8, columns), BF16), ((8, columns), F32), ((ranks, width), F32)),
         "spread",
     )(got)
-    crosses, other_expr, their_dot = lax.optimization_barrier(
-        (exchange(sent, CHIPS), swap(expr), swap(dot))
+    crosses, other_expr, their_dot, their_masses = lax.optimization_barrier(
+        (exchange(sent, CHIPS), swap(expr), swap(dot), swap(masses))
     )
     crosses = crosses.reshape(others * 8, columns)
     own_grad = ((rows, width), F32)

time: 261 us -> 261 us (level)
  transfers between devices with their start and end apart: 14 -> 14, of which waited for: 9 -> 10; matrix products, arithmetic and copies ran while one was open for 1% -> 1% of each run, Pallas kernels for 1% -> 1%
where the time goes in v16:
time: 261 us; the launch traced here: 260 us
  blocking collectives  150 us (57%)
  starting transfers between devices  59 us (23%)
  waiting for transfers between devices  25.8 us (10%)
  Pallas kernels  18.6 us (7%)
    all_to_all x12, blocking collectives, exchange(): return lax.all_to_all(chunks, axes, 0, 0, tiled=False)  150 us
    ppermute x7, starting transfers between devices, swap(): return lax.ppermute(value, 'c', [(0, 1), (1, 0)])  30.5 us
    all_to_all x4, starting transfers between devices, exchange(): return lax.all_to_all(chunks, axes, 0, 0, tiled=False)  23.6 us
    all_to_all x4, waiting for transfers between devices, exchange(): return lax.all_to_all(chunks, axes, 0, 0, tiled=False)  20.2 us
    pallas_call x9, Pallas kernels, shards(): on_chip(next_pass, (sent_shape, v_shape) + last, 'next_pass')  9.6 us
    ppermute x7, waiting for transfers between devices, swap(): return lax.ppermute(value, 'c', [(0, 1), (1, 0)])  5.67 us
  transfers between devices with their start and end apart: 14, of which 10 were waited for; matrix products, arithmetic and copies ran while one was open for 1% of the time, Pallas kernels for 1%

profile of v16, /device:TPU:1, one launch (start us, length us, event | category | flops | bytes accessed | tf_op | source)
XLA Modules:
  0.0 259.8 jit_solution(14106667868706361992)
XLA Ops:
  2.9 3.3 %collective-permute-start = (f32[32,3,4,128]{3,2,1,0:T(4,128)S(1)}, f32[32,3,4,128]{3,2,1,0:T(4,128)S(1)}, u32[]{:S(2)}, u32[]{:S(2)}) collective-permute-start(f32[32,3,4,128]{3,2,1,0:T(4,128)S(1)} %get-tuple-element.65), channel_id=1, source_target_pairs={{0,4},{4,0},{1,5},{5,1},{2,6},{6,2},{3,7},{7,3},{8,12},{12,8},{9,1... | collective-permute-start | bytes 589832 | tf_op jit(solution)/shard_map/ppermute | solution.py:38
  8.0 9.6 %all-to-all-start = ((f32[32,3,4,128]{3,2,1,0:T(4,128)}), f32[32,3,4,128]{3,2,1,0:T(4,128)S(1)}, u32[]{:S(2)}, u32[]{:S(2)}) async-start(f32[32,3,4,128]{3,2,1,0:T(4,128)} %add.18), calls=%async_computation | async-start | bytes 393216 | tf_op jit(solution)/shard_map/all_to_all | solution.py:29
  22.5 4.5 %all-to-all-done.got_ref = f32[32,3,4,128]{3,2,1,0:T(4,128)S(1)} async-done(((f32[32,3,4,128]{3,2,1,0:T(4,128)}), f32[32,3,4,128]{3,2,1,0:T(4,128)S(1)}, u32[]{:S(2)}, u32[]{:S(2)}) %all-to-all-start) | async-done | bytes 196640 | tf_op jit(solution)/shard_map/all_to_all | solution.py:29
  27.7 4.0 %all-to-all-start.1 = ((f32[4,16,128]{2,1,0:T(8,128)}), f32[4,16,128]{2,1,0:T(8,128)S(1)}, u32[]{:S(2)}, u32[]{:S(2)}) async-start(f32[4,16,128]{2,1,0:T(8,128)} %chunk.1), calls=%async_computation.1 | async-start | bytes 65536 | tf_op jit(solution)/shard_map/all_to_all | solution.py:29
  31.7 3.2 %collective-permute-start.4 = (bf16[512,512]{1,0:T(8,128)(2,1)S(1)}, bf16[512,512]{1,0:T(8,128)(2,1)S(1)}, u32[]{:S(2)}, u32[]{:S(2)}) collective-permute-start(bf16[512,512]{1,0:T(8,128)(2,1)S(1)} %copy-done.2), channel_id=1, source_target_pairs={{0,4},{4,0},{1,5},{5,1},{2,6},{6,2},{3,7},{7,3},{8,12},{12,8},{9,1... | collective-permute-start | bytes 1572872 | tf_op jit(solution)/shard_map/ppermute | solution.py:38
  36.7 6.1 %all-to-all-start.2 = ((bf16[32,8,512]{2,1,0:T(8,128)(2,1)}), bf16[32,8,512]{2,1,0:T(8,128)(2,1)S(1)}, u32[]{:S(2)}, u32[]{:S(2)}) async-start(bf16[32,8,512]{2,1,0:T(8,128)(2,1)} %get-tuple-element.68), calls=%async_computation.2 | async-start | bytes 524288 | tf_op jit(solution)/shard_map/all_to_all | solution.py:29
  43.6 2.5 collective-permute-start.6
  47.2 5.3 %all-to-all-done.2 = bf16[32,8,512]{2,1,0:T(8,128)(2,1)S(1)} async-done(((bf16[32,8,512]{2,1,0:T(8,128)(2,1)}), bf16[32,8,512]{2,1,0:T(8,128)(2,1)S(1)}, u32[]{:S(2)}, u32[]{:S(2)}) %all-to-all-start.2) | async-done | bytes 262176 | tf_op jit(solution)/shard_map/all_to_all | solution.py:29
  52.5 4.5 %collective-permute-start.7 = (bf16[256,512]{1,0:T(8,128)(2,1)S(1)}, bf16[256,512]{1,0:T(8,128)(2,1)S(1)}, u32[]{:S(2)}, u32[]{:S(2)}) collective-permute-start(bf16[256,512]{1,0:T(8,128)(2,1)S(1)} %bitcast.27), channel_id=1, source_target_pairs={{0,4},{4,0},{1,5},{5,1},{2,6},{6,2},{3,7},{7,3},{8,12},{12,8},{9,1... | collective-permute-start | bytes 786440 | tf_op jit(solution)/shard_map/ppermute | solution.py:38
  59.6 14.3 %all_to_all.80.peak_ref = f32[64,3,1,128]{3,2,1,0:T(1,128)S(1)} all-to-all(f32[64,3,1,128]{3,2,1,0:T(1,128)S(1)} %get-tuple-element.78), channel_id=1, replica_groups=mesh['y'=4,'z'=8,'c'=2,'x'=4] {'y','z','c'}, dimensions={0} | all-to-all | bytes 196608 | tf_op jit(solution)/shard_map/all_to_all | solution.py:29
  78.1 12.3 %all_to_all.81.got_ref = bf16[32,8,128]{2,1,0:T(8,128)(2,1)S(1)} all-to-all(bf16[32,8,128]{2,1,0:T(8,128)(2,1)S(1)} %first_other.1), channel_id=1, replica_groups=mesh['y'=4,'z'=8,'c'=2,'x'=4] {'y','z'}, dimensions={0} | all-to-all | bytes 131072 | tf_op jit(solution)/shard_map/all_to_all | solution.py:29
  91.5 12.0 %all_to_all.82.got_ref = bf16[32,8,128]{2,1,0:T(8,128)(2,1)S(1)} all-to-all(bf16[32,8,128]{2,1,0:T(8,128)(2,1)S(1)} %get-tuple-element.84), channel_id=1, replica_groups=mesh['y'=4,'z'=8,'c'=2,'x'=4] {'y','z'}, dimensions={0} | all-to-all | bytes 131072 | tf_op jit(solution)/shard_map/all_to_all | solution.py:29
  104.6 12.0 %all_to_all.83.got_ref = bf16[32,8,128]{2,1,0:T(8,128)(2,1)S(1)} all-to-all(bf16[32,8,128]{2,1,0:T(8,128)(2,1)S(1)} %get-tuple-element.86), channel_id=1, replica_groups=mesh['y'=4,'z'=8,'c'=2,'x'=4] {'y','z'}, dimensions={0} | all-to-all | bytes 131072 | tf_op jit(solution)/shard_map/all_to_all | solution.py:29
  117.6 11.9 %all_to_all.84.got_ref = bf16[32,8,128]{2,1,0:T(8,128)(2,1)S(1)} all-to-all(bf16[32,8,128]{2,1,0:T(8,128)(2,1)S(1)} %get-tuple-element.88), channel_id=1, replica_groups=mesh['y'=4,'z'=8,'c'=2,'x'=4] {'y','z'}, dimensions={0} | all-to-all | bytes 131072 | tf_op jit(solution)/shard_map/all_to_all | solution.py:29
  130.6 11.8 %all_to_all.85.got_ref = bf16[32,8,128]{2,1,0:T(8,128)(2,1)S(1)} all-to-all(bf16[32,8,128]{2,1,0:T(8,128)(2,1)S(1)} %get-tuple-element.90), channel_id=1, replica_groups=mesh['y'=4,'z'=8,'c'=2,'x'=4] {'y','z'}, dimensions={0} | all-to-all | bytes 131072 | tf_op jit(solution)/shard_map/all_to_all | solution.py:29
  143.5 11.8 %all_to_all.86.got_ref = bf16[32,8,128]{2,1,0:T(8,128)(2,1)S(1)} all-to-all(bf16[32,8,128]{2,1,0:T(8,128)(2,1)S(1)} %get-tuple-element.92), channel_id=1, replica_groups=mesh['y'=4,'z'=8,'c'=2,'x'=4] {'y','z'}, dimensions={0} | all-to-all | bytes 131072 | tf_op jit(solution)/shard_map/all_to_all | solution.py:29
  156.4 11.8 %all_to_all.87.got_ref = bf16[32,8,128]{2,1,0:T(8,128)(2,1)S(1)} all-to-all(bf16[32,8,128]{2,1,0:T(8,128)(2,1)S(1)} %get-tuple-element.94), channel_id=1, replica_groups=mesh['y'=4,'z'=8,'c'=2,'x'=4] {'y','z'}, dimensions={0} | all-to-all | bytes 131072 | tf_op jit(solution)/shard_map/all_to_all | solution.py:29
  169.3 11.8 %all_to_all.88.got_ref = bf16[32,8,128]{2,1,0:T(8,128)(2,1)S(1)} all-to-all(bf16[32,8,128]{2,1,0:T(8,128)(2,1)S(1)} %get-tuple-element.96), channel_id=1, replica_groups=mesh['y'=4,'z'=8,'c'=2,'x'=4] {'y','z'}, dimensions={0} | all-to-all | bytes 131072 | tf_op jit(solution)/shard_map/all_to_all | solution.py:29
  182.2 11.9 %all_to_all.89.got_ref = bf16[32,8,128]{2,1,0:T(8,128)(2,1)S(1)} all-to-all(bf16[32,8,128]{2,1,0:T(8,128)(2,1)S(1)} %get-tuple-element.98), channel_id=1, replica_groups=mesh['y'=4,'z'=8,'c'=2,'x'=4] {'y','z'}, dimensions={0} | all-to-all | bytes 131072 | tf_op jit(solution)/shard_map/all_to_all | solution.py:29
  195.2 11.8 %all_to_all.90.got_ref = bf16[32,8,128]{2,1,0:T(8,128)(2,1)S(1)} all-to-all(bf16[32,8,128]{2,1,0:T(8,128)(2,1)S(1)} %get-tuple-element.100), channel_id=1, replica_groups=mesh['y'=4,'z'=8,'c'=2,'x'=4] {'y','z'}, dimensions={0} | all-to-all | bytes 131072 | tf_op jit(solution)/shard_map/all_to_all | solution.py:29
  208.7 3.9 %all-to-all-start.14 = ((f32[32,8,512]{2,1,0:T(8,128)}), f32[32,8,512]{2,1,0:T(8,128)S(1)}, u32[]{:S(2)}, u32[]{:S(2)}) async-start(f32[32,8,512]{2,1,0:T(8,128)} %bitcast.6), calls=%async_computation.14 | async-start | bytes 1048576 | tf_op jit(solution)/shard_map/all_to_all | solution.py:29
  214.9 9.3 %all-to-all-done.14 = f32[32,8,512]{2,1,0:T(8,128)S(1)} async-done(((f32[32,8,512]{2,1,0:T(8,128)}), f32[32,8,512]{2,1,0:T(8,128)S(1)}, u32[]{:S(2)}, u32[]{:S(2)}) %all-to-all-start.14) | async-done | bytes 524320 | tf_op jit(solution)/shard_map/all_to_all | solution.py:29
  224.3 16.9 %all_to_all.91 = bf16[32,8,512]{2,1,0:T(8,128)(2,1)S(1)} all-to-all(bf16[32,8,512]{2,1,0:T(8,128)(2,1)S(1)} %broadcast_in_dim.26), channel_id=1, replica_groups=mesh['y'=4,'z'=8,'c'=2,'x'=4] {'y','z'}, dimensions={0} | all-to-all | bytes 524288 | tf_op jit(solution)/shard_map/all_to_all | solution.py:29
  241.2 16.3 %collective-permute-start.9 = (bf16[256,512]{1,0:T(8,128)(2,1)S(1)}, bf16[256,512]{1,0:T(8,128)(2,1)S(1)}, u32[]{:S(2)}, u32[]{:S(2)}) collective-permute-start(bf16[256,512]{1,0:T(8,128)(2,1)S(1)} %bitcast.30), channel_id=1, source_target_pairs={{0,4},{4,0},{1,5},{5,1},{2,6},{6,2},{3,7},{7,3},{8,12},{12,8},{9,1... | collective-permute-start | bytes 786440 | tf_op jit(solution)/shard_map/ppermute | solution.py:38
  (65 shorter events, 36.0 us)
Async XLA Ops:
  2.9 4.4 %collective-permute-start = (f32[32,3,4,128]{3,2,1,0:T(4,128)S(1)}, f32[32,3,4,128]{3,2,1,0:T(4,128)S(1)}, u32[]{:S(2)}, u32[]{:S(2)}) collective-permute-start(f32[32,3,4,128]{3,2,1,0:T(4,128)S(1)} %get-tuple-element.65), channel_id=1, source_target_pairs={{0,4},{4,0},{1,5},{5,1},{2,6},{6,2},{3,7},{7,3},{8,12},{12,8},{9,1... | collective-permute-start | bytes 589832 | tf_op jit(solution)/shard_map/ppermute | solution.py:38
  7.3 24.4 %copy-start.2 = (bf16[512,512]{1,0:T(8,128)(2,1)S(1)}, bf16[512,512]{1,0:T(8,128)(2,1)}, u32[]{:S(2)}) copy-start(bf16[512,512]{1,0:T(8,128)(2,1)} %expr_ref.1) | copy-start | bytes 1572868
  8.0 9.6 %copy-start.3 = (bf16[2,512,128]{2,1,0:T(8,128)(2,1)S(1)}, bf16[2,512,128]{2,1,0:T(8,128)(2,1)}, u32[]{:S(2)}) copy-start(bf16[2,512,128]{2,1,0:T(8,128)(2,1)} %get-tuple-element.66.refs_0_) | copy-start | bytes 786436
  8.0 19.0 %all-to-all-start = ((f32[32,3,4,128]{3,2,1,0:T(4,128)}), f32[32,3,4,128]{3,2,1,0:T(4,128)S(1)}, u32[]{:S(2)}, u32[]{:S(2)}) async-start(f32[32,3,4,128]{3,2,1,0:T(4,128)} %add.18), calls=%async_computation | async-start | bytes 393216 | tf_op jit(solution)/shard_map/all_to_all | solution.py:29
  17.6 9.4 %copy-start.4 = (f32[128]{0:T(128)S(1)}, f32[128]{0:T(128)}, u32[]{:S(2)}) copy-start(f32[128]{0:T(128)} %param.12) | copy-start | bytes 1540
  17.7 17.3 %collective-permute-start.1 = (bf16[2,512,128]{2,1,0:T(8,128)(2,1)S(1)}, bf16[2,512,128]{2,1,0:T(8,128)(2,1)S(1)}, u32[]{:S(2)}, u32[]{:S(2)}) collective-permute-start(bf16[2,512,128]{2,1,0:T(8,128)(2,1)S(1)} %copy-done.3), channel_id=1, source_target_pairs={{0,1},{1,2},{2,3},{3,0},{4,5},{5,6},{6,7},{7,4},{8,9},{9,10},{10,1... | collective-permute-start | bytes 786440 | tf_op jit(solution)/shard_map/ppermute | solution.py:363
  18.9 16.0 %collective-permute-start.2 = (bf16[2,512,128]{2,1,0:T(8,128)(2,1)S(1)}, bf16[2,512,128]{2,1,0:T(8,128)(2,1)S(1)}, u32[]{:S(2)}, u32[]{:S(2)}) collective-permute-start(bf16[2,512,128]{2,1,0:T(8,128)(2,1)S(1)} %copy-done.3), channel_id=1, source_target_pairs={{0,2},{1,3},{2,0},{3,1},{4,6},{5,7},{6,4},{7,5},{8,10},{9,11},{10,... | collective-permute-start | bytes 786440 | tf_op jit(solution)/shard_map/ppermute | solution.py:363
  21.4 13.5 %collective-permute-start.3 = (bf16[2,512,128]{2,1,0:T(8,128)(2,1)S(1)}, bf16[2,512,128]{2,1,0:T(8,128)(2,1)S(1)}, u32[]{:S(2)}, u32[]{:S(2)}) collective-permute-start(bf16[2,512,128]{2,1,0:T(8,128)(2,1)S(1)} %copy-done.3), channel_id=1, source_target_pairs={{0,3},{1,0},{2,1},{3,2},{4,7},{5,4},{6,5},{7,6},{8,11},{9,8},{10,9... | collective-permute-start | bytes 786440 | tf_op jit(solution)/shard_map/ppermute | solution.py:363
  27.7 8.3 %all-to-all-start.1 = ((f32[4,16,128]{2,1,0:T(8,128)}), f32[4,16,128]{2,1,0:T(8,128)S(1)}, u32[]{:S(2)}, u32[]{:S(2)}) async-start(f32[4,16,128]{2,1,0:T(8,128)} %chunk.1), calls=%async_computation.1 | async-start | bytes 65536 | tf_op jit(solution)/shard_map/all_to_all | solution.py:29
  31.7 15.2 %collective-permute-start.4 = (bf16[512,512]{1,0:T(8,128)(2,1)S(1)}, bf16[512,512]{1,0:T(8,128)(2,1)S(1)}, u32[]{:S(2)}, u32[]{:S(2)}) collective-permute-start(bf16[512,512]{1,0:T(8,128)(2,1)S(1)} %copy-done.2), channel_id=1, source_target_pairs={{0,4},{4,0},{1,5},{5,1},{2,6},{6,2},{3,7},{7,3},{8,12},{12,8},{9,1... | collective-permute-start | bytes 1572872 | tf_op jit(solution)/shard_map/ppermute | solution.py:38
  36.0 6.9 %copy-start.8 = (f32[512]{0:T(512)S(1)}, f32[512]{0:T(512)}, u32[]{:S(2)}) copy-start(f32[512]{0:T(512)} %param.13) | copy-start | bytes 6148
  36.7 21.5 %copy-start = (bf16[512,256]{1,0:T(8,128)(2,1)S(1)}, bf16[512,256]{1,0:T(8,128)(2,1)}, u32[]{:S(2)}) copy-start(bf16[512,256]{1,0:T(8,128)(2,1)} %x_ref.1) | copy-start | bytes 786436
  36.7 21.5 %copy-start.1 = (bf16[512,256]{1,0:T(8,128)(2,1)S(1)}, bf16[512,256]{1,0:T(8,128)(2,1)}, u32[]{:S(2)}) copy-start(bf16[512,256]{1,0:T(8,128)(2,1)} %y_ref.1) | copy-start | bytes 786436
  36.7 15.8 %all-to-all-start.2 = ((bf16[32,8,512]{2,1,0:T(8,128)(2,1)}), bf16[32,8,512]{2,1,0:T(8,128)(2,1)S(1)}, u32[]{:S(2)}, u32[]{:S(2)}) async-start(bf16[32,8,512]{2,1,0:T(8,128)(2,1)} %get-tuple-element.68), calls=%async_computation.2 | async-start | bytes 524288 | tf_op jit(solution)/shard_map/all_to_all | solution.py:29
  42.9 0.7 copy-start.7
  43.6 3.4 %collective-permute-start.6 = (f32[2,512]{1,0:T(2,128)S(1)}, f32[2,512]{1,0:T(2,128)S(1)}, u32[]{:S(2)}, u32[]{:S(2)}) collective-permute-start(f32[2,512]{1,0:T(2,128)S(1)} %pad_maximum_fusion.mass_ref), channel_id=1, source_target_pairs={{0,4},{4,0},{1,5},{5,1},{2,6},{6,2},{3,7},{7,3},{8,12},{12,8},{9,1... | collective-permute-start | bytes 12296 | tf_op jit(solution)/shard_map/ppermute | solution.py:38
  46.1 1.2 collective-permute-start.5
  52.5 5.7 %collective-permute-start.7 = (bf16[256,512]{1,0:T(8,128)(2,1)S(1)}, bf16[256,512]{1,0:T(8,128)(2,1)S(1)}, u32[]{:S(2)}, u32[]{:S(2)}) collective-permute-start(bf16[256,512]{1,0:T(8,128)(2,1)S(1)} %bitcast.27), channel_id=1, source_target_pairs={{0,4},{4,0},{1,5},{5,1},{2,6},{6,2},{3,7},{7,3},{8,12},{12,8},{9,1... | collective-permute-start | bytes 786440 | tf_op jit(solution)/shard_map/ppermute | solution.py:38
  74.6 2.8 %collective-permute-start.8 = (bf16[1024,512]{1,0:T(8,128)(2,1)S(1)}, bf16[1024,512]{1,0:T(8,128)(2,1)S(1)}, u32[]{:S(2)}, u32[]{:S(2)}) collective-permute-start(bf16[1024,512]{1,0:T(8,128)(2,1)S(1)} %get-tuple-element.82.kern_ref.own_ref), channel_id=1, source_target_pairs={{0,4},{4,0},{1,5},{5,1},{2,6},{6,2},{3,7},{7,3},{8,12},{12,8},{9,1... | collective-permute-start | bytes 3145736 | tf_op jit(solution)/shard_map/ppermute | solution.py:38
  208.7 15.5 %all-to-all-start.14 = ((f32[32,8,512]{2,1,0:T(8,128)}), f32[32,8,512]{2,1,0:T(8,128)S(1)}, u32[]{:S(2)}, u32[]{:S(2)}) async-start(f32[32,8,512]{2,1,0:T(8,128)} %bitcast.6), calls=%async_computation.14 | async-start | bytes 1048576 | tf_op jit(solution)/shard_map/all_to_all | solution.py:29
  212.9 1.0 copy-start.5
  212.9 1.0 copy-start.6
  241.2 17.5 %collective-permute-start.9 = (bf16[256,512]{1,0:T(8,128)(2,1)S(1)}, bf16[256,512]{1,0:T(8,128)(2,1)S(1)}, u32[]{:S(2)}, u32[]{:S(2)}) collective-permute-start(bf16[256,512]{1,0:T(8,128)(2,1)S(1)} %bitcast.30), channel_id=1, source_target_pairs={{0,4},{4,0},{1,5},{5,1},{2,6},{6,2},{3,7},{7,3},{8,12},{12,8},{9,1... | collective-permute-start | bytes 786440 | tf_op jit(solution)/shard_map/ppermute | solution.py:38
